TPU v7x, 32 devices: a whole 2x2x4 slice. The times are simulated.
32 devices in a mesh: dp: 8 (over z, y), seq: 4 (over x, core).
Axes of the slice: x: 2, y: 2, z: 4, core: 2. Of those that a mesh axis runs over, the one named last changes fastest.
Arguments:
- tokens: bfloat16 [8, 4096, 1024], P('dp', 'seq'), may hold values from -6 to 6
- lengths: int32 [8, 8], P('dp'), may hold values from 1 to 2048, 3584 in all within a row
- cotangent: bfloat16 [8, 4096, 1024], P('dp', 'seq'), may hold values from -6 to 6
- norm_gain: float32 [1024], P(('dp', 'seq')), may hold values from 0.5 to 1.5
- norm_shift: float32 [1024], P(('dp', 'seq')), may hold values from -1.75 to 1.75
- value_weight: float32 [1024, 3072], P(('dp', 'seq')), may hold values from -0.1875 to 0.1875
- value_bias: float32 [3072], P(('dp', 'seq')), may hold values from -1.75 to 1.75
- reduce_weight: float32 [1024, 512], P(('dp', 'seq')), may hold values from -0.1875 to 0.1875
- reduce_bias: float32 [512], P(('dp', 'seq')), may hold values from -1.75 to 1.75
- decay_rates: float32 [512], P(('dp', 'seq')), may hold values from 6e-05 to 0.034
- skip_gain: float32 [512], P(('dp', 'seq')), may hold values from -6 to 6
- state_weight: float32 [512, 512], P(('dp', 'seq')), may hold values from -0.25 to 0.25
- expand_weight: float32 [512, 3072], P(('dp', 'seq')), may hold values from -0.25 to 0.25
- expand_bias: float32 [3072], P(('dp', 'seq')), may hold values from -1.75 to 1.75
- out_weight: float32 [3072, 1024], P(('dp', 'seq')), may hold values from -0.21875 to 0.21875
- out_bias: float32 [1024], P(('dp', 'seq')), may hold values from -1.75 to 1.75
Outputs:
- output: bfloat16 [8, 4096, 1024], P('dp', 'seq')
- grad_tokens: bfloat16 [8, 4096, 1024], P('dp', 'seq')
- grad_norm_gain: float32 [1024], P(('dp', 'seq'))
- grad_norm_shift: float32 [1024], P(('dp', 'seq'))
- grad_value_weight: float32 [1024, 3072], P(('dp', 'seq'))
- grad_value_bias: float32 [3072], P(('dp', 'seq'))
- grad_reduce_weight: float32 [1024, 512], P(('dp', 'seq'))
- grad_reduce_bias: float32 [512], P(('dp', 'seq'))
- grad_decay_rates: float32 [512], P(('dp', 'seq'))
- grad_skip_gain: float32 [512], P(('dp', 'seq'))
- grad_state_weight: float32 [512, 512], P(('dp', 'seq'))
- grad_expand_weight: float32 [512, 3072], P(('dp', 'seq'))
- grad_expand_bias: float32 [3072], P(('dp', 'seq'))
- grad_out_weight: float32 [3072, 1024], P(('dp', 'seq'))
- grad_out_bias: float32 [1024], P(('dp', 'seq'))
Inputs may be any that keep to these rules, and one draw needn't show every extreme that they name: Each row's 8 lengths sum to 3584 and the rest of the row is padding; the largest length of each row is 2048.
All inputs are finite; a program needn't handle non-finite values.
Results may differ from a plain program's by a relative error of at most 0.011.
Values may be sent and summed in bfloat16 or wider, within the bound.
No kernel may reach another device: no remote copies, remote signals or barrier semaphores. Data moves between devices by JAX's collectives and lax.ppermute only.
A program may use at most 192 MiB of HBM per device.

v0:
```python
import jax
import jax.numpy as jnp
from jax import lax
from jax.sharding import PartitionSpec as P

EPSILON = 1e-05


def carried_in(part, axis, combine, identity, reverse):
    count = lax.axis_size(axis)
    place = lax.axis_index(axis)
    ahead = count - 1 - place if reverse else place
    gathered = jax.tree.map(lambda a: lax.all_gather(a, axis), part)
    state = jax.tree.map(lambda a, e: jnp.zeros_like(a) + jnp.asarray(e, a.dtype), part, identity)

    def one(lap, state):
        source = count - 1 - lap if reverse else lap
        return combine(
            state, jax.tree.map(lambda a: lax.dynamic_index_in_dim(a, source, 0, False), gathered)
        )

    return lax.fori_loop(0, ahead, one, state)


def compose(earlier, latter):
    return (earlier[0] * latter[0], latter[0] * earlier[1] + latter[1])


def layer_norm(token_rows, scale, offset):
    center = token_rows - jnp.mean(token_rows, axis=-1, keepdims=True)
    inverse = lax.rsqrt(jnp.mean(center * center, axis=-1, keepdims=True) + EPSILON)
    return center * inverse * scale + offset


def decay_terms(rates):
    return (jnp.exp(-rates), jnp.sqrt(-jnp.expm1(-2.0 * rates)))


def row_flags(row_lengths, positions):
    doc_ends = jnp.cumsum(row_lengths, axis=-1)
    starts = jnp.any(positions[..., None] == doc_ends[..., None, :-1], axis=-1) | (positions == 0)
    live_mask = positions < doc_ends[..., -1:]
    return (starts, live_mask)


def column_sum(values):
    return jnp.sum(values.astype(jnp.float32), axis=0)


def on_device(
    tokens,
    lengths,
    cotangent,
    norm_gain,
    norm_shift,
    value_weight,
    value_bias,
    reduce_weight,
    reduce_bias,
    decay_rates,
    skip_gain,
    state_weight,
    expand_weight,
    expand_bias,
    out_weight,
    out_bias,
):
    half = jnp.bfloat16
    single = jnp.float32
    gathered = (
        lax.all_gather(norm_gain.astype(half), ("dp", "seq"), axis=0, tiled=True),
        lax.all_gather(norm_shift.astype(half), ("dp", "seq"), axis=0, tiled=True),
        lax.all_gather(value_weight.astype(half), ("dp", "seq"), axis=0, tiled=True),
        lax.all_gather(value_bias.astype(half), ("dp", "seq"), axis=0, tiled=True),
        lax.all_gather(reduce_weight.astype(half), ("dp", "seq"), axis=0, tiled=True),
        lax.all_gather(reduce_bias.astype(half), ("dp", "seq"), axis=0, tiled=True),
        lax.all_gather(decay_rates.astype(half), ("dp", "seq"), axis=0, tiled=True),
        lax.all_gather(skip_gain.astype(half), ("dp", "seq"), axis=0, tiled=True),
        lax.all_gather(state_weight.astype(half), ("dp", "seq"), axis=0, tiled=True),
        lax.all_gather(expand_weight.astype(half), ("dp", "seq"), axis=0, tiled=True),
        lax.all_gather(expand_bias.astype(half), ("dp", "seq"), axis=0, tiled=True),
        lax.all_gather(out_weight.astype(half), ("dp", "seq"), axis=0, tiled=True),
        lax.all_gather(out_bias.astype(half), ("dp", "seq"), axis=0, tiled=True),
    )
    norm_scale = gathered[0].astype(single)
    norm_offset = gathered[1].astype(single)
    value_mat = gathered[2]
    value_add = gathered[3].astype(single)
    reduce_mat = gathered[4]
    reduce_add = gathered[5].astype(single)
    rate_vec = gathered[6].astype(single)
    skip_vec = gathered[7].astype(single)
    state_mat = gathered[8]
    expand_mat = gathered[9]
    expand_add = gathered[10].astype(single)
    out_mat = gathered[11]
    out_add = gathered[12].astype(single)
    row_count, block, width = tokens.shape
    channels = state_mat.shape[0]
    positions = lax.axis_index("seq") * block + jnp.arange(block, dtype=jnp.int32)
    starts, live_mask = row_flags(lengths, positions[None, :])
    keep_flags = (1.0 - starts.astype(single))[..., None]
    live_rows = live_mask.astype(single).reshape(-1, 1)
    token_rows = tokens.reshape(row_count * block, width).astype(single)
    normed, norm_pull = jax.vjp(layer_norm, token_rows, norm_scale, norm_offset)
    normed_low = normed.astype(half)
    value_pre = jnp.dot(normed_low, value_mat, preferred_element_type=single) + value_add
    values_act, value_pull = jax.vjp(jax.nn.gelu, value_pre)
    reduce_pre = jnp.dot(normed_low, reduce_mat, preferred_element_type=single) + reduce_add
    reduced_act, reduce_pull = jax.vjp(jax.nn.gelu, reduce_pre)
    (decays, inflow), decay_pull = jax.vjp(decay_terms, rate_vec)
    retain = decays * keep_flags
    reduced_rows = reduced_act.reshape(row_count, block, channels)
    cumul, local_states = lax.associative_scan(compose, (retain, inflow * reduced_rows), axis=1)
    unit_map = (jnp.ones((row_count, channels), single), jnp.zeros((row_count, channels), single))
    carried = carried_in((cumul[:, -1], local_states[:, -1]), "seq", compose, unit_map, False)[1]
    states = local_states + cumul * carried[:, None, :]
    states_low = states.reshape(-1, channels).astype(half)
    ssm_out = jnp.dot(states_low, state_mat, preferred_element_type=single) + skip_vec * reduced_act
    ssm_low = ssm_out.astype(half)
    expand_pre = jnp.dot(ssm_low, expand_mat, preferred_element_type=single) + expand_add
    gated_low = (values_act * expand_pre).astype(half)
    branch = jnp.dot(gated_low, out_mat, preferred_element_type=single) + out_add
    output = (token_rows + live_rows * branch).astype(half).reshape(tokens.shape)
    regathered = (
        lax.all_gather(norm_gain.astype(half), ("dp", "seq"), axis=0, tiled=True),
        lax.all_gather(norm_shift.astype(half), ("dp", "seq"), axis=0, tiled=True),
        lax.all_gather(value_weight.astype(half), ("dp", "seq"), axis=0, tiled=True),
        lax.all_gather(value_bias.astype(half), ("dp", "seq"), axis=0, tiled=True),
        lax.all_gather(reduce_weight.astype(half), ("dp", "seq"), axis=0, tiled=True),
        lax.all_gather(reduce_bias.astype(half), ("dp", "seq"), axis=0, tiled=True),
        lax.all_gather(decay_rates.astype(half), ("dp", "seq"), axis=0, tiled=True),
        lax.all_gather(skip_gain.astype(half), ("dp", "seq"), axis=0, tiled=True),
        lax.all_gather(state_weight.astype(half), ("dp", "seq"), axis=0, tiled=True),
        lax.all_gather(expand_weight.astype(half), ("dp", "seq"), axis=0, tiled=True),
        lax.all_gather(expand_bias.astype(half), ("dp", "seq"), axis=0, tiled=True),
        lax.all_gather(out_weight.astype(half), ("dp", "seq"), axis=0, tiled=True),
        lax.all_gather(out_bias.astype(half), ("dp", "seq"), axis=0, tiled=True),
    )
    value_mat = regathered[2]
    reduce_mat = regathered[4]
    state_mat = regathered[8]
    expand_mat = regathered[9]
    out_mat = regathered[11]
    cot_rows = cotangent.reshape(-1, width).astype(single)
    branch_grad = (live_rows * cot_rows).astype(half)
    grad_out_add = column_sum(branch_grad)
    grad_out_mat = jnp.einsum("tg,td->gd", gated_low, branch_grad, preferred_element_type=single)
    gated_grad = jnp.einsum("td,gd->tg", branch_grad, out_mat, preferred_element_type=single)
    expand_grad = (gated_grad * values_act).astype(half)
    value_grad = gated_grad * expand_pre
    grad_expand_add = column_sum(expand_grad)
    grad_expand_mat = jnp.einsum("tr,tg->rg", ssm_low, expand_grad, preferred_element_type=single)
    ssm_grad = jnp.einsum(
        "tg,rg->tr", expand_grad, expand_mat, preferred_element_type=single
    ).astype(half)
    grad_skip = jnp.sum(ssm_grad.astype(single) * reduced_act, axis=0)
    grad_state_mat = jnp.einsum("tr,ts->rs", states_low, ssm_grad, preferred_element_type=single)
    state_grad = jnp.einsum(
        "ts,rs->tr", ssm_grad, state_mat, preferred_element_type=single
    ).reshape(row_count, block, channels)
    suffix, local_flow = lax.associative_scan(
        compose, (retain, retain * state_grad), reverse=True, axis=1
    )
    flow_in = carried_in((suffix[:, 0], local_flow[:, 0]), "seq", compose, unit_map, True)[1]
    flows = local_flow + suffix * flow_in[:, None, :]
    total_grad = state_grad + jnp.concatenate([flows[:, 1:], flow_in[:, None, :]], axis=1)
    prev_states = jnp.concatenate([carried[:, None, :], states[:, :-1]], axis=1)
    grad_decays = jnp.sum(total_grad * keep_flags * prev_states, axis=(0, 1))
    grad_inflow = jnp.sum(total_grad * reduced_rows, axis=(0, 1))
    grad_rates = decay_pull((grad_decays, grad_inflow))[0]
    reduced_grad = ssm_grad.astype(single) * skip_vec + (inflow * total_grad).reshape(-1, channels)
    reduce_low = reduce_pull(reduced_grad)[0].astype(half)
    value_low = value_pull(value_grad)[0].astype(half)
    grad_value_add = column_sum(value_low)
    grad_reduce_add = column_sum(reduce_low)
    grad_value_mat = jnp.einsum("td,tg->dg", normed_low, value_low, preferred_element_type=single)
    grad_reduce_mat = jnp.einsum("td,tr->dr", normed_low, reduce_low, preferred_element_type=single)
    normed_grad = jnp.einsum(
        "tg,dg->td", value_low, value_mat, preferred_element_type=single
    ) + jnp.einsum("tr,dr->td", reduce_low, reduce_mat, preferred_element_type=single)
    token_grad, grad_scale, grad_offset = norm_pull(normed_grad)
    grad_tokens = (cot_rows + token_grad).astype(half).reshape(tokens.shape)
    head_sums = (
        lax.psum_scatter(grad_out_mat, ("dp", "seq"), scatter_dimension=0, tiled=True),
        lax.psum_scatter(grad_out_add, ("dp", "seq"), scatter_dimension=0, tiled=True),
    )
    middle_sums = (
        lax.psum_scatter(grad_expand_mat, ("dp", "seq"), scatter_dimension=0, tiled=True),
        lax.psum_scatter(grad_expand_add, ("dp", "seq"), scatter_dimension=0, tiled=True),
        lax.psum_scatter(grad_state_mat, ("dp", "seq"), scatter_dimension=0, tiled=True),
        lax.psum_scatter(grad_rates, ("dp", "seq"), scatter_dimension=0, tiled=True),
        lax.psum_scatter(grad_skip, ("dp", "seq"), scatter_dimension=0, tiled=True),
    )
    tail_sums = (
        lax.psum_scatter(grad_value_mat, ("dp", "seq"), scatter_dimension=0, tiled=True),
        lax.psum_scatter(grad_value_add, ("dp", "seq"), scatter_dimension=0, tiled=True),
        lax.psum_scatter(grad_reduce_mat, ("dp", "seq"), scatter_dimension=0, tiled=True),
        lax.psum_scatter(grad_reduce_add, ("dp", "seq"), scatter_dimension=0, tiled=True),
        lax.psum_scatter(grad_scale, ("dp", "seq"), scatter_dimension=0, tiled=True),
        lax.psum_scatter(grad_offset, ("dp", "seq"), scatter_dimension=0, tiled=True),
    )
    return (
        output,
        grad_tokens,
        tail_sums[4],
        tail_sums[5],
        tail_sums[0],
        tail_sums[1],
        tail_sums[2],
        tail_sums[3],
        middle_sums[3],
        middle_sums[4],
        middle_sums[2],
        middle_sums[0],
        middle_sums[1],
        head_sums[0],
        head_sums[1],
    )


def solution(mesh):
    return jax.shard_map(
        on_device,
        mesh=mesh,
        in_specs=(
            P("dp", "seq", None),
            P("dp", None),
            P("dp", "seq", None),
            P(("dp", "seq")),
            P(("dp", "seq")),
            P(("dp", "seq"), None),
            P(("dp", "seq")),
            P(("dp", "seq"), None),
            P(("dp", "seq")),
            P(("dp", "seq")),
            P(("dp", "seq")),
            P(("dp", "seq"), None),
            P(("dp", "seq"), None),
            P(("dp", "seq")),
            P(("dp", "seq"), None),
            P(("dp", "seq")),
        ),
        out_specs=(
            P("dp", "seq", None),
            P("dp", "seq", None),
            P(("dp", "seq")),
            P(("dp", "seq")),
            P(("dp", "seq"), None),
            P(("dp", "seq")),
            P(("dp", "seq"), None),
            P(("dp", "seq")),
            P(("dp", "seq")),
            P(("dp", "seq")),
            P(("dp", "seq"), None),
            P(("dp", "seq"), None),
            P(("dp", "seq")),
            P(("dp", "seq"), None),
            P(("dp", "seq")),
        ),
        check_vma=False,
    )
```

profile of v0, /device:TPU:0, one launch (start us, length us, event | category | flops | bytes accessed | tf_op | source)
XLA Modules:
  0.0 1442.0 jit_solution(10074119750575866104)
XLA Ops:
  16.0 42.5 %all-reduce.97 = (bf16[1024]{0:T(1024)(128)(2,1)}, bf16[512]{0:T(512)(128)(2,1)S(1)}, bf16[512]{0:T(512)(128)(2,1)S(1)}, bf16[1024]{0:T(1024)(128)(2,1)S(1)}, bf...) all-reduce(bf16[1024]{0:T(1024)(128)(2,1)S(1)} %dynamic-update-slic, ...), channel_id=1, replica_groups=mesh['dp'=8,'seq'=4] {'dp','seq'}, use_global_device_ids=true, to_apply=%add.87 | all-reduce | flops 10752 | bytes 43008
  65.0 6.5 slice.625
  73.4 6.3 slice.721
  81.4 46.0 %all_gather.65 = bf16[512,512]{1,0:T(8,128)(2,1)} all-gather(bf16[16,512]{1,0:T(8,128)(2,1)S(1)} %convert_element_type.169), channel_id=1, replica_groups=mesh['dp'=8,'seq'=4] {'dp','seq'}, dimensions={0}, use_global_device_ids=true | all-gather | bytes 540672 | tf_op jit(solution)/shard_map/all_gather | solution.py:79
  129.8 8.9 slice.723
  138.7 5.3 slice.729
  143.9 9.1 slice.722
  159.0 6.3 slice.627
  165.3 6.3 slice.628
  171.5 3.7 multiply_add_fusion.2
  175.2 3.8 slice.633
  179.0 3.7 slice.634
  270.0 3.8 slice.696
  275.8 6.4 slice.698
  303.2 4.6 pad.261
  310.2 8.7 pad.263
  320.8 4.6 pad.280
  325.4 4.6 pad.281
  337.3 8.7 pad.262
  346.1 4.7 pad.283
  352.2 4.7 pad.282
  357.6 5.1 all_gather.64
  363.5 5.7 all_gather.63
  369.2 4.5 multiply_add_fusion
  378.2 8.6 fusion.94
  386.9 12.8 fusion.85
  399.7 26.4 %convert_reduce_fusion = (f32[3072]{0:T(1024)}, bf16[1024,3072]{1,0:T(8,128)(2,1)S(1)}, bf16[1024,3072]{1,0:T(8,128)(2,1)}, f32[3072]{0:T(1024)}, bf16[1024,3072]{1,0:T(8,128)(2,1)}) fusion(f32[1024,3072]{1,0:T(8,128)} %fusion.85, f32[3072]{0:T(1024)S(1)} %copy-done.86, f32[1024,3072]{1,0:T(8,128)} %fusion.94, f32[3072]{0:T(1024)S(1)} %copy-done.87, ...), kind=kOutput, calls=%fused_computation.13 | convolution fusion | flops 6546253824 | bytes 52482048 | tf_op jit(solution)/shard_map/td,gd->tg/dot_general | solution.py:149
  426.1 7.6 convolution_convert_fusion
  437.5 6.2 slice.724
  443.7 6.2 slice.726
  449.9 8.9 slice.725
  458.9 8.9 slice.727
  467.7 4.0 multiply_add_fusion.1
  471.8 3.7 slice.732
  475.4 3.6 slice.733
  479.1 3.7 slice.731
  482.7 3.7 slice.735
  574.7 3.7 slice.730
  578.4 3.7 slice.795
  584.7 6.2 slice.797
  595.8 9.2 slice.798
  650.2 4.6 pad.300
  654.8 4.7 pad.301
  659.5 4.6 pad.321
  666.0 4.7 pad.320
  678.9 8.7 pad.302
  687.6 8.7 pad.303
  697.1 5.1 all_gather.72
  704.6 8.7 pad.322
  713.2 8.6 pad.323
  722.6 5.1 all_gather.71
  728.0 4.2 add.666
  734.1 16.7 %rev.9 = f32[1,1024,512]{2,1,0:T(8,128)} reverse(f32[1,1024,512]{2,1,0:T(8,128)} %add.666), dimensions={1} | reverse | bytes 4194304 | tf_op jit(solution)/shard_map/rev | solution.py:162
  750.8 16.6 %rev.8 = f32[1,1024,512]{2,1,0:T(8,128)} reverse(f32[1,1024,512]{2,1,0:T(8,128)} %add.656), dimensions={1} | reverse | bytes 4194304 | tf_op jit(solution)/shard_map/rev | solution.py:162
  781.5 8.1 fusion.97
  789.7 13.3 fusion.81
  803.7 12.4 fusion.74
  816.8 10.8 fusion.95
  834.8 38.0 %all-reduce.96 = (f32[1024]{0:T(1024)S(1)}, f32[1024]{0:T(1024)S(1)}, f32[3072]{0:T(1024)S(1)}, f32[512]{0:T(512)S(1)}, f32[512]{0:T(512)S(1)}, /*index=5*/f32[5...) all-reduce(f32[1024]{0:T(1024)S(1)} %get-tuple-element.145, ...), channel_id=2, replica_groups=mesh['dp'=8,'seq'=4] {'dp','seq'}, use_global_device_ids=true, to_apply=%region_11.12.clone | all-reduce | flops 10752 | bytes 86016
  877.5 11.7 fusion.33
  889.2 105.2 %reduce-scatter.8.cloned.1.call-done = f32[32,512]{1,0:T(8,128)} async-done(((f32[1024,512]{1,0:T(8,128)}), f32[32,512]{1,0:T(8,128)}) %reduce-scatter.8.cloned.1.call-update) | async-done | bytes 65552 | tf_op jit(solution)/shard_map/reduce_scatter | solution.py:198
  994.4 116.7 %reduce-scatter.12.cloned.1.call-done = f32[16,3072]{1,0:T(8,128)} async-done(((f32[512,3072]{1,0:T(8,128)}), f32[16,3072]{1,0:T(8,128)}) %reduce-scatter.12.cloned.1.call-update) | async-done | bytes 196624 | tf_op jit(solution)/shard_map/reduce_scatter | solution.py:189
  1111.1 162.7 %reduce-scatter.6.cloned.1.call-done = f32[32,3072]{1,0:T(8,128)} async-done(((f32[1024,3072]{1,0:T(8,128)}), f32[32,3072]{1,0:T(8,128)}) %reduce-scatter.6.cloned.1.call-update) | async-done | bytes 393232 | tf_op jit(solution)/shard_map/reduce_scatter | solution.py:196
  1273.8 161.5 %reduce-scatter.14.cloned.1.call-done = f32[96,1024]{1,0:T(8,128)} async-done(((f32[3072,1024]{1,0:T(8,128)}), f32[96,1024]{1,0:T(8,128)}) %reduce-scatter.14.cloned.1.call-update) | async-done | bytes 393232 | tf_op jit(solution)/shard_map/reduce_scatter | solution.py:185
  (654 shorter events, 342.8 us)
Async XLA Ops:
  7.3 51.8 %copy-start.132 = (s32[1,8]{1,0:T(1,128)S(1)}, s32[1,8]{1,0:T(1,128)}, u32[]{:S(2)}) copy-start(s32[1,8]{1,0:T(1,128)} %param.21) | copy-start | bytes 100
  7.3 145.8 %all-gather.7.cloned.1.call-start = ((), (), s32[]{:S(2)}) async-start(), calls=%async_computation.6 | async-start | bytes 1081344 | tf_op jit(solution)/shard_map/all_gather | solution.py:75
  8.8 369.4 %all-gather.9.cloned.1.call-start = ((), (), s32[]{:S(2)}) async-start(), calls=%async_computation.7 | async-start | bytes 3244032 | tf_op jit(solution)/shard_map/all_gather | solution.py:80
  10.5 376.4 %all-gather.5.cloned.1.call-start = ((), (), s32[]{:S(2)}) async-start(), calls=%async_computation.5 | async-start | bytes 6488064 | tf_op jit(solution)/shard_map/all_gather | solution.py:73
  12.2 387.5 %all-gather.11.cloned.1.call-start = ((), (), s32[]{:S(2)}) async-start(), calls=%async_computation.8 | async-start | bytes 6488064 | tf_op jit(solution)/shard_map/all_gather | solution.py:82
  14.0 875.2 %reduce-scatter.10.cloned.1.call-start = ((), (), s32[]{:S(2)}) async-start(), calls=%async_computation.11 | async-start | bytes 1081344 | tf_op jit(solution)/shard_map/reduce_scatter | solution.py:191
  58.5 97.1 %copy-start.74 = (f32[512]{0:T(512)}, f32[512]{0:T(512)S(1)}, u32[]{:S(2)}) copy-start(f32[512]{0:T(512)S(1)} %get-tuple-element.287) | copy-start | bytes 6148
  65.0 14.7 %copy-start = (bf16[1,1024,1024]{2,1,0:T(8,128)(2,1)S(1)}, bf16[1,1024,1024]{2,1,0:T(8,128)(2,1)}, u32[]{:S(2)}) copy-start(bf16[1,1024,1024]{2,1,0:T(8,128)(2,1)} %param.20) | copy-start | bytes 6291460
  79.6 73.4 %copy-start.52 = (f32[1024]{0:T(1024)}, f32[1024]{0:T(1024)S(1)}, u32[]{:S(2)}) copy-start(f32[1024]{0:T(1024)S(1)} %convert_element_type.154) | copy-start | bytes 12292
  79.7 73.4 %copy-start.120 = (f32[1024]{0:T(1024)}, f32[1024]{0:T(1024)S(1)}, u32[]{:S(2)}) copy-start(f32[1024]{0:T(1024)S(1)} %convert_element_type.156) | copy-start | bytes 12292
  80.0 73.0 %copy-start.50 = (f32[1024]{0:T(1024)}, f32[1024]{0:T(1024)S(1)}, u32[]{:S(2)}) copy-start(f32[1024]{0:T(1024)S(1)} %broadcast_multiply_fusion.1) | copy-start | bytes 12292
  80.7 46.6 %copy-start.64 = (f32[1024]{0:T(1024)}, f32[1024]{0:T(1024)S(1)}, u32[]{:S(2)}) copy-start(f32[1024]{0:T(1024)S(1)} %fusion.18) | copy-start | bytes 12292
  80.7 72.3 %copy-start.61 = (f32[1024]{0:T(1024)}, f32[1024]{0:T(1024)S(1)}, u32[]{:S(2)}) copy-start(f32[1024]{0:T(1024)S(1)} %fusion.57) | copy-start | bytes 12292
  80.8 74.9 %copy-start.71 = (f32[512]{0:T(512)}, f32[512]{0:T(512)S(1)}, u32[]{:S(2)}) copy-start(f32[512]{0:T(512)S(1)} %convert_element_type.165) | copy-start | bytes 6148
  267.9 15.5 %copy-start.82 = (f32[1,2,512]{2,1,0:T(2,128)S(1)}, f32[1,2,512]{2,1,0:T(2,128)}, u32[]{:S(2)}) copy-start(f32[1,2,512]{2,1,0:T(2,128)} %slice.675) | copy-start | bytes 12292
  267.9 15.5 %copy-start.83 = (f32[1,2,512]{2,1,0:T(2,128)S(1)}, f32[1,2,512]{2,1,0:T(2,128)}, u32[]{:S(2)}) copy-start(f32[1,2,512]{2,1,0:T(2,128)} %slice.676) | copy-start | bytes 12292
  267.9 15.5 %copy-start.84 = (f32[1,2,512]{2,1,0:T(2,128)S(1)}, f32[1,2,512]{2,1,0:T(2,128)}, u32[]{:S(2)}) copy-start(f32[1,2,512]{2,1,0:T(2,128)} %slice.674) | copy-start | bytes 12292
  267.9 15.5 %copy-start.85 = (f32[1,2,512]{2,1,0:T(2,128)S(1)}, f32[1,2,512]{2,1,0:T(2,128)}, u32[]{:S(2)}) copy-start(f32[1,2,512]{2,1,0:T(2,128)} %slice.678) | copy-start | bytes 12292
  267.9 15.6 %copy-start.59 = (f32[1,4,512]{2,1,0:T(4,128)S(1)}, f32[1,4,512]{2,1,0:T(4,128)}, u32[]{:S(2)}) copy-start(f32[1,4,512]{2,1,0:T(4,128)} %get-tuple-element.273) | copy-start | bytes 24580
  267.9 15.6 %copy-start.60 = (f32[1,4,512]{2,1,0:T(4,128)S(1)}, f32[1,4,512]{2,1,0:T(4,128)}, u32[]{:S(2)}) copy-start(f32[1,4,512]{2,1,0:T(4,128)} %get-tuple-element.274) | copy-start | bytes 24580
  267.9 15.7 %copy-start.67 = (f32[1,3,512]{2,1,0:T(4,128)S(1)}, f32[1,3,512]{2,1,0:T(4,128)}, u32[]{:S(2)}) copy-start(f32[1,3,512]{2,1,0:T(4,128)} %slice.667) | copy-start | bytes 18436
  267.9 15.7 %copy-start.68 = (f32[1,3,512]{2,1,0:T(4,128)S(1)}, f32[1,3,512]{2,1,0:T(4,128)}, u32[]{:S(2)}) copy-start(f32[1,3,512]{2,1,0:T(4,128)} %slice.684) | copy-start | bytes 18436
  267.9 15.8 %copy-start.109 = (f32[1,1,512]{2,1,0:T(1,128)S(1)}, f32[1,1,512]{2,1,0:T(1,128)}, u32[]{:S(2)}) copy-start(f32[1,1,512]{2,1,0:T(1,128)} %slice.861) | copy-start | bytes 6148
  267.9 15.8 %copy-start.108 = (f32[1,1,512]{2,1,0:T(1,128)S(1)}, f32[1,1,512]{2,1,0:T(1,128)}, u32[]{:S(2)}) copy-start(f32[1,1,512]{2,1,0:T(1,128)} %slice.829) | copy-start | bytes 6148
  270.0 13.8 copy-start.56
  270.0 15.3 %copy-start.46 = (f32[1,15,512]{2,1,0:T(8,128)S(1)}, f32[1,15,512]{2,1,0:T(8,128)}, u32[]{:S(2)}) copy-start(f32[1,15,512]{2,1,0:T(8,128)} %slice.655) | copy-start | bytes 92164
  270.0 15.3 %copy-start.47 = (f32[1,15,512]{2,1,0:T(8,128)S(1)}, f32[1,15,512]{2,1,0:T(8,128)}, u32[]{:S(2)}) copy-start(f32[1,15,512]{2,1,0:T(8,128)} %slice.688) | copy-start | bytes 92164
  275.8 11.1 copy-start.43
  275.8 11.1 copy-start.44
  275.8 11.1 copy-start.105
  337.3 8.7 copy-start.26
  378.2 8.7 copy-start.51
  378.2 8.7 copy-start.53
  378.2 8.7 copy-start.62
  378.2 8.7 copy-start.121
  386.9 12.8 copy-start.78
  386.9 12.8 copy-start.86
  386.9 12.8 copy-start.87
  595.6 9.3 copy-start.116
  595.6 9.3 copy-start.117
  595.6 9.3 copy-start.80
  595.6 9.4 copy-start.114
  595.6 9.4 copy-start.115
  595.6 9.4 copy-start.81
  595.7 9.5 copy-start.69
  595.7 9.5 copy-start.70
  595.7 9.5 copy-start.113
  595.7 9.5 copy-start.112
  595.7 9.6 copy-start.57
  595.7 9.6 copy-start.58
  595.7 9.6 copy-start.111
  595.7 9.7 copy-start.110
  595.7 9.7 copy-start.48
  595.7 9.7 copy-start.49
  595.8 11.9 copy-start.45
  631.7 10.3 copy-start.39
  650.2 14.0 copy-start.97
  687.6 14.6 %copy-start.106 = (f32[1,1,512]{2,1,0:T(1,128)S(1)}, f32[1,1,512]{2,1,0:T(1,128)}, u32[]{:S(2)}) copy-start(f32[1,1,512]{2,1,0:T(1,128)} %get-tuple-element.201) | copy-start | bytes 6148
  727.8 266.7 %reduce-scatter.8.cloned.1.call-start = ((), (), s32[]{:S(2)}) async-start(), calls=%async_computation.10 | async-start | bytes 2162688 | tf_op jit(solution)/shard_map/reduce_scatter | solution.py:198
  780.3 330.8 %reduce-scatter.12.cloned.1.call-start = ((), (), s32[]{:S(2)}) async-start(), calls=%async_computation.12 | async-start | bytes 6488064 | tf_op jit(solution)/shard_map/reduce_scatter | solution.py:189
  789.7 484.1 %reduce-scatter.6.cloned.1.call-start = ((), (), s32[]{:S(2)}) async-start(), calls=%async_computation.9 | async-start | bytes 12976128 | tf_op jit(solution)/shard_map/reduce_scatter | solution.py:196
  803.0 632.3 %reduce-scatter.14.cloned.1.call-start = ((), (), s32[]{:S(2)}) async-start(), calls=%async_computation.13 | async-start | bytes 12976128 | tf_op jit(solution)/shard_map/reduce_scatter | solution.py:185
  816.8 10.9 copy-start.28
  816.8 10.9 copy-start.38
  (78 other events, 277.8 us)
Sparse Core Ops, SparseCore 0:
  11.5 56.3 all-gather.6
  70.8 58.5 all-gather.8
  132.9 68.7 all-gather.4
  204.4 68.0 all-gather.10
  727.9 130.9 reduce-scatter.9
  861.6 132.7 reduce-scatter.7
  1000.6 110.4 reduce-scatter.11
  1118.8 154.9 reduce-scatter.5
  1280.4 154.8 reduce-scatter.13
where the time goes:
time: 1460 us; the launch traced here: 1440 us
  waiting for transfers between devices  546 us (37%)
  local copies, waits for them, and re-layouts  468 us (32%)
  blocking collectives  148 us (10%)
  other arithmetic  139 us (10%)
  matrix products  124 us (8%)
  between operations  16.2 us (1%)
    slice x72, local copies, waits for them, and re-layouts, on_device(): lax.associative_scan(compose, (retain, retain * state_grad), reverse=True...  175 us
    reduce_scatter x1, waiting for transfers between devices, on_device(): lax.psum_scatter(grad_value_mat, ('dp', 'seq'), scatter_dimension=0, tile...  163 us
    reduce_scatter x1, waiting for transfers between devices, on_device(): lax.psum_scatter(grad_out_mat, ('dp', 'seq'), scatter_dimension=0, tiled=...  162 us
    slice x67, local copies, waits for them, and re-layouts, on_device(): lax.associative_scan(compose, (retain, inflow * reduced_rows), axis=1)  119 us
    reduce_scatter x1, waiting for transfers between devices, on_device(): lax.psum_scatter(grad_expand_mat, ('dp', 'seq'), scatter_dimension=0, til...  117 us
    reduce_scatter x1, waiting for transfers between devices, on_device(): lax.psum_scatter(grad_reduce_mat, ('dp', 'seq'), scatter_dimension=0, til...  105 us
    unnamed x2, blocking collectives  80.5 us
    pad x36, local copies, waits for them, and re-layouts, on_device(): lax.associative_scan(compose, (retain, retain * state_grad), reverse=True...  72.4 us
  transfers between devices with their start and end apart: 9, of which 4 were waited for; matrix products, arithmetic and copies ran while one was open for 28% of the time, Pallas kernels for 0%

commit v1 on v0

v1 whole, which is shorter than its diff:
```python
import jax
import jax.numpy as jnp
from jax import lax
from jax.experimental import pallas as pl
from jax.experimental.pallas import tpu as pltpu
from jax.sharding import PartitionSpec as P

EPSILON = 1e-05
HALF = jnp.bfloat16
SINGLE = jnp.float32
MAIN = 5
SEGMENTS = 8
MIB = 1 << 20


def log2(n):
    return n.bit_length() - 1


def device_number():
    return lax.axis_index("dp") * lax.axis_size("seq") + lax.axis_index("seq")


def low_bits():
    return log2(lax.axis_size("dp") * lax.axis_size("seq")) - MAIN


def exchange(values, bit):
    inner = log2(lax.axis_size("seq"))
    axis, place = ("seq", bit) if bit < inner else ("dp", bit - inner)
    count = lax.axis_size(axis)
    return lax.ppermute(values, axis, [(i, i ^ (1 << place)) for i in range(count)])


def gather_low(values):
    for bit in range(low_bits()):
        other = exchange(values, bit)
        upper = (device_number() >> bit) & 1
        values = jnp.where(
            upper == 1, jnp.concatenate([other, values]), jnp.concatenate([values, other])
        )
    return values


def reduce_low(values):
    for bit in reversed(range(low_bits())):
        upper = (device_number() >> bit) & 1
        halves = values.reshape((2, values.shape[0] // 2) + values.shape[1:])
        mine = lax.dynamic_index_in_dim(halves, upper, 0, False)
        theirs = lax.dynamic_index_in_dim(halves, 1 - upper, 0, False)
        values = mine + exchange(theirs, bit)
    return values


def join(own, other):
    return jnp.concatenate([own, other])


def gather_chunk(rows, split):
    base = low_bits()
    core, bit_x, bit_y, bit_z, bit_far = (base + i for i in range(MAIN))
    held = rows[None]
    held = join(held, exchange(held, bit_far))
    held = join(held, exchange(held, bit_z))
    first, second = held[:, :split], held[:, split:]
    parts = []
    if split:
        from_y = exchange(first, bit_y)
        from_x = exchange(second, bit_x)
        first, second = join(first, from_y), join(second, from_x)
        from_x = exchange(first, bit_x)
        from_y = exchange(second, bit_y)
        first, second = join(first, from_x), join(second, from_y)
        parts = [first, exchange(first, core), second, exchange(second, core)]
    else:
        second = join(second, exchange(second, bit_y))
        second = join(second, exchange(second, bit_x))
        parts = [second, exchange(second, core)]
    return parts


def spot(rel, x_first):
    core = rel & 1
    bit_x, bit_y = (rel >> 1) & 1, (rel >> 2) & 1
    bit_z, bit_far = (rel >> 3) & 1, (rel >> 4) & 1
    if x_first:
        return core, bit_x * 8 + bit_y * 4 + bit_z * 2 + bit_far
    return core, bit_y * 8 + bit_x * 4 + bit_z * 2 + bit_far


def place_weights(parts, pieces, shapes, me):
    width = parts[0].shape[-1]
    pairs = len(parts) // 2

    def body(me_ref, *refs):
        ins, outs, sems = refs[: 2 * pairs], refs[2 * pairs : -1], refs[-1]
        mine = me_ref[0]

        def one(shard, carry):
            rel = shard ^ mine
            for which, row, rows, out, held, to_row, to_col in pieces:
                core, k = spot(rel, which == 0)
                target = outs[out].at[
                    pl.ds(pl.multiple_of(shard * held + to_row, 8), rows), pl.ds(to_col, width)
                ]

                @pl.when(core == 0)
                def _():
                    pltpu.make_async_copy(
                        ins[2 * which].at[k, pl.ds(row, rows)], target, sems.at[out]
                    ).start()

                @pl.when(core == 1)
                def _():
                    pltpu.make_async_copy(
                        ins[2 * which + 1].at[k, pl.ds(row, rows)], target, sems.at[out]
                    ).start()

            return carry

        lax.fori_loop(0, 1 << MAIN, one, 0)
        for i, out in enumerate(outs):
            pltpu.make_async_copy(out, out, sems.at[i]).wait()

    return pl.pallas_call(
        body,
        out_shape=[jax.ShapeDtypeStruct(s, HALF) for s in shapes],
        in_specs=[pl.BlockSpec(memory_space=pltpu.SMEM)]
        + [pl.BlockSpec(memory_space=pl.ANY)] * len(parts),
        out_specs=[pl.BlockSpec(memory_space=pl.ANY)] * len(shapes),
        scratch_shapes=[pltpu.SemaphoreType.DMA((len(shapes),))],
    )(me, *parts)


def weight_grad(left, right, shard_rows, column_block, row_block, me, name):
    tokens, height = left.shape
    width = right.shape[1]
    column_blocks, row_blocks = width // column_block, height // row_block
    per_block = row_block // shard_rows
    half = 1 << (MAIN - 1)

    def body(me_ref, left_ref, right_ref, send_ref, keep_ref):
        mine = me_ref[0]
        product = lax.dot_general(
            left_ref[...], right_ref[...], (((0,), (0,)), ((), ())), preferred_element_type=SINGLE
        ).astype(HALF)
        for s in range(per_block):
            shard = pl.program_id(1) * per_block + s
            core, k = spot(shard ^ mine, True)
            part = product[s * shard_rows : (s + 1) * shard_rows]

            @pl.when(core == 1)
            def _():
                send_ref[k] = part

            @pl.when(core == 0)
            def _():
                keep_ref[k] = part

    shape = jax.ShapeDtypeStruct((half, column_blocks * shard_rows, column_block), HALF)
    spec = pl.BlockSpec((half, shard_rows, column_block), lambda j, i: (0, j, 0))
    return pl.pallas_call(
        body,
        name=name,
        out_shape=[shape, shape],
        grid=(column_blocks, row_blocks),
        in_specs=[
            pl.BlockSpec(memory_space=pltpu.SMEM),
            pl.BlockSpec((tokens, row_block), lambda j, i: (0, i)),
            pl.BlockSpec((tokens, column_block), lambda j, i: (0, j)),
        ],
        out_specs=[spec, spec],
        compiler_params=pltpu.CompilerParams(vmem_limit_bytes=48 * MIB),
        cost_estimate=pl.CostEstimate(
            flops=2 * tokens * height * width,
            bytes_accessed=2 * tokens * (height + width) + 2 * height * width,
            transcendentals=0,
        ),
    )(me, left, right)


def add_low(first, second):
    return (first.astype(SINGLE) + second.astype(SINGLE)).astype(HALF)


def reduce_chunk(send, keep, split):
    base = low_bits()
    core, bit_x, bit_y, bit_z, bit_far = (base + i for i in range(MAIN))
    rows, width = send.shape[1:]
    total = add_low(keep, exchange(send, core)).reshape(2, 2, 4, rows, width)
    second = total[:, :, :, split:]
    if split:
        first = total[:, :, :, :split]
        from_x = exchange(first[1], bit_x)
        from_y = exchange(second[:, 1], bit_y)
        first, second = add_low(first[0], from_x), add_low(second[:, 0], from_y)
        from_y = exchange(first[1], bit_y)
        from_x = exchange(second[1], bit_x)
        first, second = add_low(first[0], from_y), add_low(second[0], from_x)
        total = jnp.concatenate([first, second], axis=1)
    else:
        second = add_low(second[0], exchange(second[1], bit_x))
        total = add_low(second[0], exchange(second[1], bit_y))
    total = add_low(total[:2], exchange(total[2:], bit_z))
    return total[0].astype(SINGLE) + exchange(total[1], bit_far).astype(SINGLE)


def keep_mask(ends_ref, first, shape, span):
    place = first + lax.broadcasted_iota(jnp.int32, shape, 0) * span
    start = place == 0
    for i in range(7):
        start = start | (place == ends_ref[i])
    return jnp.where(start, 0.0, 1.0)


def scan_states(ends, base, inputs, decays, reverse, name):
    block, channels = inputs.shape
    span = block // SEGMENTS
    lanes = 128

    def body(ends_ref, base_ref, in_ref, decay_ref, state_ref, product_ref):
        decay = jnp.broadcast_to(decay_ref[...], (SEGMENTS, lanes))
        first = base_ref[0]

        def at(k):
            return pl.ds(k, SEGMENTS, stride=span)

        def one(lap, carry):
            k = span - 1 - lap if reverse else lap
            state, product = carry
            a = decay * keep_mask(ends_ref, first + (k + 1 if reverse else k), (SEGMENTS, lanes), span)
            state, product = a * state + in_ref[at(k), :], product * a
            state_ref[at(k), :] = state
            product_ref[at(k), :] = product
            return (state, product)

        zero = jnp.zeros((SEGMENTS, lanes), SINGLE)
        state, product = lax.fori_loop(0, span, one, (zero, zero + 1.0), unroll=8)
        carry, through = zero[:1], zero[:1] + 1.0
        carries, throughs = [None] * SEGMENTS, [None] * SEGMENTS
        order = range(SEGMENTS)[::-1] if reverse else range(SEGMENTS)
        for s in order:
            carries[s], throughs[s] = carry, through
            carry = product[s : s + 1] * carry + state[s : s + 1]
            through = product[s : s + 1] * through
        carry_in = jnp.concatenate(carries, axis=0)
        through_in = jnp.concatenate(throughs, axis=0)

        def two(k, carry):
            product = product_ref[at(k), :]
            state_ref[at(k), :] = state_ref[at(k), :] + product * carry_in
            product_ref[at(k), :] = product * through_in
            return carry

        lax.fori_loop(0, span, two, 0, unroll=8)

    shape = jax.ShapeDtypeStruct((block, channels), SINGLE)
    spec = pl.BlockSpec((block, lanes), lambda i: (0, i))
    return pl.pallas_call(
        body,
        name=name,
        out_shape=[shape, shape],
        grid=(channels // lanes,),
        in_specs=[
            pl.BlockSpec(memory_space=pltpu.SMEM),
            pl.BlockSpec(memory_space=pltpu.SMEM),
            spec,
            pl.BlockSpec((1, lanes), lambda i: (0, i)),
        ],
        out_specs=[spec, spec],
        compiler_params=pltpu.CompilerParams(vmem_limit_bytes=24 * MIB),
    )(ends, base, inputs, decays)


def carried_in(through, ending, reverse):
    count, place = lax.axis_size("seq"), lax.axis_index("seq")
    gathered = lax.all_gather(jnp.stack([through, ending]), "seq")
    state = jnp.zeros_like(ending)
    for lap in range(count):
        source = count - 1 - lap if reverse else lap
        before = source > place if reverse else source < place
        state = jnp.where(before, gathered[source, 0] * state + gathered[source, 1], state)
    return state


def layer_norm(token_rows, scale, offset):
    center = token_rows - jnp.mean(token_rows, axis=-1, keepdims=True)
    inverse = lax.rsqrt(jnp.mean(center * center, axis=-1, keepdims=True) + EPSILON)
    return center * inverse * scale + offset


def decay_terms(rates):
    return (jnp.exp(-rates), jnp.sqrt(-jnp.expm1(-2.0 * rates)))


def column_sum(values):
    return jnp.sum(values.astype(SINGLE), axis=0)


def column_blocks(shard, width):
    return jnp.concatenate(
        [shard[:, i : i + width] for i in range(0, shard.shape[1], width)], axis=0
    )


def from_column_blocks(rows, count):
    height = rows.shape[0] // count
    return jnp.concatenate([rows[i * height : (i + 1) * height] for i in range(count)], axis=1)


def on_device(
    tokens,
    lengths,
    cotangent,
    norm_gain,
    norm_shift,
    value_weight,
    value_bias,
    reduce_weight,
    reduce_bias,
    decay_rates,
    skip_gain,
    state_weight,
    expand_weight,
    expand_bias,
    out_weight,
    out_bias,
):
    half, single = HALF, SINGLE
    shards = 1 << MAIN
    me = (device_number() >> low_bits()).reshape(1).astype(jnp.int32)
    low = lambda a: gather_low(a.astype(half))
    vectors = [
        low(v)
        for v in (
            norm_gain,
            norm_shift,
            value_bias,
            reduce_bias,
            decay_rates,
            skip_gain,
            expand_bias,
            out_bias,
        )
    ]
    sizes = [v.shape[0] for v in vectors]
    used = sum(sizes)
    reduce_shard, state_shard = low(reduce_weight), low(state_weight)
    value_shard, expand_shard, out_shard = low(value_weight), low(expand_weight), low(out_weight)
    channels = state_shard.shape[1]
    width = tokens.shape[-1]
    gate = value_shard.shape[1]
    blocks = gate // width

    vector_rows = jnp.pad(jnp.concatenate(vectors)[None], ((0, 7), (0, channels - used)))
    small = jnp.concatenate([reduce_shard, state_shard, vector_rows], axis=0)
    small_parts = gather_chunk(small, 0)
    value_parts = gather_chunk(column_blocks(value_shard, width), 48)
    expand_parts = gather_chunk(column_blocks(expand_shard, width), 24)
    out_parts = gather_chunk(out_shard, 48)

    reduce_mat, state_mat, vector_mat = place_weights(
        small_parts,
        [(0, 0, 32, 0, 32, 0, 0), (0, 32, 16, 1, 16, 0, 0), (0, 48, 8, 2, 8, 0, 0)],
        [(width, channels), (channels, channels), (8 * shards, channels)],
        me,
    )
    (value_mat,) = place_weights(
        value_parts,
        [
            (0, 0, 32, 0, 32, 0, 0),
            (0, 32, 16, 0, 32, 0, width),
            (1, 0, 16, 0, 32, 16, width),
            (1, 16, 32, 0, 32, 0, 2 * width),
        ],
        [(width, gate)],
        me,
    )
    (expand_mat,) = place_weights(
        expand_parts,
        [
            (0, 0, 16, 0, 16, 0, 0),
            (0, 16, 8, 0, 16, 0, width),
            (1, 0, 8, 0, 16, 8, width),
            (1, 8, 16, 0, 16, 0, 2 * width),
        ],
        [(channels, gate)],
        me,
    )
    (out_mat,) = place_weights(
        out_parts,
        [(0, 0, 48, 0, 96, 0, 0), (1, 0, 48, 0, 96, 48, 0)],
        [(gate, width)],
        me,
    )
    vector_table = vector_mat.reshape(shards, 8, channels)[:, 0].astype(single)
    places = [sum(sizes[:i]) for i in range(len(sizes))]
    (
        norm_scale,
        norm_offset,
        value_add,
        reduce_add,
        rate_vec,
        skip_vec,
        expand_add,
        out_add,
    ) = [vector_table[:, p : p + n].reshape(-1) for p, n in zip(places, sizes)]

    row_count, block, _ = tokens.shape
    base = (lax.axis_index("seq") * block).reshape(1).astype(jnp.int32)
    positions = base + jnp.arange(block, dtype=jnp.int32)
    doc_ends = jnp.cumsum(lengths, axis=-1).reshape(-1)
    starts = jnp.any(positions[:, None] == doc_ends[None, :-1], axis=-1) | (positions == 0)
    keep_flags = (1.0 - starts.astype(single))[:, None]
    live_rows = (positions < doc_ends[-1]).astype(single)[:, None]
    token_rows = tokens.reshape(block, width).astype(single)

    normed, norm_pull = jax.vjp(layer_norm, token_rows, norm_scale, norm_offset)
    normed_low = normed.astype(half)
    reduce_pre = jnp.dot(normed_low, reduce_mat, preferred_element_type=single) + reduce_add
    reduced_act, reduce_pull = jax.vjp(jax.nn.gelu, reduce_pre)
    (decays, inflow), decay_pull = jax.vjp(decay_terms, rate_vec)
    local_states, cumul = scan_states(
        doc_ends, base, inflow * reduced_act, decays[None], False, "forward_scan"
    )
    carried = carried_in(cumul[-1], local_states[-1], False)
    value_pre = jnp.dot(normed_low, value_mat, preferred_element_type=single) + value_add
    values_act, value_pull = jax.vjp(jax.nn.gelu, value_pre)
    states = local_states + cumul * carried[None]
    states_low = states.astype(half)
    ssm_out = jnp.dot(states_low, state_mat, preferred_element_type=single) + skip_vec * reduced_act
    ssm_low = ssm_out.astype(half)
    expand_pre = jnp.dot(ssm_low, expand_mat, preferred_element_type=single) + expand_add
    gated_low = (values_act * expand_pre).astype(half)

    cot_rows = cotangent.reshape(-1, width).astype(single)
    branch_grad = (live_rows * cot_rows).astype(half)
    out_grads = weight_grad(gated_low, branch_grad, 96, width, 768, me, "grad_out")
    out_sum = reduce_chunk(*out_grads, 48)

    branch = jnp.dot(gated_low, out_mat, preferred_element_type=single) + out_add
    output = (token_rows + live_rows * branch).astype(half).reshape(tokens.shape)
    grad_out_add = column_sum(branch_grad)
    gated_grad = jnp.einsum("td,gd->tg", branch_grad, out_mat, preferred_element_type=single)
    expand_grad = (gated_grad * values_act).astype(half)
    value_grad = gated_grad * expand_pre
    value_low = value_pull(value_grad)[0].astype(half)
    expand_grads = weight_grad(ssm_low, expand_grad, 16, width, 512, me, "grad_expand")
    expand_sum = reduce_chunk(*expand_grads, 24)
    value_grads = weight_grad(normed_low, value_low, 32, width, 512, me, "grad_value")
    value_sum = reduce_chunk(*value_grads, 48)
    grad_expand_add = column_sum(expand_grad)
    grad_value_add = column_sum(value_low)
    ssm_grad = jnp.einsum(
        "tg,rg->tr", expand_grad, expand_mat, preferred_element_type=single
    ).astype(half)
    grad_skip = jnp.sum(ssm_grad.astype(single) * reduced_act, axis=0)
    state_send, state_keep = weight_grad(states_low, ssm_grad, 16, channels, 512, me, "grad_state")
    state_grad = jnp.einsum("ts,rs->tr", ssm_grad, state_mat, preferred_element_type=single)
    local_total, suffix = scan_states(doc_ends, base, state_grad, decays[None], True, "reverse_scan")
    flow_in = carried_in(suffix[0], local_total[0], True)
    total_grad = local_total + suffix * flow_in[None]
    prev_states = jnp.concatenate([carried[None], states[:-1]], axis=0)
    grad_decays = jnp.sum(total_grad * keep_flags * prev_states, axis=0)
    grad_inflow = jnp.sum(total_grad * reduced_act, axis=0)
    grad_rates = decay_pull((grad_decays, grad_inflow))[0]
    reduced_grad = ssm_grad.astype(single) * skip_vec + inflow * total_grad
    reduce_low_grad = reduce_pull(reduced_grad)[0].astype(half)
    grad_reduce_add = column_sum(reduce_low_grad)
    reduce_send, reduce_keep = weight_grad(
        normed_low, reduce_low_grad, 32, channels, 512, me, "grad_reduce"
    )
    normed_grad = jnp.einsum(
        "tg,dg->td", value_low, value_mat, preferred_element_type=single
    ) + jnp.einsum("tr,dr->td", reduce_low_grad, reduce_mat, preferred_element_type=single)
    token_grad, grad_scale, grad_offset = norm_pull(normed_grad)
    grad_tokens = (cot_rows + token_grad).astype(half).reshape(tokens.shape)

    sums = (
        grad_scale,
        grad_offset,
        grad_value_add,
        grad_reduce_add,
        grad_rates,
        grad_skip,
        grad_expand_add,
        grad_out_add,
    )
    table = jnp.concatenate([v.reshape(shards, -1) for v in sums], axis=1).astype(half)
    table = jnp.pad(table[:, None], ((0, 0), (0, 7), (0, channels - used)))
    k = jnp.arange(shards // 2, dtype=jnp.int32)
    rel = ((k >> 3) & 1) * 2 + ((k >> 2) & 1) * 4 + ((k >> 1) & 1) * 8 + (k & 1) * 16
    small_sum = reduce_chunk(
        jnp.concatenate([reduce_send, state_send, table[(rel + 1) ^ me]], axis=1),
        jnp.concatenate([reduce_keep, state_keep, table[rel ^ me]], axis=1),
        0,
    )
    vector_sum = small_sum[48]
    vector_sums = [reduce_low(vector_sum[p : p + n]) for p, n in zip(places, sizes)]
    return (
        output,
        grad_tokens,
        vector_sums[0],
        vector_sums[1],
        reduce_low(from_column_blocks(value_sum, blocks)),
        vector_sums[2],
        reduce_low(small_sum[:32]),
        vector_sums[3],
        vector_sums[4],
        vector_sums[5],
        reduce_low(small_sum[32:48]),
        reduce_low(from_column_blocks(expand_sum, blocks)),
        vector_sums[6],
        reduce_low(out_sum),
        vector_sums[7],
    )


def solution(mesh):
    rows, vector, matrix = P("dp", "seq", None), P(("dp", "seq")), P(("dp", "seq"), None)
    return jax.shard_map(
        on_device,
        mesh=mesh,
        in_specs=(
            rows,
            P("dp", None),
            rows,
            vector,
            vector,
            matrix,
            vector,
            matrix,
            vector,
            vector,
            vector,
            matrix,
            matrix,
            vector,
            matrix,
            vector,
        ),
        out_specs=(
            rows,
            rows,
            vector,
            vector,
            matrix,
            vector,
            matrix,
            vector,
            vector,
            vector,
            matrix,
            matrix,
            vector,
            matrix,
            vector,
        ),
        check_vma=False,
    )
```

time: 1460 us -> 974 us (0.67)
  Pallas kernels: 0 us -> 605 us
  local copies, waits for them, and re-layouts: 468 us -> 23.7 us
  waiting for transfers between devices: 546 us -> 125 us
  blocking collectives: 148 us -> 10.4 us
  other arithmetic: 139 us -> 59.8 us
  starting transfers between devices: 0.37 us -> 58.3 us
  matrix products: 124 us -> 80.2 us
    pallas_call x0 -> x11, Pallas kernels: none -> 605 us  [the longest x4 537 us: place_weights(): pl.pallas_call(body, out_shape=[jax.ShapeDtypeStruct(s, HALF) for s in sh...]
    reduce_scatter x5 -> x0, waiting for transfers between devices: 546 us -> none  [the longest x1 163 us: on_device(): lax.psum_scatter(grad_value_mat, ('dp', 'seq'), scatter_dimension=0, tile...]
    slice x140 -> x23, local copies, waits for them, and re-layouts: 295 us -> 5.04 us  [the longest x3 1.77 us: on_device(): vector_sum[p:p + n]]
    ppermute x0 -> x55, waiting for transfers between devices: none -> 125 us  [exchange(): lax.ppermute(values, axis, [(i, i ^ 1 << place) for i in range(count)])]
    pad x72 -> x0, local copies, waits for them, and re-layouts: 120 us -> none  [the longest x36 72.4 us: on_device(): lax.associative_scan(compose, (retain, retain * state_grad), reverse=True...]
    add x81 -> x5, other arithmetic: 86.8 us -> 0.88 us  [the longest x4 0.87 us: reduce_chunk(): return total[0].astype(SINGLE) + exchange(total[1], bit_far).astype(SINGLE)]
    unnamed x2 -> x0, blocking collectives: 80.5 us -> none
    ppermute x0 -> x55, starting transfers between devices: none -> 58.3 us  [exchange(): lax.ppermute(values, axis, [(i, i ^ 1 << place) for i in range(count)])]
  transfers between devices with their start and end apart: 9 -> 55, of which waited for: 4 -> 28; matrix products, arithmetic and copies ran while one was open for 28% -> 12% of each run, Pallas kernels for 0% -> 40%
where the time goes in v1:
time: 974 us; the launch traced here: 965 us
  Pallas kernels  605 us (62%)
  waiting for transfers between devices  125 us (13%)
  matrix products  80.2 us (8%)
  other arithmetic  59.8 us (6%)
  starting transfers between devices  58.3 us (6%)
  local copies, waits for them, and re-layouts  23.7 us (2%)
  blocking collectives  10.4 us (1%)
    pallas_call x4, Pallas kernels, place_weights(): pl.pallas_call(body, out_shape=[jax.ShapeDtypeStruct(s, HALF) for s in sh...  537 us
    ppermute x55, waiting for transfers between devices, exchange(): lax.ppermute(values, axis, [(i, i ^ 1 << place) for i in range(count)])  125 us
    ppermute x55, starting transfers between devices, exchange(): lax.ppermute(values, axis, [(i, i ^ 1 << place) for i in range(count)])  58.3 us
    pallas_call x5, Pallas kernels, weight_grad(): pl.pallas_call(body, name=name, out_shape=[shape, shape], grid=(column_bl...  44.5 us
    pallas_call x2, Pallas kernels, scan_states(): pl.pallas_call(body, name=name, out_shape=[shape, shape], grid=(channels...  23.8 us
    dot_general x1, matrix products, on_device(): jnp.einsum('td,gd->tg', branch_grad, out_mat, preferred_element_type=single)  22.8 us
  transfers between devices with their start and end apart: 55, of which 28 were waited for; matrix products, arithmetic and copies ran while one was open for 12% of the time, Pallas kernels for 40%

profile of v1, /device:TPU:0, one launch (start us, length us, event | category | flops | bytes accessed | tf_op | source)
XLA Modules:
  0.0 964.7 jit_solution(10434089942350614595)
XLA Ops:
  7.8 4.1 collective-permute-start
  14.0 3.0 collective-permute-start.5
  22.7 2.8 collective-permute-start.1
  26.1 3.7 collective-permute-done.13
  29.9 7.6 collective-permute-done.1
  39.4 2.4 collective-permute-done.14
  45.8 3.9 collective-permute-done.18
  53.8 4.6 collective-permute-done.22
  60.1 7.8 collective-permute-done.16
  71.8 4.6 collective-permute-done.23
  82.9 5.6 collective-permute-done.10
  93.9 96.4 %shard_map.273 = bf16[512,3072]{1,0:T(8,128)(2,1)} custom-call(s32[1]{0:T(128)} %bitcast.2.me_ref, bf16[16,24,1024]{2,1,0:T(8,128)(2,1)} %copy-done.20, bf16[16,24,1024]{2,1,0:T(8,128)(2,1)} %copy-done.33, bf16[16,24,1024]{2,1,0:T(8,128)(2,1)} %copy-done.21, bf16[16,24,1024]{2,1,0:T(8,128)(2,1)} %copy-done.34), custom_call_target="tpu_custom_call" | custom-call | tf_op jit(solution)/shard_map/pallas_call | solution.py:125
  190.3 2.7 pad_maximum_fusion.2.refs_0_
  193.2 2.5 pad_maximum_fusion.3.refs_2_
  196.0 2.4 pad_maximum_fusion.refs_0_
  198.7 2.5 pad_maximum_fusion.1.refs_2_
  201.4 56.7 %shard_map.271 = (bf16[1024,512]{1,0:T(8,128)(2,1)}, bf16[512,512]{1,0:T(8,128)(2,1)}, bf16[256,512]{1,0:T(8,128)(2,1)}) custom-call(s32[1]{0:T(128)} %bitcast.2.me_ref, bf16[16,56,512]{2,1,0:T(8,128)(2,1)} %constant_dynamic-update-slice_fusion.refs_0_, bf16[16,56,512]{2,1,0:T(8,128)(2,1)} %collective-permute-done.4.refs_1_), custom_call_target="tpu_custom_call" | custom-call | tf_op jit(solution)/shard_map/pallas_call | solution.py:125
  260.7 2.5 fusion.16.left_ref
  265.0 12.1 %forward_scan.1 = (f32[1024,512]{1,0:T(8,128)S(1)}, f32[1024,512]{1,0:T(8,128)S(1)}) custom-call(s32[8]{0:T(128)S(1)} %bitcast.313, s32[1]{0:T(128)} %bitcast.9.base_ref, f32[1024,512]{1,0:T(8,128)S(1)} %get-tuple-element.127.in_ref, f32[1,512]{1,0:T(1,128)S(1)} %exp.19.decay_ref), custom_call_target="tpu_custom_call" | custom-call | tf_op jit(solution)/shard_map/forward_scan/pallas_call | solution.py:259
  277.2 5.2 all-gather.2
  284.3 2.3 add_convert_fusion.3.left_ref
  286.6 191.9 %shard_map.272 = bf16[1024,3072]{1,0:T(8,128)(2,1)} custom-call(s32[1]{0:T(128)} %bitcast.2.me_ref, bf16[16,48,1024]{2,1,0:T(8,128)(2,1)} %pad_maximum_fusion.refs_0_, bf16[16,48,1024]{2,1,0:T(8,128)(2,1)} %collective-permute-done.9.refs_1_, bf16[16,48,1024]{2,1,0:T(8,128)(2,1)} %pad_maximum_fusion.1.refs_2_, ...), custom_call_target="tpu_custom_call" | custom-call | tf_op jit(solution)/shard_map/pallas_call | solution.py:125
  478.5 9.5 fusion.98
  488.1 10.3 %multiply_convert_fusion.1 = (bf16[1024,3072]{1,0:T(8,128)(2,1)}, f32[1024,3072]{1,0:T(8,128)}) fusion(f32[3072]{0:T(1024)S(1)} %add.386, f32[1024,3072]{1,0:T(8,128)S(1)} %fusion.98, f32[3072]{0:T(1024)S(1)} %add.370, bf16[1024,512]{1,0:T(8,128)(2,1)S(1)} %copy-done.8, bf16[512,3072]{1,0:T(8,128)(2,1)S(1)} %copy-done.22), kind=kOutput, calls=%fused_computation.12 | convolution fusion | flops 3258974208 | bytes 35676160 | tf_op jit(solution)/shard_map/dot_general | solution.py:433
  498.4 191.7 %shard_map.274 = bf16[3072,1024]{1,0:T(8,128)(2,1)} custom-call(s32[1]{0:T(128)} %bitcast.2.me_ref, bf16[16,48,1024]{2,1,0:T(8,128)(2,1)} %pad_maximum_fusion.2.refs_0_, bf16[16,48,1024]{2,1,0:T(8,128)(2,1)} %collective-permute-done.25.refs_1_, bf16[16,48,1024]{2,1,0:T(8,128)(2,1)} %pad_maximum_fusion.3.refs_2_, ...), custom_call_target="tpu_custom_call" | custom-call | tf_op jit(solution)/shard_map/pallas_call | solution.py:125
  690.1 22.8 %fusion.82 = (bf16[3072]{0:T(1024)(128)(2,1)}, bf16[1024,3072]{1,0:T(8,128)(2,1)}, bf16[3072]{0:T(1024)(128)(2,1)S(1)}, bf16[1024,3072]{1,0:T(8,128)(2,1)S(1)}) fusion(f32[1024,3072]{1,0:T(8,128)} %copy-done.48, f32[3072]{0:T(1024)S(1)} %add.370, f32[1024,3072]{1,0:T(8,128)} %get-tuple-element.130, f32[3072]{0:T(1024)S(1)} %add.386, ...), kind=kOutput, calls=%fused_computation.256 | convolution fusion | flops 6530525184 | bytes 46174208 | tf_op jit(solution)/shard_map/td,gd->tg/dot_general | solution.py:444
  713.0 2.6 copy-done.47
  715.6 3.4 convolution_convert_fusion.right_ref
  719.0 10.8 %grad_state.1 = (bf16[16,16,512]{2,1,0:T(8,128)(2,1)S(1)}, bf16[16,16,512]{2,1,0:T(8,128)(2,1)S(1)}) custom-call(s32[1]{0:T(128)} %bitcast.2.me_ref, bf16[1024,512]{1,0:T(8,128)(2,1)S(1)} %get-tuple-element.67.left_ref, bf16[1024,512]{1,0:T(8,128)(2,1)S(1)} %convolution_convert_fusion.right_ref), custom_call_target="tpu_custom_call" | custom-call | flops 536870912 | bytes 2621440 | tf_op jit(solution)/shard_map/grad_state/pallas_call | solution.py:162
  731.8 7.1 grad_expand.1
  740.1 11.7 %reverse_scan.1 = (f32[1024,512]{1,0:T(8,128)S(1)}, f32[1024,512]{1,0:T(8,128)S(1)}) custom-call(s32[8]{0:T(128)S(1)} %bitcast.314, s32[1]{0:T(128)} %bitcast.9.base_ref, f32[1024,512]{1,0:T(8,128)S(1)} %fusion.99.in_ref, f32[1,512]{1,0:T(1,128)S(1)} %exp.19.decay_ref), custom_call_target="tpu_custom_call" | custom-call | tf_op jit(solution)/shard_map/reverse_scan/pallas_call | solution.py:259
  751.9 5.2 all-gather.3
  757.1 2.3 fusion.24
  759.4 1.8 fusion.80
  761.3 2.1 grad_reduce.1
  763.4 3.3 fusion.100
  770.9 13.0 %grad_value.1 = (bf16[16,96,1024]{2,1,0:T(8,128)(2,1)S(1)}, bf16[16,96,1024]{2,1,0:T(8,128)(2,1)}) custom-call(s32[1]{0:T(128)} %bitcast.2.me_ref, bf16[1024,1024]{1,0:T(8,128)(2,1)S(1)} %copy-done.2, bf16[1024,3072]{1,0:T(8,128)(2,1)} %get-tuple-element.66.right_ref), custom_call_target="tpu_custom_call" | custom-call | flops 6442450944 | bytes 14680064 | tf_op jit(solution)/shard_map/grad_value/pallas_call | solution.py:162
  784.0 13.8 %fusion.76 = (bf16[1024]{0:T(1024)(128)(2,1)S(1)}, f32[1024]{0:T(1024)S(1)}, f32[1024,1024]{1,0:T(8,128)}) fusion(f32[1024]{0:T(1024)S(1)} %mul.414, f32[1024]{0:T(1024)S(1)} %broadcast_multiply_fusion.1, bf16[1,1024,1024]{2,1,0:T(8,128)(2,1)S(1)} %copy-done.11, f32[1024,1024]{1,0:T(8,128)S(1)} %copy-done.46, ...), kind=kOutput, calls=%fused_computation.252 | convolution fusion | flops 6449788928 | bytes 23083008 | tf_op jit(solution)/shard_map/tg,dg->td/dot_general | solution.py:473
  798.5 4.4 fusion.17
  805.2 2.0 fusion.42
  807.7 12.2 %fusion.33 = bf16[1,1024,1024]{2,1,0:T(8,128)(2,1)} fusion(bf16[1,1024,1024]{2,1,0:T(8,128)(2,1)} %param.16, f32[1024]{0:T(1024)} %add.389, f32[1024]{0:T(1024)S(1)} %copy-done.40, bf16[1024,3072]{1,0:T(8,128)(2,1)} %get-tuple-element.129.left_ref, bf16[3072,1024]{1,0:T(8,128)(2,1)} %shard_map.274), kind=kOutput, calls=%fused_computation.52 | convolution fusion | flops 6447693824 | bytes 16785408 | tf_op jit(solution)/shard_map/dot_general | solution.py:441
  820.7 11.4 %grad_out.1 = (bf16[16,96,1024]{2,1,0:T(8,128)(2,1)S(1)}, bf16[16,96,1024]{2,1,0:T(8,128)(2,1)}) custom-call(s32[1]{0:T(128)} %bitcast.2.me_ref, bf16[1024,3072]{1,0:T(8,128)(2,1)} %get-tuple-element.129.left_ref, bf16[1024,1024]{1,0:T(8,128)(2,1)S(1)} %get-tuple-element.57.right_ref), custom_call_target="tpu_custom_call" | custom-call | flops 6442450944 | bytes 14680064 | tf_op jit(solution)/shard_map/grad_out/pallas_call | solution.py:162
  834.8 2.7 fusion.32
  837.6 9.2 collective-permute-done.30
  847.8 2.1 add_convert_fusion.2
  849.9 4.1 collective-permute-done.31
  854.3 4.7 collective-permute-done.32
  859.1 2.6 collective-permute-start.33
  864.8 5.8 collective-permute-done.42
  873.5 3.2 collective-permute-done.45
  878.5 2.1 collective-permute-start.46
  881.2 3.5 collective-permute-done.46
  887.7 2.7 collective-permute-done.47
  891.1 3.4 add_convert_fusion.1
  894.6 2.1 collective-permute-start.35
  901.2 14.0 %collective-permute-done.35 = bf16[2,4,48,1024]{3,2,1,0:T(8,128)(2,1)S(1)} collective-permute-done((bf16[2,4,48,1024]{3,2,1,0:T(8,128)(2,1)S(1)}, bf16[2,4,48,1024]{3,2,1,0:T(8,128)(2,1)S(1)}, u32[]{:S(2)}, u32[]{:S(2)}) %collective-permute-start.35) | collective-permute-done | bytes 786464 | tf_op jit(solution)/shard_map/ppermute | solution.py:32
  915.2 2.1 collective-permute-done.37
  918.1 2.1 collective-permute-start.36
  920.2 11.5 %collective-permute-done.49 = bf16[2,4,48,1024]{3,2,1,0:T(8,128)(2,1)S(1)} collective-permute-done((bf16[2,4,48,1024]{3,2,1,0:T(8,128)(2,1)S(1)}, bf16[2,4,48,1024]{3,2,1,0:T(8,128)(2,1)S(1)}, u32[]{:S(2)}, u32[]{:S(2)}) %collective-permute-start.49) | collective-permute-done | bytes 786464 | tf_op jit(solution)/shard_map/ppermute | solution.py:32
  936.8 2.5 collective-permute-start.39
  942.4 2.3 collective-permute-start.53
  944.7 3.8 collective-permute-done.39
  948.7 6.7 collective-permute-done.53
  958.3 5.2 collective-permute-done.54
  (334 shorter events, 94.9 us)
Async XLA Ops:
  0.7 16.5 %copy-start.45 = (s32[1,8]{1,0:T(1,128)S(1)}, s32[1,8]{1,0:T(1,128)}, u32[]{:S(2)}) copy-start(s32[1,8]{1,0:T(1,128)} %param.17) | copy-start | bytes 100
  0.7 18.6 %copy-start.10 = (bf16[1,1024,1024]{2,1,0:T(8,128)(2,1)S(1)}, bf16[1,1024,1024]{2,1,0:T(8,128)(2,1)}, u32[]{:S(2)}) copy-start(bf16[1,1024,1024]{2,1,0:T(8,128)(2,1)} %param.16) | copy-start | bytes 6291460
  7.8 14.9 %collective-permute-start = (bf16[1,56,512]{2,1,0:T(8,128)(2,1)S(1)}, bf16[1,56,512]{2,1,0:T(8,128)(2,1)S(1)}, u32[]{:S(2)}, u32[]{:S(2)}) collective-permute-start(bf16[1,56,512]{2,1,0:T(8,128)(2,1)S(1)} %fusion.58), channel_id=1, source_target_pairs={{0,16},{4,20},{8,24},{12,28},{16,0},{20,4},{24,8},{28,12},{1,17},{... | collective-permute-start | bytes 172040 | tf_op jit(solution)/shard_map/ppermute | solution.py:32
  12.9 16.9 %collective-permute-start.13 = (bf16[1,48,1024]{2,1,0:T(8,128)(2,1)S(1)}, bf16[1,48,1024]{2,1,0:T(8,128)(2,1)S(1)}, u32[]{:S(2)}, u32[]{:S(2)}) collective-permute-start(bf16[1,48,1024]{2,1,0:T(8,128)(2,1)S(1)} %maximum_bitcast_fusion.1), channel_id=1, source_target_pairs={{0,16},{4,20},{8,24},{12,28},{16,0},{20,4},{24,8},{28,12},{1,17},{... | collective-permute-start | bytes 294920 | tf_op jit(solution)/shard_map/ppermute | solution.py:32
  14.0 25.2 %collective-permute-start.5 = (bf16[1,96,1024]{2,1,0:T(8,128)(2,1)S(1)}, bf16[1,96,1024]{2,1,0:T(8,128)(2,1)S(1)}, u32[]{:S(2)}, u32[]{:S(2)}) collective-permute-start(bf16[1,96,1024]{2,1,0:T(8,128)(2,1)S(1)} %maximum_bitcast_fusion), channel_id=1, source_target_pairs={{0,16},{4,20},{8,24},{12,28},{16,0},{20,4},{24,8},{28,12},{1,17},{... | collective-permute-start | bytes 589832 | tf_op jit(solution)/shard_map/ppermute | solution.py:32
  17.0 26.4 %collective-permute-start.21 = (bf16[1,96,1024]{2,1,0:T(8,128)(2,1)S(1)}, bf16[1,96,1024]{2,1,0:T(8,128)(2,1)S(1)}, u32[]{:S(2)}, u32[]{:S(2)}) collective-permute-start(bf16[1,96,1024]{2,1,0:T(8,128)(2,1)S(1)} %convert_bitcast_fusion.1), channel_id=1, source_target_pairs={{0,16},{4,20},{8,24},{12,28},{16,0},{20,4},{24,8},{28,12},{1,17},{... | collective-permute-start | bytes 589832 | tf_op jit(solution)/shard_map/ppermute | solution.py:32
  22.7 14.8 %collective-permute-start.1 = (bf16[2,56,512]{2,1,0:T(8,128)(2,1)S(1)}, bf16[2,56,512]{2,1,0:T(8,128)(2,1)S(1)}, u32[]{:S(2)}, u32[]{:S(2)}) collective-permute-start(bf16[2,56,512]{2,1,0:T(8,128)(2,1)S(1)} %pad_maximum_fusion.25), channel_id=1, source_target_pairs={{0,8},{4,12},{8,0},{12,4},{16,24},{20,28},{24,16},{28,20},{1,9},{5... | collective-permute-start | bytes 344072 | tf_op jit(solution)/shard_map/ppermute | solution.py:32
  29.8 11.9 %collective-permute-start.14 = (bf16[2,48,1024]{2,1,0:T(8,128)(2,1)S(1)}, bf16[2,48,1024]{2,1,0:T(8,128)(2,1)S(1)}, u32[]{:S(2)}, u32[]{:S(2)}) collective-permute-start(bf16[2,48,1024]{2,1,0:T(8,128)(2,1)S(1)} %pad_maximum_fusion.23), channel_id=1, source_target_pairs={{0,8},{4,12},{8,0},{12,4},{16,24},{20,28},{24,16},{28,20},{1,9},{5... | collective-permute-start | bytes 589832 | tf_op jit(solution)/shard_map/ppermute | solution.py:32
  37.6 7.6 collective-permute-start.2
  39.3 13.8 %collective-permute-start.6 = (bf16[2,96,1024]{2,1,0:T(8,128)(2,1)S(1)}, bf16[2,96,1024]{2,1,0:T(8,128)(2,1)S(1)}, u32[]{:S(2)}, u32[]{:S(2)}) collective-permute-start(bf16[2,96,1024]{2,1,0:T(8,128)(2,1)S(1)} %pad_maximum_fusion.15), channel_id=1, source_target_pairs={{0,8},{4,12},{8,0},{12,4},{16,24},{20,28},{24,16},{28,20},{1,9},{5... | collective-permute-start | bytes 1179656 | tf_op jit(solution)/shard_map/ppermute | solution.py:32
  41.8 7.9 collective-permute-start.18
  43.5 14.9 %collective-permute-start.22 = (bf16[2,96,1024]{2,1,0:T(8,128)(2,1)S(1)}, bf16[2,96,1024]{2,1,0:T(8,128)(2,1)S(1)}, u32[]{:S(2)}, u32[]{:S(2)}) collective-permute-start(bf16[2,96,1024]{2,1,0:T(8,128)(2,1)S(1)} %pad_maximum_fusion.19), channel_id=1, source_target_pairs={{0,8},{4,12},{8,0},{12,4},{16,24},{20,28},{24,16},{28,20},{1,9},{5... | collective-permute-start | bytes 1179656 | tf_op jit(solution)/shard_map/ppermute | solution.py:32
  43.6 7.8 collective-permute-start.15
  45.3 24.6 %collective-permute-start.3 = (bf16[8,56,512]{2,1,0:T(8,128)(2,1)S(1)}, bf16[8,56,512]{2,1,0:T(8,128)(2,1)S(1)}, u32[]{:S(2)}, u32[]{:S(2)}) collective-permute-start(bf16[8,56,512]{2,1,0:T(8,128)(2,1)S(1)} %pad_maximum_fusion.12), channel_id=1, source_target_pairs={{0,2},{1,3},{2,0},{3,1},{4,6},{5,7},{6,4},{7,5},{8,10},{9,11},{10,... | collective-permute-start | bytes 1376264 | tf_op jit(solution)/shard_map/ppermute | solution.py:32
  49.7 19.9 %collective-permute-start.19 = (bf16[8,24,1024]{2,1,0:T(8,128)(2,1)S(1)}, bf16[8,24,1024]{2,1,0:T(8,128)(2,1)S(1)}, u32[]{:S(2)}, u32[]{:S(2)}) collective-permute-start(bf16[8,24,1024]{2,1,0:T(8,128)(2,1)S(1)} %pad_maximum_fusion.18), channel_id=1, source_target_pairs={{0,4},{4,0},{8,12},{12,8},{16,20},{20,16},{24,28},{28,24},{1,5},{5... | collective-permute-start | bytes 1179656 | tf_op jit(solution)/shard_map/ppermute | solution.py:32
  51.5 16.5 %collective-permute-start.16 = (bf16[8,24,1024]{2,1,0:T(8,128)(2,1)S(1)}, bf16[8,24,1024]{2,1,0:T(8,128)(2,1)S(1)}, u32[]{:S(2)}, u32[]{:S(2)}) collective-permute-start(bf16[8,24,1024]{2,1,0:T(8,128)(2,1)S(1)} %pad_maximum_fusion.17), channel_id=1, source_target_pairs={{0,2},{1,3},{2,0},{3,1},{4,6},{5,7},{6,4},{7,5},{8,10},{9,11},{10,... | collective-permute-start | bytes 1179656 | tf_op jit(solution)/shard_map/ppermute | solution.py:32
  53.2 27.3 %collective-permute-start.7 = (bf16[4,48,1024]{2,1,0:T(8,128)(2,1)S(1)}, bf16[4,48,1024]{2,1,0:T(8,128)(2,1)S(1)}, u32[]{:S(2)}, u32[]{:S(2)}) collective-permute-start(bf16[4,48,1024]{2,1,0:T(8,128)(2,1)S(1)} %get-tuple-element.82), channel_id=1, source_target_pairs={{0,4},{4,0},{8,12},{12,8},{16,20},{20,16},{24,28},{28,24},{1,5},{5... | collective-permute-start | bytes 1179656 | tf_op jit(solution)/shard_map/ppermute | solution.py:32
  58.5 20.2 %copy-start.19 = (bf16[4,48,1024]{2,1,0:T(8,128)(2,1)}, bf16[4,48,1024]{2,1,0:T(8,128)(2,1)S(1)}, u32[]{:S(2)}) copy-start(bf16[4,48,1024]{2,1,0:T(8,128)(2,1)S(1)} %get-tuple-element.80) | copy-start | bytes 1179652
  58.5 20.2 %collective-permute-start.26 = (bf16[4,48,1024]{2,1,0:T(8,128)(2,1)S(1)}, bf16[4,48,1024]{2,1,0:T(8,128)(2,1)S(1)}, u32[]{:S(2)}, u32[]{:S(2)}) collective-permute-start(bf16[4,48,1024]{2,1,0:T(8,128)(2,1)S(1)} %get-tuple-element.79), channel_id=1, source_target_pairs={{0,2},{1,3},{2,0},{3,1},{4,6},{5,7},{6,4},{7,5},{8,10},{9,11},{10,... | collective-permute-start | bytes 1179656 | tf_op jit(solution)/shard_map/ppermute | solution.py:32
  68.0 8.5 collective-permute-start.23
  69.7 21.9 %collective-permute-start.17 = (bf16[16,24,1024]{2,1,0:T(8,128)(2,1)S(1)}, bf16[16,24,1024]{2,1,0:T(8,128)(2,1)S(1)}, u32[]{:S(2)}, u32[]{:S(2)}) collective-permute-start(bf16[16,24,1024]{2,1,0:T(8,128)(2,1)S(1)} %pad_maximum_fusion.7.refs_0_), channel_id=1, source_target_pairs={{0,1},{1,0},{2,3},{3,2},{4,5},{5,4},{6,7},{7,6},{8,9},{9,8},{10,11... | collective-permute-start | bytes 2359304 | tf_op jit(solution)/shard_map/ppermute | solution.py:32
  69.9 21.8 %collective-permute-start.20 = (bf16[16,24,1024]{2,1,0:T(8,128)(2,1)S(1)}, bf16[16,24,1024]{2,1,0:T(8,128)(2,1)S(1)}, u32[]{:S(2)}, u32[]{:S(2)}) collective-permute-start(bf16[16,24,1024]{2,1,0:T(8,128)(2,1)S(1)} %pad_maximum_fusion.8.refs_2_), channel_id=1, source_target_pairs={{0,1},{1,0},{2,3},{3,2},{4,5},{5,4},{6,7},{7,6},{8,9},{9,8},{10,11... | collective-permute-start | bytes 2359304 | tf_op jit(solution)/shard_map/ppermute | solution.py:32
  76.4 12.1 %collective-permute-start.10 = (bf16[4,48,1024]{2,1,0:T(8,128)(2,1)S(1)}, bf16[4,48,1024]{2,1,0:T(8,128)(2,1)S(1)}, u32[]{:S(2)}, u32[]{:S(2)}) collective-permute-start(bf16[4,48,1024]{2,1,0:T(8,128)(2,1)S(1)} %get-tuple-element.81), channel_id=1, source_target_pairs={{0,2},{1,3},{2,0},{3,1},{4,6},{5,7},{6,4},{7,5},{8,10},{9,11},{10,... | collective-permute-start | bytes 1179656 | tf_op jit(solution)/shard_map/ppermute | solution.py:32
  78.7 111.6 %collective-permute-start.24 = (bf16[8,48,1024]{2,1,0:T(8,128)(2,1)}, bf16[8,48,1024]{2,1,0:T(8,128)(2,1)}, u32[]{:S(2)}, u32[]{:S(2)}) collective-permute-start(bf16[8,48,1024]{2,1,0:T(8,128)(2,1)} %pad_maximum_fusion.10), channel_id=1, source_target_pairs={{0,2},{1,3},{2,0},{3,1},{4,6},{5,7},{6,4},{7,5},{8,10},{9,11},{10,... | collective-permute-start | bytes 2359304 | tf_op jit(solution)/shard_map/ppermute | solution.py:32
  80.5 112.7 %collective-permute-start.27 = (bf16[8,48,1024]{2,1,0:T(8,128)(2,1)}, bf16[8,48,1024]{2,1,0:T(8,128)(2,1)}, u32[]{:S(2)}, u32[]{:S(2)}) collective-permute-start(bf16[8,48,1024]{2,1,0:T(8,128)(2,1)} %pad_maximum_fusion.11), channel_id=1, source_target_pairs={{0,4},{4,0},{8,12},{12,8},{16,20},{20,16},{24,28},{28,24},{1,5},{5... | collective-permute-start | bytes 2359304 | tf_op jit(solution)/shard_map/ppermute | solution.py:32
  88.5 107.5 %collective-permute-start.8 = (bf16[8,48,1024]{2,1,0:T(8,128)(2,1)}, bf16[8,48,1024]{2,1,0:T(8,128)(2,1)}, u32[]{:S(2)}, u32[]{:S(2)}) collective-permute-start(bf16[8,48,1024]{2,1,0:T(8,128)(2,1)} %pad_maximum_fusion.5), channel_id=1, source_target_pairs={{0,2},{1,3},{2,0},{3,1},{4,6},{5,7},{6,4},{7,5},{8,10},{9,11},{10,... | collective-permute-start | bytes 2359304 | tf_op jit(solution)/shard_map/ppermute | solution.py:32
  91.6 109.8 %collective-permute-start.4 = (bf16[16,56,512]{2,1,0:T(8,128)(2,1)}, bf16[16,56,512]{2,1,0:T(8,128)(2,1)}, u32[]{:S(2)}, u32[]{:S(2)}) collective-permute-start(bf16[16,56,512]{2,1,0:T(8,128)(2,1)} %constant_dynamic-update-slice_fusion.refs_0_), channel_id=1, source_target_pairs={{0,1},{1,0},{2,3},{3,2},{4,5},{5,4},{6,7},{7,6},{8,9},{9,8},{10,11... | collective-permute-start | bytes 2752520 | tf_op jit(solution)/shard_map/ppermute | solution.py:32
  91.7 106.9 %collective-permute-start.11 = (bf16[8,48,1024]{2,1,0:T(8,128)(2,1)}, bf16[8,48,1024]{2,1,0:T(8,128)(2,1)}, u32[]{:S(2)}, u32[]{:S(2)}) collective-permute-start(bf16[8,48,1024]{2,1,0:T(8,128)(2,1)} %pad_maximum_fusion.6), channel_id=1, source_target_pairs={{0,4},{4,0},{8,12},{12,8},{16,20},{20,16},{24,28},{28,24},{1,5},{5... | collective-permute-start | bytes 2359304 | tf_op jit(solution)/shard_map/ppermute | solution.py:32
  193.0 305.3 %collective-permute-start.25 = (bf16[16,48,1024]{2,1,0:T(8,128)(2,1)}, bf16[16,48,1024]{2,1,0:T(8,128)(2,1)}, u32[]{:S(2)}, u32[]{:S(2)}) collective-permute-start(bf16[16,48,1024]{2,1,0:T(8,128)(2,1)} %pad_maximum_fusion.2.refs_0_), channel_id=1, source_target_pairs={{0,1},{1,0},{2,3},{3,2},{4,5},{5,4},{6,7},{7,6},{8,9},{9,8},{10,11... | collective-permute-start | bytes 4718600 | tf_op jit(solution)/shard_map/ppermute | solution.py:32
  195.7 302.7 %collective-permute-start.28 = (bf16[16,48,1024]{2,1,0:T(8,128)(2,1)}, bf16[16,48,1024]{2,1,0:T(8,128)(2,1)}, u32[]{:S(2)}, u32[]{:S(2)}) collective-permute-start(bf16[16,48,1024]{2,1,0:T(8,128)(2,1)} %pad_maximum_fusion.3.refs_2_), channel_id=1, source_target_pairs={{0,1},{1,0},{2,3},{3,2},{4,5},{5,4},{6,7},{7,6},{8,9},{9,8},{10,11... | collective-permute-start | bytes 4718600 | tf_op jit(solution)/shard_map/ppermute | solution.py:32
  198.5 88.1 %collective-permute-start.9 = (bf16[16,48,1024]{2,1,0:T(8,128)(2,1)}, bf16[16,48,1024]{2,1,0:T(8,128)(2,1)}, u32[]{:S(2)}, u32[]{:S(2)}) collective-permute-start(bf16[16,48,1024]{2,1,0:T(8,128)(2,1)} %pad_maximum_fusion.refs_0_), channel_id=1, source_target_pairs={{0,1},{1,0},{2,3},{3,2},{4,5},{5,4},{6,7},{7,6},{8,9},{9,8},{10,11... | collective-permute-start | bytes 4718600 | tf_op jit(solution)/shard_map/ppermute | solution.py:32
  201.1 85.5 %collective-permute-start.12 = (bf16[16,48,1024]{2,1,0:T(8,128)(2,1)}, bf16[16,48,1024]{2,1,0:T(8,128)(2,1)}, u32[]{:S(2)}, u32[]{:S(2)}) collective-permute-start(bf16[16,48,1024]{2,1,0:T(8,128)(2,1)} %pad_maximum_fusion.1.refs_2_), channel_id=1, source_target_pairs={{0,1},{1,0},{2,3},{3,2},{4,5},{5,4},{6,7},{7,6},{8,9},{9,8},{10,11... | collective-permute-start | bytes 4718600 | tf_op jit(solution)/shard_map/ppermute | solution.py:32
  265.0 19.3 %copy-start.16 = (f32[1024,512]{1,0:T(8,128)}, f32[1024,512]{1,0:T(8,128)S(1)}, u32[]{:S(2)}) copy-start(f32[1024,512]{1,0:T(8,128)S(1)} %get-tuple-element.128) | copy-start | bytes 6291460
  690.1 25.5 %copy-start.23 = (bf16[512,3072]{1,0:T(8,128)(2,1)S(1)}, bf16[512,3072]{1,0:T(8,128)(2,1)}, u32[]{:S(2)}) copy-start(bf16[512,3072]{1,0:T(8,128)(2,1)} %shard_map.273) | copy-start | bytes 9437188
  731.8 25.3 %copy-start.18 = (f32[1024,512]{1,0:T(8,128)S(1)}, f32[1024,512]{1,0:T(8,128)}, u32[]{:S(2)}) copy-start(f32[1024,512]{1,0:T(8,128)} %get-tuple-element.68) | copy-start | bytes 6291460
  740.1 19.3 %copy-start.3 = (bf16[16,48,1024]{2,1,0:T(8,128)(2,1)}, bf16[16,48,1024]{2,1,0:T(8,128)(2,1)S(1)}, u32[]{:S(2)}) copy-start(bf16[16,48,1024]{2,1,0:T(8,128)(2,1)S(1)} %get-tuple-element.45) | copy-start | bytes 4718596
  740.1 17.0 %copy-start.17 = (f32[1024,512]{1,0:T(8,128)S(1)}, f32[1024,512]{1,0:T(8,128)}, u32[]{:S(2)}) copy-start(f32[1024,512]{1,0:T(8,128)} %copy-done.16) | copy-start | bytes 6291460
  769.0 78.8 %collective-permute-start.41 = (bf16[16,48,1024]{2,1,0:T(8,128)(2,1)}, bf16[16,48,1024]{2,1,0:T(8,128)(2,1)}, u32[]{:S(2)}, u32[]{:S(2)}) collective-permute-start(bf16[16,48,1024]{2,1,0:T(8,128)(2,1)} %copy-done.7), channel_id=1, source_target_pairs={{0,1},{1,0},{2,3},{3,2},{4,5},{5,4},{6,7},{7,6},{8,9},{9,8},{10,11... | collective-permute-start | bytes 4718600 | tf_op jit(solution)/shard_map/ppermute | solution.py:32
  807.2 25.1 %collective-permute-start.29 = (bf16[16,56,512]{2,1,0:T(8,128)(2,1)}, bf16[16,56,512]{2,1,0:T(8,128)(2,1)}, u32[]{:S(2)}, u32[]{:S(2)}) collective-permute-start(bf16[16,56,512]{2,1,0:T(8,128)(2,1)} %fusion.42), channel_id=1, source_target_pairs={{0,1},{1,0},{2,3},{3,2},{4,5},{5,4},{6,7},{7,6},{8,9},{9,8},{10,11... | collective-permute-start | bytes 2752520 | tf_op jit(solution)/shard_map/ppermute | solution.py:32
  807.4 83.7 %collective-permute-start.34 = (bf16[16,96,1024]{2,1,0:T(8,128)(2,1)}, bf16[16,96,1024]{2,1,0:T(8,128)(2,1)}, u32[]{:S(2)}, u32[]{:S(2)}) collective-permute-start(bf16[16,96,1024]{2,1,0:T(8,128)(2,1)} %copy-done.6), channel_id=1, source_target_pairs={{0,1},{1,0},{2,3},{3,2},{4,5},{5,4},{6,7},{7,6},{8,9},{9,8},{10,11... | collective-permute-start | bytes 9437192 | tf_op jit(solution)/shard_map/ppermute | solution.py:32
  832.1 65.5 %collective-permute-start.48 = (bf16[16,96,1024]{2,1,0:T(8,128)(2,1)S(1)}, bf16[16,96,1024]{2,1,0:T(8,128)(2,1)S(1)}, u32[]{:S(2)}, u32[]{:S(2)}) collective-permute-start(bf16[16,96,1024]{2,1,0:T(8,128)(2,1)S(1)} %get-tuple-element.48), channel_id=1, source_target_pairs={{0,1},{1,0},{2,3},{3,2},{4,5},{5,4},{6,7},{7,6},{8,9},{9,8},{10,11... | collective-permute-start | bytes 9437192 | tf_op jit(solution)/shard_map/ppermute | solution.py:32
  834.0 12.8 %collective-permute-start.30 = (bf16[2,4,56,512]{3,2,1,0:T(8,128)(2,1)S(1)}, bf16[2,4,56,512]{3,2,1,0:T(8,128)(2,1)S(1)}, u32[]{:S(2)}, u32[]{:S(2)}) collective-permute-start(bf16[2,4,56,512]{3,2,1,0:T(8,128)(2,1)S(1)} %bitcast.328), channel_id=1, source_target_pairs={{0,2},{1,3},{2,0},{3,1},{4,6},{5,7},{6,4},{7,5},{8,10},{9,11},{10,... | collective-permute-start | bytes 1376264 | tf_op jit(solution)/shard_map/ppermute | solution.py:32
  847.0 7.1 collective-permute-start.31
  854.2 4.9 collective-permute-start.32
  859.1 5.2 collective-permute-start.33
  861.7 8.9 collective-permute-start.42
  862.6 8.0 collective-permute-start.44
  871.0 5.7 collective-permute-start.45
  872.7 18.4 %copy-start.24 = (bf16[16,96,1024]{2,1,0:T(8,128)(2,1)S(1)}, bf16[16,96,1024]{2,1,0:T(8,128)(2,1)}, u32[]{:S(2)}) copy-start(bf16[16,96,1024]{2,1,0:T(8,128)(2,1)} %get-tuple-element.43) | copy-start | bytes 9437188
  872.7 5.7 collective-permute-start.43
  878.5 6.2 collective-permute-start.46
  884.8 5.6 collective-permute-start.47
  894.6 20.5 %collective-permute-start.35 = (bf16[2,4,48,1024]{3,2,1,0:T(8,128)(2,1)S(1)}, bf16[2,4,48,1024]{3,2,1,0:T(8,128)(2,1)S(1)}, u32[]{:S(2)}, u32[]{:S(2)}) collective-permute-start(bf16[2,4,48,1024]{3,2,1,0:T(8,128)(2,1)S(1)} %slice_bitcast_fusion.6), channel_id=1, source_target_pairs={{0,2},{1,3},{2,0},{3,1},{4,6},{5,7},{6,4},{7,5},{8,10},{9,11},{10,... | collective-permute-start | bytes 2359304 | tf_op jit(solution)/shard_map/ppermute | solution.py:32
  896.7 20.5 %collective-permute-start.37 = (bf16[2,4,48,1024]{3,2,1,0:T(8,128)(2,1)S(1)}, bf16[2,4,48,1024]{3,2,1,0:T(8,128)(2,1)S(1)}, u32[]{:S(2)}, u32[]{:S(2)}) collective-permute-start(bf16[2,4,48,1024]{3,2,1,0:T(8,128)(2,1)S(1)} %slice_bitcast_fusion.4), channel_id=1, source_target_pairs={{0,4},{4,0},{8,12},{12,8},{16,20},{20,16},{24,28},{28,24},{1,5},{5... | collective-permute-start | bytes 2359304 | tf_op jit(solution)/shard_map/ppermute | solution.py:32
  899.3 32.4 %collective-permute-start.49 = (bf16[2,4,48,1024]{3,2,1,0:T(8,128)(2,1)S(1)}, bf16[2,4,48,1024]{3,2,1,0:T(8,128)(2,1)S(1)}, u32[]{:S(2)}, u32[]{:S(2)}) collective-permute-start(bf16[2,4,48,1024]{3,2,1,0:T(8,128)(2,1)S(1)} %slice_bitcast_fusion.2), channel_id=1, source_target_pairs={{0,2},{1,3},{2,0},{3,1},{4,6},{5,7},{6,4},{7,5},{8,10},{9,11},{10,... | collective-permute-start | bytes 2359304 | tf_op jit(solution)/shard_map/ppermute | solution.py:32
  900.7 31.7 %collective-permute-start.51 = (bf16[2,4,48,1024]{3,2,1,0:T(8,128)(2,1)S(1)}, bf16[2,4,48,1024]{3,2,1,0:T(8,128)(2,1)S(1)}, u32[]{:S(2)}, u32[]{:S(2)}) collective-permute-start(bf16[2,4,48,1024]{3,2,1,0:T(8,128)(2,1)S(1)} %slice_bitcast_fusion), channel_id=1, source_target_pairs={{0,4},{4,0},{8,12},{12,8},{16,20},{20,16},{24,28},{28,24},{1,5},{5... | collective-permute-start | bytes 2359304 | tf_op jit(solution)/shard_map/ppermute | solution.py:32
  918.0 17.9 %collective-permute-start.38 = (bf16[4,48,1024]{2,1,0:T(8,128)(2,1)S(1)}, bf16[4,48,1024]{2,1,0:T(8,128)(2,1)S(1)}, u32[]{:S(2)}, u32[]{:S(2)}) collective-permute-start(bf16[4,48,1024]{2,1,0:T(8,128)(2,1)S(1)} %slice_bitcast_fusion.16), channel_id=1, source_target_pairs={{0,2},{1,3},{2,0},{3,1},{4,6},{5,7},{6,4},{7,5},{8,10},{9,11},{10,... | collective-permute-start | bytes 1179656 | tf_op jit(solution)/shard_map/ppermute | solution.py:32
  918.1 18.4 %collective-permute-start.36 = (bf16[4,48,1024]{2,1,0:T(8,128)(2,1)S(1)}, bf16[4,48,1024]{2,1,0:T(8,128)(2,1)S(1)}, u32[]{:S(2)}, u32[]{:S(2)}) collective-permute-start(bf16[4,48,1024]{2,1,0:T(8,128)(2,1)S(1)} %slice_bitcast_fusion.18), channel_id=1, source_target_pairs={{0,4},{4,0},{8,12},{12,8},{16,20},{20,16},{24,28},{28,24},{1,5},{5... | collective-permute-start | bytes 1179656 | tf_op jit(solution)/shard_map/ppermute | solution.py:32
  933.1 7.8 collective-permute-start.52
  934.4 7.8 collective-permute-start.50
  936.8 11.7 %collective-permute-start.39 = (bf16[2,96,1024]{2,1,0:T(8,128)(2,1)S(1)}, bf16[2,96,1024]{2,1,0:T(8,128)(2,1)S(1)}, u32[]{:S(2)}, u32[]{:S(2)}) collective-permute-start(bf16[2,96,1024]{2,1,0:T(8,128)(2,1)S(1)} %pad_maximum_fusion.14), channel_id=1, source_target_pairs={{0,8},{4,12},{8,0},{12,4},{16,24},{20,28},{24,16},{28,20},{1,9},{5... | collective-permute-start | bytes 1179656 | tf_op jit(solution)/shard_map/ppermute | solution.py:32
  942.4 13.0 %collective-permute-start.53 = (bf16[2,96,1024]{2,1,0:T(8,128)(2,1)S(1)}, bf16[2,96,1024]{2,1,0:T(8,128)(2,1)S(1)}, u32[]{:S(2)}, u32[]{:S(2)}) collective-permute-start(bf16[2,96,1024]{2,1,0:T(8,128)(2,1)S(1)} %pad_maximum_fusion.13), channel_id=1, source_target_pairs={{0,8},{4,12},{8,0},{12,4},{16,24},{20,28},{24,16},{28,20},{1,9},{5... | collective-permute-start | bytes 1179656 | tf_op jit(solution)/shard_map/ppermute | solution.py:32
  948.6 8.8 collective-permute-start.40
  955.5 7.9 collective-permute-start.54
  (40 other events, 250.7 us)

commit v2 on v1

v2 whole, which is shorter than its diff:
```python
import jax
import jax.numpy as jnp
from jax import lax
from jax.experimental import pallas as pl
from jax.experimental.pallas import tpu as pltpu
from jax.sharding import PartitionSpec as P

EPSILON = 1e-05
HALF = jnp.bfloat16
SINGLE = jnp.float32
MAIN = 5
SEGMENTS = 8
MIB = 1 << 20


def log2(n):
    return n.bit_length() - 1


def device_number():
    return lax.axis_index("dp") * lax.axis_size("seq") + lax.axis_index("seq")


def low_bits():
    return log2(lax.axis_size("dp") * lax.axis_size("seq")) - MAIN


def exchange(values, bit):
    inner = log2(lax.axis_size("seq"))
    axis, place = ("seq", bit) if bit < inner else ("dp", bit - inner)
    count = lax.axis_size(axis)
    return lax.ppermute(values, axis, [(i, i ^ (1 << place)) for i in range(count)])


def gather_low(values):
    for bit in range(low_bits()):
        other = exchange(values, bit)
        upper = (device_number() >> bit) & 1
        values = jnp.where(
            upper == 1, jnp.concatenate([other, values]), jnp.concatenate([values, other])
        )
    return values


def reduce_low(values):
    for bit in reversed(range(low_bits())):
        upper = (device_number() >> bit) & 1
        halves = values.reshape((2, values.shape[0] // 2) + values.shape[1:])
        mine = lax.dynamic_index_in_dim(halves, upper, 0, False)
        theirs = lax.dynamic_index_in_dim(halves, 1 - upper, 0, False)
        values = mine + exchange(theirs, bit)
    return values


def join(own, other):
    return jnp.concatenate([own, other])


def gather_chunk(rows, split):
    base = low_bits()
    core, bit_x, bit_y, bit_z, bit_far = (base + i for i in range(MAIN))
    held = rows[None]
    held = join(held, exchange(held, bit_far))
    held = join(held, exchange(held, bit_z))
    first, second = held[:, :split], held[:, split:]
    parts = []
    if split:
        from_y = exchange(first, bit_y)
        from_x = exchange(second, bit_x)
        first, second = join(first, from_y), join(second, from_x)
        from_x = exchange(first, bit_x)
        from_y = exchange(second, bit_y)
        first, second = join(first, from_x), join(second, from_y)
        parts = [first, exchange(first, core), second, exchange(second, core)]
    else:
        second = join(second, exchange(second, bit_y))
        second = join(second, exchange(second, bit_x))
        parts = [second, exchange(second, core)]
    return parts


def spot(rel, x_first):
    core = rel & 1
    bit_x, bit_y = (rel >> 1) & 1, (rel >> 2) & 1
    bit_z, bit_far = (rel >> 3) & 1, (rel >> 4) & 1
    if x_first:
        return core, bit_x * 8 + bit_y * 4 + bit_z * 2 + bit_far
    return core, bit_y * 8 + bit_x * 4 + bit_z * 2 + bit_far


def load_weights(mine, parts, target, pieces, sems):
    def one(shard, carry):
        rel = shard ^ mine
        for pair, row, rows, group, held, to_row in pieces:
            core, k = spot(rel, pair == 0)
            to = target.at[group, pl.ds(pl.multiple_of(shard * held + to_row, 16), rows)]
            for side in range(2):

                @pl.when(core == side)
                def _():
                    source = parts[2 * pair + side].at[k, pl.ds(row, rows)]
                    pltpu.make_async_copy(source, to, sems.at[group]).start()

        return carry

    lax.fori_loop(0, 1 << MAIN, one, 0)


def await_weights(target, group, sems):
    pltpu.make_async_copy(target.at[group], target.at[group], sems.at[group]).wait()


REDUCE_PIECES = [(0, 0, 32, 0, 32, 0)]
STATE_PIECES = [(0, 32, 16, 0, 16, 0)]
VALUE_PIECES = [
    (0, 0, 32, 0, 32, 0),
    (0, 32, 16, 1, 32, 0),
    (1, 0, 16, 1, 32, 16),
    (1, 16, 32, 2, 32, 0),
]
EXPAND_PIECES = [(0, 0, 16, 0, 16, 0), (0, 16, 16, 1, 16, 0), (1, 0, 16, 2, 16, 0)]
OUT_PIECES = [(0, 0, 48, 0, 96, 0), (1, 0, 48, 0, 96, 48)]

SMEM = pl.BlockSpec(memory_space=pltpu.SMEM)
ANY = pl.BlockSpec(memory_space=pl.ANY)


def whole(*shape):
    return pl.BlockSpec(shape, lambda *_: (0,) * len(shape))


def dot(left, right, left_dim=1, right_dim=0):
    return lax.dot_general(
        left, right, (((left_dim,), (right_dim,)), ((), ())), preferred_element_type=SINGLE
    )


def gelu_pair(v):
    c, d = 0.7978845608028654, 0.7978845608028654 * 0.044715
    square = v * v
    h = 0.5 + 0.5 * jnp.tanh(v * (c + d * square))
    act = v * h
    return act, h + 2.0 * act * (1.0 - h) * (c + 3.0 * d * square)


def norm_terms(x):
    center = x - jnp.mean(x, axis=-1, keepdims=True)
    inverse = lax.rsqrt(jnp.mean(center * center, axis=-1, keepdims=True) + EPSILON)
    return center * inverse, inverse


def lanes_joined(ref, rows):
    return jnp.concatenate([ref[c, rows, :] for c in range(ref.shape[0])], axis=1)


def scan_block(ends_ref, first, decay, value_ref, product_ref, reverse):
    columns, block, lanes = value_ref.shape
    span = block // SEGMENTS
    decays = [
        jnp.broadcast_to(decay[:, c * lanes : (c + 1) * lanes], (SEGMENTS, lanes))
        for c in range(columns)
    ]

    def one(lap, carry):
        k = span - 1 - lap if reverse else lap
        mask = keep_mask(ends_ref, first + (k + 1 if reverse else k), (SEGMENTS, lanes), span)
        at = pl.ds(k, SEGMENTS, stride=span)
        states, products = [], []
        for c in range(columns):
            a = decays[c] * mask
            states.append(a * carry[0][c] + value_ref[c, at, :])
            products.append(a * carry[1][c])
        for c in range(columns):
            value_ref[c, at, :] = states[c]
            product_ref[c, at, :] = products[c]
        return (states, products)

    zero = [jnp.zeros((SEGMENTS, lanes), SINGLE)] * columns
    ones = [jnp.ones((SEGMENTS, lanes), SINGLE)] * columns
    states, products = lax.fori_loop(0, span, one, (zero, ones), unroll=4)
    return jnp.concatenate(products, axis=1), jnp.concatenate(states, axis=1)


def span_carries(product, state, carry, reverse):
    carries = [None] * SEGMENTS
    for s in range(SEGMENTS)[::-1] if reverse else range(SEGMENTS):
        carries[s] = carry
        carry = product[s : s + 1] * carry + state[s : s + 1]
    return carries, carry


def block_carry(place, maps_ref, reverse):
    count = maps_ref.shape[0]
    carry = jnp.zeros((1, maps_ref.shape[2]), SINGLE)
    for s in range(count)[::-1] if reverse else range(count):
        rel = s ^ place
        inside = s > place if reverse else s < place
        moved = maps_ref[rel, 0:1, :] * carry + maps_ref[rel, 1:2, :]
        carry = jnp.where(inside, moved, carry)
    return carry


def whole_map(product, state, reverse):
    zero = jnp.zeros((1, product.shape[1]), SINGLE)
    _, ending = span_carries(product, state, zero, reverse)
    through = zero + 1.0
    for s in range(SEGMENTS):
        through = through * product[s : s + 1]
    return through, ending


def gather_maps(maps):
    held = maps[None]
    for bit in range(log2(lax.axis_size("seq"))):
        held = join(held, exchange(held, bit))
    return held


def reduce_kernel(scalars, tokens, gain, shift, bias, decay, inflow, parts):
    block, width = tokens.shape
    channels = bias.shape[1]
    tile = 256
    columns = channels // 128

    def body(me, ends, base, x_ref, gain_ref, shift_ref, bias_ref, decay_ref, inflow_ref, p0, p1,
             normed_ref, act_ref, slope_ref, state_ref, product_ref, span_ref, map_ref,
             weight, sems):
        load_weights(me[0], (p0, p1), weight, REDUCE_PIECES, sems)
        for t in range(block // tile):
            rows = pl.ds(t * tile, tile)
            n, _ = norm_terms(x_ref[rows, :].astype(SINGLE))
            normed_ref[rows, :] = (n * gain_ref[...] + shift_ref[...]).astype(HALF)
        await_weights(weight, 0, sems)
        for t in range(block // tile):
            rows = pl.ds(t * tile, tile)
            act, slope = gelu_pair(dot(normed_ref[rows, :], weight[0]) + bias_ref[...])
            act_ref[rows, :] = act
            slope_ref[rows, :] = slope.astype(HALF)
            flow = act * inflow_ref[...]
            for c in range(columns):
                state_ref[c, rows, :] = flow[:, c * 128 : (c + 1) * 128]
        product, state = scan_block(ends, base[0], decay_ref[...], state_ref, product_ref, False)
        span_ref[0], span_ref[1] = product, state
        map_ref[0:1, :], map_ref[1:2, :] = whole_map(product, state, False)

    vm = pl.BlockSpec(memory_space=pltpu.VMEM)
    return pl.pallas_call(
        body,
        name="reduce_forward",
        out_shape=[
            jax.ShapeDtypeStruct((block, width), HALF),
            jax.ShapeDtypeStruct((block, channels), SINGLE),
            jax.ShapeDtypeStruct((block, channels), HALF),
            jax.ShapeDtypeStruct((columns, block, 128), SINGLE),
            jax.ShapeDtypeStruct((columns, block, 128), SINGLE),
            jax.ShapeDtypeStruct((2, SEGMENTS, channels), SINGLE),
            jax.ShapeDtypeStruct((2, channels), SINGLE),
        ],
        in_specs=[SMEM] * 3 + [vm] * 6 + [ANY] * 2,
        out_specs=[vm] * 7,
        scratch_shapes=[
            pltpu.VMEM((1, width, channels), HALF),
            pltpu.SemaphoreType.DMA((1,)),
        ],
        compiler_params=pltpu.CompilerParams(vmem_limit_bytes=40 * MIB),
        cost_estimate=pl.CostEstimate(
            flops=2 * block * width * channels,
            bytes_accessed=16 * MIB,
            transcendentals=block * channels,
        ),
    )(*scalars[:3], tokens, gain, shift, bias, decay, inflow, *parts)


def value_kernel(me, normed, bias, parts):
    block, width = normed.shape
    gate = bias.shape[1]
    tile, sub = 256, 256
    groups = gate // width

    def body(me, x_ref, bias_ref, p0, p1, p2, p3, act_ref, slope_ref, weight, sems):
        j, t = pl.program_id(0), pl.program_id(1)

        @pl.when((j == 0) & (t == 0))
        def _():
            load_weights(me[0], (p0, p1, p2, p3), weight, VALUE_PIECES, sems)

        for g in range(groups):

            @pl.when((j == g) & (t == 0))
            def _():
                await_weights(weight, g, sems)

        for c in range(width // sub):
            cols = pl.ds(c * sub, sub)
            pre = dot(x_ref[...], weight[j, :, cols]) + bias_ref[:, cols]
            act, slope = gelu_pair(pre)
            act_ref[:, cols] = act.astype(HALF)
            slope_ref[:, cols] = slope.astype(HALF)

    shape = jax.ShapeDtypeStruct((block, gate), HALF)
    spec = pl.BlockSpec((tile, width), lambda j, t: (t, j))
    return pl.pallas_call(
        body,
        name="value_forward",
        out_shape=[shape, shape],
        grid=(groups, block // tile),
        in_specs=[
            SMEM,
            pl.BlockSpec((tile, width), lambda j, t: (t, 0)),
            pl.BlockSpec((1, width), lambda j, t: (0, j)),
        ]
        + [ANY] * 4,
        out_specs=[spec, spec],
        scratch_shapes=[
            pltpu.VMEM((groups, width, width), HALF),
            pltpu.SemaphoreType.DMA((groups,)),
        ],
        compiler_params=pltpu.CompilerParams(vmem_limit_bytes=40 * MIB),
        cost_estimate=pl.CostEstimate(
            flops=2 * block * width * gate,
            bytes_accessed=20 * MIB,
            transcendentals=block * gate,
        ),
    )(me, normed, bias, *parts)


def expand_kernel(me, place, maps, spans, states, products, act, skip, inflow, bias, va, vd,
                  small_parts, parts):
    columns, block, _ = states.shape
    channels = act.shape[1]
    gate = bias.shape[1]
    tile, sub = 256, 512
    groups, width = 3, gate // 3
    span = block // SEGMENTS

    def body(me, place_ref, maps_ref, span_ref, state_ref, product_ref, act_ref, skip_ref,
             inflow_ref, bias_ref, va_ref, vd_ref, s0, s1, p0, p1, p2, p3,
             gated_ref, slope_ref, low_ref, prior_ref, ssm_ref,
             carry_ref, small, weight, small_sems, sems):
        t = pl.program_id(0)

        @pl.when(t == 0)
        def _():
            load_weights(me[0], (s0, s1), small, STATE_PIECES, small_sems)
            load_weights(me[0], (p0, p1, p2, p3), weight, EXPAND_PIECES, sems)
            entering = block_carry(place_ref[0], maps_ref, False)
            carries, _ = span_carries(span_ref[0], span_ref[1], entering, False)
            for s in range(SEGMENTS):
                carry_ref[s] = jnp.broadcast_to(carries[s], (8, channels))
            await_weights(small, 0, small_sems)
            for g in range(groups):
                await_weights(weight, g, sems)

        pieces = []
        for s in range(tile // span):
            rows = pl.ds(s * span, span)
            carry = carry_ref[t * (tile // span) + s][:1]
            pieces.append(
                lanes_joined(state_ref, rows) + lanes_joined(product_ref, rows) * carry
            )
        state = jnp.concatenate(pieces, axis=0)
        low = state.astype(HALF)
        low_ref[...] = low
        prior_ref[...] = (state - inflow_ref[...] * act_ref[...]).astype(HALF)
        ssm = (dot(low, small[0]) + skip_ref[...] * act_ref[...]).astype(HALF)
        ssm_ref[...] = ssm
        for g in range(groups):
            for c in range(width // sub):
                cols = pl.ds(g * width + c * sub, sub)
                pre = dot(ssm, weight[g, :, c * sub : (c + 1) * sub]) + bias_ref[:, cols]
                gated_ref[:, cols] = (va_ref[:, cols].astype(SINGLE) * pre).astype(HALF)
                slope_ref[:, cols] = (vd_ref[:, cols].astype(SINGLE) * pre).astype(HALF)

    tall = pl.BlockSpec((columns, tile, 128), lambda t: (0, t, 0))
    narrow = pl.BlockSpec((tile, channels), lambda t: (t, 0))
    wide = pl.BlockSpec((tile, gate), lambda t: (t, 0))
    return pl.pallas_call(
        body,
        name="expand_forward",
        out_shape=[jax.ShapeDtypeStruct((block, gate), HALF)] * 2
        + [jax.ShapeDtypeStruct((block, channels), HALF)] * 3,
        grid=(block // tile,),
        in_specs=[
            SMEM,
            SMEM,
            whole(*maps.shape),
            whole(*spans.shape),
            tall,
            tall,
            narrow,
            whole(1, channels),
            whole(1, channels),
            whole(1, gate),
            wide,
            wide,
        ]
        + [ANY] * 6,
        out_specs=[wide, wide, narrow, narrow, narrow],
        scratch_shapes=[
            pltpu.VMEM((SEGMENTS, 8, channels), SINGLE),
            pltpu.VMEM((1, channels, channels), HALF),
            pltpu.VMEM((groups, channels, width), HALF),
            pltpu.SemaphoreType.DMA((1,)),
            pltpu.SemaphoreType.DMA((groups,)),
        ],
        compiler_params=pltpu.CompilerParams(vmem_limit_bytes=48 * MIB),
        cost_estimate=pl.CostEstimate(
            flops=2 * block * channels * (gate + channels),
            bytes_accessed=36 * MIB,
            transcendentals=0,
        ),
    )(me, place, maps, spans, states, products, act, skip, inflow, bias, va, vd,
      *small_parts, *parts)


def out_kernel(me, live, base, gated, tokens, bias, parts):
    block, gate = gated.shape
    width = tokens.shape[1]
    tile = 256

    def body(me, live_ref, base_ref, gated_ref, x_ref, bias_ref, p0, p1, p2, p3,
             out_ref, weight, sems):
        t = pl.program_id(0)

        @pl.when(t == 0)
        def _():
            load_weights(me[0], (p0, p1, p2, p3), weight, OUT_PIECES, sems)
            await_weights(weight, 0, sems)

        place = base_ref[0] + t * tile + lax.broadcasted_iota(jnp.int32, (tile, 1), 0)
        branch = dot(gated_ref[...], weight[0]) + bias_ref[...]
        branch = jnp.where(place < live_ref[0], branch, 0.0)
        out_ref[...] = (x_ref[...].astype(SINGLE) + branch).astype(HALF)

    return pl.pallas_call(
        body,
        name="out_forward",
        out_shape=jax.ShapeDtypeStruct((block, width), HALF),
        grid=(block // tile,),
        in_specs=[
            SMEM,
            SMEM,
            SMEM,
            pl.BlockSpec((tile, gate), lambda t: (t, 0)),
            pl.BlockSpec((tile, width), lambda t: (t, 0)),
            whole(1, width),
        ]
        + [ANY] * 4,
        out_specs=pl.BlockSpec((tile, width), lambda t: (t, 0)),
        scratch_shapes=[
            pltpu.VMEM((1, gate, width), HALF),
            pltpu.SemaphoreType.DMA((1,)),
        ],
        compiler_params=pltpu.CompilerParams(vmem_limit_bytes=40 * MIB),
        cost_estimate=pl.CostEstimate(
            flops=2 * block * width * gate, bytes_accessed=16 * MIB, transcendentals=0
        ),
    )(me, live, base, gated, tokens, bias, *parts)


def fold(values):
    return jnp.sum(values.reshape(values.shape[0] // 8, 8, values.shape[1]), axis=0)


def gate_kernel(me, branch_grad, va, slope, parts):
    block, width = branch_grad.shape
    gate = va.shape[1]
    tile, sub = 256, 512

    def body(me, grad_ref, va_ref, slope_ref, p0, p1, p2, p3,
             expand_ref, value_ref, expand_sum, value_sum, weight, sems):
        t = pl.program_id(0)

        @pl.when(t == 0)
        def _():
            load_weights(me[0], (p0, p1, p2, p3), weight, OUT_PIECES, sems)
            expand_sum[...] = jnp.zeros_like(expand_sum)
            value_sum[...] = jnp.zeros_like(value_sum)
            await_weights(weight, 0, sems)

        grad = grad_ref[...]
        for c in range(gate // sub):
            cols = pl.ds(c * sub, sub)
            gated_grad = dot(grad, weight[0, c * sub : (c + 1) * sub, :], 1, 1)
            expand = gated_grad * va_ref[:, cols].astype(SINGLE)
            value = gated_grad * slope_ref[:, cols].astype(SINGLE)
            expand_ref[:, cols] = expand.astype(HALF)
            value_ref[:, cols] = value.astype(HALF)
            expand_sum[:, cols] += fold(expand)
            value_sum[:, cols] += fold(value)

    wide = pl.BlockSpec((tile, gate), lambda t: (t, 0))
    return pl.pallas_call(
        body,
        name="gate_backward",
        out_shape=[jax.ShapeDtypeStruct((block, gate), HALF)] * 2
        + [jax.ShapeDtypeStruct((8, gate), SINGLE)] * 2,
        grid=(block // tile,),
        in_specs=[SMEM, pl.BlockSpec((tile, width), lambda t: (t, 0)), wide, wide] + [ANY] * 4,
        out_specs=[wide, wide, whole(8, gate), whole(8, gate)],
        scratch_shapes=[
            pltpu.VMEM((1, gate, width), HALF),
            pltpu.SemaphoreType.DMA((1,)),
        ],
        compiler_params=pltpu.CompilerParams(vmem_limit_bytes=48 * MIB),
        cost_estimate=pl.CostEstimate(
            flops=2 * block * width * gate, bytes_accessed=32 * MIB, transcendentals=0
        ),
    )(me, branch_grad, va, slope, *parts)


def state_kernel(me, ends, base, expand_grad, act, decay, small_parts, parts):
    block, gate = expand_grad.shape
    channels = act.shape[1]
    tile = 256
    groups, width = 3, gate // 3
    columns = channels // 128

    def body(me, ends_ref, base_ref, grad_ref, act_ref, decay_ref, s0, s1, p0, p1, p2, p3,
             ssm_ref, total_ref, product_ref, span_ref, map_ref, skip_sum,
             small, weight, small_sems, sems):
        t = pl.program_id(0)

        @pl.when(t == 0)
        def _():
            load_weights(me[0], (s0, s1), small, STATE_PIECES, small_sems)
            load_weights(me[0], (p0, p1, p2, p3), weight, EXPAND_PIECES, sems)
            skip_sum[...] = jnp.zeros_like(skip_sum)
            await_weights(small, 0, small_sems)
            for g in range(groups):
                await_weights(weight, g, sems)

        ssm = dot(grad_ref[:, :width], weight[0], 1, 1)
        for g in range(1, groups):
            ssm += dot(grad_ref[:, g * width : (g + 1) * width], weight[g], 1, 1)
        low = ssm.astype(HALF)
        ssm_ref[...] = low
        skip_sum[...] += fold(ssm * act_ref[...])
        state = dot(low, small[0], 1, 1)
        rows = pl.ds(pl.multiple_of(t * tile, tile), tile)
        for c in range(columns):
            total_ref[c, rows, :] = state[:, c * 128 : (c + 1) * 128]

        @pl.when(t == block // tile - 1)
        def _():
            product, state = scan_block(
                ends_ref, base_ref[0], decay_ref[...], total_ref, product_ref, True
            )
            span_ref[0], span_ref[1] = product, state
            map_ref[0:1, :], map_ref[1:2, :] = whole_map(product, state, True)

    narrow = pl.BlockSpec((tile, channels), lambda t: (t, 0))
    return pl.pallas_call(
        body,
        name="state_backward",
        out_shape=[
            jax.ShapeDtypeStruct((block, channels), HALF),
            jax.ShapeDtypeStruct((columns, block, 128), SINGLE),
            jax.ShapeDtypeStruct((columns, block, 128), SINGLE),
            jax.ShapeDtypeStruct((2, SEGMENTS, channels), SINGLE),
            jax.ShapeDtypeStruct((2, channels), SINGLE),
            jax.ShapeDtypeStruct((8, channels), SINGLE),
        ],
        grid=(block // tile,),
        in_specs=[SMEM] * 3
        + [pl.BlockSpec((tile, gate), lambda t: (t, 0)), narrow, whole(1, channels)]
        + [ANY] * 6,
        out_specs=[
            narrow,
            whole(columns, block, 128),
            whole(columns, block, 128),
            whole(2, SEGMENTS, channels),
            whole(2, channels),
            whole(8, channels),
        ],
        scratch_shapes=[
            pltpu.VMEM((1, channels, channels), HALF),
            pltpu.VMEM((groups, channels, width), HALF),
            pltpu.SemaphoreType.DMA((1,)),
            pltpu.SemaphoreType.DMA((groups,)),
        ],
        compiler_params=pltpu.CompilerParams(vmem_limit_bytes=40 * MIB),
        cost_estimate=pl.CostEstimate(
            flops=2 * block * channels * (gate + channels),
            bytes_accessed=16 * MIB,
            transcendentals=0,
        ),
    )(me, ends, base, expand_grad, act, decay, *small_parts, *parts)


def input_kernel(me, place, maps, spans, totals, products, act, prior, ssm_grad, slope, skip,
                 inflow, gain, tokens, cotangent, value_grad, small_parts, parts):
    block, width = tokens.shape
    channels = act.shape[1]
    gate = value_grad.shape[1]
    tile = 256
    groups = gate // width
    columns = channels // 128
    span = block // SEGMENTS

    def body(me, place_ref, maps_ref, span_ref, total_ref, product_ref, act_ref, prior_ref,
             ssm_ref, slope_ref, skip_ref, inflow_ref, gain_ref, x_ref, cot_ref, value_ref,
             s0, s1, p0, p1, p2, p3,
             reduce_ref, out_ref, channel_sums, norm_sums,
             carry_ref, small, weight, small_sems, sems):
        t = pl.program_id(0)

        @pl.when(t == 0)
        def _():
            load_weights(me[0], (s0, s1), small, REDUCE_PIECES, small_sems)
            load_weights(me[0], (p0, p1, p2, p3), weight, VALUE_PIECES, sems)
            entering = block_carry(place_ref[0], maps_ref, True)
            carries, _ = span_carries(span_ref[0], span_ref[1], entering, True)
            for s in range(SEGMENTS):
                carry_ref[s] = jnp.broadcast_to(carries[s], (8, channels))
            channel_sums[...] = jnp.zeros_like(channel_sums)
            norm_sums[...] = jnp.zeros_like(norm_sums)

        pieces = []
        for s in range(tile // span):
            rows = pl.ds(s * span, span)
            carry = carry_ref[t * (tile // span) + s][:1]
            pieces.append(
                lanes_joined(total_ref, rows) + lanes_joined(product_ref, rows) * carry
            )
        total = jnp.concatenate(pieces, axis=0)
        channel_sums[0] += fold(total * prior_ref[...].astype(SINGLE))
        channel_sums[1] += fold(total * act_ref[...])
        reduced = ssm_ref[...].astype(SINGLE) * skip_ref[...] + inflow_ref[...] * total
        reduced = reduced * slope_ref[...].astype(SINGLE)
        channel_sums[2] += fold(reduced)
        low = reduced.astype(HALF)
        reduce_ref[...] = low

        @pl.when(t == 0)
        def _():
            await_weights(small, 0, small_sems)
            for g in range(groups):
                await_weights(weight, g, sems)

        grad = dot(low, small[0], 1, 1)
        for g in range(groups):
            grad += dot(value_ref[:, g * width : (g + 1) * width], weight[g], 1, 1)
        n, inverse = norm_terms(x_ref[...].astype(SINGLE))
        norm_sums[0] += fold(grad * n)
        norm_sums[1] += fold(grad)
        h = grad * gain_ref[...]
        mean_h = jnp.mean(h, axis=-1, keepdims=True)
        mean_hn = jnp.mean(h * n, axis=-1, keepdims=True)
        back = inverse * (h - mean_h - n * mean_hn)
        out_ref[...] = (cot_ref[...].astype(SINGLE) + back).astype(HALF)

    tall = pl.BlockSpec((columns, tile, 128), lambda t: (0, t, 0))
    narrow = pl.BlockSpec((tile, channels), lambda t: (t, 0))
    full = pl.BlockSpec((tile, width), lambda t: (t, 0))
    wide = pl.BlockSpec((tile, gate), lambda t: (t, 0))
    return pl.pallas_call(
        body,
        name="input_backward",
        out_shape=[
            jax.ShapeDtypeStruct((block, channels), HALF),
            jax.ShapeDtypeStruct((block, width), HALF),
            jax.ShapeDtypeStruct((3, 8, channels), SINGLE),
            jax.ShapeDtypeStruct((2, 8, width), SINGLE),
        ],
        grid=(block // tile,),
        in_specs=[
            SMEM,
            SMEM,
            whole(*maps.shape),
            whole(*spans.shape),
            tall,
            tall,
            narrow,
            narrow,
            narrow,
            narrow,
            whole(1, channels),
            whole(1, channels),
            whole(1, width),
            full,
            full,
            wide,
        ]
        + [ANY] * 6,
        out_specs=[narrow, full, whole(3, 8, channels), whole(2, 8, width)],
        scratch_shapes=[
            pltpu.VMEM((SEGMENTS, 8, channels), SINGLE),
            pltpu.VMEM((1, width, channels), HALF),
            pltpu.VMEM((groups, width, width), HALF),
            pltpu.SemaphoreType.DMA((1,)),
            pltpu.SemaphoreType.DMA((groups,)),
        ],
        compiler_params=pltpu.CompilerParams(vmem_limit_bytes=40 * MIB),
        cost_estimate=pl.CostEstimate(
            flops=2 * block * width * (gate + channels),
            bytes_accessed=30 * MIB,
            transcendentals=0,
        ),
    )(me, place, maps, spans, totals, products, act, prior, ssm_grad, slope, skip, inflow, gain,
      tokens, cotangent, value_grad, *small_parts, *parts)


def weight_grad(left, right, shard_rows, column_block, row_block, me, name):
    tokens, height = left.shape
    width = right.shape[1]
    column_blocks, row_blocks = width // column_block, height // row_block
    per_block = row_block // shard_rows
    half = 1 << (MAIN - 1)

    def body(me_ref, left_ref, right_ref, send_ref, keep_ref):
        mine = me_ref[0]
        product = lax.dot_general(
            left_ref[...], right_ref[...], (((0,), (0,)), ((), ())), preferred_element_type=SINGLE
        ).astype(HALF)
        for s in range(per_block):
            shard = pl.program_id(1) * per_block + s
            core, k = spot(shard ^ mine, True)
            part = product[s * shard_rows : (s + 1) * shard_rows]

            @pl.when(core == 1)
            def _():
                send_ref[k] = part

            @pl.when(core == 0)
            def _():
                keep_ref[k] = part

    shape = jax.ShapeDtypeStruct((half, column_blocks * shard_rows, column_block), HALF)
    spec = pl.BlockSpec((half, shard_rows, column_block), lambda j, i: (0, j, 0))
    return pl.pallas_call(
        body,
        name=name,
        out_shape=[shape, shape],
        grid=(column_blocks, row_blocks),
        in_specs=[
            pl.BlockSpec(memory_space=pltpu.SMEM),
            pl.BlockSpec((tokens, row_block), lambda j, i: (0, i)),
            pl.BlockSpec((tokens, column_block), lambda j, i: (0, j)),
        ],
        out_specs=[spec, spec],
        compiler_params=pltpu.CompilerParams(vmem_limit_bytes=48 * MIB),
        cost_estimate=pl.CostEstimate(
            flops=2 * tokens * height * width,
            bytes_accessed=2 * tokens * (height + width) + 2 * height * width,
            transcendentals=0,
        ),
    )(me, left, right)


def add_low(first, second):
    return (first.astype(SINGLE) + second.astype(SINGLE)).astype(HALF)


def reduce_chunk(send, keep, split):
    base = low_bits()
    core, bit_x, bit_y, bit_z, bit_far = (base + i for i in range(MAIN))
    rows, width = send.shape[1:]
    total = add_low(keep, exchange(send, core)).reshape(2, 2, 4, rows, width)
    second = total[:, :, :, split:]
    if split:
        first = total[:, :, :, :split]
        from_x = exchange(first[1], bit_x)
        from_y = exchange(second[:, 1], bit_y)
        first, second = add_low(first[0], from_x), add_low(second[:, 0], from_y)
        from_y = exchange(first[1], bit_y)
        from_x = exchange(second[1], bit_x)
        first, second = add_low(first[0], from_y), add_low(second[0], from_x)
        total = jnp.concatenate([first, second], axis=1)
    else:
        second = add_low(second[0], exchange(second[1], bit_x))
        total = add_low(second[0], exchange(second[1], bit_y))
    total = add_low(total[:2], exchange(total[2:], bit_z))
    return total[0].astype(SINGLE) + exchange(total[1], bit_far).astype(SINGLE)


def keep_mask(ends_ref, first, shape, span):
    place = first + lax.broadcasted_iota(jnp.int32, shape, 0) * span
    start = place == 0
    for i in range(7):
        start = start | (place == ends_ref[i])
    return jnp.where(start, 0.0, 1.0)


def decay_terms(rates):
    return (jnp.exp(-rates), jnp.sqrt(-jnp.expm1(-2.0 * rates)))


def column_sum(values):
    return jnp.sum(values.astype(SINGLE), axis=0)


def column_blocks(shard, width):
    return jnp.concatenate(
        [shard[:, i : i + width] for i in range(0, shard.shape[1], width)], axis=0
    )


def from_column_blocks(rows, count):
    height = rows.shape[0] // count
    return jnp.concatenate([rows[i * height : (i + 1) * height] for i in range(count)], axis=1)


def on_device(
    tokens,
    lengths,
    cotangent,
    norm_gain,
    norm_shift,
    value_weight,
    value_bias,
    reduce_weight,
    reduce_bias,
    decay_rates,
    skip_gain,
    state_weight,
    expand_weight,
    expand_bias,
    out_weight,
    out_bias,
):
    half, single = HALF, SINGLE
    shards = 1 << MAIN
    me = (device_number() >> low_bits()).reshape(1).astype(jnp.int32)
    low = lambda a: gather_low(a.astype(half))
    vectors = [
        low(v)
        for v in (
            norm_gain,
            norm_shift,
            value_bias,
            reduce_bias,
            decay_rates,
            skip_gain,
            expand_bias,
            out_bias,
        )
    ]
    sizes = [v.shape[0] for v in vectors]
    used = sum(sizes)
    reduce_shard, state_shard = low(reduce_weight), low(state_weight)
    value_shard, expand_shard, out_shard = low(value_weight), low(expand_weight), low(out_weight)
    channels = state_shard.shape[1]
    width = tokens.shape[-1]
    gate = value_shard.shape[1]
    blocks = gate // width

    vector_rows = jnp.pad(jnp.concatenate(vectors)[None], ((0, 7), (0, channels - used)))
    small = jnp.concatenate([reduce_shard, state_shard, vector_rows], axis=0)
    small_parts = gather_chunk(small, 0)
    value_parts = gather_chunk(column_blocks(value_shard, width), 48)
    expand_parts = gather_chunk(column_blocks(expand_shard, width), 32)
    out_parts = gather_chunk(out_shard, 48)

    row_count, block, _ = tokens.shape
    place = lax.axis_index("seq").reshape(1).astype(jnp.int32)
    base = place * block
    positions = base + jnp.arange(block, dtype=jnp.int32)
    ends = jnp.cumsum(lengths, axis=-1).reshape(-1)
    live = ends[-1:]
    token_rows, cot_rows = tokens.reshape(block, width), cotangent.reshape(block, width)
    branch_grad = jnp.where((positions < live)[:, None], cot_rows, jnp.zeros_like(cot_rows))
    grad_out_add = column_sum(branch_grad)

    k = jnp.arange(shards, dtype=jnp.int32) ^ me
    spots = (k & 1) * 16 + spot(k, True)[1]
    table = jnp.concatenate([p[:, 48] for p in small_parts])[spots].astype(single)
    places = [sum(sizes[:i]) for i in range(len(sizes))]
    gain, shift, value_add, reduce_add, rates, skip, expand_add, out_add = [
        table[:, p : p + n].reshape(1, -1) for p, n in zip(places, sizes)
    ]
    decays, inflow = decay_terms(rates)

    normed, act, reduce_slope, states, products, spans, own_map = reduce_kernel(
        (me, ends, base), token_rows, gain, shift, reduce_add, decays, inflow, small_parts
    )
    maps = gather_maps(own_map)
    value_act, value_slope = value_kernel(me, normed, value_add, value_parts)
    gated, gate_slope, states_low, prior, ssm_low = expand_kernel(
        me, place, maps, spans, states, products, act, skip, inflow, expand_add, value_act,
        value_slope, small_parts, expand_parts
    )
    out_grads = weight_grad(gated, branch_grad, 96, width, 768, me, "grad_out")
    out_sum = reduce_chunk(*out_grads, 48)

    expand_grad, value_grad, expand_fold, value_fold = gate_kernel(
        me, branch_grad, value_act, gate_slope, out_parts
    )
    value_grads = weight_grad(normed, value_grad, 32, width, 512, me, "grad_value")
    value_sum = reduce_chunk(*value_grads, 48)
    expand_grads = weight_grad(ssm_low, expand_grad, 16, width, 512, me, "grad_expand")
    expand_sum = reduce_chunk(*expand_grads, 32)
    ssm_grad, totals, suffixes, back_spans, back_map, skip_fold = state_kernel(
        me, ends, base, expand_grad, act, decays, small_parts, expand_parts
    )
    back_maps = gather_maps(back_map)
    state_send, state_keep = weight_grad(states_low, ssm_grad, 16, channels, 512, me, "grad_state")
    reduce_grad, grad_tokens, channel_folds, norm_folds = input_kernel(
        me, place, back_maps, back_spans, totals, suffixes, act, prior, ssm_grad, reduce_slope,
        skip, inflow, gain, token_rows, cot_rows, value_grad, small_parts, value_parts
    )
    reduce_send, reduce_keep = weight_grad(
        normed, reduce_grad, 32, channels, 512, me, "grad_reduce"
    )
    output = out_kernel(me, live, base, gated, token_rows, out_add, out_parts)

    decay_sum, inflow_sum, grad_reduce_add = jnp.sum(channel_folds, axis=1)
    grad_scale, grad_offset = jnp.sum(norm_folds, axis=1)
    inflow_pull = jnp.exp(-2.0 * rates[0]) / inflow[0]
    grad_rates = inflow_pull * inflow_sum - decay_sum
    grad_skip = jnp.sum(skip_fold, axis=0)
    grad_expand_add, grad_value_add = jnp.sum(expand_fold, axis=0), jnp.sum(value_fold, axis=0)

    sums = (
        grad_scale,
        grad_offset,
        grad_value_add,
        grad_reduce_add,
        grad_rates,
        grad_skip,
        grad_expand_add,
        grad_out_add,
    )
    table = jnp.concatenate([v.reshape(shards, -1) for v in sums], axis=1).astype(half)
    table = jnp.pad(table[:, None], ((0, 0), (0, 7), (0, channels - used)))
    k = jnp.arange(shards // 2, dtype=jnp.int32)
    rel = ((k >> 3) & 1) * 2 + ((k >> 2) & 1) * 4 + ((k >> 1) & 1) * 8 + (k & 1) * 16
    small_sum = reduce_chunk(
        jnp.concatenate([reduce_send, state_send, table[(rel + 1) ^ me]], axis=1),
        jnp.concatenate([reduce_keep, state_keep, table[rel ^ me]], axis=1),
        0,
    )
    vector_sum = small_sum[48]
    vector_sums = [reduce_low(vector_sum[p : p + n]) for p, n in zip(places, sizes)]
    return (
        output.reshape(tokens.shape),
        grad_tokens.reshape(tokens.shape),
        vector_sums[0],
        vector_sums[1],
        reduce_low(from_column_blocks(value_sum, blocks)),
        vector_sums[2],
        reduce_low(small_sum[:32]),
        vector_sums[3],
        vector_sums[4],
        vector_sums[5],
        reduce_low(small_sum[32:48]),
        reduce_low(from_column_blocks(expand_sum, blocks)),
        vector_sums[6],
        reduce_low(out_sum),
        vector_sums[7],
    )


def solution(mesh):
    rows, vector, matrix = P("dp", "seq", None), P(("dp", "seq")), P(("dp", "seq"), None)
    return jax.shard_map(
        on_device,
        mesh=mesh,
        in_specs=(
            rows,
            P("dp", None),
            rows,
            vector,
            vector,
            matrix,
            vector,
            matrix,
            vector,
            vector,
            vector,
            matrix,
            matrix,
            vector,
            matrix,
            vector,
        ),
        out_specs=(
            rows,
            rows,
            vector,
            vector,
            matrix,
            vector,
            matrix,
            vector,
            vector,
            vector,
            matrix,
            matrix,
            vector,
            matrix,
            vector,
        ),
        check_vma=False,
    )
```

time: 974 us -> 455 us (0.47)
  Pallas kernels: 605 us -> 155 us
  matrix products: 80.2 us -> 0 us
  local copies, waits for them, and re-layouts: 23.7 us -> 45.6 us
  waiting for transfers between devices: 125 us -> 140 us
  other arithmetic: 59.8 us -> 45.4 us
  blocking collectives: 10.4 us -> 0 us
    pallas_call x6 -> x7, Pallas kernels: 561 us -> 118 us  [the longest x1 21.9 us: input_kernel(): pl.pallas_call(body, name='input_backward', out_shape=[jax.ShapeDtypeStru...]
    dot_general x10 -> x0, matrix products: 80.2 us -> none  [the longest x1 22.8 us: on_device(): jnp.einsum('td,gd->tg', branch_grad, out_mat, preferred_element_type=single)]
    unnamed x101 -> x143, local copies, waits for them, and re-layouts: 9.31 us -> 29.7 us
    ppermute x55 -> x59, waiting for transfers between devices: 125 us -> 140 us  [exchange(): lax.ppermute(values, axis, [(i, i ^ 1 << place) for i in range(count)])]
    all_gather x2 -> x0, blocking collectives: 10.4 us -> none  [carried_in(): gathered = lax.all_gather(jnp.stack([through, ending]), 'seq')]
    ppermute x55 -> x59, starting transfers between devices: 58.3 us -> 61.1 us  [exchange(): lax.ppermute(values, axis, [(i, i ^ 1 << place) for i in range(count)])]
  transfers between devices with their start and end apart: 55 -> 59, of which waited for: 28 -> 25; matrix products, arithmetic and copies ran while one was open for 12% -> 12% of each run, Pallas kernels for 40% -> 27%
where the time goes in v2:
time: 455 us; the launch traced here: 450 us
  Pallas kernels  155 us (34%)
  waiting for transfers between devices  140 us (31%)
  starting transfers between devices  61.1 us (13%)
  local copies, waits for them, and re-layouts  45.6 us (10%)
  other arithmetic  45.4 us (10%)
    ppermute x59, waiting for transfers between devices, exchange(): lax.ppermute(values, axis, [(i, i ^ 1 << place) for i in range(count)])  140 us
    ppermute x59, starting transfers between devices, exchange(): lax.ppermute(values, axis, [(i, i ^ 1 << place) for i in range(count)])  61.1 us
    pallas_call x5, Pallas kernels, weight_grad(): pl.pallas_call(body, name=name, out_shape=[shape, shape], grid=(column_bl...  36.7 us
    unnamed x143, local copies, waits for them, and re-layouts  29.7 us
    pallas_call x1, Pallas kernels, input_kernel(): pl.pallas_call(body, name='input_backward', out_shape=[jax.ShapeDtypeStru...  21.9 us
    pallas_call x1, Pallas kernels, value_kernel(): pl.pallas_call(body, name='value_forward', out_shape=[shape, shape], grid...  21.7 us
    pallas_call x1, Pallas kernels, gate_kernel(): pl.pallas_call(body, name='gate_backward', out_shape=[jax.ShapeDtypeStruc...  17.6 us
    pallas_call x1, Pallas kernels, expand_kernel(): pl.pallas_call(body, name='expand_forward', out_shape=[jax.ShapeDtypeStru...  16.8 us
  transfers between devices with their start and end apart: 59, of which 25 were waited for; matrix products, arithmetic and copies ran while one was open for 12% of the time, Pallas kernels for 27%

profile of v2, /device:TPU:0, one launch (start us, length us, event | category | flops | bytes accessed | tf_op | source)
XLA Modules:
  0.0 449.5 jit_solution(15977000193820811205)
XLA Ops:
  7.8 4.1 collective-permute-start
  14.0 3.0 collective-permute-start.7
  20.8 1.9 fusion.40
  23.4 2.8 collective-permute-start.1
  26.8 3.0 collective-permute-done.15
  29.9 9.1 %collective-permute-done.1 = bf16[2,56,512]{2,1,0:T(8,128)(2,1)S(1)} collective-permute-done((bf16[2,56,512]{2,1,0:T(8,128)(2,1)S(1)}, bf16[2,56,512]{2,1,0:T(8,128)(2,1)S(1)}, u32[]{:S(2)}, u32[]{:S(2)}) %collective-permute-start.1) | collective-permute-done | bytes 114720 | tf_op jit(solution)/shard_map/ppermute | solution.py:32
  39.0 1.7 collective-permute-start.2
  41.5 2.1 collective-permute-start.24
  46.8 6.7 %collective-permute-done.8 = bf16[2,96,1024]{2,1,0:T(8,128)(2,1)S(1)} collective-permute-done((bf16[2,96,1024]{2,1,0:T(8,128)(2,1)S(1)}, bf16[2,96,1024]{2,1,0:T(8,128)(2,1)S(1)}, u32[]{:S(2)}, u32[]{:S(2)}) %collective-permute-start.8) | collective-permute-done | bytes 393248 | tf_op jit(solution)/shard_map/ppermute | solution.py:32
  55.7 3.5 collective-permute-done.24
  59.3 1.6 collective-permute-start.28
  61.6 6.8 %collective-permute-done.12 = bf16[4,48,1024]{2,1,0:T(8,128)(2,1)S(1)} collective-permute-done((bf16[4,48,1024]{2,1,0:T(8,128)(2,1)S(1)}, bf16[4,48,1024]{2,1,0:T(8,128)(2,1)S(1)}, u32[]{:S(2)}, u32[]{:S(2)}) %collective-permute-start.12) | collective-permute-done | bytes 393248 | tf_op jit(solution)/shard_map/ppermute | solution.py:32
  70.7 1.6 collective-permute-start.10
  73.0 3.8 collective-permute-done.28
  82.2 20.7 %collective-permute-done.25 = bf16[4,48,1024]{2,1,0:T(8,128)(2,1)S(1)} collective-permute-done((bf16[4,48,1024]{2,1,0:T(8,128)(2,1)S(1)}, bf16[4,48,1024]{2,1,0:T(8,128)(2,1)S(1)}, u32[]{:S(2)}, u32[]{:S(2)}) %collective-permute-start.25) | collective-permute-done | bytes 393248 | tf_op jit(solution)/shard_map/ppermute | solution.py:32
  107.6 8.0 %collective-permute-done.29 = bf16[8,48,1024]{2,1,0:T(8,128)(2,1)S(1)} collective-permute-done((bf16[8,48,1024]{2,1,0:T(8,128)(2,1)S(1)}, bf16[8,48,1024]{2,1,0:T(8,128)(2,1)S(1)}, u32[]{:S(2)}, u32[]{:S(2)}) %collective-permute-start.29) | collective-permute-done | bytes 786464 | tf_op jit(solution)/shard_map/ppermute | solution.py:32
  122.2 1.6 copy-done.12
  123.8 10.9 %reduce_forward.1 = (bf16[1024,1024]{1,0:T(8,128)(2,1)S(1)}, f32[1024,512]{1,0:T(8,128)S(1)}, bf16[1024,512]{1,0:T(8,128)(2,1)S(1)}, f32[4,1024,128]{2,1,0:T(8,1...) custom-call(s32[1]{0:T(128)} %bitcast.me.me_ref, s32[8]{0:T(128)S(1)} %bitcast.203, ...), custom_call_target="tpu_custom_call" | custom-call | flops 1073741824 | bytes 16777216 | tf_op jit(solution)/shard_map/reduce_forward/pallas_call | solution.py:247
  137.6 3.2 pad_maximum_fusion.2.p0
  141.4 1.6 collective-permute-start.6
  143.0 2.1 pad_maximum_fusion.4.p0
  145.2 1.8 pad_maximum_fusion.12.p2
  148.6 1.6 copy-done.43
  150.2 21.7 %value_forward.1 = (bf16[1024,3072]{1,0:T(8,128)(2,1)}, bf16[1024,3072]{1,0:T(8,128)(2,1)}) custom-call(s32[1]{0:T(128)} %bitcast.me.me_ref, bf16[1024,1024]{1,0:T(8,128)(2,1)S(1)} %copy-done.43, f32[1,3072]{1,0:T(1,128)S(1)} %reshape.475.bias_ref, bf16[16,48,1024]{2,1,0:T(8,128)(2,1)S(1)} %pad_maximum_fusion.p0, ...), custom_call_target="tpu_custom_call" | custom-call | flops 6442450944 | bytes 20971520 | tf_op jit(solution)/shard_map/value_forward/pallas_call | solution.py:302
  171.9 16.8 %expand_forward.1 = (bf16[1024,3072]{1,0:T(8,128)(2,1)}, bf16[1024,3072]{1,0:T(8,128)(2,1)}, bf16[1024,512]{1,0:T(8,128)(2,1)S(1)}, bf16[1024,512]{1,0:T(8,128)(2,1)S(1)}, bf16[1024,512]{1,0:T(8,128)(2,1)S(1)}) custom-call(s32[1]{0:T(128)} %bitcast.me.me_ref, s32[1]{0:T(128)} %bitcast.2.place_ref, f32[4,2,512]{2,1,0:T(2,128)S(1)} %pad_maximum_fusion.28.maps_ref, ...), custom_call_target="tpu_custom_call" | custom-call | flops 3758096384 | bytes 37748736 | tf_op jit(solution)/shard_map/expand_forward/pallas_call | solution.py:377
  189.8 17.6 %gate_backward.1 = (bf16[1024,3072]{1,0:T(8,128)(2,1)}, bf16[1024,3072]{1,0:T(8,128)(2,1)}, f32[8,3072]{1,0:T(8,128)S(1)}, f32[8,3072]{1,0:T(8,128)S(1)}) custom-call(s32[1]{0:T(128)} %bitcast.me.me_ref, bf16[1024,1024]{1,0:T(8,128)(2,1)} %get-tuple-element.96.grad_ref.right_ref, bf16[1024,3072]{1,0:T(8,128)(2,1)} %get-tuple-element.59.va_ref, ...), custom_call_target="tpu_custom_call" | custom-call | flops 6442450944 | bytes 33554432 | tf_op jit(solution)/shard_map/gate_backward/pallas_call | solution.py:493
  208.1 16.1 %state_backward.1 = (bf16[1024,512]{1,0:T(8,128)(2,1)S(1)}, f32[4,1024,128]{2,1,0:T(8,128)S(1)}, f32[4,1024,128]{2,1,0:T(8,128)S(1)}, f32[2,8,512]{2,1,0:T(8,128...) custom-call(s32[1]{0:T(128)} %bitcast.me.me_ref, s32[8]{0:T(128)S(1)} %bitcast.204, s32[1]{0:T(128)} %mul.141.base.base_ref, ...), custom_call_target="tpu_custom_call" | custom-call | flops 3758096384 | bytes 16777216 | tf_op jit(solution)/shard_map/state_backward/pallas_call | solution.py:553
  226.8 8.3 %grad_expand.1 = (bf16[16,48,1024]{2,1,0:T(8,128)(2,1)}, bf16[16,48,1024]{2,1,0:T(8,128)(2,1)S(1)}) custom-call(s32[1]{0:T(128)} %bitcast.me.me_ref, bf16[1024,512]{1,0:T(8,128)(2,1)S(1)} %get-tuple-element.86.left_ref, bf16[1024,3072]{1,0:T(8,128)(2,1)} %get-tuple-element.63.grad_ref.right_ref), custom_call_target="tpu_custom_call" | custom-call | flops 3221225472 | bytes 10485760 | tf_op jit(solution)/shard_map/grad_expand/pallas_call | solution.py:731
  248.0 1.6 copy-done.17
  254.1 21.9 %input_backward.1 = (bf16[1024,512]{1,0:T(8,128)(2,1)S(1)}, bf16[1024,1024]{1,0:T(8,128)(2,1)}, f32[3,8,512]{2,1,0:T(8,128)S(1)}, f32[2,8,1024]{2,1,0:T(8,128)S(1)}) custom-call(s32[1]{0:T(128)} %bitcast.me.me_ref, s32[1]{0:T(128)} %bitcast.2.place_ref, f32[4,2,512]{2,1,0:T(2,128)S(1)} %pad_maximum_fusion.29.maps_ref, ...), custom_call_target="tpu_custom_call" | custom-call | flops 7516192768 | bytes 31457280 | tf_op jit(solution)/shard_map/input_backward/pallas_call | solution.py:657
  278.3 1.6 copy-done.44
  279.9 2.1 grad_reduce.1
  284.4 1.7 copy-done.45
  286.2 12.9 %grad_value.1 = (bf16[16,96,1024]{2,1,0:T(8,128)(2,1)}, bf16[16,96,1024]{2,1,0:T(8,128)(2,1)}) custom-call(s32[1]{0:T(128)} %bitcast.me.me_ref, bf16[1024,1024]{1,0:T(8,128)(2,1)S(1)} %copy-done.45, bf16[1024,3072]{1,0:T(8,128)(2,1)} %get-tuple-element.71.value_ref.right_ref), custom_call_target="tpu_custom_call" | custom-call | flops 6442450944 | bytes 14680064 | tf_op jit(solution)/shard_map/grad_value/pallas_call | solution.py:731
  299.5 12.2 %grad_out.1 = (bf16[16,96,1024]{2,1,0:T(8,128)(2,1)}, bf16[16,96,1024]{2,1,0:T(8,128)(2,1)}) custom-call(s32[1]{0:T(128)} %bitcast.me.me_ref, bf16[1024,3072]{1,0:T(8,128)(2,1)} %get-tuple-element.61.gated_ref.left_ref, bf16[1024,1024]{1,0:T(8,128)(2,1)S(1)} %copy-done.20), custom_call_target="tpu_custom_call" | custom-call | flops 6442450944 | bytes 14680064 | tf_op jit(solution)/shard_map/grad_out/pallas_call | solution.py:731
  314.2 13.3 %out_forward.1 = bf16[1024,1024]{1,0:T(8,128)(2,1)} custom-call(s32[1]{0:T(128)} %bitcast.me.me_ref, s32[1]{0:T(128)} %bitcast.1.live_ref, s32[1]{0:T(128)} %mul.141.base.base_ref, bf16[1024,3072]{1,0:T(8,128)(2,1)} %get-tuple-element.61.gated_ref.left_ref, bf16[1024,1024]{1,0:T(8,128)(2,1)S(1)} %bitcast.196, f32[1,1024]{1,0:T(1,128)S(1)} %copy-done.37, ...), custom_call_target="tpu_custom_call" | custom-call | flops 6442450944 | bytes 16777216 | tf_op jit(solution)/shard_map/out_forward/pallas_call | solution.py:435
  327.7 1.8 collective-permute-start.35
  329.5 2.1 add_convert_fusion.2
  331.6 4.0 collective-permute-done.35
  335.8 1.8 collective-permute-start.48
  337.6 2.9 collective-permute-done.36
  340.6 2.9 collective-permute-start.37
  344.1 1.6 collective-permute-done.37
  346.5 11.0 %collective-permute-done.46 = bf16[2,4,32,1024]{3,2,1,0:T(8,128)(2,1)S(1)} collective-permute-done((bf16[2,4,32,1024]{3,2,1,0:T(8,128)(2,1)S(1)}, bf16[2,4,32,1024]{3,2,1,0:T(8,128)(2,1)S(1)}, u32[]{:S(2)}, u32[]{:S(2)}) %collective-permute-start.46) | collective-permute-done | bytes 524320 | tf_op jit(solution)/shard_map/ppermute | solution.py:32
  357.8 1.8 collective-permute-start.47
  360.2 4.0 collective-permute-done.47
  366.3 4.8 %collective-permute-done.50 = bf16[2,48,1024]{2,1,0:T(8,128)(2,1)S(1)} collective-permute-done((bf16[2,48,1024]{2,1,0:T(8,128)(2,1)S(1)}, bf16[2,48,1024]{2,1,0:T(8,128)(2,1)S(1)}, u32[]{:S(2)}, u32[]{:S(2)}) %collective-permute-start.50) | collective-permute-done | bytes 196640 | tf_op jit(solution)/shard_map/ppermute | solution.py:32
  373.4 4.2 collective-permute-done.51
  378.3 3.4 add_convert_fusion.1
  382.2 1.8 collective-permute-start.41
  384.0 3.4 add_convert_fusion
  387.5 1.8 collective-permute-start.53
  389.7 12.6 %collective-permute-done.39 = bf16[2,4,48,1024]{3,2,1,0:T(8,128)(2,1)S(1)} collective-permute-done((bf16[2,4,48,1024]{3,2,1,0:T(8,128)(2,1)S(1)}, bf16[2,4,48,1024]{3,2,1,0:T(8,128)(2,1)S(1)}, u32[]{:S(2)}, u32[]{:S(2)}) %collective-permute-start.39) | collective-permute-done | bytes 786464 | tf_op jit(solution)/shard_map/ppermute | solution.py:32
  403.5 1.8 collective-permute-start.42
  405.4 1.8 collective-permute-start.40
  407.2 11.2 %collective-permute-done.53 = bf16[2,4,48,1024]{3,2,1,0:T(8,128)(2,1)S(1)} collective-permute-done((bf16[2,4,48,1024]{3,2,1,0:T(8,128)(2,1)S(1)}, bf16[2,4,48,1024]{3,2,1,0:T(8,128)(2,1)S(1)}, u32[]{:S(2)}, u32[]{:S(2)}) %collective-permute-start.53) | collective-permute-done | bytes 786464 | tf_op jit(solution)/shard_map/ppermute | solution.py:32
  419.3 1.8 collective-permute-start.56
  421.1 1.8 collective-permute-start.54
  424.6 2.6 collective-permute-done.56
  427.3 1.7 collective-permute-done.54
  429.9 5.3 %collective-permute-done.43 = bf16[2,96,1024]{2,1,0:T(8,128)(2,1)S(1)} collective-permute-done((bf16[2,96,1024]{2,1,0:T(8,128)(2,1)S(1)}, bf16[2,96,1024]{2,1,0:T(8,128)(2,1)S(1)}, u32[]{:S(2)}, u32[]{:S(2)}) %collective-permute-start.43) | collective-permute-done | bytes 393248 | tf_op jit(solution)/shard_map/ppermute | solution.py:32
  435.4 4.0 collective-permute-done.57
  439.6 4.4 collective-permute-done.44
  444.9 3.4 collective-permute-done.58
  (366 shorter events, 90.5 us)
Async XLA Ops:
  7.8 15.6 %collective-permute-start = (bf16[1,56,512]{2,1,0:T(8,128)(2,1)S(1)}, bf16[1,56,512]{2,1,0:T(8,128)(2,1)S(1)}, u32[]{:S(2)}, u32[]{:S(2)}) collective-permute-start(bf16[1,56,512]{2,1,0:T(8,128)(2,1)S(1)} %fusion.23), channel_id=1, source_target_pairs={{0,16},{4,20},{8,24},{12,28},{16,0},{20,4},{24,8},{28,12},{1,17},{... | collective-permute-start | bytes 172040 | tf_op jit(solution)/shard_map/ppermute | solution.py:32
  12.9 16.9 %collective-permute-start.15 = (bf16[1,48,1024]{2,1,0:T(8,128)(2,1)S(1)}, bf16[1,48,1024]{2,1,0:T(8,128)(2,1)S(1)}, u32[]{:S(2)}, u32[]{:S(2)}) collective-permute-start(bf16[1,48,1024]{2,1,0:T(8,128)(2,1)S(1)} %maximum_bitcast_fusion.1), channel_id=1, source_target_pairs={{0,16},{4,20},{8,24},{12,28},{16,0},{20,4},{24,8},{28,12},{1,17},{... | collective-permute-start | bytes 294920 | tf_op jit(solution)/shard_map/ppermute | solution.py:32
  14.0 27.3 %collective-permute-start.7 = (bf16[1,96,1024]{2,1,0:T(8,128)(2,1)S(1)}, bf16[1,96,1024]{2,1,0:T(8,128)(2,1)S(1)}, u32[]{:S(2)}, u32[]{:S(2)}) collective-permute-start(bf16[1,96,1024]{2,1,0:T(8,128)(2,1)S(1)} %maximum_bitcast_fusion), channel_id=1, source_target_pairs={{0,16},{4,20},{8,24},{12,28},{16,0},{20,4},{24,8},{28,12},{1,17},{... | collective-permute-start | bytes 589832 | tf_op jit(solution)/shard_map/ppermute | solution.py:32
  18.0 23.4 %collective-permute-start.23 = (bf16[1,96,1024]{2,1,0:T(8,128)(2,1)S(1)}, bf16[1,96,1024]{2,1,0:T(8,128)(2,1)S(1)}, u32[]{:S(2)}, u32[]{:S(2)}) collective-permute-start(bf16[1,96,1024]{2,1,0:T(8,128)(2,1)S(1)} %convert_bitcast_fusion), channel_id=1, source_target_pairs={{0,16},{4,20},{8,24},{12,28},{16,0},{20,4},{24,8},{28,12},{1,17},{... | collective-permute-start | bytes 589832 | tf_op jit(solution)/shard_map/ppermute | solution.py:32
  19.0 102.1 %copy-start.46 = (s32[1,8]{1,0:T(1,128)}, s32[1,8]{1,0:T(1,128)S(1)}, u32[]{:S(2)}) copy-start(s32[1,8]{1,0:T(1,128)S(1)} %reduce_window_sum.11) | copy-start | bytes 100
  23.4 15.5 %collective-permute-start.1 = (bf16[2,56,512]{2,1,0:T(8,128)(2,1)S(1)}, bf16[2,56,512]{2,1,0:T(8,128)(2,1)S(1)}, u32[]{:S(2)}, u32[]{:S(2)}) collective-permute-start(bf16[2,56,512]{2,1,0:T(8,128)(2,1)S(1)} %pad_maximum_fusion.26), channel_id=1, source_target_pairs={{0,8},{4,12},{8,0},{12,4},{16,24},{20,28},{24,16},{28,20},{1,9},{5... | collective-permute-start | bytes 344072 | tf_op jit(solution)/shard_map/ppermute | solution.py:32
  29.8 13.7 %collective-permute-start.16 = (bf16[2,48,1024]{2,1,0:T(8,128)(2,1)S(1)}, bf16[2,48,1024]{2,1,0:T(8,128)(2,1)S(1)}, u32[]{:S(2)}, u32[]{:S(2)}) collective-permute-start(bf16[2,48,1024]{2,1,0:T(8,128)(2,1)S(1)} %pad_maximum_fusion.23), channel_id=1, source_target_pairs={{0,8},{4,12},{8,0},{12,4},{16,24},{20,28},{24,16},{28,20},{1,9},{5... | collective-permute-start | bytes 589832 | tf_op jit(solution)/shard_map/ppermute | solution.py:32
  39.0 6.2 %collective-permute-start.2 = (bf16[4,56,512]{2,1,0:T(8,128)(2,1)S(1)}, bf16[4,56,512]{2,1,0:T(8,128)(2,1)S(1)}, u32[]{:S(2)}, u32[]{:S(2)}) collective-permute-start(bf16[4,56,512]{2,1,0:T(8,128)(2,1)S(1)} %pad_maximum_fusion.21), channel_id=1, source_target_pairs={{0,4},{4,0},{8,12},{12,8},{16,20},{20,16},{24,28},{28,24},{1,5},{5... | collective-permute-start | bytes 688136 | tf_op jit(solution)/shard_map/ppermute | solution.py:32
  41.3 12.1 %collective-permute-start.8 = (bf16[2,96,1024]{2,1,0:T(8,128)(2,1)S(1)}, bf16[2,96,1024]{2,1,0:T(8,128)(2,1)S(1)}, u32[]{:S(2)}, u32[]{:S(2)}) collective-permute-start(bf16[2,96,1024]{2,1,0:T(8,128)(2,1)S(1)} %pad_maximum_fusion.16), channel_id=1, source_target_pairs={{0,8},{4,12},{8,0},{12,4},{16,24},{20,28},{24,16},{28,20},{1,9},{5... | collective-permute-start | bytes 1179656 | tf_op jit(solution)/shard_map/ppermute | solution.py:32
  41.5 17.6 %collective-permute-start.24 = (bf16[2,96,1024]{2,1,0:T(8,128)(2,1)S(1)}, bf16[2,96,1024]{2,1,0:T(8,128)(2,1)S(1)}, u32[]{:S(2)}, u32[]{:S(2)}) collective-permute-start(bf16[2,96,1024]{2,1,0:T(8,128)(2,1)S(1)} %pad_maximum_fusion.18), channel_id=1, source_target_pairs={{0,8},{4,12},{8,0},{12,4},{16,24},{20,28},{24,16},{28,20},{1,9},{5... | collective-permute-start | bytes 1179656 | tf_op jit(solution)/shard_map/ppermute | solution.py:32
  43.6 34.5 %collective-permute-start.20 = (bf16[4,16,1024]{2,1,0:T(8,128)(2,1)S(1)}, bf16[4,16,1024]{2,1,0:T(8,128)(2,1)S(1)}, u32[]{:S(2)}, u32[]{:S(2)}) collective-permute-start(bf16[4,16,1024]{2,1,0:T(8,128)(2,1)S(1)} %pad_maximum_fusion.25), channel_id=1, source_target_pairs={{0,2},{1,3},{2,0},{3,1},{4,6},{5,7},{6,4},{7,5},{8,10},{9,11},{10,... | collective-permute-start | bytes 393224 | tf_op jit(solution)/shard_map/ppermute | solution.py:32
  45.3 25.4 %collective-permute-start.3 = (bf16[8,56,512]{2,1,0:T(8,128)(2,1)S(1)}, bf16[8,56,512]{2,1,0:T(8,128)(2,1)S(1)}, u32[]{:S(2)}, u32[]{:S(2)}) collective-permute-start(bf16[8,56,512]{2,1,0:T(8,128)(2,1)S(1)} %pad_maximum_fusion.13), channel_id=1, source_target_pairs={{0,2},{1,3},{2,0},{3,1},{4,6},{5,7},{6,4},{7,5},{8,10},{9,11},{10,... | collective-permute-start | bytes 1376264 | tf_op jit(solution)/shard_map/ppermute | solution.py:32
  53.6 14.8 %collective-permute-start.12 = (bf16[4,48,1024]{2,1,0:T(8,128)(2,1)S(1)}, bf16[4,48,1024]{2,1,0:T(8,128)(2,1)S(1)}, u32[]{:S(2)}, u32[]{:S(2)}) collective-permute-start(bf16[4,48,1024]{2,1,0:T(8,128)(2,1)S(1)} %get-tuple-element.105), channel_id=1, source_target_pairs={{0,2},{1,3},{2,0},{3,1},{4,6},{5,7},{6,4},{7,5},{8,10},{9,11},{10,... | collective-permute-start | bytes 1179656 | tf_op jit(solution)/shard_map/ppermute | solution.py:32
  55.2 14.5 %collective-permute-start.9 = (bf16[4,48,1024]{2,1,0:T(8,128)(2,1)S(1)}, bf16[4,48,1024]{2,1,0:T(8,128)(2,1)S(1)}, u32[]{:S(2)}, u32[]{:S(2)}) collective-permute-start(bf16[4,48,1024]{2,1,0:T(8,128)(2,1)S(1)} %get-tuple-element.106), channel_id=1, source_target_pairs={{0,4},{4,0},{8,12},{12,8},{16,20},{20,16},{24,28},{28,24},{1,5},{5... | collective-permute-start | bytes 1179656 | tf_op jit(solution)/shard_map/ppermute | solution.py:32
  59.3 44.9 %copy-start.49 = (bf16[4,48,1024]{2,1,0:T(8,128)(2,1)}, bf16[4,48,1024]{2,1,0:T(8,128)(2,1)S(1)}, u32[]{:S(2)}) copy-start(bf16[4,48,1024]{2,1,0:T(8,128)(2,1)S(1)} %get-tuple-element.104) | copy-start | bytes 1179652
  59.3 17.6 %collective-permute-start.28 = (bf16[4,48,1024]{2,1,0:T(8,128)(2,1)S(1)}, bf16[4,48,1024]{2,1,0:T(8,128)(2,1)S(1)}, u32[]{:S(2)}, u32[]{:S(2)}) collective-permute-start(bf16[4,48,1024]{2,1,0:T(8,128)(2,1)S(1)} %get-tuple-element.103), channel_id=1, source_target_pairs={{0,2},{1,3},{2,0},{3,1},{4,6},{5,7},{6,4},{7,5},{8,10},{9,11},{10,... | collective-permute-start | bytes 1179656 | tf_op jit(solution)/shard_map/ppermute | solution.py:32
  68.4 9.8 %collective-permute-start.17 = (bf16[4,32,1024]{2,1,0:T(8,128)(2,1)S(1)}, bf16[4,32,1024]{2,1,0:T(8,128)(2,1)S(1)}, u32[]{:S(2)}, u32[]{:S(2)}) collective-permute-start(bf16[4,32,1024]{2,1,0:T(8,128)(2,1)S(1)} %slice.420), channel_id=1, source_target_pairs={{0,4},{4,0},{8,12},{12,8},{16,20},{20,16},{24,28},{28,24},{1,5},{5... | collective-permute-start | bytes 786440 | tf_op jit(solution)/shard_map/ppermute | solution.py:32
  69.7 35.4 %collective-permute-start.13 = (bf16[8,48,1024]{2,1,0:T(8,128)(2,1)S(1)}, bf16[8,48,1024]{2,1,0:T(8,128)(2,1)S(1)}, u32[]{:S(2)}, u32[]{:S(2)}) collective-permute-start(bf16[8,48,1024]{2,1,0:T(8,128)(2,1)S(1)} %pad_maximum_fusion.7), channel_id=1, source_target_pairs={{0,4},{4,0},{8,12},{12,8},{16,20},{20,16},{24,28},{28,24},{1,5},{5... | collective-permute-start | bytes 2359304 | tf_op jit(solution)/shard_map/ppermute | solution.py:32
  70.7 36.2 %collective-permute-start.10 = (bf16[8,48,1024]{2,1,0:T(8,128)(2,1)S(1)}, bf16[8,48,1024]{2,1,0:T(8,128)(2,1)S(1)}, u32[]{:S(2)}, u32[]{:S(2)}) collective-permute-start(bf16[8,48,1024]{2,1,0:T(8,128)(2,1)S(1)} %pad_maximum_fusion.6), channel_id=1, source_target_pairs={{0,2},{1,3},{2,0},{3,1},{4,6},{5,7},{6,4},{7,5},{8,10},{9,11},{10,... | collective-permute-start | bytes 2359304 | tf_op jit(solution)/shard_map/ppermute | solution.py:32
  76.8 26.1 %collective-permute-start.25 = (bf16[4,48,1024]{2,1,0:T(8,128)(2,1)S(1)}, bf16[4,48,1024]{2,1,0:T(8,128)(2,1)S(1)}, u32[]{:S(2)}, u32[]{:S(2)}) collective-permute-start(bf16[4,48,1024]{2,1,0:T(8,128)(2,1)S(1)} %get-tuple-element.104), channel_id=1, source_target_pairs={{0,4},{4,0},{8,12},{12,8},{16,20},{20,16},{24,28},{28,24},{1,5},{5... | collective-permute-start | bytes 1179656 | tf_op jit(solution)/shard_map/ppermute | solution.py:32
  78.1 38.7 %collective-permute-start.4 = (bf16[16,56,512]{2,1,0:T(8,128)(2,1)}, bf16[16,56,512]{2,1,0:T(8,128)(2,1)S(1)}, u32[]{:S(2)}, u32[]{:S(2)}) collective-permute-start(bf16[16,56,512]{2,1,0:T(8,128)(2,1)} %constant_dynamic-update-slice_fusion.p0.s0), channel_id=1, source_target_pairs={{0,1},{1,0},{2,3},{3,2},{4,5},{5,4},{6,7},{7,6},{8,9},{9,8},{10,11... | collective-permute-start | bytes 2752520 | tf_op jit(solution)/shard_map/ppermute | solution.py:32
  78.2 37.3 %collective-permute-start.29 = (bf16[8,48,1024]{2,1,0:T(8,128)(2,1)S(1)}, bf16[8,48,1024]{2,1,0:T(8,128)(2,1)S(1)}, u32[]{:S(2)}, u32[]{:S(2)}) collective-permute-start(bf16[8,48,1024]{2,1,0:T(8,128)(2,1)S(1)} %pad_maximum_fusion.10), channel_id=1, source_target_pairs={{0,4},{4,0},{8,12},{12,8},{16,20},{20,16},{24,28},{28,24},{1,5},{5... | collective-permute-start | bytes 2359304 | tf_op jit(solution)/shard_map/ppermute | solution.py:32
  102.9 37.9 %collective-permute-start.21 = (bf16[8,16,1024]{2,1,0:T(8,128)(2,1)}, bf16[8,16,1024]{2,1,0:T(8,128)(2,1)}, u32[]{:S(2)}, u32[]{:S(2)}) collective-permute-start(bf16[8,16,1024]{2,1,0:T(8,128)(2,1)} %pad_maximum_fusion.20), channel_id=1, source_target_pairs={{0,4},{4,0},{8,12},{12,8},{16,20},{20,16},{24,28},{28,24},{1,5},{5... | collective-permute-start | bytes 786440 | tf_op jit(solution)/shard_map/ppermute | solution.py:32
  105.1 36.3 %collective-permute-start.18 = (bf16[8,32,1024]{2,1,0:T(8,128)(2,1)}, bf16[8,32,1024]{2,1,0:T(8,128)(2,1)}, u32[]{:S(2)}, u32[]{:S(2)}) collective-permute-start(bf16[8,32,1024]{2,1,0:T(8,128)(2,1)} %pad_maximum_fusion.11), channel_id=1, source_target_pairs={{0,2},{1,3},{2,0},{3,1},{4,6},{5,7},{6,4},{7,5},{8,10},{9,11},{10,... | collective-permute-start | bytes 1572872 | tf_op jit(solution)/shard_map/ppermute | solution.py:32
  106.8 41.8 %copy-start.2 = (bf16[16,48,1024]{2,1,0:T(8,128)(2,1)}, bf16[16,48,1024]{2,1,0:T(8,128)(2,1)S(1)}, u32[]{:S(2)}) copy-start(bf16[16,48,1024]{2,1,0:T(8,128)(2,1)S(1)} %pad_maximum_fusion.1.p2) | copy-start | bytes 4718596
  106.8 30.7 %collective-permute-start.26 = (bf16[8,48,1024]{2,1,0:T(8,128)(2,1)}, bf16[8,48,1024]{2,1,0:T(8,128)(2,1)}, u32[]{:S(2)}, u32[]{:S(2)}) collective-permute-start(bf16[8,48,1024]{2,1,0:T(8,128)(2,1)} %pad_maximum_fusion.9), channel_id=1, source_target_pairs={{0,2},{1,3},{2,0},{3,1},{4,6},{5,7},{6,4},{7,5},{8,10},{9,11},{10,... | collective-permute-start | bytes 2359304 | tf_op jit(solution)/shard_map/ppermute | solution.py:32
  107.6 41.0 %copy-start.4 = (bf16[16,48,1024]{2,1,0:T(8,128)(2,1)}, bf16[16,48,1024]{2,1,0:T(8,128)(2,1)S(1)}, u32[]{:S(2)}) copy-start(bf16[16,48,1024]{2,1,0:T(8,128)(2,1)S(1)} %pad_maximum_fusion.p0) | copy-start | bytes 4718596
  115.6 32.5 %collective-permute-start.11 = (bf16[16,48,1024]{2,1,0:T(8,128)(2,1)S(1)}, bf16[16,48,1024]{2,1,0:T(8,128)(2,1)}, u32[]{:S(2)}, u32[]{:S(2)}) collective-permute-start(bf16[16,48,1024]{2,1,0:T(8,128)(2,1)S(1)} %pad_maximum_fusion.p0), channel_id=1, source_target_pairs={{0,1},{1,0},{2,3},{3,2},{4,5},{5,4},{6,7},{7,6},{8,9},{9,8},{10,11... | collective-permute-start | bytes 4718600 | tf_op jit(solution)/shard_map/ppermute | solution.py:32
  116.9 31.7 %collective-permute-start.14 = (bf16[16,48,1024]{2,1,0:T(8,128)(2,1)S(1)}, bf16[16,48,1024]{2,1,0:T(8,128)(2,1)}, u32[]{:S(2)}, u32[]{:S(2)}) collective-permute-start(bf16[16,48,1024]{2,1,0:T(8,128)(2,1)S(1)} %pad_maximum_fusion.1.p2), channel_id=1, source_target_pairs={{0,1},{1,0},{2,3},{3,2},{4,5},{5,4},{6,7},{7,6},{8,9},{9,8},{10,11... | collective-permute-start | bytes 4718600 | tf_op jit(solution)/shard_map/ppermute | solution.py:32
  121.0 50.9 %copy-start.30 = (f32[1,512]{1,0:T(1,128)}, f32[1,512]{1,0:T(1,128)S(1)}, u32[]{:S(2)}) copy-start(f32[1,512]{1,0:T(1,128)S(1)} %sqrt.8.inflow_ref) | copy-start | bytes 6148
  137.5 3.7 collective-permute-start.5
  140.8 49.0 %collective-permute-start.27 = (bf16[16,48,1024]{2,1,0:T(8,128)(2,1)}, bf16[16,48,1024]{2,1,0:T(8,128)(2,1)}, u32[]{:S(2)}, u32[]{:S(2)}) collective-permute-start(bf16[16,48,1024]{2,1,0:T(8,128)(2,1)} %pad_maximum_fusion.2.p0), channel_id=1, source_target_pairs={{0,1},{1,0},{2,3},{3,2},{4,5},{5,4},{6,7},{7,6},{8,9},{9,8},{10,11... | collective-permute-start | bytes 4718600 | tf_op jit(solution)/shard_map/ppermute | solution.py:32
  141.2 48.6 %collective-permute-start.30 = (bf16[16,48,1024]{2,1,0:T(8,128)(2,1)}, bf16[16,48,1024]{2,1,0:T(8,128)(2,1)}, u32[]{:S(2)}, u32[]{:S(2)}) collective-permute-start(bf16[16,48,1024]{2,1,0:T(8,128)(2,1)} %pad_maximum_fusion.3.p2), channel_id=1, source_target_pairs={{0,1},{1,0},{2,3},{3,2},{4,5},{5,4},{6,7},{7,6},{8,9},{9,8},{10,11... | collective-permute-start | bytes 4718600 | tf_op jit(solution)/shard_map/ppermute | solution.py:32
  141.4 3.7 collective-permute-start.6
  145.1 26.8 %collective-permute-start.19 = (bf16[16,32,1024]{2,1,0:T(8,128)(2,1)}, bf16[16,32,1024]{2,1,0:T(8,128)(2,1)}, u32[]{:S(2)}, u32[]{:S(2)}) collective-permute-start(bf16[16,32,1024]{2,1,0:T(8,128)(2,1)} %pad_maximum_fusion.4.p0), channel_id=1, source_target_pairs={{0,1},{1,0},{2,3},{3,2},{4,5},{5,4},{6,7},{7,6},{8,9},{9,8},{10,11... | collective-permute-start | bytes 3145736 | tf_op jit(solution)/shard_map/ppermute | solution.py:32
  148.1 23.8 %collective-permute-start.22 = (bf16[16,16,1024]{2,1,0:T(8,128)(2,1)}, bf16[16,16,1024]{2,1,0:T(8,128)(2,1)S(1)}, u32[]{:S(2)}, u32[]{:S(2)}) collective-permute-start(bf16[16,16,1024]{2,1,0:T(8,128)(2,1)} %pad_maximum_fusion.12.p2), channel_id=1, source_target_pairs={{0,1},{1,0},{2,3},{3,2},{4,5},{5,4},{6,7},{7,6},{8,9},{9,8},{10,11... | collective-permute-start | bytes 1572872 | tf_op jit(solution)/shard_map/ppermute | solution.py:32
  226.8 8.6 %collective-permute-start.31 = (f32[1,2,512]{2,1,0:T(2,128)S(1)}, f32[1,2,512]{2,1,0:T(2,128)S(1)}, u32[]{:S(2)}, u32[]{:S(2)}) collective-permute-start(f32[1,2,512]{2,1,0:T(2,128)S(1)} %bitcast.200), channel_id=1, source_target_pairs={{0,1},{1,0},{2,3},{3,2},{4,5},{5,4},{6,7},{7,6},{8,9},{9,8},{10,11... | collective-permute-start | bytes 12296 | tf_op jit(solution)/shard_map/ppermute | solution.py:32
  235.1 94.4 %collective-permute-start.45 = (bf16[16,48,1024]{2,1,0:T(8,128)(2,1)}, bf16[16,48,1024]{2,1,0:T(8,128)(2,1)}, u32[]{:S(2)}, u32[]{:S(2)}) collective-permute-start(bf16[16,48,1024]{2,1,0:T(8,128)(2,1)} %get-tuple-element.88), channel_id=1, source_target_pairs={{0,1},{1,0},{2,3},{3,2},{4,5},{5,4},{6,7},{7,6},{8,9},{9,8},{10,11... | collective-permute-start | bytes 4718600 | tf_op jit(solution)/shard_map/ppermute | solution.py:32
  236.0 8.9 %collective-permute-start.32 = (f32[2,2,512]{2,1,0:T(2,128)}, f32[2,2,512]{2,1,0:T(2,128)}, u32[]{:S(2)}, u32[]{:S(2)}) collective-permute-start(f32[2,2,512]{2,1,0:T(2,128)} %pad_maximum_fusion.31), channel_id=1, source_target_pairs={{0,2},{1,3},{2,0},{3,1},{4,6},{5,7},{6,4},{7,5},{8,10},{9,11},{10,... | collective-permute-start | bytes 24584 | tf_op jit(solution)/shard_map/ppermute | solution.py:32
  284.3 28.3 %collective-permute-start.33 = (bf16[16,56,512]{2,1,0:T(8,128)(2,1)S(1)}, bf16[16,56,512]{2,1,0:T(8,128)(2,1)S(1)}, u32[]{:S(2)}, u32[]{:S(2)}) collective-permute-start(bf16[16,56,512]{2,1,0:T(8,128)(2,1)S(1)} %fusion.8), channel_id=1, source_target_pairs={{0,1},{1,0},{2,3},{3,2},{4,5},{5,4},{6,7},{7,6},{8,9},{9,8},{10,11... | collective-permute-start | bytes 2752520 | tf_op jit(solution)/shard_map/ppermute | solution.py:32
  299.1 79.2 %collective-permute-start.38 = (bf16[16,96,1024]{2,1,0:T(8,128)(2,1)}, bf16[16,96,1024]{2,1,0:T(8,128)(2,1)}, u32[]{:S(2)}, u32[]{:S(2)}) collective-permute-start(bf16[16,96,1024]{2,1,0:T(8,128)(2,1)} %get-tuple-element.85), channel_id=1, source_target_pairs={{0,1},{1,0},{2,3},{3,2},{4,5},{5,4},{6,7},{7,6},{8,9},{9,8},{10,11... | collective-permute-start | bytes 9437192 | tf_op jit(solution)/shard_map/ppermute | solution.py:32
  311.7 72.3 %collective-permute-start.52 = (bf16[16,96,1024]{2,1,0:T(8,128)(2,1)}, bf16[16,96,1024]{2,1,0:T(8,128)(2,1)}, u32[]{:S(2)}, u32[]{:S(2)}) collective-permute-start(bf16[16,96,1024]{2,1,0:T(8,128)(2,1)} %get-tuple-element.90), channel_id=1, source_target_pairs={{0,1},{1,0},{2,3},{3,2},{4,5},{5,4},{6,7},{7,6},{8,9},{9,8},{10,11... | collective-permute-start | bytes 9437192 | tf_op jit(solution)/shard_map/ppermute | solution.py:32
  313.0 14.6 %collective-permute-start.34 = (bf16[2,4,56,512]{3,2,1,0:T(8,128)(2,1)S(1)}, bf16[2,4,56,512]{3,2,1,0:T(8,128)(2,1)S(1)}, u32[]{:S(2)}, u32[]{:S(2)}) collective-permute-start(bf16[2,4,56,512]{3,2,1,0:T(8,128)(2,1)S(1)} %bitcast.219), channel_id=1, source_target_pairs={{0,2},{1,3},{2,0},{3,1},{4,6},{5,7},{6,4},{7,5},{8,10},{9,11},{10,... | collective-permute-start | bytes 1376264 | tf_op jit(solution)/shard_map/ppermute | solution.py:32
  327.7 7.9 %collective-permute-start.35 = (bf16[4,56,512]{2,1,0:T(8,128)(2,1)S(1)}, bf16[4,56,512]{2,1,0:T(8,128)(2,1)S(1)}, u32[]{:S(2)}, u32[]{:S(2)}) collective-permute-start(bf16[4,56,512]{2,1,0:T(8,128)(2,1)S(1)} %slice_bitcast_fusion.22), channel_id=1, source_target_pairs={{0,4},{4,0},{8,12},{12,8},{16,20},{20,16},{24,28},{28,24},{1,5},{5... | collective-permute-start | bytes 688136 | tf_op jit(solution)/shard_map/ppermute | solution.py:32
  335.7 4.9 %collective-permute-start.36 = (bf16[2,56,512]{2,1,0:T(8,128)(2,1)S(1)}, bf16[2,56,512]{2,1,0:T(8,128)(2,1)S(1)}, u32[]{:S(2)}, u32[]{:S(2)}) collective-permute-start(bf16[2,56,512]{2,1,0:T(8,128)(2,1)S(1)} %slice.429), channel_id=1, source_target_pairs={{0,8},{4,12},{8,0},{12,4},{16,24},{20,28},{24,16},{28,20},{1,9},{5... | collective-permute-start | bytes 344072 | tf_op jit(solution)/shard_map/ppermute | solution.py:32
  335.8 10.0 %collective-permute-start.48 = (bf16[2,4,16,1024]{3,2,1,0:T(8,128)(2,1)S(1)}, bf16[2,4,16,1024]{3,2,1,0:T(8,128)(2,1)S(1)}, u32[]{:S(2)}, u32[]{:S(2)}) collective-permute-start(bf16[2,4,16,1024]{3,2,1,0:T(8,128)(2,1)S(1)} %slice_bitcast_fusion.18), channel_id=1, source_target_pairs={{0,4},{4,0},{8,12},{12,8},{16,20},{20,16},{24,28},{28,24},{1,5},{5... | collective-permute-start | bytes 786440 | tf_op jit(solution)/shard_map/ppermute | solution.py:32
  340.6 5.1 %collective-permute-start.37 = (bf16[56,512]{1,0:T(8,128)(2,1)S(1)}, bf16[56,512]{1,0:T(8,128)(2,1)S(1)}, u32[]{:S(2)}, u32[]{:S(2)}) collective-permute-start(bf16[56,512]{1,0:T(8,128)(2,1)S(1)} %slice_bitcast_fusion.32), channel_id=1, source_target_pairs={{0,16},{4,20},{8,24},{12,28},{16,0},{20,4},{24,8},{28,12},{1,17},{... | collective-permute-start | bytes 172040 | tf_op jit(solution)/shard_map/ppermute | solution.py:32
  343.6 14.0 %collective-permute-start.46 = (bf16[2,4,32,1024]{3,2,1,0:T(8,128)(2,1)S(1)}, bf16[2,4,32,1024]{3,2,1,0:T(8,128)(2,1)S(1)}, u32[]{:S(2)}, u32[]{:S(2)}) collective-permute-start(bf16[2,4,32,1024]{3,2,1,0:T(8,128)(2,1)S(1)} %slice_bitcast_fusion.8), channel_id=1, source_target_pairs={{0,2},{1,3},{2,0},{3,1},{4,6},{5,7},{6,4},{7,5},{8,10},{9,11},{10,... | collective-permute-start | bytes 1572872 | tf_op jit(solution)/shard_map/ppermute | solution.py:32
  345.9 14.3 %collective-permute-start.49 = (bf16[4,16,1024]{2,1,0:T(8,128)(2,1)S(1)}, bf16[4,16,1024]{2,1,0:T(8,128)(2,1)S(1)}, u32[]{:S(2)}, u32[]{:S(2)}) collective-permute-start(bf16[4,16,1024]{2,1,0:T(8,128)(2,1)S(1)} %slice_bitcast_fusion.28), channel_id=1, source_target_pairs={{0,2},{1,3},{2,0},{3,1},{4,6},{5,7},{6,4},{7,5},{8,10},{9,11},{10,... | collective-permute-start | bytes 393224 | tf_op jit(solution)/shard_map/ppermute | solution.py:32
  357.8 6.4 %collective-permute-start.47 = (bf16[4,32,1024]{2,1,0:T(8,128)(2,1)S(1)}, bf16[4,32,1024]{2,1,0:T(8,128)(2,1)S(1)}, u32[]{:S(2)}, u32[]{:S(2)}) collective-permute-start(bf16[4,32,1024]{2,1,0:T(8,128)(2,1)S(1)} %slice_bitcast_fusion.20), channel_id=1, source_target_pairs={{0,4},{4,0},{8,12},{12,8},{16,20},{20,16},{24,28},{28,24},{1,5},{5... | collective-permute-start | bytes 786440 | tf_op jit(solution)/shard_map/ppermute | solution.py:32
  364.3 6.8 %collective-permute-start.50 = (bf16[2,48,1024]{2,1,0:T(8,128)(2,1)S(1)}, bf16[2,48,1024]{2,1,0:T(8,128)(2,1)S(1)}, u32[]{:S(2)}, u32[]{:S(2)}) collective-permute-start(bf16[2,48,1024]{2,1,0:T(8,128)(2,1)S(1)} %pad_maximum_fusion.22), channel_id=1, source_target_pairs={{0,8},{4,12},{8,0},{12,4},{16,24},{20,28},{24,16},{28,20},{1,9},{5... | collective-permute-start | bytes 589832 | tf_op jit(solution)/shard_map/ppermute | solution.py:32
  371.2 6.4 %collective-permute-start.51 = (bf16[48,1024]{1,0:T(8,128)(2,1)S(1)}, bf16[48,1024]{1,0:T(8,128)(2,1)S(1)}, u32[]{:S(2)}, u32[]{:S(2)}) collective-permute-start(bf16[48,1024]{1,0:T(8,128)(2,1)S(1)} %slice_bitcast_fusion.30), channel_id=1, source_target_pairs={{0,16},{4,20},{8,24},{12,28},{16,0},{20,4},{24,8},{28,12},{1,17},{... | collective-permute-start | bytes 294920 | tf_op jit(solution)/shard_map/ppermute | solution.py:32
  381.8 20.5 %collective-permute-start.39 = (bf16[2,4,48,1024]{3,2,1,0:T(8,128)(2,1)S(1)}, bf16[2,4,48,1024]{3,2,1,0:T(8,128)(2,1)S(1)}, u32[]{:S(2)}, u32[]{:S(2)}) collective-permute-start(bf16[2,4,48,1024]{3,2,1,0:T(8,128)(2,1)S(1)} %slice_bitcast_fusion.6), channel_id=1, source_target_pairs={{0,2},{1,3},{2,0},{3,1},{4,6},{5,7},{6,4},{7,5},{8,10},{9,11},{10,... | collective-permute-start | bytes 2359304 | tf_op jit(solution)/shard_map/ppermute | solution.py:32
  382.2 20.5 %collective-permute-start.41 = (bf16[2,4,48,1024]{3,2,1,0:T(8,128)(2,1)S(1)}, bf16[2,4,48,1024]{3,2,1,0:T(8,128)(2,1)S(1)}, u32[]{:S(2)}, u32[]{:S(2)}) collective-permute-start(bf16[2,4,48,1024]{3,2,1,0:T(8,128)(2,1)S(1)} %slice_bitcast_fusion.4), channel_id=1, source_target_pairs={{0,4},{4,0},{8,12},{12,8},{16,20},{20,16},{24,28},{28,24},{1,5},{5... | collective-permute-start | bytes 2359304 | tf_op jit(solution)/shard_map/ppermute | solution.py:32
  387.5 30.9 %collective-permute-start.53 = (bf16[2,4,48,1024]{3,2,1,0:T(8,128)(2,1)S(1)}, bf16[2,4,48,1024]{3,2,1,0:T(8,128)(2,1)S(1)}, u32[]{:S(2)}, u32[]{:S(2)}) collective-permute-start(bf16[2,4,48,1024]{3,2,1,0:T(8,128)(2,1)S(1)} %slice_bitcast_fusion.2), channel_id=1, source_target_pairs={{0,2},{1,3},{2,0},{3,1},{4,6},{5,7},{6,4},{7,5},{8,10},{9,11},{10,... | collective-permute-start | bytes 2359304 | tf_op jit(solution)/shard_map/ppermute | solution.py:32
  389.4 29.2 %collective-permute-start.55 = (bf16[2,4,48,1024]{3,2,1,0:T(8,128)(2,1)S(1)}, bf16[2,4,48,1024]{3,2,1,0:T(8,128)(2,1)S(1)}, u32[]{:S(2)}, u32[]{:S(2)}) collective-permute-start(bf16[2,4,48,1024]{3,2,1,0:T(8,128)(2,1)S(1)} %slice_bitcast_fusion), channel_id=1, source_target_pairs={{0,4},{4,0},{8,12},{12,8},{16,20},{20,16},{24,28},{28,24},{1,5},{5... | collective-permute-start | bytes 2359304 | tf_op jit(solution)/shard_map/ppermute | solution.py:32
  403.5 19.4 %collective-permute-start.42 = (bf16[4,48,1024]{2,1,0:T(8,128)(2,1)S(1)}, bf16[4,48,1024]{2,1,0:T(8,128)(2,1)S(1)}, u32[]{:S(2)}, u32[]{:S(2)}) collective-permute-start(bf16[4,48,1024]{2,1,0:T(8,128)(2,1)S(1)} %slice_bitcast_fusion.14), channel_id=1, source_target_pairs={{0,2},{1,3},{2,0},{3,1},{4,6},{5,7},{6,4},{7,5},{8,10},{9,11},{10,... | collective-permute-start | bytes 1179656 | tf_op jit(solution)/shard_map/ppermute | solution.py:32
  405.4 17.7 %collective-permute-start.40 = (bf16[4,48,1024]{2,1,0:T(8,128)(2,1)S(1)}, bf16[4,48,1024]{2,1,0:T(8,128)(2,1)S(1)}, u32[]{:S(2)}, u32[]{:S(2)}) collective-permute-start(bf16[4,48,1024]{2,1,0:T(8,128)(2,1)S(1)} %slice_bitcast_fusion.16), channel_id=1, source_target_pairs={{0,4},{4,0},{8,12},{12,8},{16,20},{20,16},{24,28},{28,24},{1,5},{5... | collective-permute-start | bytes 1179656 | tf_op jit(solution)/shard_map/ppermute | solution.py:32
  419.3 7.8 %collective-permute-start.56 = (bf16[4,48,1024]{2,1,0:T(8,128)(2,1)S(1)}, bf16[4,48,1024]{2,1,0:T(8,128)(2,1)S(1)}, u32[]{:S(2)}, u32[]{:S(2)}) collective-permute-start(bf16[4,48,1024]{2,1,0:T(8,128)(2,1)S(1)} %slice_bitcast_fusion.10), channel_id=1, source_target_pairs={{0,2},{1,3},{2,0},{3,1},{4,6},{5,7},{6,4},{7,5},{8,10},{9,11},{10,... | collective-permute-start | bytes 1179656 | tf_op jit(solution)/shard_map/ppermute | solution.py:32
  421.1 7.8 %collective-permute-start.54 = (bf16[4,48,1024]{2,1,0:T(8,128)(2,1)S(1)}, bf16[4,48,1024]{2,1,0:T(8,128)(2,1)S(1)}, u32[]{:S(2)}, u32[]{:S(2)}) collective-permute-start(bf16[4,48,1024]{2,1,0:T(8,128)(2,1)S(1)} %slice_bitcast_fusion.12), channel_id=1, source_target_pairs={{0,4},{4,0},{8,12},{12,8},{16,20},{20,16},{24,28},{28,24},{1,5},{5... | collective-permute-start | bytes 1179656 | tf_op jit(solution)/shard_map/ppermute | solution.py:32
  423.3 11.9 %collective-permute-start.43 = (bf16[2,96,1024]{2,1,0:T(8,128)(2,1)S(1)}, bf16[2,96,1024]{2,1,0:T(8,128)(2,1)S(1)}, u32[]{:S(2)}, u32[]{:S(2)}) collective-permute-start(bf16[2,96,1024]{2,1,0:T(8,128)(2,1)S(1)} %pad_maximum_fusion.15), channel_id=1, source_target_pairs={{0,8},{4,12},{8,0},{12,4},{16,24},{20,28},{24,16},{28,20},{1,9},{5... | collective-permute-start | bytes 1179656 | tf_op jit(solution)/shard_map/ppermute | solution.py:32
  429.1 10.2 %collective-permute-start.57 = (bf16[2,96,1024]{2,1,0:T(8,128)(2,1)S(1)}, bf16[2,96,1024]{2,1,0:T(8,128)(2,1)S(1)}, u32[]{:S(2)}, u32[]{:S(2)}) collective-permute-start(bf16[2,96,1024]{2,1,0:T(8,128)(2,1)S(1)} %pad_maximum_fusion.14), channel_id=1, source_target_pairs={{0,8},{4,12},{8,0},{12,4},{16,24},{20,28},{24,16},{28,20},{1,9},{5... | collective-permute-start | bytes 1179656 | tf_op jit(solution)/shard_map/ppermute | solution.py:32
  435.3 8.7 %collective-permute-start.44 = (bf16[96,1024]{1,0:T(8,128)(2,1)S(1)}, bf16[96,1024]{1,0:T(8,128)(2,1)S(1)}, u32[]{:S(2)}, u32[]{:S(2)}) collective-permute-start(bf16[96,1024]{1,0:T(8,128)(2,1)S(1)} %slice_bitcast_fusion.26), channel_id=1, source_target_pairs={{0,16},{4,20},{8,24},{12,28},{16,0},{20,4},{24,8},{28,12},{1,17},{... | collective-permute-start | bytes 589832 | tf_op jit(solution)/shard_map/ppermute | solution.py:32
  439.5 8.7 %collective-permute-start.58 = (bf16[96,1024]{1,0:T(8,128)(2,1)S(1)}, bf16[96,1024]{1,0:T(8,128)(2,1)S(1)}, u32[]{:S(2)}, u32[]{:S(2)}) collective-permute-start(bf16[96,1024]{1,0:T(8,128)(2,1)S(1)} %slice_bitcast_fusion.24), channel_id=1, source_target_pairs={{0,16},{4,20},{8,24},{12,28},{16,0},{20,4},{24,8},{28,12},{1,17},{... | collective-permute-start | bytes 589832 | tf_op jit(solution)/shard_map/ppermute | solution.py:32
  (64 other events, 496.2 us)

commit v3 on v2

v3 whole, which is shorter than its diff:
```python
import jax
import jax.numpy as jnp
from jax import lax
from jax.experimental import pallas as pl
from jax.experimental.pallas import tpu as pltpu
from jax.sharding import PartitionSpec as P

EPSILON = 1e-05
HALF = jnp.bfloat16
SINGLE = jnp.float32
MAIN = 5
SEGMENTS = 8
MIB = 1 << 20


def log2(n):
    return n.bit_length() - 1


def device_number():
    return lax.axis_index("dp") * lax.axis_size("seq") + lax.axis_index("seq")


def low_bits():
    return log2(lax.axis_size("dp") * lax.axis_size("seq")) - MAIN


def exchange(values, *bits):
    inner = log2(lax.axis_size("seq"))
    axis, first = ("seq", 0) if bits[0] < inner else ("dp", inner)
    flip = sum(1 << (bit - first) for bit in bits)
    return lax.ppermute(values, axis, [(i, i ^ flip) for i in range(lax.axis_size(axis))])


def gather_low(values):
    for bit in range(low_bits()):
        other = exchange(values, bit)
        upper = (device_number() >> bit) & 1
        values = jnp.where(
            upper == 1, jnp.concatenate([other, values]), jnp.concatenate([values, other])
        )
    return values


def reduce_low(values):
    for bit in reversed(range(low_bits())):
        upper = (device_number() >> bit) & 1
        halves = values.reshape((2, values.shape[0] // 2) + values.shape[1:])
        mine = lax.dynamic_index_in_dim(halves, upper, 0, False)
        theirs = lax.dynamic_index_in_dim(halves, 1 - upper, 0, False)
        values = mine + exchange(theirs, bit)
    return values


def join(own, other):
    return jnp.concatenate([own, other])


def gather_steps(rows, split):
    core, bit_x, bit_y, bit_z, bit_far = (low_bits() + i for i in range(MAIN))
    held = rows[None]
    if not split:
        others = yield [exchange(held, *bits) for bits in ((bit_far,), (bit_z,), (bit_z, bit_far))]
        held = jnp.concatenate([held, *others])
        (other,) = yield [exchange(held, bit_y)]
        held = join(held, other)
        other, held_core = yield [exchange(held, bit_x), exchange(held, core)]
        (other_core,) = yield [exchange(other, core)]
        return [held, other, held_core, other_core]
    (other,) = yield [exchange(held, bit_far)]
    held = join(held, other)
    (other,) = yield [exchange(held, bit_z)]
    held = join(held, other)
    first, second = held[:, :split], held[:, split:]
    from_y, from_x = yield [exchange(first, bit_y), exchange(second, bit_x)]
    first, second = join(first, from_y), join(second, from_x)
    from_x, from_y, *near = yield [
        exchange(first, bit_x),
        exchange(second, bit_y),
        exchange(first, core),
        exchange(second, core),
    ]
    far = yield [exchange(from_x, core), exchange(from_y, core)]
    return [first, from_x, near[0], far[0], second, from_y, near[1], far[1]]


def spot(rel, x_first):
    core = rel & 1
    bit_x, bit_y = (rel >> 1) & 1, (rel >> 2) & 1
    bit_z, bit_far = (rel >> 3) & 1, (rel >> 4) & 1
    if x_first:
        return core, bit_x * 8 + bit_y * 4 + bit_z * 2 + bit_far
    return core, bit_y * 8 + bit_x * 4 + bit_z * 2 + bit_far


def load_weights(mine, parts, target, pieces, sems):
    def one(k, carry):
        bits = ((k >> 2) & 1, ((k >> 1) & 1) * 8 + (k & 1) * 16)
        for four, row, rows, group, held, to_row in pieces:
            lead_bit, other_bit = (2, 4) if four == 0 else (4, 2)
            for side in range(4):
                rel = (side >> 1) + (side & 1) * lead_bit + bits[0] * other_bit + bits[1]
                shard = rel ^ mine
                to = group
                if group is None:
                    per_group = target.shape[1] // held
                    to, shard = shard // per_group, shard % per_group
                at = pl.multiple_of(shard * held + to_row, 16)
                source = parts[4 * four + side].at[k, pl.ds(row, rows)]
                pltpu.make_async_copy(source, target.at[to, pl.ds(at, rows)], sems.at[to]).start()
        return carry

    lax.fori_loop(0, 8, one, 0)


def await_weights(target, group, sems):
    pltpu.make_async_copy(target.at[group], target.at[group], sems.at[group]).wait()


REDUCE_PIECES = [(0, 0, 32, 0, 32, 0)]
STATE_PIECES = [(0, 32, 16, 0, 16, 0)]
EXPAND_PIECES = [(g // 2, 16 * (g % 2), 16, g, 16, 0) for g in range(4)]
OUT_PIECES = [(0, 0, 48, None, 96, 0), (1, 0, 48, None, 96, 48)]

SMEM = pl.BlockSpec(memory_space=pltpu.SMEM)
FAR = pl.BlockSpec(memory_space=pltpu.HBM)


def cost(micros):
    return pl.CostEstimate(flops=int(micros * 1e9), bytes_accessed=MIB, transcendentals=0)

ROOM = pltpu.CompilerParams(vmem_limit_bytes=60 * MIB)


def whole(*shape):
    return pl.BlockSpec(shape, lambda *_: (0,) * len(shape))


def dot(left, right, left_dim=1, right_dim=0):
    return lax.dot_general(
        left, right, (((left_dim,), (right_dim,)), ((), ())), preferred_element_type=SINGLE
    )


def gelu_pair(v):
    c, d = 0.7978845608028654, 0.7978845608028654 * 0.044715
    square = v * v
    h = 0.5 + 0.5 * jnp.tanh(v * (c + d * square))
    act = v * h
    return act, h + 2.0 * act * (1.0 - h) * (c + 3.0 * d * square)


def norm_terms(x):
    center = x - jnp.mean(x, axis=-1, keepdims=True)
    inverse = lax.rsqrt(jnp.mean(center * center, axis=-1, keepdims=True) + EPSILON)
    return center * inverse, inverse


def lanes_joined(ref, rows):
    return jnp.concatenate([ref[c, rows, :] for c in range(ref.shape[0])], axis=1)


def powers(decay, count, rows):
    power, out = decay, jnp.ones((rows, decay.shape[1]), SINGLE)
    for bit in range(8):
        out = jnp.where((count >> bit) & 1 == 1, out * power, out)
        power = power * power
    return out


def starts_near(ends_ref, places, reverse):
    far = jnp.full(places.shape, 1 << 20, jnp.int32)
    for i in range(7):
        away = ends_ref[i] - places if reverse else places - ends_ref[i]
        far = jnp.where(away >= (1 if reverse else 0), jnp.minimum(far, away), far)
    return far


def scan_block(ends_ref, first, decay, value_ref, reverse):
    columns, block, lanes = value_ref.shape
    span = block // SEGMENTS
    row = lax.broadcasted_iota(jnp.int32, (8, lanes), 0)
    order = 7 - row if reverse else row
    factors = []
    for c in range(columns):
        one = jnp.broadcast_to(decay[:, c * lanes : (c + 1) * lanes], (8, lanes))
        two = one * one
        steps = [jnp.where(order >= d, f, 0.0) for d, f in ((1, one), (2, two), (4, two * two))]
        factors.append(steps + [powers(one, order + 1, 8)])

    def tile(lap, carry):
        k = span // 8 - 1 - lap if reverse else lap
        out = []
        for s in range(SEGMENTS):
            at = pl.multiple_of(s * span + k * 8, 8)
            near = starts_near(ends_ref, first + at + row, reverse) + (0 if reverse else 1)
            for c in range(columns):
                x = value_ref[c, pl.ds(at, 8), :]
                for step, d in enumerate((1, 2, 4)):
                    moved = pltpu.roll(x, 8 - d if reverse else d, 0)
                    x = x + jnp.where(near > d, factors[c][step], 0.0) * moved
                whole_way = jnp.where(near > order + 1, factors[c][3], 0.0)
                x = x + whole_way * carry[s * columns + c]
                value_ref[c, pl.ds(at, 8), :] = x
                edge = x[:1] if reverse else x[7:]
                out.append(jnp.broadcast_to(edge, (8, lanes)))
        return out

    zero = [jnp.zeros((8, lanes), SINGLE)] * (columns * SEGMENTS)
    ends = lax.fori_loop(0, span // 8, tile, zero)
    states, products = [], []
    power = decay
    for _ in range(log2(span)):
        power = power * power
    for s in range(SEGMENTS):
        states.append(
            jnp.concatenate([ends[s * columns + c][:1] for c in range(columns)], axis=1)
        )
        low = first + s * span + (1 if reverse else 0)
        broken = jnp.int32(0)
        for i in range(7):
            inside = (ends_ref[i] >= low) & (ends_ref[i] < low + span)
            broken = jnp.where(inside, 1, broken)
        products.append(jnp.where(broken == 1, 0.0, power))
    return jnp.concatenate(products, axis=0), jnp.concatenate(states, axis=0)


def span_products(ends_ref, first, table, lanes, reverse):
    span, channels = table.shape
    row = lax.broadcasted_iota(jnp.int32, (span, lanes), 0)
    near = starts_near(ends_ref, first + row, reverse)
    kept = near > (span - row if reverse else row)
    return jnp.where(jnp.concatenate([kept] * (channels // lanes), axis=1), table, 0.0)


def span_table(decay, span, reverse):
    row = lax.broadcasted_iota(jnp.int32, (span, decay.shape[1]), 0)
    return powers(decay, span - row if reverse else row + 1, span)


def span_carries(product, state, carry, reverse):
    carries = [None] * SEGMENTS
    for s in range(SEGMENTS)[::-1] if reverse else range(SEGMENTS):
        carries[s] = carry
        carry = product[s : s + 1] * carry + state[s : s + 1]
    return carries, carry


def block_carry(place, maps_ref, reverse):
    count = maps_ref.shape[0]
    carry = jnp.zeros((1, maps_ref.shape[2]), SINGLE)
    for s in range(count)[::-1] if reverse else range(count):
        rel = s ^ place
        inside = s > place if reverse else s < place
        moved = maps_ref[rel, 0:1, :] * carry + maps_ref[rel, 1:2, :]
        carry = jnp.where(inside, moved, carry)
    return carry


def whole_map(product, state, reverse):
    zero = jnp.zeros((1, product.shape[1]), SINGLE)
    _, ending = span_carries(product, state, zero, reverse)
    through = zero + 1.0
    for s in range(SEGMENTS):
        through = through * product[s : s + 1]
    return through, ending


def gather_maps(maps):
    held = maps[None]
    for bit in range(log2(lax.axis_size("seq"))):
        held = join(held, exchange(held, bit))
    return held


def reduce_kernel(scalars, tokens, gain, shift, bias, decay, inflow, parts):
    block, width = tokens.shape
    channels = bias.shape[1]
    tile = 256
    columns = channels // 128

    def body(me, ends, base, x_ref, gain_ref, shift_ref, bias_ref, decay_ref, inflow_ref, s0, s1, s2, s3,
             normed_ref, act_ref, slope_ref, state_ref, span_ref, map_ref,
             weight, sems):
        load_weights(me[0], (s0, s1, s2, s3), weight, REDUCE_PIECES, sems)

        def norm(t, carry):
            rows = pl.ds(pl.multiple_of(t * tile, tile), tile)
            n, _ = norm_terms(x_ref[rows, :].astype(SINGLE))
            normed_ref[rows, :] = (n * gain_ref[...] + shift_ref[...]).astype(HALF)
            return carry

        lax.fori_loop(0, block // tile, norm, 0)
        await_weights(weight, 0, sems)

        def reduce(t, carry):
            rows = pl.ds(pl.multiple_of(t * tile, tile), tile)
            act, slope = gelu_pair(dot(normed_ref[rows, :], weight[0]) + bias_ref[...])
            act_ref[rows, :] = act
            slope_ref[rows, :] = slope.astype(HALF)
            flow = act * inflow_ref[...]
            for c in range(columns):
                state_ref[c, rows, :] = flow[:, c * 128 : (c + 1) * 128]
            return carry

        lax.fori_loop(0, block // tile, reduce, 0)
        product, state = scan_block(ends, base[0], decay_ref[...], state_ref, False)
        span_ref[0], span_ref[1] = product, state
        map_ref[0:1, :], map_ref[1:2, :] = whole_map(product, state, False)

    vm = pl.BlockSpec(memory_space=pltpu.VMEM)
    return pl.pallas_call(
        body,
        name="reduce_forward",
        out_shape=[
            jax.ShapeDtypeStruct((block, width), HALF),
            jax.ShapeDtypeStruct((block, channels), SINGLE),
            jax.ShapeDtypeStruct((block, channels), HALF),
            jax.ShapeDtypeStruct((columns, block, 128), SINGLE),
            jax.ShapeDtypeStruct((2, SEGMENTS, channels), SINGLE),
            jax.ShapeDtypeStruct((2, channels), SINGLE),
        ],
        in_specs=[SMEM] * 3 + [vm] * 6 + [FAR] * 4,
        out_specs=[vm] * 6,
        scratch_shapes=[
            pltpu.VMEM((1, width, channels), HALF),
            pltpu.SemaphoreType.DMA((1,)),
        ],
        compiler_params=ROOM,
        cost_estimate=cost(8),
    )(*scalars[:3], tokens, gain, shift, bias, decay, inflow, *parts)


def staged(count, product, finish):
    ahead = product(0)
    for c in range(count):
        now = ahead
        if c + 1 < count:
            ahead = product(c + 1)
        finish(c, now)


def once(*shape):
    return pl.BlockSpec(shape, lambda *_: (0,) * len(shape), pipeline_mode=pl.Buffered(1))


def states_kernel(me, place, ends, base, maps, spans, states, act, skip, inflow, decay, parts):
    columns, block, lanes = states.shape
    channels = act.shape[1]
    span = block // SEGMENTS

    def body(me, place_ref, ends_ref, base_ref, maps_ref, span_ref, state_ref, act_ref, skip_ref,
             inflow_ref, decay_ref, s0, s1, s2, s3, low_ref, prior_ref, ssm_ref,
             carry_ref, weight, sems):
        load_weights(me[0], (s0, s1, s2, s3), weight, STATE_PIECES, sems)
        entering = block_carry(place_ref[0], maps_ref, False)
        carries, _ = span_carries(span_ref[0], span_ref[1], entering, False)
        table = span_table(decay_ref[...], span, False)
        for s in range(SEGMENTS):
            carry_ref[s] = jnp.broadcast_to(carries[s], (8, channels))

        def one_span(s, done):
            rows = pl.ds(pl.multiple_of(s * span, span), span)
            product = span_products(ends_ref, base_ref[0] + s * span, table, lanes, False)
            state = lanes_joined(state_ref, rows) + product * carry_ref[s][:1]
            low_ref[rows, :] = state.astype(HALF)
            prior_ref[rows, :] = (state - inflow_ref[...] * act_ref[rows, :]).astype(HALF)
            return done

        lax.fori_loop(0, SEGMENTS, one_span, 0)
        await_weights(weight, 0, sems)
        ssm = dot(low_ref[...], weight[0]) + skip_ref[...] * act_ref[...]
        ssm_ref[...] = ssm.astype(HALF)

    vm = pl.BlockSpec(memory_space=pltpu.VMEM)
    return pl.pallas_call(
        body,
        name="states_forward",
        out_shape=[jax.ShapeDtypeStruct((block, channels), HALF)] * 3,
        in_specs=[SMEM] * 4 + [vm] * 7 + [FAR] * 4,
        out_specs=[vm] * 3,
        scratch_shapes=[
            pltpu.VMEM((SEGMENTS, 8, channels), SINGLE),
            pltpu.VMEM((1, channels, channels), HALF), pltpu.SemaphoreType.DMA((1,))],
        compiler_params=ROOM,
        cost_estimate=cost(3),
    )(me, place, ends, base, maps, spans, states, act, skip, inflow, decay, *parts)


def forward_kernel(me, normed, ssm, branch_grad, value_bias, expand_bias, value_weight,
                   expand_parts):
    block, width = normed.shape
    channels = ssm.shape[1]
    gate = value_bias.shape[1]
    groups, sub = 4, 256
    depth = gate // groups

    def body(me, x_ref, ssm_ref, grad_ref, value_bias_ref, expand_bias_ref, value,
             q0, q1, q2, q3, q4, q5, q6, q7, act_ref, gated_ref, slope_ref, sum_ref,
             expand, expand_sems):
        j = pl.program_id(0)

        @pl.when(j == 0)
        def _():
            load_weights(
                me[0], (q0, q1, q2, q3, q4, q5, q6, q7), expand, EXPAND_PIECES, expand_sems
            )

        for g in range(groups):

            @pl.when(j == g)
            def _():
                await_weights(expand, g, expand_sems)

        for c in range(depth // sub):
            cols = pl.ds(c * sub, sub)
            pre = dot(x_ref[...], value[:, cols]) + value_bias_ref[:, cols]
            act, slope = gelu_pair(pre)
            pre = dot(ssm_ref[...], expand[j, :, cols]) + expand_bias_ref[:, cols]
            act_ref[:, cols] = act.astype(HALF)
            gated_ref[:, cols] = (act * pre).astype(HALF)
            slope_ref[:, cols] = (slope * pre).astype(HALF)
        for c in range(width // sub):
            cols = pl.ds(c * sub, sub)
            sum_ref[:, cols] = dot(gated_ref[...], grad_ref[:, cols], 0, 0).astype(HALF)

    wide = pl.BlockSpec((block, depth), lambda j: (0, j))
    bias = pl.BlockSpec((1, depth), lambda j: (0, j))
    return pl.pallas_call(
        body,
        name="gate_forward",
        out_shape=[jax.ShapeDtypeStruct((block, gate), HALF)] * 3
        + [jax.ShapeDtypeStruct((gate, width), HALF)],
        grid=(groups,),
        in_specs=[
            SMEM,
            once(block, width),
            once(block, channels),
            once(block, width),
            bias,
            bias,
            pl.BlockSpec((width, depth), lambda j: (0, j)),
        ]
        + [FAR] * 8,
        out_specs=[wide] * 3 + [pl.BlockSpec((depth, width), lambda j: (j, 0))],
        scratch_shapes=[
            pltpu.VMEM((groups, channels, depth), HALF),
            pltpu.SemaphoreType.DMA((groups,)),
        ],
        compiler_params=ROOM,
        cost_estimate=cost(16),
    )(me, normed, ssm, branch_grad, value_bias, expand_bias, value_weight,
      *expand_parts)


def fold(values):
    return jnp.sum(values.reshape(values.shape[0] // 8, 8, values.shape[1]), axis=0)


def out_kernel(me, live, base, gated, tokens, bias, parts):
    block, gate = gated.shape
    width = tokens.shape[1]
    tile, sub, groups = block // 2, 256, 4
    depth = gate // groups

    def body(me, live_ref, base_ref, gated_ref, x_ref, bias_ref, p0, p1, p2, p3, p4, p5, p6, p7,
             out_ref, weight, sems):
        t = pl.program_id(0)

        @pl.when(t == 0)
        def _():
            load_weights(me[0], (p0, p1, p2, p3, p4, p5, p6, p7), weight, OUT_PIECES, sems)
            await_weights(weight, 0, sems)

        place = base_ref[0] + t * tile + lax.broadcasted_iota(jnp.int32, (tile, 1), 0)

        def column(c, carry):
            cols = pl.ds(pl.multiple_of(c * sub, sub), sub)
            branch = dot(gated_ref[...], weight[0, :, cols]) + bias_ref[:, cols]
            branch = jnp.where(place < live_ref[0], branch, 0.0)
            out_ref[:, cols] = (x_ref[:, cols].astype(SINGLE) + branch).astype(HALF)
            return carry

        lax.fori_loop(0, width // sub, column, 0)

    return pl.pallas_call(
        body,
        name="out_forward",
        out_shape=jax.ShapeDtypeStruct((block, width), HALF),
        grid=(block // tile,),
        in_specs=[
            SMEM,
            SMEM,
            SMEM,
            pl.BlockSpec((tile, gate), lambda t: (t, 0)),
            pl.BlockSpec((tile, width), lambda t: (t, 0)),
            whole(1, width),
        ]
        + [FAR] * 8,
        out_specs=pl.BlockSpec((tile, width), lambda t: (t, 0)),
        scratch_shapes=[pltpu.VMEM((1, gate, width), HALF), pltpu.SemaphoreType.DMA((1,))],
        compiler_params=ROOM,
        cost_estimate=cost(6),
    )(me, live, base, gated, tokens, bias, *parts)


def put_halves(mine, made, send_ref, keep_ref):
    half, rows, _ = send_ref.shape
    for k in range(half):
        rel = ((k >> 3) & 1) * 2 + ((k >> 2) & 1) * 4 + ((k >> 1) & 1) * 8 + (k & 1) * 16
        for side, ref in ((0, keep_ref), (1, send_ref)):
            ref[k] = made[pl.ds(pl.multiple_of(((rel + side) ^ mine) * rows, rows), rows), :]


def gate_kernel(me, branch_grad, normed, ssm, act, slope, parts, expand_parts):
    block, width = branch_grad.shape
    gate, channels = act.shape[1], ssm.shape[1]
    groups, sub = 4, 256
    depth = gate // groups
    half = 1 << (MAIN - 1)
    value_rows, expand_rows = width // (2 * half), channels // (2 * half)

    def body(me, grad_ref, x_ref, ssm_ref, act_ref, slope_ref, p0, p1, p2, p3, p4, p5, p6, p7,
             q0, q1, q2, q3, q4, q5, q6, q7, value_ref, expand_sum, value_sum, state_ref,
             value_send, value_keep, expand_send, expand_keep,
             expand_ref, made, made_low, weight, expand_weight, sems, expand_sems):
        j = pl.program_id(0)

        @pl.when(j == 0)
        def _():
            load_weights(me[0], (p0, p1, p2, p3, p4, p5, p6, p7), weight, OUT_PIECES, sems)
            load_weights(
                me[0], (q0, q1, q2, q3, q4, q5, q6, q7), expand_weight, EXPAND_PIECES, expand_sems
            )
            state_ref[...] = jnp.zeros_like(state_ref)

        for g in range(groups):

            @pl.when(j == g)
            def _():
                await_weights(weight, g, sems)
                await_weights(expand_weight, g, expand_sems)

        for c in range(depth // sub):
            cols = pl.ds(c * sub, sub)
            gated_grad = dot(grad_ref[...], weight[j, cols, :], 1, 1)
            expand = gated_grad * act_ref[:, cols].astype(SINGLE)
            value = gated_grad * slope_ref[:, cols].astype(SINGLE)
            expand_ref[:, cols] = expand.astype(HALF)
            value_ref[:, cols] = value.astype(HALF)
            expand_sum[:, cols] = fold(expand)
            value_sum[:, cols] = fold(value)
        for c in range(depth // sub):
            cols = pl.ds(c * sub, sub)
            made[:, cols] = dot(x_ref[...], value_ref[:, cols], 0, 0).astype(HALF)
            made_low[:, cols] = dot(ssm_ref[...], expand_ref[:, cols], 0, 0).astype(HALF)
        state_ref[...] += dot(expand_ref[...], expand_weight[j], 1, 1)
        put_halves(me[0], made, value_send, value_keep)
        put_halves(me[0], made_low, expand_send, expand_keep)

    wide = pl.BlockSpec((block, depth), lambda j: (0, j))
    sums = pl.BlockSpec((8, depth), lambda j: (0, j))
    halves = [
        (jax.ShapeDtypeStruct((half, groups * rows, depth), HALF),
         pl.BlockSpec((half, rows, depth), lambda j: (0, j, 0)))
        for rows in (value_rows, value_rows, expand_rows, expand_rows)
    ]
    return pl.pallas_call(
        body,
        name="gate_backward",
        out_shape=[jax.ShapeDtypeStruct((block, gate), HALF)]
        + [jax.ShapeDtypeStruct((8, gate), SINGLE)] * 2
        + [jax.ShapeDtypeStruct((block, channels), SINGLE)]
        + [h[0] for h in halves],
        grid=(groups,),
        in_specs=[
            SMEM,
            once(block, width),
            once(block, width),
            once(block, channels),
            wide,
            wide,
        ]
        + [FAR] * 16,
        out_specs=[wide, sums, sums, once(block, channels)] + [h[1] for h in halves],
        scratch_shapes=[
            pltpu.VMEM((block, depth), HALF),
            pltpu.VMEM((width, depth), HALF),
            pltpu.VMEM((channels, depth), HALF),
            pltpu.VMEM((groups, depth, width), HALF),
            pltpu.VMEM((groups, channels, depth), HALF),
            pltpu.SemaphoreType.DMA((groups,)),
            pltpu.SemaphoreType.DMA((groups,)),
        ],
        compiler_params=ROOM,
        cost_estimate=cost(16),
    )(me, branch_grad, normed, ssm, act, slope, *parts, *expand_parts)


def state_kernel(me, ends, base, ssm_grad, act, decay, parts):
    block, channels = ssm_grad.shape
    columns, tile = channels // 128, 256

    def body(me, ends_ref, base_ref, grad_ref, act_ref, decay_ref, s0, s1, s2, s3,
             ssm_ref, total_ref, span_ref, map_ref, skip_sum, weight, sems):
        load_weights(me[0], (s0, s1, s2, s3), weight, STATE_PIECES, sems)
        sums = jnp.zeros((8, channels), SINGLE)
        for t in range(block // tile):
            rows = pl.ds(t * tile, tile)
            grad = grad_ref[rows, :]
            ssm_ref[rows, :] = grad.astype(HALF)
            sums += fold(grad * act_ref[rows, :])
        skip_sum[...] = sums
        await_weights(weight, 0, sems)
        for c in range(channels // 256):
            state = dot(ssm_ref[...], weight[0, c * 256 : (c + 1) * 256, :], 1, 1)
            total_ref[2 * c], total_ref[2 * c + 1] = state[:, :128], state[:, 128:]
        product, ending = scan_block(ends_ref, base_ref[0], decay_ref[...], total_ref, True)
        span_ref[0], span_ref[1] = product, ending
        map_ref[0:1, :], map_ref[1:2, :] = whole_map(product, ending, True)

    vm = pl.BlockSpec(memory_space=pltpu.VMEM)
    return pl.pallas_call(
        body,
        name="state_backward",
        out_shape=[
            jax.ShapeDtypeStruct((block, channels), HALF),
            jax.ShapeDtypeStruct((columns, block, 128), SINGLE),
            jax.ShapeDtypeStruct((2, SEGMENTS, channels), SINGLE),
            jax.ShapeDtypeStruct((2, channels), SINGLE),
            jax.ShapeDtypeStruct((8, channels), SINGLE),
        ],
        in_specs=[SMEM] * 3 + [vm] * 3 + [FAR] * 4,
        out_specs=[vm] * 5,
        scratch_shapes=[pltpu.VMEM((1, channels, channels), HALF), pltpu.SemaphoreType.DMA((1,))],
        compiler_params=ROOM,
        cost_estimate=cost(4),
    )(me, ends, base, ssm_grad, act, decay, *parts)


def input_kernel(me, place, ends, base, maps, spans, totals, act, prior, ssm_grad, slope, skip,
                 inflow, decay, gain, tokens, cotangent, value_grad, weight,
                 small_parts):
    block, width = tokens.shape
    channels = act.shape[1]
    gate = value_grad.shape[1]
    tile, sub = 256, 256
    columns = channels // 128
    span = block // SEGMENTS

    def body(me, place_ref, ends_ref, base_ref, maps_ref, span_ref, total_ref, act_ref,
             prior_ref, ssm_ref, slope_ref, skip_ref, inflow_ref, decay_ref, gain_ref,
             weight_ref, x_far, cot_far, value_far, s0, s1, s2, s3,
             reduce_ref, out_ref, channel_sums, norm_sums, carry_ref, grads, small,
             x_ref, cot_ref, value_ref, small_sems, sems):
        j = pl.program_id(0)
        value_copy = pltpu.make_async_copy(value_far, value_ref, sems.at[0])
        x_copy = pltpu.make_async_copy(x_far, x_ref, sems.at[1])
        cot_copy = pltpu.make_async_copy(cot_far, cot_ref, sems.at[2])

        @pl.when(j == 0)
        def _():
            load_weights(me[0], (s0, s1, s2, s3), small, REDUCE_PIECES, small_sems)
            value_copy.start()
            x_copy.start()
            cot_copy.start()
            entering = block_carry(place_ref[0], maps_ref, True)
            carries, _ = span_carries(span_ref[0], span_ref[1], entering, True)
            table = span_table(decay_ref[...], span, True)
            for s in range(SEGMENTS):
                carry_ref[s] = jnp.broadcast_to(carries[s], (8, channels))

            def one_span(s, sums):
                rows = pl.ds(pl.multiple_of(s * span, span), span)
                product = span_products(ends_ref, base_ref[0] + s * span, table, 128, True)
                total = lanes_joined(total_ref, rows) + product * carry_ref[s][:1]
                reduced = ssm_ref[rows, :].astype(SINGLE) * skip_ref[...] + inflow_ref[...] * total
                reduced = reduced * slope_ref[rows, :].astype(SINGLE)
                reduce_ref[rows, :] = reduced.astype(HALF)
                terms = (total * prior_ref[rows, :].astype(SINGLE), total * act_ref[rows, :], reduced)
                return [old + fold(new) for old, new in zip(sums, terms)]

            sums = [jnp.zeros((8, channels), SINGLE)] * 3
            sums = lax.fori_loop(0, SEGMENTS, one_span, sums)
            for i in range(3):
                channel_sums[i] = sums[i]
            await_weights(small, 0, small_sems)
            value_copy.wait()

        at = pl.ds(pl.multiple_of(j * sub, sub), sub)
        grads[j] = dot(value_ref[...], weight_ref[...], 1, 1) + dot(
            reduce_ref[...], small[0, at, :], 1, 1
        )

        @pl.when(j == width // sub - 1)
        def _():
            x_copy.wait()
            cot_copy.wait()
            norm_sums[...] = jnp.zeros_like(norm_sums)

            def norm_back(t, carry):
                rows = pl.ds(pl.multiple_of(t * tile, tile), tile)
                grad = lanes_joined(grads, rows)
                n, inverse = norm_terms(x_ref[rows, :].astype(SINGLE))
                norm_sums[0] += fold(grad * n)
                norm_sums[1] += fold(grad)
                h = grad * gain_ref[...]
                mean_h = jnp.mean(h, axis=-1, keepdims=True)
                mean_hn = jnp.mean(h * n, axis=-1, keepdims=True)
                back = inverse * (h - mean_h - n * mean_hn)
                out_ref[rows, :] = (cot_ref[rows, :].astype(SINGLE) + back).astype(HALF)
                return carry

            lax.fori_loop(0, block // tile, norm_back, 0)

    tall = once(columns, block, 128)
    narrow = once(block, channels)
    return pl.pallas_call(
        body,
        name="input_backward",
        out_shape=[
            jax.ShapeDtypeStruct((block, channels), HALF),
            jax.ShapeDtypeStruct((block, width), HALF),
            jax.ShapeDtypeStruct((3, 8, channels), SINGLE),
            jax.ShapeDtypeStruct((2, 8, width), SINGLE),
        ],
        grid=(width // sub,),
        in_specs=[
            SMEM,
            SMEM,
            SMEM,
            SMEM,
            whole(*maps.shape),
            whole(*spans.shape),
            tall,
            narrow,
            narrow,
            narrow,
            narrow,
            whole(1, channels),
            whole(1, channels),
            whole(1, channels),
            whole(1, width),
            pl.BlockSpec((sub, gate), lambda j: (j, 0)),
        ]
        + [FAR] * 7,
        out_specs=[narrow, once(block, width), whole(3, 8, channels), whole(2, 8, width)],
        scratch_shapes=[
            pltpu.VMEM((SEGMENTS, 8, channels), SINGLE),
            pltpu.VMEM((width // sub, block, sub), SINGLE),
            pltpu.VMEM((1, width, channels), HALF),
            pltpu.VMEM((block, width), HALF),
            pltpu.VMEM((block, width), HALF),
            pltpu.VMEM((block, gate), HALF),
            pltpu.SemaphoreType.DMA((1,)),
            pltpu.SemaphoreType.DMA((3,)),
        ],
        compiler_params=ROOM,
        cost_estimate=cost(10),
    )(me, place, ends, base, maps, spans, totals, act, prior, ssm_grad, slope, skip, inflow, decay,
      gain, weight, tokens, cotangent, value_grad, *small_parts)


def unpack_kernel(me, sizes, parts):
    shards = 1 << MAIN
    lanes = 128
    rates_at = 4

    def body(me, *refs):
        ins, outs, table = refs[:4], refs[4:-1], refs[-1]
        for side in range(4):
            for k in range(8):
                rel = (side >> 1) + (side & 1) * 2 + ((k >> 2) & 1) * 4
                rel += ((k >> 1) & 1) * 8 + (k & 1) * 16
                table[rel ^ me[0]] = ins[side][k, :, :lanes].astype(SINGLE)
        for i, n in enumerate(sizes):
            for shard in range(shards):
                outs[i][:, shard * n : (shard + 1) * n] = table[shard, i : i + 1, :n]
        rates = outs[rates_at][...]
        decay_ref, inflow_ref, pull_ref = outs[len(sizes) :]
        inflow = jnp.sqrt(one_less_exp(2.0 * rates))
        decay_ref[...] = jnp.exp(-rates)
        inflow_ref[...] = inflow
        pull_ref[...] = jnp.exp(-2.0 * rates) / inflow

    channels = parts[0].shape[2]
    rows = parts[0].shape[1]
    widths = [n * shards for n in sizes] + [sizes[rates_at] * shards] * 3
    return pl.pallas_call(
        body,
        name="unpack",
        out_shape=[jax.ShapeDtypeStruct((1, n), SINGLE) for n in widths],
        grid=(1,),
        in_specs=[SMEM]
        + [pl.BlockSpec((8, 8, channels), lambda i: (0, rows // 8 - 1, 0))] * 4,
        out_specs=[whole(1, n) for n in widths],
        scratch_shapes=[pltpu.VMEM((shards, 8, lanes), SINGLE)],
        compiler_params=ROOM,
        cost_estimate=cost(1),
    )(me, *parts)


def sums_kernel(me, sizes, norm_folds, value_fold, channel_folds, pull, skip_fold, expand_fold,
                out_fold):
    shards = 1 << MAIN
    half = shards // 2
    channels = skip_fold.shape[1]
    lanes = 128

    def body(me, norm_ref, value_ref, channel_ref, pull_ref, skip_ref, expand_ref, out_ref,
             send_ref, keep_ref, table):
        def total(values):
            return jnp.sum(values, axis=0, keepdims=True)

        rates = pull_ref[...] * total(channel_ref[1]) - total(channel_ref[0])
        rows = (
            total(norm_ref[0]),
            total(norm_ref[1]),
            total(value_ref[...]),
            total(channel_ref[2]),
            rates,
            total(skip_ref[...]),
            total(expand_ref[...]),
            total(out_ref[...]),
        )
        table[...] = jnp.zeros_like(table)
        for i, (n, row) in enumerate(zip(sizes, rows)):
            for shard in range(shards):
                table[shard, i : i + 1, :n] = row[:, shard * n : (shard + 1) * n]
        send_ref[...] = jnp.zeros_like(send_ref)
        keep_ref[...] = jnp.zeros_like(keep_ref)
        for k in range(half):
            rel = ((k >> 3) & 1) * 2 + ((k >> 2) & 1) * 4 + ((k >> 1) & 1) * 8 + (k & 1) * 16
            keep_ref[k, :, :lanes] = table[rel ^ me[0]].astype(HALF)
            send_ref[k, :, :lanes] = table[(rel + 1) ^ me[0]].astype(HALF)

    vm = pl.BlockSpec(memory_space=pltpu.VMEM)
    shape = jax.ShapeDtypeStruct((half, 8, channels), HALF)
    return pl.pallas_call(
        body,
        name="vector_sums",
        out_shape=[shape, shape],
        in_specs=[SMEM] + [vm] * 7,
        out_specs=[vm] * 2,
        scratch_shapes=[pltpu.VMEM((shards, 8, lanes), SINGLE)],
        compiler_params=ROOM,
        cost_estimate=cost(0.1),
    )(me, norm_folds, value_fold, channel_folds, pull, skip_fold, expand_fold, out_fold)


def finish_kernel(sizes, wide, small, high, low, gate):
    groups = gate // wide[0].shape[1]

    def body(w0, w1, w2, s0, s1, s2, *outs):
        def total(refs, rows):
            first, second, third = (ref[rows, :].astype(SINGLE) for ref in refs)
            return first + second + third

        width = w0.shape[1]
        value_ref, expand_ref, reduce_ref, state_ref = outs[:4]
        for g in range(groups):
            cols = pl.ds(g * width, width)
            value_ref[:, cols] = total((w0, w1, w2), pl.ds(g * high, high))
            expand_ref[:, cols] = total((w0, w1, w2), pl.ds(groups * high + g * low, low))
        reduce_ref[...] = total((s0, s1, s2), pl.ds(0, high))
        state_ref[...] = total((s0, s1, s2), pl.ds(high, low))
        rows = total((s0, s1, s2), pl.ds(high + low, 8))
        for i, n in enumerate(sizes):
            outs[4 + i][...] = rows[i : i + 1, :n]

    channels = small[0].shape[1]
    vm = pl.BlockSpec(memory_space=pltpu.VMEM)
    shapes = [(high, gate), (low, gate), (high, channels), (low, channels)]
    shapes += [(1, n) for n in sizes]
    return pl.pallas_call(
        body,
        name="finish",
        out_shape=[jax.ShapeDtypeStruct(s, SINGLE) for s in shapes],
        in_specs=[vm] * 6,
        out_specs=[vm] * len(shapes),
        compiler_params=ROOM,
        cost_estimate=cost(1),
    )(*wide, *small)


def pack_kernel(vectors, reduce_shard, state_shard, expand_shard, out_shard):
    channels = state_shard.shape[1]
    high, low = reduce_shard.shape[0], state_shard.shape[0]
    groups, depth = 4, expand_shard.shape[1] // 4

    def body(*refs):
        vector_refs, refs = refs[: len(vectors)], refs[len(vectors) :]
        reduce_ref, state_ref, expand_ref, out_ref, small, expand, out, table = refs
        table[...] = jnp.zeros_like(table)
        for i, ref in enumerate(vector_refs):
            table[i : i + 1, : ref.shape[1]] = ref[...]
        small[:high, :] = reduce_ref[...].astype(HALF)
        small[high : high + low, :] = state_ref[...].astype(HALF)
        small[high + low :, :] = table[...].astype(HALF)
        for g in range(groups):
            cols = pl.ds(g * depth, depth)
            expand[g * low : (g + 1) * low, :] = expand_ref[:, cols].astype(HALF)
        out[...] = out_ref[...].astype(HALF)

    vm = pl.BlockSpec(memory_space=pltpu.VMEM)
    return pl.pallas_call(
        body,
        name="pack",
        out_shape=[
            jax.ShapeDtypeStruct((high + low + len(vectors), channels), HALF),
            jax.ShapeDtypeStruct((groups * low, depth), HALF),
            jax.ShapeDtypeStruct(out_shard.shape, HALF),
        ],
        in_specs=[vm] * (len(vectors) + 4),
        out_specs=[vm] * 3,
        scratch_shapes=[pltpu.VMEM((len(vectors), channels), SINGLE)],
        compiler_params=ROOM,
        cost_estimate=cost(1),
    )(*[v[None] for v in vectors], reduce_shard, state_shard, expand_shard, out_shard)


def weight_grad(left, right, column_block, me, name, micros):
    tokens, height = left.shape
    width = right.shape[1]
    blocks, sub = width // column_block, 256
    half = 1 << (MAIN - 1)
    shard_rows = height // (2 * half)

    def body(me_ref, left_ref, right_ref, send_ref, keep_ref, made):
        mine = me_ref[0]

        def product(c):
            return dot(left_ref[...], right_ref[:, c * sub : (c + 1) * sub], 0, 0)

        def finish(c, value):
            made[:, pl.ds(c * sub, sub)] = value.astype(HALF)

        staged(column_block // sub, product, finish)
        put_halves(mine, made, send_ref, keep_ref)

    shape = jax.ShapeDtypeStruct((half, blocks * shard_rows, column_block), HALF)
    spec = pl.BlockSpec((half, shard_rows, column_block), lambda j: (0, j, 0))
    return pl.pallas_call(
        body,
        name=name,
        out_shape=[shape, shape],
        grid=(blocks,),
        in_specs=[
            SMEM,
            once(tokens, height),
            pl.BlockSpec((tokens, column_block), lambda j: (0, j)),
        ],
        out_specs=[spec, spec],
        scratch_shapes=[pltpu.VMEM((height, column_block), HALF)],
        compiler_params=ROOM,
        cost_estimate=cost(micros),
    )(me, left, right)


def add_low(first, second):
    return (first.astype(SINGLE) + second.astype(SINGLE)).astype(HALF)


def core_exchange(values):
    return exchange(values, low_bits())


def reduce_steps(pairs, split):
    bit_x, bit_y, bit_z, bit_far = (low_bits() + i for i in range(1, MAIN))
    total = [[a.reshape((2, 2, 4) + a.shape[1:]) for a in pair] for pair in pairs]

    def added(x, y, first, last):
        parts, at = [], 0
        for keep, other in total:
            low, high = max(first - at, 0), min(last - at, keep.shape[3])
            if low < high:
                parts.append(add_low(keep[x, y, :, low:high], other[x, y, :, low:high]))
            at += keep.shape[3]
        return parts[0] if len(parts) == 1 else jnp.concatenate(parts, axis=-2)

    rows = sum(keep.shape[1] for keep, _ in pairs)
    every = slice(None)
    if split:
        from_x, from_y = yield [
            exchange(added(1, every, 0, split), bit_x),
            exchange(added(every, 1, split, rows), bit_y),
        ]
        kept_x, kept_y = added(0, every, 0, split), added(every, 0, split, rows)
        last_y, last_x = yield [
            exchange(add_low(kept_x[1], from_x[1]), bit_y),
            exchange(add_low(kept_y[1], from_y[1]), bit_x),
        ]
        first = add_low(add_low(kept_x[0], from_x[0]), last_y)
        second = add_low(add_low(kept_y[0], from_y[0]), last_x)
        total = jnp.concatenate([first, second], axis=1)
    else:
        (other,) = yield [exchange(added(1, every, 0, rows), bit_x)]
        kept = added(0, every, 0, rows)
        (last,) = yield [exchange(add_low(kept[1], other[1]), bit_y)]
        total = add_low(add_low(kept[0], other[0]), last)
    (other,) = yield [exchange(total[2:], bit_z)]
    (last,) = yield [exchange(add_low(total[1], other[1]), bit_far)]
    return total[0], other[0], last


class Run:
    def __init__(self, steps):
        self.steps, self.result = steps, None
        self.pending = next(steps)

    def step(self):
        try:
            self.pending = self.steps.send(self.pending)
        except StopIteration as stop:
            self.pending, self.result = None, stop.value


def tie(values):
    return lax.optimization_barrier(values)


def one_less_exp(y):
    series = jnp.ones_like(y)
    for n in range(9, 1, -1):
        series = 1.0 - series * y * (1.0 / n)
    return jnp.where(y < 0.5, y * series, 1.0 - jnp.exp(-y))


def on_device(
    tokens,
    lengths,
    cotangent,
    norm_gain,
    norm_shift,
    value_weight,
    value_bias,
    reduce_weight,
    reduce_bias,
    decay_rates,
    skip_gain,
    state_weight,
    expand_weight,
    expand_bias,
    out_weight,
    out_bias,
):
    half, single = HALF, SINGLE
    shards = 1 << MAIN
    me = (device_number() >> low_bits()).reshape(1).astype(jnp.int32)
    value_mat = lax.all_gather(value_weight.astype(half), ("dp", "seq"), axis=0, tiled=True)
    vectors = [
        gather_low(v)
        for v in (
            norm_gain,
            norm_shift,
            value_bias,
            reduce_bias,
            decay_rates,
            skip_gain,
            expand_bias,
            out_bias,
        )
    ]
    sizes = [v.shape[0] for v in vectors]
    small, expand_rows, out_rows = pack_kernel(
        vectors,
        gather_low(reduce_weight),
        gather_low(state_weight),
        gather_low(expand_weight),
        gather_low(out_weight),
    )
    channels = state_weight.shape[1]
    width = tokens.shape[-1]
    blocks = value_weight.shape[1] // width
    small_run = Run(gather_steps(small, 0))
    small_run.pending, expand_rows, out_rows = tie((small_run.pending, expand_rows, out_rows))
    small_run.step()
    expand_run = Run(gather_steps(expand_rows, 32))
    small_run.pending, expand_run.pending, out_rows = tie(
        (small_run.pending, expand_run.pending, out_rows)
    )
    small_run.step()
    expand_run.step()
    out_run = Run(gather_steps(out_rows, 48))
    small_run.pending, expand_run.pending, out_run.pending = tie(
        (small_run.pending, expand_run.pending, out_run.pending)
    )
    small_run.step()
    expand_run.step()
    out_run.step()
    small_run.step()
    small_parts = small_run.result

    row_count, block, _ = tokens.shape
    place = lax.axis_index("seq").reshape(1).astype(jnp.int32)
    base = place * block
    positions = base + jnp.arange(block, dtype=jnp.int32)
    ends = jnp.cumsum(lengths, axis=-1).reshape(-1)
    live = ends[-1:]
    token_rows, cot_rows = tokens.reshape(block, width), cotangent.reshape(block, width)
    branch_grad = jnp.where((positions < live)[:, None], cot_rows, jnp.zeros_like(cot_rows))
    out_fold = fold(branch_grad.astype(single))

    vectors = unpack_kernel(me, sizes, small_parts)
    gain, shift, value_add, reduce_add, _, skip, expand_add, out_add = vectors[:8]
    decays, inflow, inflow_pull = vectors[8:]
    expand_run.pending, out_run.pending, me = tie(
        (expand_run.pending, out_run.pending, me)
    )
    expand_run.step()
    out_run.step()

    normed, act, reduce_slope, states, spans, own_map = reduce_kernel(
        (me, ends, base), token_rows, gain, shift, reduce_add, decays, inflow, small_parts
    )
    own_map, me = tie((own_map, me))
    maps = gather_maps(own_map)
    states_low, prior, ssm_low = states_kernel(
        me, place, ends, base, maps, spans, states, act, skip, inflow, decays, small_parts
    )
    expand_run.pending, out_run.pending, ssm_low, me = tie(
        (expand_run.pending, out_run.pending, ssm_low, me)
    )
    expand_run.step()
    expand_run.pending, me = tie((expand_run.pending, me))
    expand_run.step()
    expand_parts = expand_run.result
    out_run.step()

    value_act, gated, gate_slope, out_grads = forward_kernel(
        me, normed, ssm_low, branch_grad, value_add, expand_add, value_mat, expand_parts
    )
    out_run.pending, gated, me = tie((out_run.pending, gated, me))
    out_run.step()
    out_run.pending, me = tie((out_run.pending, me))
    out_run.step()
    out_parts = out_run.result
    out_sum = lax.psum_scatter(out_grads, ("dp", "seq"), scatter_dimension=0, tiled=True)
    value_grad, expand_fold, value_fold, ssm_grad, *halves = gate_kernel(
        me, branch_grad, normed, ssm_low, value_act, gate_slope, out_parts, expand_parts
    )
    halves, me = tie((halves, me))

    others = [core_exchange(halves[0]), core_exchange(halves[2])]
    ssm_grad, totals, back_spans, back_map, skip_fold = state_kernel(
        me, ends, base, ssm_grad, act, decays, small_parts
    )
    state_halves = weight_grad(states_low, ssm_grad, channels, me, "grad_state", 1)
    others, state_halves, back_map, me = tie((others, state_halves, back_map, me))

    wide_run = Run(reduce_steps([(halves[1], others[0]), (halves[3], others[1])], 96))
    back_maps = gather_maps(back_map)
    reduce_grad, grad_tokens, channel_folds, norm_folds = input_kernel(
        me, place, ends, base, back_maps, back_spans, totals, act, prior, ssm_grad, reduce_slope,
        skip, inflow, decays, gain, token_rows, cot_rows, value_grad, value_mat, small_parts
    )
    wide_run.pending, reduce_grad, norm_folds, me = tie(
        (wide_run.pending, reduce_grad, norm_folds, me)
    )

    wide_run.step()
    reduce_halves = weight_grad(normed, reduce_grad, channels, me, "grad_reduce", 2)
    table_halves = sums_kernel(
        me, sizes, norm_folds, value_fold, channel_folds, inflow_pull, skip_fold, expand_fold,
        out_fold
    )
    small_others = [core_exchange(h[0]) for h in (reduce_halves, state_halves, table_halves)]
    small_run = Run(
        reduce_steps(
            [
                (halves[1], other)
                for halves, other in zip((reduce_halves, state_halves, table_halves), small_others)
            ],
            0,
        )
    )
    output = out_kernel(me, live, base, gated, token_rows, out_add, out_parts)
    wide_run.pending, small_run.pending, output, out_sum = tie(
        (wide_run.pending, small_run.pending, output, out_sum)
    )

    wide_run.step()
    small_run.step()
    wide_run.pending, small_run.pending = tie((wide_run.pending, small_run.pending))

    for run in (small_run, wide_run):
        while run.result is None:
            run.step()
    value_sum, expand_sum, reduce_sum, state_sum, *vector_sums = finish_kernel(
        sizes, wide_run.result, small_run.result, width // shards, channels // shards, width * blocks
    )
    vector_sums = [reduce_low(v[0]) for v in vector_sums]
    return (
        output.reshape(tokens.shape),
        grad_tokens.reshape(tokens.shape),
        vector_sums[0],
        vector_sums[1],
        reduce_low(value_sum),
        vector_sums[2],
        reduce_low(reduce_sum),
        vector_sums[3],
        vector_sums[4],
        vector_sums[5],
        reduce_low(state_sum),
        reduce_low(expand_sum),
        vector_sums[6],
        out_sum.astype(single),
        vector_sums[7],
    )


def solution(mesh):
    rows, vector, matrix = P("dp", "seq", None), P(("dp", "seq")), P(("dp", "seq"), None)
    return jax.shard_map(
        on_device,
        mesh=mesh,
        in_specs=(
            rows,
            P("dp", None),
            rows,
            vector,
            vector,
            matrix,
            vector,
            matrix,
            vector,
            vector,
            vector,
            matrix,
            matrix,
            vector,
            matrix,
            vector,
        ),
        out_specs=(
            rows,
            rows,
            vector,
            vector,
            matrix,
            vector,
            matrix,
            vector,
            vector,
            vector,
            matrix,
            matrix,
            vector,
            matrix,
            vector,
        ),
        check_vma=False,
    )
```

time: 455 us -> 308 us (0.68)
  waiting for transfers between devices: 140 us -> 76.9 us
  local copies, waits for them, and re-layouts: 45.6 us -> 6.28 us
  Pallas kernels: 155 us -> 136 us
  starting transfers between devices: 61.1 us -> 42.8 us
  other arithmetic: 45.4 us -> 29.7 us
  between operations: 2.45 us -> 14.6 us
    ppermute x59 -> x46, waiting for transfers between devices: 140 us -> 76.9 us  [exchange(): lax.ppermute(values, axis, [(i, i ^ flip) for i in range(lax.axis_size(ax...]
    unnamed x143 -> x50, local copies, waits for them, and re-layouts: 29.7 us -> 3.48 us
    pallas_call x7 -> x8, Pallas kernels: 75.2 us -> 49.9 us  [the longest x1 28.9 us: forward_kernel(): pl.pallas_call(body, name='gate_forward', out_shape=[jax.ShapeDtypeStruct...]
    ppermute x59 -> x46, starting transfers between devices: 61.1 us -> 42.8 us  [exchange(): lax.ppermute(values, axis, [(i, i ^ flip) for i in range(lax.axis_size(ax...]
    pallas_call x1, Pallas kernels: 17.6 us -> 31.5 us  [gate_kernel(): pl.pallas_call(body, name='gate_backward', out_shape=[jax.ShapeDtypeStruc...]
    concatenate x25 -> x12, other arithmetic: 13.2 us -> 4.51 us  [join(): return jnp.concatenate([own, other])]
    pallas_call x1, Pallas kernels: 16.1 us -> 7.88 us  [state_kernel(): pl.pallas_call(body, name='state_backward', out_shape=[jax.ShapeDtypeStru...]
    convert_element_type x13 -> x2, other arithmetic: 8.97 us -> 2.48 us  [the longest x1 1.7 us: on_device(): value_weight.astype(half)]
  transfers between devices with their start and end apart: 59 -> 48, of which waited for: 25 -> 23; matrix products, arithmetic and copies ran while one was open for 12% -> 9% of each run, Pallas kernels for 27% -> 44%
where the time goes in v3:
time: 308 us; the launch traced here: 307 us
  Pallas kernels  136 us (44%)
  waiting for transfers between devices  76.9 us (25%)
  starting transfers between devices  42.8 us (14%)
  other arithmetic  29.7 us (10%)
  between operations  14.6 us (5%)
  local copies, waits for them, and re-layouts  6.28 us (2%)
    ppermute x46, waiting for transfers between devices, exchange(): lax.ppermute(values, axis, [(i, i ^ flip) for i in range(lax.axis_size(ax...  76.9 us
    ppermute x46, starting transfers between devices, exchange(): lax.ppermute(values, axis, [(i, i ^ flip) for i in range(lax.axis_size(ax...  42.8 us
    pallas_call x1, Pallas kernels, gate_kernel(): pl.pallas_call(body, name='gate_backward', out_shape=[jax.ShapeDtypeStruc...  31.5 us
    pallas_call x1, Pallas kernels, forward_kernel(): pl.pallas_call(body, name='gate_forward', out_shape=[jax.ShapeDtypeStruct...  28.9 us
    pallas_call x1, Pallas kernels, input_kernel(): pl.pallas_call(body, name='input_backward', out_shape=[jax.ShapeDtypeStru...  20.5 us
    pallas_call x1, Pallas kernels, out_kernel(): pl.pallas_call(body, name='out_forward', out_shape=jax.ShapeDtypeStruct((...  15.1 us
    convert_element_type x13, other arithmetic, add_low(): return (first.astype(SINGLE) + second.astype(SINGLE)).astype(HALF)  15 us
    pallas_call x1, Pallas kernels, reduce_kernel(): pl.pallas_call(body, name='reduce_forward', out_shape=[jax.ShapeDtypeStru...  11.3 us
  transfers between devices with their start and end apart: 48, of which 23 were waited for; matrix products, arithmetic and copies ran while one was open for 9% of the time, Pallas kernels for 44%

profile of v3, /device:TPU:0, one launch (start us, length us, event | category | flops | bytes accessed | tf_op | source)
XLA Modules:
  0.0 306.6 jit_solution(13037306287047711858)
XLA Ops:
  7.2 1.7 convert_element_type.327
  9.0 2.0 pack.1
  11.0 5.1 %collective-permute-start.2 = (bf16[1,56,512]{2,1,0:T(8,128)(2,1)}, bf16[1,56,512]{2,1,0:T(8,128)(2,1)S(1)}, u32[]{:S(2)}, u32[]{:S(2)}) collective-permute-start(bf16[1,56,512]{2,1,0:T(8,128)(2,1)} %bitcast.148), channel_id=1, source_target_pairs={{0,24},{4,28},{8,16},{12,20},{16,8},{20,12},{24,0},{28,4},{1,25},{... | collective-permute-start | bytes 172040 | tf_op jit(solution)/shard_map/ppermute | solution.py:32
  17.6 1.3 collective-permute-done.2
  19.0 1.7 collective-permute-done.1
  20.6 1.2 collective-permute-done
  21.8 1.6 collective-permute-start.4
  24.2 1.6 collective-permute-start.3
  25.9 3.8 %collective-permute-done.4 = bf16[1,64,768]{2,1,0:T(8,128)(2,1)S(1)} collective-permute-done((bf16[1,64,768]{2,1,0:T(8,128)(2,1)}, bf16[1,64,768]{2,1,0:T(8,128)(2,1)S(1)}, u32[]{:S(2)}, u32[]{:S(2)}) %collective-permute-start.4) | collective-permute-done | bytes 98336 | tf_op jit(solution)/shard_map/ppermute | solution.py:32
  29.7 1.5 collective-permute-done.3
  31.3 1.5 collective-permute-start.5
  32.9 1.0 collective-permute-start.7
  33.9 1.9 collective-permute-start.8
  35.8 7.4 %collective-permute-done.7 = bf16[2,64,768]{2,1,0:T(8,128)(2,1)S(1)} collective-permute-done((bf16[2,64,768]{2,1,0:T(8,128)(2,1)S(1)}, bf16[2,64,768]{2,1,0:T(8,128)(2,1)S(1)}, u32[]{:S(2)}, u32[]{:S(2)}) %collective-permute-start.7) | collective-permute-done | bytes 196640 | tf_op jit(solution)/shard_map/ppermute | solution.py:32
  43.3 5.8 %collective-permute-done.8 = bf16[1,96,1024]{2,1,0:T(8,128)(2,1)S(1)} collective-permute-done((bf16[1,96,1024]{2,1,0:T(8,128)(2,1)S(1)}, bf16[1,96,1024]{2,1,0:T(8,128)(2,1)S(1)}, u32[]{:S(2)}, u32[]{:S(2)}) %collective-permute-start.8) | collective-permute-done | bytes 196640 | tf_op jit(solution)/shard_map/ppermute | solution.py:32
  52.3 5.2 %collective-permute-done.10 = bf16[4,32,768]{2,1,0:T(8,128)(2,1)S(1)} collective-permute-done((bf16[4,32,768]{2,1,0:T(8,128)(2,1)S(1)}, bf16[4,32,768]{2,1,0:T(8,128)(2,1)S(1)}, u32[]{:S(2)}, u32[]{:S(2)}) %collective-permute-start.10) | collective-permute-done | bytes 196640 | tf_op jit(solution)/shard_map/ppermute | solution.py:32
  57.6 4.6 %collective-permute-done.11 = bf16[2,96,1024]{2,1,0:T(8,128)(2,1)S(1)} collective-permute-done((bf16[2,96,1024]{2,1,0:T(8,128)(2,1)S(1)}, bf16[2,96,1024]{2,1,0:T(8,128)(2,1)S(1)}, u32[]{:S(2)}, u32[]{:S(2)}) %collective-permute-start.11) | collective-permute-done | bytes 393248 | tf_op jit(solution)/shard_map/ppermute | solution.py:32
  64.1 1.9 unpack.1
  66.0 11.3 %reduce_forward.1 = (bf16[1024,1024]{1,0:T(8,128)(2,1)}, f32[1024,512]{1,0:T(8,128)}, bf16[1024,512]{1,0:T(8,128)(2,1)}, f32[4,1024,128]{2,1,0:T(8,128)}, f32[2,8,512]{2,1,0:T(8,128)}, /*index=5*/f32[2,512]{1,0:T(2,128)}) custom-call(s32[1]{0:T(128)} %bitcast.11.me.me_ref, s32[8]{0:T(128)} %bitcast.171, s32[1]{0:T(128)} %mul.7.base.base_ref, ...), custom_call_target="tpu_custom_call" | custom-call | flops 8000000000 | bytes 1048576 | tf_op jit(solution)/shard_map/reduce_forward/pallas_call | solution.py:312
  77.5 1.2 collective-permute-done.19
  78.7 1.6 collective-permute-start.20
  80.4 3.5 %collective-permute-done.20 = f32[2,2,512]{2,1,0:T(2,128)S(1)} collective-permute-done((f32[2,2,512]{2,1,0:T(2,128)S(1)}, f32[2,2,512]{2,1,0:T(2,128)S(1)}, u32[]{:S(2)}, u32[]{:S(2)}) %collective-permute-start.20) | collective-permute-done | bytes 8224 | tf_op jit(solution)/shard_map/ppermute | solution.py:32
  84.4 1.5 collective-permute-start.16
  86.5 5.8 %states_forward.1 = (bf16[1024,512]{1,0:T(8,128)(2,1)}, bf16[1024,512]{1,0:T(8,128)(2,1)}, bf16[1024,512]{1,0:T(8,128)(2,1)}) custom-call(s32[1]{0:T(128)} %bitcast.11.me.me_ref, s32[1]{0:T(128)} %bitcast.13.place_ref, s32[8]{0:T(128)} %bitcast.172, s32[1]{0:T(128)} %mul.7.base.base_ref, f32[4,2,512]{2,1,0:T(2,128)} %pad_maximum_fusion.14.maps_ref, ...), custom_call_target="tpu_custom_call" | custom-call | flops 3000000000 | bytes 1048576 | tf_op jit(solution)/shard_map/states_forward/pallas_call | solution.py:376
  92.4 2.1 collective-permute-done.17
  95.3 1.5 broadcast_select_fusion.grad_ref
  96.8 1.1 pad_maximum_fusion.3.p4
  98.0 1.6 collective-permute-start.22
  99.6 2.0 pad_maximum_fusion.2.p0
  101.7 1.3 collective-permute-start.21
  103.0 28.9 %gate_forward.1 = (bf16[1024,3072]{1,0:T(8,128)(2,1)}, bf16[1024,3072]{1,0:T(8,128)(2,1)}, bf16[1024,3072]{1,0:T(8,128)(2,1)}, bf16[3072,1024]{1,0:T(8,128)(2,1)}) custom-call(s32[1]{0:T(128)} %bitcast.11.me.me_ref, bf16[1024,1024]{1,0:T(8,128)(2,1)} %get-tuple-element.175.x_ref.left_ref, bf16[1024,512]{1,0:T(8,128)(2,1)} %get-tuple-element.176.ssm_ref, ...), custom_call_target="tpu_custom_call" | custom-call | flops 16000000000 | bytes 1048576 | tf_op jit(solution)/shard_map/gate_forward/pallas_call | solution.py:429
  132.5 2.3 collective-permute-done.27.p3
  135.7 31.5 %gate_backward.1 = (bf16[1024,3072]{1,0:T(8,128)(2,1)}, f32[8,3072]{1,0:T(8,128)}, f32[8,3072]{1,0:T(8,128)}, f32[1024,512]{1,0:T(8,128)}, bf16[16,128,768]{2,1,...) custom-call(s32[1]{0:T(128)} %bitcast.11.me.me_ref, ...), custom_call_target="tpu_custom_call" | custom-call | flops 16000000000 | bytes 1048576 | tf_op jit(solution)/shard_map/gate_backward/pallas_call | solution.py:568
  168.7 1.1 convert_reduce_fusion.out_ref
  169.8 7.9 %state_backward.1 = (bf16[1024,512]{1,0:T(8,128)(2,1)}, f32[4,1024,128]{2,1,0:T(8,128)}, f32[2,8,512]{2,1,0:T(8,128)}, f32[2,512]{1,0:T(2,128)}, f32[8,512]{1,0:T(8,128)}) custom-call(s32[1]{0:T(128)} %bitcast.11.me.me_ref, s32[8]{0:T(128)} %bitcast.173, s32[1]{0:T(128)} %mul.7.base.base_ref, f32[1024,512]{1,0:T(8,128)} %get-tuple-element.203.grad_ref, ...), custom_call_target="tpu_custom_call" | custom-call | flops 4000000000 | bytes 1048576 | tf_op jit(solution)/shard_map/state_backward/pallas_call | solution.py:623
  177.7 3.2 %grad_state.1 = (bf16[16,16,512]{2,1,0:T(8,128)(2,1)}, bf16[16,16,512]{2,1,0:T(8,128)(2,1)}) custom-call(s32[1]{0:T(128)} %bitcast.11.me.me_ref, bf16[1024,512]{1,0:T(8,128)(2,1)} %get-tuple-element.202.left_ref, bf16[1024,512]{1,0:T(8,128)(2,1)} %get-tuple-element.204.right_ref.ssm_ref), custom_call_target="tpu_custom_call" | custom-call | flops 1000000000 | bytes 1048576 | tf_op jit(solution)/shard_map/grad_state/pallas_call | solution.py:943
  181.5 2.0 fusion.6
  183.8 2.4 fusion
  186.2 1.3 fusion.15
  188.5 1.1 pad_maximum_fusion
  189.8 1.8 collective-permute-start.31
  192.2 20.5 %input_backward.1 = (bf16[1024,512]{1,0:T(8,128)(2,1)}, bf16[1024,1024]{1,0:T(8,128)(2,1)}, f32[3,8,512]{2,1,0:T(8,128)}, f32[2,8,1024]{2,1,0:T(8,128)}) custom-call(s32[1]{0:T(128)} %bitcast.11.me.me_ref, s32[1]{0:T(128)} %bitcast.13.place_ref, s32[8]{0:T(128)} %bitcast.174, s32[1]{0:T(128)} %mul.7.base.base_ref, f32[4,2,512]{2,1,0:T(2,128)} %pad_maximum_fusion.15.maps_ref, ...), custom_call_target="tpu_custom_call" | custom-call | flops 10000000000 | bytes 1048576 | tf_op jit(solution)/shard_map/input_backward/pallas_call | solution.py:718
  212.7 1.7 add_convert_fusion.13
  214.4 9.7 %collective-permute-done.32 = bf16[2,4,96,768]{3,2,1,0:T(8,128)(2,1)} collective-permute-done((bf16[2,4,96,768]{3,2,1,0:T(8,128)(2,1)}, bf16[2,4,96,768]{3,2,1,0:T(8,128)(2,1)}, u32[]{:S(2)}, u32[]{:S(2)}) %collective-permute-start.32) | collective-permute-done | bytes 1179680 | tf_op jit(solution)/shard_map/ppermute | solution.py:32
  224.3 2.0 vector_sums.1
  226.2 4.1 %grad_reduce.1 = (bf16[16,32,512]{2,1,0:T(8,128)(2,1)}, bf16[16,32,512]{2,1,0:T(8,128)(2,1)}) custom-call(s32[1]{0:T(128)} %bitcast.11.me.me_ref, bf16[1024,1024]{1,0:T(8,128)(2,1)} %get-tuple-element.175.x_ref.left_ref, bf16[1024,512]{1,0:T(8,128)(2,1)} %get-tuple-element.223.right_ref), custom_call_target="tpu_custom_call" | custom-call | flops 2000000000 | bytes 1048576 | tf_op jit(solution)/shard_map/grad_reduce/pallas_call | solution.py:943
  230.9 2.1 fusion.7
  233.0 1.4 collective-permute-start.36
  234.4 1.2 fusion.9
  237.3 1.5 collective-permute-start.40
  238.8 15.1 %out_forward.1 = bf16[1024,1024]{1,0:T(8,128)(2,1)} custom-call(s32[1]{0:T(128)} %bitcast.11.me.me_ref, s32[1]{0:T(128)} %bitcast.36.live_ref, s32[1]{0:T(128)} %mul.7.base.base_ref, bf16[1024,3072]{1,0:T(8,128)(2,1)} %get-tuple-element.236.gated_ref, bf16[1024,1024]{1,0:T(8,128)(2,1)} %bitcast.160, f32[1,1024]{1,0:T(1,128)} %get-tuple-element.237.bias_ref, ...), custom_call_target="tpu_custom_call" | custom-call | flops 6000000000 | bytes 1048576 | tf_op jit(solution)/shard_map/out_forward/pallas_call | solution.py:486
  254.0 5.8 %collective-permute-done.40 = bf16[2,4,56,512]{3,2,1,0:T(8,128)(2,1)} collective-permute-done((bf16[2,4,56,512]{3,2,1,0:T(8,128)(2,1)}, bf16[2,4,56,512]{3,2,1,0:T(8,128)(2,1)}, u32[]{:S(2)}, u32[]{:S(2)}) %collective-permute-start.40) | collective-permute-done | bytes 458784 | tf_op jit(solution)/shard_map/ppermute | solution.py:32
  259.8 2.0 fusion.1
  261.9 1.6 collective-permute-start.41
  263.5 1.0 fusion.17
  264.5 1.5 collective-permute-start.42
  267.6 3.4 %collective-permute-done.42 = bf16[4,56,512]{2,1,0:T(8,128)(2,1)S(1)} collective-permute-done((bf16[4,56,512]{2,1,0:T(8,128)(2,1)S(1)}, bf16[4,56,512]{2,1,0:T(8,128)(2,1)S(1)}, u32[]{:S(2)}, u32[]{:S(2)}) %collective-permute-start.42) | collective-permute-done | bytes 229408 | tf_op jit(solution)/shard_map/ppermute | solution.py:32
  271.0 5.4 %collective-permute-done.41 = bf16[2,192,768]{2,1,0:T(8,128)(2,1)S(1)} collective-permute-done((bf16[2,192,768]{2,1,0:T(8,128)(2,1)S(1)}, bf16[2,192,768]{2,1,0:T(8,128)(2,1)S(1)}, u32[]{:S(2)}, u32[]{:S(2)}) %collective-permute-start.41) | collective-permute-done | bytes 589856 | tf_op jit(solution)/shard_map/ppermute | solution.py:32
  277.1 1.0 fusion.13
  278.2 1.6 collective-permute-start.44
  279.8 2.4 collective-permute-start.43
  283.5 3.3 %collective-permute-start.45 = (bf16[56,512]{1,0:T(8,128)(2,1)S(1)}, bf16[56,512]{1,0:T(8,128)(2,1)S(1)}, u32[]{:S(2)}, u32[]{:S(2)}) collective-permute-start(bf16[56,512]{1,0:T(8,128)(2,1)S(1)} %fusion.19), channel_id=1, source_target_pairs={{0,16},{4,20},{8,24},{12,28},{16,0},{20,4},{24,8},{28,12},{1,17},{... | collective-permute-start | bytes 172040 | tf_op jit(solution)/shard_map/ppermute | solution.py:32
  287.5 8.8 %collective-permute-done.45.s2 = bf16[56,512]{1,0:T(8,128)(2,1)S(1)} collective-permute-done((bf16[56,512]{1,0:T(8,128)(2,1)S(1)}, bf16[56,512]{1,0:T(8,128)(2,1)S(1)}, u32[]{:S(2)}, u32[]{:S(2)}) %collective-permute-start.45) | collective-permute-done | bytes 57376 | tf_op jit(solution)/shard_map/ppermute | solution.py:32
  297.7 2.1 finish.1
  (144 shorter events, 23.9 us)
Async XLA Ops:
  7.2 95.8 %all-gather.2.cloned.1.call-start = ((), (), s32[]{:S(2)}) async-start(), calls=%async_computation.1 | async-start | bytes 6488064 | tf_op jit(solution)/shard_map/all_gather | solution.py:1050
  8.9 250.8 %reduce-scatter.2.cloned.1.call-start = ((), (), s32[]{:S(2)}) async-start(), calls=%async_computation.2 | async-start | bytes 6488064 | tf_op jit(solution)/shard_map/reduce_scatter | solution.py:1138
  11.0 21.9 %copy-start.9 = (bf16[64,768]{1,0:T(8,128)(2,1)S(1)}, bf16[64,768]{1,0:T(8,128)(2,1)}, u32[]{:S(2)}) copy-start(bf16[64,768]{1,0:T(8,128)(2,1)} %get-tuple-element.143) | copy-start | bytes 294916
  11.0 22.9 %copy-start.4 = (bf16[96,1024]{1,0:T(8,128)(2,1)S(1)}, bf16[96,1024]{1,0:T(8,128)(2,1)}, u32[]{:S(2)}) copy-start(bf16[96,1024]{1,0:T(8,128)(2,1)} %get-tuple-element.145) | copy-start | bytes 589828
  11.0 8.0 %collective-permute-start.2 = (bf16[1,56,512]{2,1,0:T(8,128)(2,1)}, bf16[1,56,512]{2,1,0:T(8,128)(2,1)S(1)}, u32[]{:S(2)}, u32[]{:S(2)}) collective-permute-start(bf16[1,56,512]{2,1,0:T(8,128)(2,1)} %bitcast.148), channel_id=1, source_target_pairs={{0,24},{4,28},{8,16},{12,20},{16,8},{20,12},{24,0},{28,4},{1,25},{... | collective-permute-start | bytes 172040 | tf_op jit(solution)/shard_map/ppermute | solution.py:32
  16.1 4.5 %collective-permute-start.1 = (bf16[1,56,512]{2,1,0:T(8,128)(2,1)}, bf16[1,56,512]{2,1,0:T(8,128)(2,1)S(1)}, u32[]{:S(2)}, u32[]{:S(2)}) collective-permute-start(bf16[1,56,512]{2,1,0:T(8,128)(2,1)} %bitcast.149), channel_id=1, source_target_pairs={{0,8},{4,12},{8,0},{12,4},{16,24},{20,28},{24,16},{28,20},{1,9},{5... | collective-permute-start | bytes 172040 | tf_op jit(solution)/shard_map/ppermute | solution.py:32
  16.1 5.7 %collective-permute-start = (bf16[1,56,512]{2,1,0:T(8,128)(2,1)}, bf16[1,56,512]{2,1,0:T(8,128)(2,1)S(1)}, u32[]{:S(2)}, u32[]{:S(2)}) collective-permute-start(bf16[1,56,512]{2,1,0:T(8,128)(2,1)} %bitcast.150), channel_id=1, source_target_pairs={{0,16},{4,20},{8,24},{12,28},{16,0},{20,4},{24,8},{28,12},{1,17},{... | collective-permute-start | bytes 172040 | tf_op jit(solution)/shard_map/ppermute | solution.py:32
  21.8 7.9 %collective-permute-start.4 = (bf16[1,64,768]{2,1,0:T(8,128)(2,1)}, bf16[1,64,768]{2,1,0:T(8,128)(2,1)S(1)}, u32[]{:S(2)}, u32[]{:S(2)}) collective-permute-start(bf16[1,64,768]{2,1,0:T(8,128)(2,1)} %bitcast.143), channel_id=1, source_target_pairs={{0,16},{4,20},{8,24},{12,28},{16,0},{20,4},{24,8},{28,12},{1,17},{... | collective-permute-start | bytes 294920 | tf_op jit(solution)/shard_map/ppermute | solution.py:32
  24.2 7.0 %collective-permute-start.3 = (bf16[4,56,512]{2,1,0:T(8,128)(2,1)S(1)}, bf16[4,56,512]{2,1,0:T(8,128)(2,1)S(1)}, u32[]{:S(2)}, u32[]{:S(2)}) collective-permute-start(bf16[4,56,512]{2,1,0:T(8,128)(2,1)S(1)} %pad_maximum_fusion.12), channel_id=1, source_target_pairs={{0,4},{4,0},{8,12},{12,8},{16,20},{20,16},{24,28},{28,24},{1,5},{5... | collective-permute-start | bytes 688136 | tf_op jit(solution)/shard_map/ppermute | solution.py:32
  31.3 18.9 %copy-start.15 = (bf16[8,56,512]{2,1,0:T(8,128)(2,1)}, bf16[8,56,512]{2,1,0:T(8,128)(2,1)S(1)}, u32[]{:S(2)}) copy-start(bf16[8,56,512]{2,1,0:T(8,128)(2,1)S(1)} %constant_dynamic-update-slice_fusion.refs_0_.s0) | copy-start | bytes 1376260
  31.3 17.8 %collective-permute-start.6 = (bf16[8,56,512]{2,1,0:T(8,128)(2,1)S(1)}, bf16[8,56,512]{2,1,0:T(8,128)(2,1)S(1)}, u32[]{:S(2)}, u32[]{:S(2)}) collective-permute-start(bf16[8,56,512]{2,1,0:T(8,128)(2,1)S(1)} %constant_dynamic-update-slice_fusion.refs_0_.s0), channel_id=1, source_target_pairs={{0,1},{1,0},{2,3},{3,2},{4,5},{5,4},{6,7},{7,6},{8,9},{9,8},{10,11... | collective-permute-start | bytes 1376264 | tf_op jit(solution)/shard_map/ppermute | solution.py:32
  31.3 18.5 %collective-permute-start.5 = (bf16[8,56,512]{2,1,0:T(8,128)(2,1)S(1)}, bf16[8,56,512]{2,1,0:T(8,128)(2,1)}, u32[]{:S(2)}, u32[]{:S(2)}) collective-permute-start(bf16[8,56,512]{2,1,0:T(8,128)(2,1)S(1)} %constant_dynamic-update-slice_fusion.refs_0_.s0), channel_id=1, source_target_pairs={{0,2},{1,3},{2,0},{3,1},{4,6},{5,7},{6,4},{7,5},{8,10},{9,11},{10,... | collective-permute-start | bytes 1376264 | tf_op jit(solution)/shard_map/ppermute | solution.py:32
  32.9 10.4 %collective-permute-start.7 = (bf16[2,64,768]{2,1,0:T(8,128)(2,1)S(1)}, bf16[2,64,768]{2,1,0:T(8,128)(2,1)S(1)}, u32[]{:S(2)}, u32[]{:S(2)}) collective-permute-start(bf16[2,64,768]{2,1,0:T(8,128)(2,1)S(1)} %pad_maximum_fusion.13), channel_id=1, source_target_pairs={{0,8},{4,12},{8,0},{12,4},{16,24},{20,28},{24,16},{28,20},{1,9},{5... | collective-permute-start | bytes 589832 | tf_op jit(solution)/shard_map/ppermute | solution.py:32
  33.9 16.9 %copy-start.21 = (s32[1,8]{1,0:T(1,128)S(1)}, s32[1,8]{1,0:T(1,128)}, u32[]{:S(2)}) copy-start(s32[1,8]{1,0:T(1,128)} %param.17) | copy-start | bytes 100
  33.9 15.1 %collective-permute-start.8 = (bf16[1,96,1024]{2,1,0:T(8,128)(2,1)S(1)}, bf16[1,96,1024]{2,1,0:T(8,128)(2,1)S(1)}, u32[]{:S(2)}, u32[]{:S(2)}) collective-permute-start(bf16[1,96,1024]{2,1,0:T(8,128)(2,1)S(1)} %bitcast.138), channel_id=1, source_target_pairs={{0,16},{4,20},{8,24},{12,28},{16,0},{20,4},{24,8},{28,12},{1,17},{... | collective-permute-start | bytes 589832 | tf_op jit(solution)/shard_map/ppermute | solution.py:32
  49.9 12.3 %collective-permute-start.11 = (bf16[2,96,1024]{2,1,0:T(8,128)(2,1)S(1)}, bf16[2,96,1024]{2,1,0:T(8,128)(2,1)S(1)}, u32[]{:S(2)}, u32[]{:S(2)}) collective-permute-start(bf16[2,96,1024]{2,1,0:T(8,128)(2,1)S(1)} %pad_maximum_fusion.8), channel_id=1, source_target_pairs={{0,8},{4,12},{8,0},{12,4},{16,24},{20,28},{24,16},{28,20},{1,9},{5... | collective-permute-start | bytes 1179656 | tf_op jit(solution)/shard_map/ppermute | solution.py:32
  50.0 14.1 %collective-permute-start.18 = (bf16[8,56,512]{2,1,0:T(8,128)(2,1)}, bf16[8,56,512]{2,1,0:T(8,128)(2,1)}, u32[]{:S(2)}, u32[]{:S(2)}) collective-permute-start(bf16[8,56,512]{2,1,0:T(8,128)(2,1)} %collective-permute-done.5.refs_1_.s1), channel_id=1, source_target_pairs={{0,1},{1,0},{2,3},{3,2},{4,5},{5,4},{6,7},{7,6},{8,9},{9,8},{10,11... | collective-permute-start | bytes 1376264 | tf_op jit(solution)/shard_map/ppermute | solution.py:32
  50.1 7.4 %collective-permute-start.10 = (bf16[4,32,768]{2,1,0:T(8,128)(2,1)S(1)}, bf16[4,32,768]{2,1,0:T(8,128)(2,1)S(1)}, u32[]{:S(2)}, u32[]{:S(2)}) collective-permute-start(bf16[4,32,768]{2,1,0:T(8,128)(2,1)S(1)} %get-tuple-element.271), channel_id=1, source_target_pairs={{0,2},{1,3},{2,0},{3,1},{4,6},{5,7},{6,4},{7,5},{8,10},{9,11},{10,... | collective-permute-start | bytes 589832 | tf_op jit(solution)/shard_map/ppermute | solution.py:32
  50.2 7.4 %collective-permute-start.9 = (bf16[4,32,768]{2,1,0:T(8,128)(2,1)S(1)}, bf16[4,32,768]{2,1,0:T(8,128)(2,1)S(1)}, u32[]{:S(2)}, u32[]{:S(2)}) collective-permute-start(bf16[4,32,768]{2,1,0:T(8,128)(2,1)S(1)} %get-tuple-element.272), channel_id=1, source_target_pairs={{0,4},{4,0},{8,12},{12,8},{16,20},{20,16},{24,28},{28,24},{1,5},{5... | collective-permute-start | bytes 589832 | tf_op jit(solution)/shard_map/ppermute | solution.py:32
  51.0 14.9 %copy-start.22 = (s32[1,8]{1,0:T(1,128)}, s32[1,8]{1,0:T(1,128)S(1)}, u32[]{:S(2)}) copy-start(s32[1,8]{1,0:T(1,128)S(1)} %reduce_window_sum.11) | copy-start | bytes 100
  62.2 3.7 %copy-start.7 = (bf16[8,32,768]{2,1,0:T(8,128)(2,1)}, bf16[8,32,768]{2,1,0:T(8,128)(2,1)S(1)}, u32[]{:S(2)}) copy-start(bf16[8,32,768]{2,1,0:T(8,128)(2,1)S(1)} %pad_maximum_fusion.10.q4) | copy-start | bytes 1179652
  62.2 22.2 %collective-permute-start.15 = (bf16[8,32,768]{2,1,0:T(8,128)(2,1)S(1)}, bf16[8,32,768]{2,1,0:T(8,128)(2,1)S(1)}, u32[]{:S(2)}, u32[]{:S(2)}) collective-permute-start(bf16[8,32,768]{2,1,0:T(8,128)(2,1)S(1)} %pad_maximum_fusion.10.q4), channel_id=1, source_target_pairs={{0,1},{1,0},{2,3},{3,2},{4,5},{5,4},{6,7},{7,6},{8,9},{9,8},{10,11... | collective-permute-start | bytes 1179656 | tf_op jit(solution)/shard_map/ppermute | solution.py:32
  62.3 30.0 %collective-permute-start.13 = (bf16[8,32,768]{2,1,0:T(8,128)(2,1)S(1)}, bf16[8,32,768]{2,1,0:T(8,128)(2,1)}, u32[]{:S(2)}, u32[]{:S(2)}) collective-permute-start(bf16[8,32,768]{2,1,0:T(8,128)(2,1)S(1)} %pad_maximum_fusion.10.q4), channel_id=1, source_target_pairs={{0,4},{4,0},{8,12},{12,8},{16,20},{20,16},{24,28},{28,24},{1,5},{5... | collective-permute-start | bytes 1179656 | tf_op jit(solution)/shard_map/ppermute | solution.py:32
  63.3 2.6 copy-start.8
  63.3 29.0 %collective-permute-start.14 = (bf16[8,32,768]{2,1,0:T(8,128)(2,1)S(1)}, bf16[8,32,768]{2,1,0:T(8,128)(2,1)}, u32[]{:S(2)}, u32[]{:S(2)}) collective-permute-start(bf16[8,32,768]{2,1,0:T(8,128)(2,1)S(1)} %pad_maximum_fusion.9.q0), channel_id=1, source_target_pairs={{0,1},{1,0},{2,3},{3,2},{4,5},{5,4},{6,7},{7,6},{8,9},{9,8},{10,11... | collective-permute-start | bytes 1179656 | tf_op jit(solution)/shard_map/ppermute | solution.py:32
  63.6 28.8 %collective-permute-start.12 = (bf16[8,32,768]{2,1,0:T(8,128)(2,1)S(1)}, bf16[8,32,768]{2,1,0:T(8,128)(2,1)}, u32[]{:S(2)}, u32[]{:S(2)}) collective-permute-start(bf16[8,32,768]{2,1,0:T(8,128)(2,1)S(1)} %pad_maximum_fusion.9.q0), channel_id=1, source_target_pairs={{0,2},{1,3},{2,0},{3,1},{4,6},{5,7},{6,4},{7,5},{8,10},{9,11},{10,... | collective-permute-start | bytes 1179656 | tf_op jit(solution)/shard_map/ppermute | solution.py:32
  77.2 1.4 collective-permute-start.19
  78.7 5.1 %collective-permute-start.20 = (f32[2,2,512]{2,1,0:T(2,128)S(1)}, f32[2,2,512]{2,1,0:T(2,128)S(1)}, u32[]{:S(2)}, u32[]{:S(2)}) collective-permute-start(f32[2,2,512]{2,1,0:T(2,128)S(1)} %pad_maximum_fusion.16), channel_id=1, source_target_pairs={{0,2},{1,3},{2,0},{3,1},{4,6},{5,7},{6,4},{7,5},{8,10},{9,11},{10,... | collective-permute-start | bytes 24584 | tf_op jit(solution)/shard_map/ppermute | solution.py:32
  83.8 10.6 %collective-permute-start.17 = (bf16[4,48,1024]{2,1,0:T(8,128)(2,1)S(1)}, bf16[4,48,1024]{2,1,0:T(8,128)(2,1)}, u32[]{:S(2)}, u32[]{:S(2)}) collective-permute-start(bf16[4,48,1024]{2,1,0:T(8,128)(2,1)S(1)} %get-tuple-element.267), channel_id=1, source_target_pairs={{0,2},{1,3},{2,0},{3,1},{4,6},{5,7},{6,4},{7,5},{8,10},{9,11},{10,... | collective-permute-start | bytes 1179656 | tf_op jit(solution)/shard_map/ppermute | solution.py:32
  84.4 10.3 %collective-permute-start.16 = (bf16[4,48,1024]{2,1,0:T(8,128)(2,1)S(1)}, bf16[4,48,1024]{2,1,0:T(8,128)(2,1)}, u32[]{:S(2)}, u32[]{:S(2)}) collective-permute-start(bf16[4,48,1024]{2,1,0:T(8,128)(2,1)S(1)} %get-tuple-element.268), channel_id=1, source_target_pairs={{0,4},{4,0},{8,12},{12,8},{16,20},{20,16},{24,28},{28,24},{1,5},{5... | collective-permute-start | bytes 1179656 | tf_op jit(solution)/shard_map/ppermute | solution.py:32
  86.5 8.7 %copy-start = (bf16[1,1024,1024]{2,1,0:T(8,128)(2,1)S(1)}, bf16[1,1024,1024]{2,1,0:T(8,128)(2,1)}, u32[]{:S(2)}) copy-start(bf16[1,1024,1024]{2,1,0:T(8,128)(2,1)} %param.18) | copy-start | bytes 6291460
  94.8 6.9 %collective-permute-start.25 = (bf16[8,32,768]{2,1,0:T(8,128)(2,1)}, bf16[8,32,768]{2,1,0:T(8,128)(2,1)}, u32[]{:S(2)}, u32[]{:S(2)}) collective-permute-start(bf16[8,32,768]{2,1,0:T(8,128)(2,1)} %collective-permute-done.12.q1), channel_id=1, source_target_pairs={{0,1},{1,0},{2,3},{3,2},{4,5},{5,4},{6,7},{7,6},{8,9},{9,8},{10,11... | collective-permute-start | bytes 1179656 | tf_op jit(solution)/shard_map/ppermute | solution.py:32
  94.8 8.2 %collective-permute-start.26 = (bf16[8,32,768]{2,1,0:T(8,128)(2,1)}, bf16[8,32,768]{2,1,0:T(8,128)(2,1)}, u32[]{:S(2)}, u32[]{:S(2)}) collective-permute-start(bf16[8,32,768]{2,1,0:T(8,128)(2,1)} %collective-permute-done.13.q5), channel_id=1, source_target_pairs={{0,1},{1,0},{2,3},{3,2},{4,5},{5,4},{6,7},{7,6},{8,9},{9,8},{10,11... | collective-permute-start | bytes 1179656 | tf_op jit(solution)/shard_map/ppermute | solution.py:32
  97.9 34.0 %copy-start.3 = (bf16[8,48,1024]{2,1,0:T(8,128)(2,1)}, bf16[8,48,1024]{2,1,0:T(8,128)(2,1)S(1)}, u32[]{:S(2)}) copy-start(bf16[8,48,1024]{2,1,0:T(8,128)(2,1)S(1)} %pad_maximum_fusion.3.p4) | copy-start | bytes 2359300
  97.9 34.0 %collective-permute-start.24 = (bf16[8,48,1024]{2,1,0:T(8,128)(2,1)S(1)}, bf16[8,48,1024]{2,1,0:T(8,128)(2,1)}, u32[]{:S(2)}, u32[]{:S(2)}) collective-permute-start(bf16[8,48,1024]{2,1,0:T(8,128)(2,1)S(1)} %pad_maximum_fusion.3.p4), channel_id=1, source_target_pairs={{0,1},{1,0},{2,3},{3,2},{4,5},{5,4},{6,7},{7,6},{8,9},{9,8},{10,11... | collective-permute-start | bytes 2359304 | tf_op jit(solution)/shard_map/ppermute | solution.py:32
  98.0 33.9 %collective-permute-start.22 = (bf16[8,48,1024]{2,1,0:T(8,128)(2,1)S(1)}, bf16[8,48,1024]{2,1,0:T(8,128)(2,1)}, u32[]{:S(2)}, u32[]{:S(2)}) collective-permute-start(bf16[8,48,1024]{2,1,0:T(8,128)(2,1)S(1)} %pad_maximum_fusion.3.p4), channel_id=1, source_target_pairs={{0,4},{4,0},{8,12},{12,8},{16,20},{20,16},{24,28},{28,24},{1,5},{5... | collective-permute-start | bytes 2359304 | tf_op jit(solution)/shard_map/ppermute | solution.py:32
  101.5 30.4 %collective-permute-start.23 = (bf16[8,48,1024]{2,1,0:T(8,128)(2,1)}, bf16[8,48,1024]{2,1,0:T(8,128)(2,1)}, u32[]{:S(2)}, u32[]{:S(2)}) collective-permute-start(bf16[8,48,1024]{2,1,0:T(8,128)(2,1)} %pad_maximum_fusion.2.p0), channel_id=1, source_target_pairs={{0,1},{1,0},{2,3},{3,2},{4,5},{5,4},{6,7},{7,6},{8,9},{9,8},{10,11... | collective-permute-start | bytes 2359304 | tf_op jit(solution)/shard_map/ppermute | solution.py:32
  101.7 30.2 %collective-permute-start.21 = (bf16[8,48,1024]{2,1,0:T(8,128)(2,1)}, bf16[8,48,1024]{2,1,0:T(8,128)(2,1)}, u32[]{:S(2)}, u32[]{:S(2)}) collective-permute-start(bf16[8,48,1024]{2,1,0:T(8,128)(2,1)} %pad_maximum_fusion.2.p0), channel_id=1, source_target_pairs={{0,2},{1,3},{2,0},{3,1},{4,6},{5,7},{6,4},{7,5},{8,10},{9,11},{10,... | collective-permute-start | bytes 2359304 | tf_op jit(solution)/shard_map/ppermute | solution.py:32
  131.9 2.9 collective-permute-start.27
  132.1 3.7 %collective-permute-start.28 = (bf16[8,48,1024]{2,1,0:T(8,128)(2,1)}, bf16[8,48,1024]{2,1,0:T(8,128)(2,1)}, u32[]{:S(2)}, u32[]{:S(2)}) collective-permute-start(bf16[8,48,1024]{2,1,0:T(8,128)(2,1)} %collective-permute-done.22.p5), channel_id=1, source_target_pairs={{0,1},{1,0},{2,3},{3,2},{4,5},{5,4},{6,7},{7,6},{8,9},{9,8},{10,11... | collective-permute-start | bytes 2359304 | tf_op jit(solution)/shard_map/ppermute | solution.py:32
  167.3 13.6 %collective-permute-start.29 = (bf16[16,128,768]{2,1,0:T(8,128)(2,1)}, bf16[16,128,768]{2,1,0:T(8,128)(2,1)}, u32[]{:S(2)}, u32[]{:S(2)}) collective-permute-start(bf16[16,128,768]{2,1,0:T(8,128)(2,1)} %get-tuple-element.199), channel_id=1, source_target_pairs={{0,1},{1,0},{2,3},{3,2},{4,5},{5,4},{6,7},{7,6},{8,9},{9,8},{10,11... | collective-permute-start | bytes 9437192 | tf_op jit(solution)/shard_map/ppermute | solution.py:32
  167.5 13.4 %collective-permute-start.30 = (bf16[16,64,768]{2,1,0:T(8,128)(2,1)}, bf16[16,64,768]{2,1,0:T(8,128)(2,1)}, u32[]{:S(2)}, u32[]{:S(2)}) collective-permute-start(bf16[16,64,768]{2,1,0:T(8,128)(2,1)} %get-tuple-element.200), channel_id=1, source_target_pairs={{0,1},{1,0},{2,3},{3,2},{4,5},{5,4},{6,7},{7,6},{8,9},{9,8},{10,11... | collective-permute-start | bytes 4718600 | tf_op jit(solution)/shard_map/ppermute | solution.py:32
  177.6 3.2 %copy-start.13 = (f32[2,512]{1,0:T(2,128)S(1)}, f32[2,512]{1,0:T(2,128)}, u32[]{:S(2)}) copy-start(f32[2,512]{1,0:T(2,128)} %get-tuple-element.212) | copy-start | bytes 12292
  177.7 3.8 %copy-start.2 = (bf16[16,64,768]{2,1,0:T(8,128)(2,1)S(1)}, bf16[16,64,768]{2,1,0:T(8,128)(2,1)}, u32[]{:S(2)}) copy-start(bf16[16,64,768]{2,1,0:T(8,128)(2,1)} %get-tuple-element.209) | copy-start | bytes 4718596
  180.9 6.6 %collective-permute-start.33 = (f32[1,2,512]{2,1,0:T(2,128)S(1)}, f32[1,2,512]{2,1,0:T(2,128)S(1)}, u32[]{:S(2)}, u32[]{:S(2)}) collective-permute-start(f32[1,2,512]{2,1,0:T(2,128)S(1)} %bitcast.152), channel_id=1, source_target_pairs={{0,1},{1,0},{2,3},{3,2},{4,5},{5,4},{6,7},{7,6},{8,9},{9,8},{10,11... | collective-permute-start | bytes 12296 | tf_op jit(solution)/shard_map/ppermute | solution.py:32
  181.1 31.6 %collective-permute-start.38 = (bf16[16,16,512]{2,1,0:T(8,128)(2,1)}, bf16[16,16,512]{2,1,0:T(8,128)(2,1)}, u32[]{:S(2)}, u32[]{:S(2)}) collective-permute-start(bf16[16,16,512]{2,1,0:T(8,128)(2,1)} %get-tuple-element.227), channel_id=1, source_target_pairs={{0,1},{1,0},{2,3},{3,2},{4,5},{5,4},{6,7},{7,6},{8,9},{9,8},{10,11... | collective-permute-start | bytes 786440 | tf_op jit(solution)/shard_map/ppermute | solution.py:32
  181.5 2.4 copy-start.1
  187.6 4.0 %collective-permute-start.34 = (f32[2,2,512]{2,1,0:T(2,128)S(1)}, f32[2,2,512]{2,1,0:T(2,128)S(1)}, u32[]{:S(2)}, u32[]{:S(2)}) collective-permute-start(f32[2,2,512]{2,1,0:T(2,128)S(1)} %pad_maximum_fusion.17), channel_id=1, source_target_pairs={{0,2},{1,3},{2,0},{3,1},{4,6},{5,7},{6,4},{7,5},{8,10},{9,11},{10,... | collective-permute-start | bytes 24584 | tf_op jit(solution)/shard_map/ppermute | solution.py:32
  189.6 34.5 %collective-permute-start.32 = (bf16[2,4,96,768]{3,2,1,0:T(8,128)(2,1)}, bf16[2,4,96,768]{3,2,1,0:T(8,128)(2,1)}, u32[]{:S(2)}, u32[]{:S(2)}) collective-permute-start(bf16[2,4,96,768]{3,2,1,0:T(8,128)(2,1)} %pad_maximum_fusion), channel_id=1, source_target_pairs={{0,4},{4,0},{8,12},{12,8},{16,20},{20,16},{24,28},{28,24},{1,5},{5... | collective-permute-start | bytes 3538952 | tf_op jit(solution)/shard_map/ppermute | solution.py:32
  189.8 34.5 %collective-permute-start.31 = (bf16[2,4,96,768]{3,2,1,0:T(8,128)(2,1)S(1)}, bf16[2,4,96,768]{3,2,1,0:T(8,128)(2,1)}, u32[]{:S(2)}, u32[]{:S(2)}) collective-permute-start(bf16[2,4,96,768]{3,2,1,0:T(8,128)(2,1)S(1)} %get-tuple-element.261), channel_id=1, source_target_pairs={{0,2},{1,3},{2,0},{3,1},{4,6},{5,7},{6,4},{7,5},{8,10},{9,11},{10,... | collective-permute-start | bytes 3538952 | tf_op jit(solution)/shard_map/ppermute | solution.py:32
  192.2 20.5 %copy-start.10 = (bf16[16,16,512]{2,1,0:T(8,128)(2,1)S(1)}, bf16[16,16,512]{2,1,0:T(8,128)(2,1)}, u32[]{:S(2)}) copy-start(bf16[16,16,512]{2,1,0:T(8,128)(2,1)} %get-tuple-element.226) | copy-start | bytes 786436
  226.2 10.0 %collective-permute-start.39 = (bf16[16,8,512]{2,1,0:T(8,128)(2,1)}, bf16[16,8,512]{2,1,0:T(8,128)(2,1)S(1)}, u32[]{:S(2)}, u32[]{:S(2)}) collective-permute-start(bf16[16,8,512]{2,1,0:T(8,128)(2,1)} %get-tuple-element.235), channel_id=1, source_target_pairs={{0,1},{1,0},{2,3},{3,2},{4,5},{5,4},{6,7},{7,6},{8,9},{9,8},{10,11... | collective-permute-start | bytes 393224 | tf_op jit(solution)/shard_map/ppermute | solution.py:32
  230.4 6.0 %collective-permute-start.37 = (bf16[16,32,512]{2,1,0:T(8,128)(2,1)}, bf16[16,32,512]{2,1,0:T(8,128)(2,1)S(1)}, u32[]{:S(2)}, u32[]{:S(2)}) collective-permute-start(bf16[16,32,512]{2,1,0:T(8,128)(2,1)} %get-tuple-element.225), channel_id=1, source_target_pairs={{0,1},{1,0},{2,3},{3,2},{4,5},{5,4},{6,7},{7,6},{8,9},{9,8},{10,11... | collective-permute-start | bytes 1572872 | tf_op jit(solution)/shard_map/ppermute | solution.py:32
  233.0 3.3 %copy-start.12 = (bf16[16,8,512]{2,1,0:T(8,128)(2,1)S(1)}, bf16[16,8,512]{2,1,0:T(8,128)(2,1)}, u32[]{:S(2)}) copy-start(bf16[16,8,512]{2,1,0:T(8,128)(2,1)} %get-tuple-element.234) | copy-start | bytes 393220
  233.0 3.4 %copy-start.5 = (bf16[16,32,512]{2,1,0:T(8,128)(2,1)S(1)}, bf16[16,32,512]{2,1,0:T(8,128)(2,1)}, u32[]{:S(2)}) copy-start(bf16[16,32,512]{2,1,0:T(8,128)(2,1)} %get-tuple-element.224) | copy-start | bytes 1572868
  233.0 21.0 %collective-permute-start.36 = (bf16[4,96,768]{2,1,0:T(8,128)(2,1)}, bf16[4,96,768]{2,1,0:T(8,128)(2,1)}, u32[]{:S(2)}, u32[]{:S(2)}) collective-permute-start(bf16[4,96,768]{2,1,0:T(8,128)(2,1)} %fusion.7), channel_id=1, source_target_pairs={{0,2},{1,3},{2,0},{3,1},{4,6},{5,7},{6,4},{7,5},{8,10},{9,11},{10,... | collective-permute-start | bytes 1769480 | tf_op jit(solution)/shard_map/ppermute | solution.py:32
  235.6 18.4 %collective-permute-start.35 = (bf16[4,96,768]{2,1,0:T(8,128)(2,1)S(1)}, bf16[4,96,768]{2,1,0:T(8,128)(2,1)}, u32[]{:S(2)}, u32[]{:S(2)}) collective-permute-start(bf16[4,96,768]{2,1,0:T(8,128)(2,1)S(1)} %fusion.9), channel_id=1, source_target_pairs={{0,4},{4,0},{8,12},{12,8},{16,20},{20,16},{24,28},{28,24},{1,5},{5... | collective-permute-start | bytes 1769480 | tf_op jit(solution)/shard_map/ppermute | solution.py:32
  237.3 22.4 %collective-permute-start.40 = (bf16[2,4,56,512]{3,2,1,0:T(8,128)(2,1)}, bf16[2,4,56,512]{3,2,1,0:T(8,128)(2,1)}, u32[]{:S(2)}, u32[]{:S(2)}) collective-permute-start(bf16[2,4,56,512]{3,2,1,0:T(8,128)(2,1)} %pad_maximum_fusion.5), channel_id=1, source_target_pairs={{0,2},{1,3},{2,0},{3,1},{4,6},{5,7},{6,4},{7,5},{8,10},{9,11},{10,... | collective-permute-start | bytes 1376264 | tf_op jit(solution)/shard_map/ppermute | solution.py:32
  261.9 4.2 %copy-start.11 = (bf16[96,1024]{1,0:T(8,128)(2,1)S(1)}, bf16[96,1024]{1,0:T(8,128)(2,1)}, u32[]{:S(2)}) copy-start(bf16[96,1024]{1,0:T(8,128)(2,1)} %reduce-scatter.2.cloned.1.call-done) | copy-start | bytes 589828
  261.9 14.4 %collective-permute-start.41 = (bf16[2,192,768]{2,1,0:T(8,128)(2,1)S(1)}, bf16[2,192,768]{2,1,0:T(8,128)(2,1)S(1)}, u32[]{:S(2)}, u32[]{:S(2)}) collective-permute-start(bf16[2,192,768]{2,1,0:T(8,128)(2,1)S(1)} %fusion.11), channel_id=1, source_target_pairs={{0,8},{4,12},{8,0},{12,4},{16,24},{20,28},{24,16},{28,20},{1,9},{5... | collective-permute-start | bytes 1769480 | tf_op jit(solution)/shard_map/ppermute | solution.py:32
  264.5 6.4 %collective-permute-start.42 = (bf16[4,56,512]{2,1,0:T(8,128)(2,1)S(1)}, bf16[4,56,512]{2,1,0:T(8,128)(2,1)S(1)}, u32[]{:S(2)}, u32[]{:S(2)}) collective-permute-start(bf16[4,56,512]{2,1,0:T(8,128)(2,1)S(1)} %fusion.17), channel_id=1, source_target_pairs={{0,4},{4,0},{8,12},{12,8},{16,20},{20,16},{24,28},{28,24},{1,5},{5... | collective-permute-start | bytes 688136 | tf_op jit(solution)/shard_map/ppermute | solution.py:32
  278.2 5.3 %collective-permute-start.44 = (bf16[2,56,512]{2,1,0:T(8,128)(2,1)S(1)}, bf16[2,56,512]{2,1,0:T(8,128)(2,1)S(1)}, u32[]{:S(2)}, u32[]{:S(2)}) collective-permute-start(bf16[2,56,512]{2,1,0:T(8,128)(2,1)S(1)} %slice.253), channel_id=1, source_target_pairs={{0,8},{4,12},{8,0},{12,4},{16,24},{20,28},{24,16},{28,20},{1,9},{5... | collective-permute-start | bytes 344072 | tf_op jit(solution)/shard_map/ppermute | solution.py:32
  279.8 16.5 %collective-permute-start.43 = (bf16[192,768]{1,0:T(8,128)(2,1)S(1)}, bf16[192,768]{1,0:T(8,128)(2,1)S(1)}, u32[]{:S(2)}, u32[]{:S(2)}) collective-permute-start(bf16[192,768]{1,0:T(8,128)(2,1)S(1)} %fusion.16), channel_id=1, source_target_pairs={{0,16},{4,20},{8,24},{12,28},{16,0},{20,4},{24,8},{28,12},{1,17},{... | collective-permute-start | bytes 884744 | tf_op jit(solution)/shard_map/ppermute | solution.py:32
  283.5 12.8 %collective-permute-start.45 = (bf16[56,512]{1,0:T(8,128)(2,1)S(1)}, bf16[56,512]{1,0:T(8,128)(2,1)S(1)}, u32[]{:S(2)}, u32[]{:S(2)}) collective-permute-start(bf16[56,512]{1,0:T(8,128)(2,1)S(1)} %fusion.19), channel_id=1, source_target_pairs={{0,16},{4,20},{8,24},{12,28},{16,0},{20,4},{24,8},{28,12},{1,17},{... | collective-permute-start | bytes 172040 | tf_op jit(solution)/shard_map/ppermute | solution.py:32
  (7 other events, 8.3 us)
Sparse Core Ops, SparseCore 0:
  10.9 85.7 all-gather.1
  132.6 127.0 reduce-scatter.1

commit v4 on v3

--- a/solution.py
+++ b/solution.py
@@ -26,10 +26,16 @@
 
 
 def exchange(values, *bits):
-    inner = log2(lax.axis_size("seq"))
-    axis, first = ("seq", 0) if bits[0] < inner else ("dp", inner)
-    flip = sum(1 << (bit - first) for bit in bits)
-    return lax.ppermute(values, axis, [(i, i ^ flip) for i in range(lax.axis_size(axis))])
+    axes = ("dp", "seq")
+    base = low_bits()
+
+    def other(i):
+        for bit in bits:
+            i ^= 1 << (bit[(i >> base) & 1] if isinstance(bit, tuple) else bit)
+        return i
+
+    count = lax.axis_size("dp") * lax.axis_size("seq")
+    return lax.ppermute(values, axes, [(i, other(i)) for i in range(count)])
 
 
 def gather_low(values):
@@ -56,57 +62,51 @@
     return jnp.concatenate([own, other])
 
 
-def gather_steps(rows, split):
-    core, bit_x, bit_y, bit_z, bit_far = (low_bits() + i for i in range(MAIN))
+def stage_bits():
+    core, bit_x, bit_y, near, far = (low_bits() + i for i in range(MAIN))
+    return core, (bit_x, bit_y), (bit_y, bit_x), near, far
+
+
+def gather_steps(rows, direct=False, early=False):
+    core, lead, second, near, far = stage_bits()
     held = rows[None]
-    if not split:
-        others = yield [exchange(held, *bits) for bits in ((bit_far,), (bit_z,), (bit_z, bit_far))]
+    if direct:
+        others = yield [(held, far), (held, near), (held, near, far)]
         held = jnp.concatenate([held, *others])
-        (other,) = yield [exchange(held, bit_y)]
+    else:
+        (other,) = yield [(held, far)]
         held = join(held, other)
-        other, held_core = yield [exchange(held, bit_x), exchange(held, core)]
-        (other_core,) = yield [exchange(other, core)]
-        return [held, other, held_core, other_core]
-    (other,) = yield [exchange(held, bit_far)]
+        (other,) = yield [(held, near)]
+        held = join(held, other)
+    (other,) = yield [(held, second)]
     held = join(held, other)
-    (other,) = yield [exchange(held, bit_z)]
-    held = join(held, other)
-    first, second = held[:, :split], held[:, split:]
-    from_y, from_x = yield [exchange(first, bit_y), exchange(second, bit_x)]
-    first, second = join(first, from_y), join(second, from_x)
-    from_x, from_y, *near = yield [
-        exchange(first, bit_x),
-        exchange(second, bit_y),
-        exchange(first, core),
-        exchange(second, core),
-    ]
-    far = yield [exchange(from_x, core), exchange(from_y, core)]
-    return [first, from_x, near[0], far[0], second, from_y, near[1], far[1]]
-
-
-def spot(rel, x_first):
-    core = rel & 1
-    bit_x, bit_y = (rel >> 1) & 1, (rel >> 2) & 1
-    bit_z, bit_far = (rel >> 3) & 1, (rel >> 4) & 1
-    if x_first:
-        return core, bit_x * 8 + bit_y * 4 + bit_z * 2 + bit_far
-    return core, bit_y * 8 + bit_x * 4 + bit_z * 2 + bit_far
+    if early:
+        other, held_there = yield [(held, lead), (held, core)]
+        (other_there,) = yield [(other, core)]
+    else:
+        (other,) = yield [(held, lead)]
+        held_there, other_there = yield [(held, core), (other, core)]
+    return [held, other, held_there, other_there]
+
+
+def shard_at(mine, side, lead, k):
+    own = 2 + 2 * (mine & 1)
+    first, second = (own, 6 - own) if side == 0 else (6 - own, own)
+    rel = side + lead * first + ((k >> 2) & 1) * second + ((k >> 1) & 1) * 8 + (k & 1) * 16
+    return rel ^ mine
 
 
 def load_weights(mine, parts, target, pieces, sems):
     def one(k, carry):
-        bits = ((k >> 2) & 1, ((k >> 1) & 1) * 8 + (k & 1) * 16)
-        for four, row, rows, group, held, to_row in pieces:
-            lead_bit, other_bit = (2, 4) if four == 0 else (4, 2)
+        for row, rows, group, held, to_row in pieces:
             for side in range(4):
-                rel = (side >> 1) + (side & 1) * lead_bit + bits[0] * other_bit + bits[1]
-                shard = rel ^ mine
+                shard = shard_at(mine, side >> 1, side & 1, k)
                 to = group
                 if group is None:
                     per_group = target.shape[1] // held
                     to, shard = shard // per_group, shard % per_group
                 at = pl.multiple_of(shard * held + to_row, 16)
-                source = parts[4 * four + side].at[k, pl.ds(row, rows)]
+                source = parts[side].at[k, pl.ds(row, rows)]
                 pltpu.make_async_copy(source, target.at[to, pl.ds(at, rows)], sems.at[to]).start()
         return carry
 
@@ -117,10 +117,10 @@
     pltpu.make_async_copy(target.at[group], target.at[group], sems.at[group]).wait()
 
 
-REDUCE_PIECES = [(0, 0, 32, 0, 32, 0)]
-STATE_PIECES = [(0, 32, 16, 0, 16, 0)]
-EXPAND_PIECES = [(g // 2, 16 * (g % 2), 16, g, 16, 0) for g in range(4)]
-OUT_PIECES = [(0, 0, 48, None, 96, 0), (1, 0, 48, None, 96, 48)]
+REDUCE_PIECES = [(0, 32, 0, 32, 0)]
+STATE_PIECES = [(32, 16, 0, 16, 0)]
+EXPAND_PIECES = [(16 * g, 16, g, 16, 0) for g in range(4)]
+OUT_PIECES = [(0, 96, None, 96, 0)]
 
 SMEM = pl.BlockSpec(memory_space=pltpu.SMEM)
 FAR = pl.BlockSpec(memory_space=pltpu.HBM)
@@ -129,7 +129,9 @@
 def cost(micros):
     return pl.CostEstimate(flops=int(micros * 1e9), bytes_accessed=MIB, transcendentals=0)
 
-ROOM = pltpu.CompilerParams(vmem_limit_bytes=60 * MIB)
+
+def room(mib):
+    return pltpu.CompilerParams(vmem_limit_bytes=mib * MIB)
 
 
 def whole(*shape):
@@ -176,7 +178,7 @@
     return far
 
 
-def scan_block(ends_ref, first, decay, value_ref, reverse):
+def scan_block(ends_ref, first, decay, source_ref, value_ref, reverse):
     columns, block, lanes = value_ref.shape
     span = block // SEGMENTS
     row = lax.broadcasted_iota(jnp.int32, (8, lanes), 0)
@@ -195,7 +197,7 @@
             at = pl.multiple_of(s * span + k * 8, 8)
             near = starts_near(ends_ref, first + at + row, reverse) + (0 if reverse else 1)
             for c in range(columns):
-                x = value_ref[c, pl.ds(at, 8), :]
+                x = source_ref[c, pl.ds(at, 8), :]
                 for step, d in enumerate((1, 2, 4)):
                     moved = pltpu.roll(x, 8 - d if reverse else d, 0)
                     x = x + jnp.where(near > d, factors[c][step], 0.0) * moved
@@ -273,15 +275,14 @@
     return held
 
 
-def reduce_kernel(scalars, tokens, gain, shift, bias, decay, inflow, parts):
+def reduce_kernel(me, tokens, gain, shift, bias, inflow, parts):
     block, width = tokens.shape
     channels = bias.shape[1]
     tile = 256
     columns = channels // 128
 
-    def body(me, ends, base, x_ref, gain_ref, shift_ref, bias_ref, decay_ref, inflow_ref, s0, s1, s2, s3,
-             normed_ref, act_ref, slope_ref, state_ref, span_ref, map_ref,
-             weight, sems):
+    def body(me, x_ref, gain_ref, shift_ref, bias_ref, inflow_ref, s0, s1, s2, s3,
+             normed_ref, act_ref, slope_ref, state_ref, weight, sems):
         load_weights(me[0], (s0, s1, s2, s3), weight, REDUCE_PIECES, sems)
 
         def norm(t, carry):
@@ -304,9 +305,6 @@
             return carry
 
         lax.fori_loop(0, block // tile, reduce, 0)
-        product, state = scan_block(ends, base[0], decay_ref[...], state_ref, False)
-        span_ref[0], span_ref[1] = product, state
-        map_ref[0:1, :], map_ref[1:2, :] = whole_map(product, state, False)
 
     vm = pl.BlockSpec(memory_space=pltpu.VMEM)
     return pl.pallas_call(
@@ -317,18 +315,42 @@
             jax.ShapeDtypeStruct((block, channels), SINGLE),
             jax.ShapeDtypeStruct((block, channels), HALF),
             jax.ShapeDtypeStruct((columns, block, 128), SINGLE),
-            jax.ShapeDtypeStruct((2, SEGMENTS, channels), SINGLE),
-            jax.ShapeDtypeStruct((2, channels), SINGLE),
         ],
-        in_specs=[SMEM] * 3 + [vm] * 6 + [FAR] * 4,
-        out_specs=[vm] * 6,
+        in_specs=[SMEM] + [vm] * 5 + [FAR] * 4,
+        out_specs=[vm] * 4,
         scratch_shapes=[
             pltpu.VMEM((1, width, channels), HALF),
             pltpu.SemaphoreType.DMA((1,)),
         ],
-        compiler_params=ROOM,
+        compiler_params=room(60),
         cost_estimate=cost(8),
-    )(*scalars[:3], tokens, gain, shift, bias, decay, inflow, *parts)
+    )(me, tokens, gain, shift, bias, inflow, *parts)
+
+
+def scan_kernel(order, ends, base, flow, decay):
+    channels = decay.shape[1]
+
+    def body(order, ends_ref, base_ref, flow_ref, decay_ref, state_ref, span_ref, map_ref):
+        product, state = scan_block(
+            ends_ref, base_ref[0], decay_ref[...], flow_ref, state_ref, False
+        )
+        span_ref[0], span_ref[1] = product, state
+        map_ref[0:1, :], map_ref[1:2, :] = whole_map(product, state, False)
+
+    vm = pl.BlockSpec(memory_space=pltpu.VMEM)
+    return pl.pallas_call(
+        body,
+        name="state_scan",
+        out_shape=[
+            jax.ShapeDtypeStruct(flow.shape, SINGLE),
+            jax.ShapeDtypeStruct((2, SEGMENTS, channels), SINGLE),
+            jax.ShapeDtypeStruct((2, channels), SINGLE),
+        ],
+        in_specs=[SMEM] * 3 + [vm] * 2,
+        out_specs=[vm] * 3,
+        compiler_params=room(20),
+        cost_estimate=cost(12),
+    )(order, ends, base, flow, decay)
 
 
 def staged(count, product, finish):
@@ -382,8 +404,8 @@
         scratch_shapes=[
             pltpu.VMEM((SEGMENTS, 8, channels), SINGLE),
             pltpu.VMEM((1, channels, channels), HALF), pltpu.SemaphoreType.DMA((1,))],
-        compiler_params=ROOM,
-        cost_estimate=cost(3),
+        compiler_params=room(20),
+        cost_estimate=cost(4),
     )(me, place, ends, base, maps, spans, states, act, skip, inflow, decay, *parts)
 
 
@@ -394,16 +416,17 @@
     gate = value_bias.shape[1]
     groups, sub = 4, 256
     depth = gate // groups
+    rows = gate >> MAIN
 
     def body(me, x_ref, ssm_ref, grad_ref, value_bias_ref, expand_bias_ref, value,
-             q0, q1, q2, q3, q4, q5, q6, q7, act_ref, gated_ref, slope_ref, sum_ref,
-             expand, expand_sems):
+             q0, q1, q2, q3, act_ref, gated_ref, slope_ref, send_ref, keep_ref,
+             made, expand, expand_sems):
         j = pl.program_id(0)
 
         @pl.when(j == 0)
         def _():
             load_weights(
-                me[0], (q0, q1, q2, q3, q4, q5, q6, q7), expand, EXPAND_PIECES, expand_sems
+                me[0], (q0, q1, q2, q3), expand, EXPAND_PIECES, expand_sems
             )
 
         for g in range(groups):
@@ -422,7 +445,13 @@
             slope_ref[:, cols] = (slope * pre).astype(HALF)
         for c in range(width // sub):
             cols = pl.ds(c * sub, sub)
-            sum_ref[:, cols] = dot(gated_ref[...], grad_ref[:, cols], 0, 0).astype(HALF)
+            made[:, cols] = dot(gated_ref[...], grad_ref[:, cols], 0, 0).astype(HALF)
+        rel_z = j ^ (me[0] >> 3)
+        place = (rel_z & 1) * 2 + (rel_z >> 1)
+        for k in range(0, 16, 4):
+            for side, ref in ((0, keep_ref), (1, send_ref)):
+                at = pl.multiple_of((shard_at(me[0], side, k >> 3, k & 7) & 7) * rows, 16)
+                ref[k + place] = made[pl.ds(at, rows), :]
 
     wide = pl.BlockSpec((block, depth), lambda j: (0, j))
     bias = pl.BlockSpec((1, depth), lambda j: (0, j))
@@ -430,7 +459,7 @@
         body,
         name="gate_forward",
         out_shape=[jax.ShapeDtypeStruct((block, gate), HALF)] * 3
-        + [jax.ShapeDtypeStruct((gate, width), HALF)],
+        + [jax.ShapeDtypeStruct((16, rows, width), HALF)] * 2,
         grid=(groups,),
         in_specs=[
             SMEM,
@@ -441,13 +470,14 @@
             bias,
             pl.BlockSpec((width, depth), lambda j: (0, j)),
         ]
-        + [FAR] * 8,
-        out_specs=[wide] * 3 + [pl.BlockSpec((depth, width), lambda j: (j, 0))],
+        + [FAR] * 4,
+        out_specs=[wide] * 3 + [once(16, rows, width)] * 2,
         scratch_shapes=[
+            pltpu.VMEM((depth, width), HALF),
             pltpu.VMEM((groups, channels, depth), HALF),
             pltpu.SemaphoreType.DMA((groups,)),
         ],
-        compiler_params=ROOM,
+        compiler_params=room(60),
         cost_estimate=cost(16),
     )(me, normed, ssm, branch_grad, value_bias, expand_bias, value_weight,
       *expand_parts)
@@ -463,13 +493,13 @@
     tile, sub, groups = block // 2, 256, 4
     depth = gate // groups
 
-    def body(me, live_ref, base_ref, gated_ref, x_ref, bias_ref, p0, p1, p2, p3, p4, p5, p6, p7,
+    def body(me, live_ref, base_ref, gated_ref, x_ref, bias_ref, p0, p1, p2, p3,
              out_ref, weight, sems):
         t = pl.program_id(0)
 
         @pl.when(t == 0)
         def _():
-            load_weights(me[0], (p0, p1, p2, p3, p4, p5, p6, p7), weight, OUT_PIECES, sems)
+            load_weights(me[0], (p0, p1, p2, p3), weight, OUT_PIECES, sems)
             await_weights(weight, 0, sems)
 
         place = base_ref[0] + t * tile + lax.broadcasted_iota(jnp.int32, (tile, 1), 0)
@@ -496,20 +526,20 @@
             pl.BlockSpec((tile, width), lambda t: (t, 0)),
             whole(1, width),
         ]
-        + [FAR] * 8,
+        + [FAR] * 4,
         out_specs=pl.BlockSpec((tile, width), lambda t: (t, 0)),
         scratch_shapes=[pltpu.VMEM((1, gate, width), HALF), pltpu.SemaphoreType.DMA((1,))],
-        compiler_params=ROOM,
-        cost_estimate=cost(6),
+        compiler_params=room(24),
+        cost_estimate=cost(12),
     )(me, live, base, gated, tokens, bias, *parts)
 
 
 def put_halves(mine, made, send_ref, keep_ref):
     half, rows, _ = send_ref.shape
     for k in range(half):
-        rel = ((k >> 3) & 1) * 2 + ((k >> 2) & 1) * 4 + ((k >> 1) & 1) * 8 + (k & 1) * 16
         for side, ref in ((0, keep_ref), (1, send_ref)):
-            ref[k] = made[pl.ds(pl.multiple_of(((rel + side) ^ mine) * rows, rows), rows), :]
+            at = shard_at(mine, side, k >> 3, k & 7) * rows
+            ref[k] = made[pl.ds(pl.multiple_of(at, rows), rows), :]
 
 
 def gate_kernel(me, branch_grad, normed, ssm, act, slope, parts, expand_parts):
@@ -520,17 +550,17 @@
     half = 1 << (MAIN - 1)
     value_rows, expand_rows = width // (2 * half), channels // (2 * half)
 
-    def body(me, grad_ref, x_ref, ssm_ref, act_ref, slope_ref, p0, p1, p2, p3, p4, p5, p6, p7,
-             q0, q1, q2, q3, q4, q5, q6, q7, value_ref, expand_sum, value_sum, state_ref,
+    def body(me, grad_ref, x_ref, ssm_ref, act_ref, slope_ref, p0, p1, p2, p3,
+             q0, q1, q2, q3, value_ref, expand_sum, value_sum, state_ref,
              value_send, value_keep, expand_send, expand_keep,
              expand_ref, made, made_low, weight, expand_weight, sems, expand_sems):
         j = pl.program_id(0)
 
         @pl.when(j == 0)
         def _():
-            load_weights(me[0], (p0, p1, p2, p3, p4, p5, p6, p7), weight, OUT_PIECES, sems)
+            load_weights(me[0], (p0, p1, p2, p3), weight, OUT_PIECES, sems)
             load_weights(
-                me[0], (q0, q1, q2, q3, q4, q5, q6, q7), expand_weight, EXPAND_PIECES, expand_sems
+                me[0], (q0, q1, q2, q3), expand_weight, EXPAND_PIECES, expand_sems
             )
             state_ref[...] = jnp.zeros_like(state_ref)
 
@@ -581,7 +611,7 @@
             wide,
             wide,
         ]
-        + [FAR] * 16,
+        + [FAR] * 8,
         out_specs=[wide, sums, sums, once(block, channels)] + [h[1] for h in halves],
         scratch_shapes=[
             pltpu.VMEM((block, depth), HALF),
@@ -592,8 +622,8 @@
             pltpu.SemaphoreType.DMA((groups,)),
             pltpu.SemaphoreType.DMA((groups,)),
         ],
-        compiler_params=ROOM,
-        cost_estimate=cost(16),
+        compiler_params=room(60),
+        cost_estimate=cost(20),
     )(me, branch_grad, normed, ssm, act, slope, *parts, *expand_parts)
 
 
@@ -615,7 +645,9 @@
         for c in range(channels // 256):
             state = dot(ssm_ref[...], weight[0, c * 256 : (c + 1) * 256, :], 1, 1)
             total_ref[2 * c], total_ref[2 * c + 1] = state[:, :128], state[:, 128:]
-        product, ending = scan_block(ends_ref, base_ref[0], decay_ref[...], total_ref, True)
+        product, ending = scan_block(
+            ends_ref, base_ref[0], decay_ref[...], total_ref, total_ref, True
+        )
         span_ref[0], span_ref[1] = product, ending
         map_ref[0:1, :], map_ref[1:2, :] = whole_map(product, ending, True)
 
@@ -633,8 +665,8 @@
         in_specs=[SMEM] * 3 + [vm] * 3 + [FAR] * 4,
         out_specs=[vm] * 5,
         scratch_shapes=[pltpu.VMEM((1, channels, channels), HALF), pltpu.SemaphoreType.DMA((1,))],
-        compiler_params=ROOM,
-        cost_estimate=cost(4),
+        compiler_params=room(20),
+        cost_estimate=cost(6),
     )(me, ends, base, ssm_grad, act, decay, *parts)
 
 
@@ -755,8 +787,8 @@
             pltpu.SemaphoreType.DMA((1,)),
             pltpu.SemaphoreType.DMA((3,)),
         ],
-        compiler_params=ROOM,
-        cost_estimate=cost(10),
+        compiler_params=room(40),
+        cost_estimate=cost(16),
     )(me, place, ends, base, maps, spans, totals, act, prior, ssm_grad, slope, skip, inflow, decay,
       gain, weight, tokens, cotangent, value_grad, *small_parts)
 
@@ -770,9 +802,7 @@
         ins, outs, table = refs[:4], refs[4:-1], refs[-1]
         for side in range(4):
             for k in range(8):
-                rel = (side >> 1) + (side & 1) * 2 + ((k >> 2) & 1) * 4
-                rel += ((k >> 1) & 1) * 8 + (k & 1) * 16
-                table[rel ^ me[0]] = ins[side][k, :, :lanes].astype(SINGLE)
+                table[shard_at(me[0], side >> 1, side & 1, k)] = ins[side][k, :, :lanes].astype(SINGLE)
         for i, n in enumerate(sizes):
             for shard in range(shards):
                 outs[i][:, shard * n : (shard + 1) * n] = table[shard, i : i + 1, :n]
@@ -795,7 +825,7 @@
         + [pl.BlockSpec((8, 8, channels), lambda i: (0, rows // 8 - 1, 0))] * 4,
         out_specs=[whole(1, n) for n in widths],
         scratch_shapes=[pltpu.VMEM((shards, 8, lanes), SINGLE)],
-        compiler_params=ROOM,
+        compiler_params=room(60),
         cost_estimate=cost(1),
     )(me, *parts)
 
@@ -830,9 +860,8 @@
         send_ref[...] = jnp.zeros_like(send_ref)
         keep_ref[...] = jnp.zeros_like(keep_ref)
         for k in range(half):
-            rel = ((k >> 3) & 1) * 2 + ((k >> 2) & 1) * 4 + ((k >> 1) & 1) * 8 + (k & 1) * 16
-            keep_ref[k, :, :lanes] = table[rel ^ me[0]].astype(HALF)
-            send_ref[k, :, :lanes] = table[(rel + 1) ^ me[0]].astype(HALF)
+            for side, ref in ((0, keep_ref), (1, send_ref)):
+                ref[k, :, :lanes] = table[shard_at(me[0], side, k >> 3, k & 7)].astype(HALF)
 
     vm = pl.BlockSpec(memory_space=pltpu.VMEM)
     shape = jax.ShapeDtypeStruct((half, 8, channels), HALF)
@@ -843,44 +872,47 @@
         in_specs=[SMEM] + [vm] * 7,
         out_specs=[vm] * 2,
         scratch_shapes=[pltpu.VMEM((shards, 8, lanes), SINGLE)],
-        compiler_params=ROOM,
-        cost_estimate=cost(0.1),
+        compiler_params=room(16),
+        cost_estimate=cost(12),
     )(me, norm_folds, value_fold, channel_folds, pull, skip_fold, expand_fold, out_fold)
 
 
-def finish_kernel(sizes, wide, small, high, low, gate):
-    groups = gate // wide[0].shape[1]
-
-    def body(w0, w1, w2, s0, s1, s2, *outs):
+def finish_kernel(sizes, value, expand, out, small, high, low, gate):
+    groups = gate // value[0].shape[1]
+
+    def body(*refs):
+        value, expand, out, small = refs[:3], refs[3:6], refs[6:9], refs[9:13]
+        outs = refs[13:]
+
         def total(refs, rows):
-            first, second, third = (ref[rows, :].astype(SINGLE) for ref in refs)
-            return first + second + third
-
-        width = w0.shape[1]
-        value_ref, expand_ref, reduce_ref, state_ref = outs[:4]
+            return sum(ref[rows, :].astype(SINGLE) for ref in refs)
+
+        width = value[0].shape[1]
+        value_ref, expand_ref, out_ref, reduce_ref, state_ref = outs[:5]
+        out_ref[...] = total(out, pl.ds(0, out_ref.shape[0]))
         for g in range(groups):
             cols = pl.ds(g * width, width)
-            value_ref[:, cols] = total((w0, w1, w2), pl.ds(g * high, high))
-            expand_ref[:, cols] = total((w0, w1, w2), pl.ds(groups * high + g * low, low))
-        reduce_ref[...] = total((s0, s1, s2), pl.ds(0, high))
-        state_ref[...] = total((s0, s1, s2), pl.ds(high, low))
-        rows = total((s0, s1, s2), pl.ds(high + low, 8))
+            value_ref[:, cols] = total(value, pl.ds(g * high, high))
+            expand_ref[:, cols] = total(expand, pl.ds(g * low, low))
+        reduce_ref[...] = total(small, pl.ds(0, high))
+        state_ref[...] = total(small, pl.ds(high, low))
+        rows = total(small, pl.ds(high + low, 8))
         for i, n in enumerate(sizes):
-            outs[4 + i][...] = rows[i : i + 1, :n]
+            outs[5 + i][...] = rows[i : i + 1, :n]
 
     channels = small[0].shape[1]
     vm = pl.BlockSpec(memory_space=pltpu.VMEM)
-    shapes = [(high, gate), (low, gate), (high, channels), (low, channels)]
+    shapes = [(high, gate), (low, gate), out[0].shape, (high, channels), (low, channels)]
     shapes += [(1, n) for n in sizes]
     return pl.pallas_call(
         body,
         name="finish",
         out_shape=[jax.ShapeDtypeStruct(s, SINGLE) for s in shapes],
-        in_specs=[vm] * 6,
+        in_specs=[vm] * 13,
         out_specs=[vm] * len(shapes),
-        compiler_params=ROOM,
+        compiler_params=room(16),
         cost_estimate=cost(1),
-    )(*wide, *small)
+    )(*value, *expand, *out, *small)
 
 
 def pack_kernel(vectors, reduce_shard, state_shard, expand_shard, out_shard):
@@ -914,7 +946,7 @@
         in_specs=[vm] * (len(vectors) + 4),
         out_specs=[vm] * 3,
         scratch_shapes=[pltpu.VMEM((len(vectors), channels), SINGLE)],
-        compiler_params=ROOM,
+        compiler_params=room(60),
         cost_estimate=cost(1),
     )(*[v[None] for v in vectors], reduce_shard, state_shard, expand_shard, out_shard)
 
@@ -952,7 +984,7 @@
         ],
         out_specs=[spec, spec],
         scratch_shapes=[pltpu.VMEM((height, column_block), HALF)],
-        compiler_params=ROOM,
+        compiler_params=room(16),
         cost_estimate=cost(micros),
     )(me, left, right)
 
@@ -965,54 +997,40 @@
     return exchange(values, low_bits())
 
 
-def reduce_steps(pairs, split):
-    bit_x, bit_y, bit_z, bit_far = (low_bits() + i for i in range(1, MAIN))
-    total = [[a.reshape((2, 2, 4) + a.shape[1:]) for a in pair] for pair in pairs]
-
-    def added(x, y, first, last):
-        parts, at = [], 0
-        for keep, other in total:
-            low, high = max(first - at, 0), min(last - at, keep.shape[3])
-            if low < high:
-                parts.append(add_low(keep[x, y, :, low:high], other[x, y, :, low:high]))
-            at += keep.shape[3]
-        return parts[0] if len(parts) == 1 else jnp.concatenate(parts, axis=-2)
-
-    rows = sum(keep.shape[1] for keep, _ in pairs)
-    every = slice(None)
-    if split:
-        from_x, from_y = yield [
-            exchange(added(1, every, 0, split), bit_x),
-            exchange(added(every, 1, split, rows), bit_y),
-        ]
-        kept_x, kept_y = added(0, every, 0, split), added(every, 0, split, rows)
-        last_y, last_x = yield [
-            exchange(add_low(kept_x[1], from_x[1]), bit_y),
-            exchange(add_low(kept_y[1], from_y[1]), bit_x),
-        ]
-        first = add_low(add_low(kept_x[0], from_x[0]), last_y)
-        second = add_low(add_low(kept_y[0], from_y[0]), last_x)
-        total = jnp.concatenate([first, second], axis=1)
-    else:
-        (other,) = yield [exchange(added(1, every, 0, rows), bit_x)]
-        kept = added(0, every, 0, rows)
-        (last,) = yield [exchange(add_low(kept[1], other[1]), bit_y)]
-        total = add_low(add_low(kept[0], other[0]), last)
-    (other,) = yield [exchange(total[2:], bit_z)]
-    (last,) = yield [exchange(add_low(total[1], other[1]), bit_far)]
-    return total[0], other[0], last
+def reduce_steps(pairs, direct=False):
+    _, lead, second, near, far = stage_bits()
+
+    def added(part):
+        parts = [add_low(keep[part], other[part]) for keep, other in pairs]
+        return parts[0] if len(parts) == 1 else jnp.concatenate(parts, axis=1)
+
+    (other,) = yield [(added(slice(8, 16)), lead)]
+    kept = added(slice(0, 8))
+    (last,) = yield [(add_low(kept[4:], other[4:]), second)]
+    total = add_low(add_low(kept[:4], other[:4]), last)
+    if direct:
+        others = yield [(total[1], far), (total[2], near), (total[3], near, far)]
+        return [total[0], *others]
+    (other,) = yield [(total[2:], near)]
+    (last,) = yield [(add_low(total[1], other[1]), far)]
+    return [total[0], other[0], last]
 
 
 class Run:
     def __init__(self, steps):
-        self.steps, self.result = steps, None
-        self.pending = next(steps)
-
-    def step(self):
+        self.steps, self.pending, self.result = steps, None, None
+
+    def step(self, token=None):
         try:
-            self.pending = self.steps.send(self.pending)
+            wanted = self.steps.send(self.pending)
         except StopIteration as stop:
             self.pending, self.result = None, stop.value
+            return token
+        arrays, bits = [w[0] for w in wanted], [w[1:] for w in wanted]
+        if token is not None:
+            arrays, token = tie((arrays, token))
+        self.pending = [exchange(array, *bit) for array, bit in zip(arrays, bits)]
+        return token
 
 
 def tie(values):
@@ -1072,25 +1090,6 @@
     channels = state_weight.shape[1]
     width = tokens.shape[-1]
     blocks = value_weight.shape[1] // width
-    small_run = Run(gather_steps(small, 0))
-    small_run.pending, expand_rows, out_rows = tie((small_run.pending, expand_rows, out_rows))
-    small_run.step()
-    expand_run = Run(gather_steps(expand_rows, 32))
-    small_run.pending, expand_run.pending, out_rows = tie(
-        (small_run.pending, expand_run.pending, out_rows)
-    )
-    small_run.step()
-    expand_run.step()
-    out_run = Run(gather_steps(out_rows, 48))
-    small_run.pending, expand_run.pending, out_run.pending = tie(
-        (small_run.pending, expand_run.pending, out_run.pending)
-    )
-    small_run.step()
-    expand_run.step()
-    out_run.step()
-    small_run.step()
-    small_parts = small_run.result
-
     row_count, block, _ = tokens.shape
     place = lax.axis_index("seq").reshape(1).astype(jnp.int32)
     base = place * block
@@ -1101,20 +1100,45 @@
     branch_grad = jnp.where((positions < live)[:, None], cot_rows, jnp.zeros_like(cot_rows))
     out_fold = fold(branch_grad.astype(single))
 
+    small_run = Run(gather_steps(small, True))
+    small_run.step()
+    small_run.pending, expand_rows, out_rows, branch_grad, out_fold, ends = tie(
+        (small_run.pending, expand_rows, out_rows, branch_grad, out_fold, ends)
+    )
+    small_run.step()
+    expand_run = Run(gather_steps(expand_rows))
+    expand_run.step()
+    small_run.pending, expand_run.pending, out_rows = tie(
+        (small_run.pending, expand_run.pending, out_rows)
+    )
+    small_run.step()
+    expand_run.step()
+    out_run = Run(gather_steps(out_rows, early=True))
+    out_run.step()
+    small_run.pending, expand_run.pending, out_run.pending = tie(
+        (small_run.pending, expand_run.pending, out_run.pending)
+    )
+    small_run.step()
+    small_run.pending, expand_run.pending, out_run.pending = tie(
+        (small_run.pending, expand_run.pending, out_run.pending)
+    )
+    small_run.step()
+    small_parts = small_run.result
+    me = expand_run.step(me)
+    me = out_run.step(me)
+
     vectors = unpack_kernel(me, sizes, small_parts)
     gain, shift, value_add, reduce_add, _, skip, expand_add, out_add = vectors[:8]
     decays, inflow, inflow_pull = vectors[8:]
-    expand_run.pending, out_run.pending, me = tie(
-        (expand_run.pending, out_run.pending, me)
-    )
-    expand_run.step()
-    out_run.step()
-
-    normed, act, reduce_slope, states, spans, own_map = reduce_kernel(
-        (me, ends, base), token_rows, gain, shift, reduce_add, decays, inflow, small_parts
-    )
-    own_map, me = tie((own_map, me))
+    normed, act, reduce_slope, flow = reduce_kernel(
+        me, token_rows, gain, shift, reduce_add, inflow, small_parts
+    )
+    flow, expand_run.pending, me = tie((flow, expand_run.pending, me))
+    me = expand_run.step(me)
+    states, spans, own_map = scan_kernel(me, ends, base, flow, decays)
+    own_map, out_run.pending, me = tie((own_map, out_run.pending, me))
     maps = gather_maps(own_map)
+    maps, me = out_run.step((maps, me))
     states_low, prior, ssm_low = states_kernel(
         me, place, ends, base, maps, spans, states, act, skip, inflow, decays, small_parts
     )
@@ -1122,72 +1146,87 @@
         (expand_run.pending, out_run.pending, ssm_low, me)
     )
     expand_run.step()
+    me = out_run.step(me)
     expand_run.pending, me = tie((expand_run.pending, me))
     expand_run.step()
     expand_parts = expand_run.result
-    out_run.step()
-
-    value_act, gated, gate_slope, out_grads = forward_kernel(
+
+    value_act, gated, gate_slope, out_send, out_keep = forward_kernel(
         me, normed, ssm_low, branch_grad, value_add, expand_add, value_mat, expand_parts
     )
     out_run.pending, gated, me = tie((out_run.pending, gated, me))
     out_run.step()
-    out_run.pending, me = tie((out_run.pending, me))
+    out_run.pending, out_other, me = tie((out_run.pending, core_exchange(out_send), me))
     out_run.step()
     out_parts = out_run.result
-    out_sum = lax.psum_scatter(out_grads, ("dp", "seq"), scatter_dimension=0, tiled=True)
+
+    out_run = Run(reduce_steps([(out_keep, out_other)]))
+    me = out_run.step(me)
     value_grad, expand_fold, value_fold, ssm_grad, *halves = gate_kernel(
         me, branch_grad, normed, ssm_low, value_act, gate_slope, out_parts, expand_parts
     )
-    halves, me = tie((halves, me))
+    out_run.pending, halves, me = tie((out_run.pending, halves, me))
 
     others = [core_exchange(halves[0]), core_exchange(halves[2])]
+    me = out_run.step(me)
     ssm_grad, totals, back_spans, back_map, skip_fold = state_kernel(
         me, ends, base, ssm_grad, act, decays, small_parts
     )
-    state_halves = weight_grad(states_low, ssm_grad, channels, me, "grad_state", 1)
-    others, state_halves, back_map, me = tie((others, state_halves, back_map, me))
-
-    wide_run = Run(reduce_steps([(halves[1], others[0]), (halves[3], others[1])], 96))
+    out_run.pending, others, ssm_grad, back_map, me = tie(
+        (out_run.pending, others, ssm_grad, back_map, me)
+    )
+
     back_maps = gather_maps(back_map)
+    value_run = Run(reduce_steps([(halves[1], others[0])]))
+    expand_run = Run(reduce_steps([(halves[3], others[1])]))
+    back_maps, me = value_run.step((back_maps, me))
+    me = out_run.step(me)
     reduce_grad, grad_tokens, channel_folds, norm_folds = input_kernel(
         me, place, ends, base, back_maps, back_spans, totals, act, prior, ssm_grad, reduce_slope,
         skip, inflow, decays, gain, token_rows, cot_rows, value_grad, value_mat, small_parts
     )
-    wide_run.pending, reduce_grad, norm_folds, me = tie(
-        (wide_run.pending, reduce_grad, norm_folds, me)
-    )
-
-    wide_run.step()
-    reduce_halves = weight_grad(normed, reduce_grad, channels, me, "grad_reduce", 2)
+    value_run.pending, out_run.pending, reduce_grad, norm_folds, me = tie(
+        (value_run.pending, out_run.pending, reduce_grad, norm_folds, me)
+    )
+
+    me = value_run.step(me)
+    me, norm_folds = expand_run.step((me, norm_folds))
+    me = out_run.step(me)
+    reduce_halves = weight_grad(normed, reduce_grad, channels, me, "grad_reduce", 6)
     table_halves = sums_kernel(
         me, sizes, norm_folds, value_fold, channel_folds, inflow_pull, skip_fold, expand_fold,
         out_fold
     )
-    small_others = [core_exchange(h[0]) for h in (reduce_halves, state_halves, table_halves)]
-    small_run = Run(
-        reduce_steps(
-            [
-                (halves[1], other)
-                for halves, other in zip((reduce_halves, state_halves, table_halves), small_others)
-            ],
-            0,
-        )
-    )
+    state_halves = weight_grad(states_low, ssm_grad, channels, me, "grad_state", 6)
+    small_halves = (reduce_halves, state_halves, table_halves)
+    reduce_halves, state_halves, table_halves, me = tie((*small_halves, me))
+    small_halves = (reduce_halves, state_halves, table_halves)
+    small_others = [core_exchange(h[0]) for h in small_halves]
     output = out_kernel(me, live, base, gated, token_rows, out_add, out_parts)
-    wide_run.pending, small_run.pending, output, out_sum = tie(
-        (wide_run.pending, small_run.pending, output, out_sum)
-    )
-
-    wide_run.step()
+    value_run.pending, expand_run.pending, out_run.pending, small_others, output = tie(
+        (value_run.pending, expand_run.pending, out_run.pending, small_others, output)
+    )
+
+    small_run = Run(reduce_steps([(h[1], other) for h, other in zip(small_halves, small_others)], True))
     small_run.step()
-    wide_run.pending, small_run.pending = tie((wide_run.pending, small_run.pending))
-
-    for run in (small_run, wide_run):
+    value_run.step()
+    expand_run.step()
+    out_run.step()
+    value_run.pending, expand_run.pending, small_run.pending = tie(
+        (value_run.pending, expand_run.pending, small_run.pending)
+    )
+
+    small_run.step()
+    value_run.step()
+    expand_run.step()
+    value_run.pending, expand_run.pending, small_run.pending = tie(
+        (value_run.pending, expand_run.pending, small_run.pending)
+    )
+    for run in (value_run, expand_run, small_run, out_run):
         while run.result is None:
             run.step()
-    value_sum, expand_sum, reduce_sum, state_sum, *vector_sums = finish_kernel(
-        sizes, wide_run.result, small_run.result, width // shards, channels // shards, width * blocks
+    value_sum, expand_sum, out_sum, reduce_sum, state_sum, *vector_sums = finish_kernel(
+        sizes, value_run.result, expand_run.result, out_run.result, small_run.result, width // shards, channels // shards, width * blocks
     )
     vector_sums = [reduce_low(v[0]) for v in vector_sums]
     return (
@@ -1204,7 +1243,7 @@
         reduce_low(state_sum),
         reduce_low(expand_sum),
         vector_sums[6],
-        out_sum.astype(single),
+        reduce_low(out_sum),
         vector_sums[7],
     )
 

time: 308 us -> 291 us (0.945)
  Pallas kernels: 136 us -> 120 us
  other arithmetic: 29.7 us -> 22.4 us
  waiting for transfers between devices: 76.9 us -> 81.8 us
    pallas_call x2, Pallas kernels: 7.34 us -> 2.11 us  [weight_grad(): pl.pallas_call(body, name=name, out_shape=[shape, shape], grid=(blocks,),...]
    ppermute x46, waiting for transfers between devices: 76.9 us -> 81.8 us  [exchange(): return lax.ppermute(values, axes, [(i, other(i)) for i in range(count)])]
    convert_element_type x13 -> x17, other arithmetic: 15 us -> 11 us  [add_low(): return (first.astype(SINGLE) + second.astype(SINGLE)).astype(HALF)]
    unnamed x50 -> x98, local copies, waits for them, and re-layouts: 3.48 us -> 7.2 us
  transfers between devices with their start and end apart: 48 -> 47, of which waited for: 23 -> 21; matrix products, arithmetic and copies ran while one was open for 9% -> 5% of each run, Pallas kernels for 44% -> 40%
where the time goes in v4:
time: 291 us
  Pallas kernels  120 us (41%)
  waiting for transfers between devices  81.8 us (28%)
  starting transfers between devices  43 us (15%)
  other arithmetic  22.4 us (8%)
  between operations  14.9 us (5%)
  local copies, waits for them, and re-layouts  8.09 us (3%)
    ppermute x46, waiting for transfers between devices, exchange(): return lax.ppermute(values, axes, [(i, other(i)) for i in range(count)])  81.8 us
    ppermute x46, starting transfers between devices, exchange(): return lax.ppermute(values, axes, [(i, other(i)) for i in range(count)])  42.9 us
    pallas_call x1, Pallas kernels, gate_kernel(): pl.pallas_call(body, name='gate_backward', out_shape=[jax.ShapeDtypeStruc...  31.2 us
    pallas_call x1, Pallas kernels, forward_kernel(): pl.pallas_call(body, name='gate_forward', out_shape=[jax.ShapeDtypeStruct...  31.1 us
    pallas_call x1, Pallas kernels, input_kernel(): pl.pallas_call(body, name='input_backward', out_shape=[jax.ShapeDtypeStru...  18.4 us
    pallas_call x1, Pallas kernels, out_kernel(): pl.pallas_call(body, name='out_forward', out_shape=jax.ShapeDtypeStruct((...  12.7 us
    convert_element_type x17, other arithmetic, add_low(): return (first.astype(SINGLE) + second.astype(SINGLE)).astype(HALF)  11 us
    pallas_call x1, Pallas kernels, reduce_kernel(): pl.pallas_call(body, name='reduce_forward', out_shape=[jax.ShapeDtypeStru...  8.44 us
  transfers between devices with their start and end apart: 47, of which 21 were waited for; matrix products, arithmetic and copies ran while one was open for 5% of the time, Pallas kernels for 40%

profile of v4, /device:TPU:0, one launch (start us, length us, event | category | flops | bytes accessed | tf_op | source)
XLA Modules:
  0.0 290.7 jit_solution(6396422309259108605)
XLA Ops:
  7.2 1.7 convert_element_type.269
  9.0 2.1 pack.1
  11.1 5.0 %collective-permute-start.2 = (bf16[1,56,512]{2,1,0:T(8,128)(2,1)}, bf16[1,56,512]{2,1,0:T(8,128)(2,1)S(1)}, u32[]{:S(2)}, u32[]{:S(2)}) collective-permute-start(bf16[1,56,512]{2,1,0:T(8,128)(2,1)} %bitcast.87), channel_id=1, source_target_pairs={{0,24},{1,25},{2,26},{3,27},{4,28},{5,29},{6,30},{7,31},{8,16},{9,... | collective-permute-start | bytes 172040 | tf_op jit(solution)/shard_map/ppermute | solution.py:38
  19.5 1.5 broadcast_select_fusion.grad_ref
  21.9 1.6 collective-permute-start.3
  23.5 1.7 collective-permute-start.4
  25.1 7.2 %collective-permute-done.4 = bf16[1,64,768]{2,1,0:T(8,128)(2,1)S(1)} collective-permute-done((bf16[1,64,768]{2,1,0:T(8,128)(2,1)S(1)}, bf16[1,64,768]{2,1,0:T(8,128)(2,1)S(1)}, u32[]{:S(2)}, u32[]{:S(2)}) %collective-permute-start.4) | collective-permute-done | bytes 98336 | tf_op jit(solution)/shard_map/ppermute | solution.py:38
  32.5 0.8 collective-permute-start.7
  33.3 3.6 %collective-permute-start.8 = (bf16[1,96,1024]{2,1,0:T(8,128)(2,1)S(1)}, bf16[1,96,1024]{2,1,0:T(8,128)(2,1)S(1)}, u32[]{:S(2)}, u32[]{:S(2)}) collective-permute-start(bf16[1,96,1024]{2,1,0:T(8,128)(2,1)S(1)} %bitcast.80), channel_id=1, source_target_pairs={{0,16},{1,17},{2,18},{3,19},{4,20},{5,21},{6,22},{7,23},{8,24},{9,... | collective-permute-start | bytes 589832 | tf_op jit(solution)/shard_map/ppermute | solution.py:38
  36.9 6.2 %collective-permute-done.7 = bf16[2,64,768]{2,1,0:T(8,128)(2,1)S(1)} collective-permute-done((bf16[2,64,768]{2,1,0:T(8,128)(2,1)S(1)}, bf16[2,64,768]{2,1,0:T(8,128)(2,1)S(1)}, u32[]{:S(2)}, u32[]{:S(2)}) %collective-permute-start.7) | collective-permute-done | bytes 196640 | tf_op jit(solution)/shard_map/ppermute | solution.py:38
  43.1 2.1 collective-permute-done.8
  45.8 1.9 collective-permute-done.9.refs_3_.s3
  47.8 1.8 pad_maximum_fusion.6
  49.6 1.8 pad_maximum_fusion.5
  51.7 1.0 collective-permute-start.10
  52.8 1.9 unpack.1
  54.6 8.4 %reduce_forward.1 = (bf16[1024,1024]{1,0:T(8,128)(2,1)}, f32[1024,512]{1,0:T(8,128)}, bf16[1024,512]{1,0:T(8,128)(2,1)}, f32[4,1024,128]{2,1,0:T(8,128)}) custom-call(s32[1]{0:T(128)} %bitcast.17.me.order.me_ref, bf16[1024,1024]{1,0:T(8,128)(2,1)} %bitcast.70, f32[1,1024]{1,0:T(1,128)} %get-tuple-element.202.gain_ref, ...), custom_call_target="tpu_custom_call" | custom-call | flops 8000000000 | bytes 1048576 | tf_op jit(solution)/shard_map/reduce_forward/pallas_call | solution.py:310
  63.1 1.1 pad_maximum_fusion.1.q0
  64.2 2.4 copy-done.17
  66.7 2.7 state_scan.1
  69.9 0.8 collective-permute-done.14
  70.7 1.0 collective-permute-start.15
  71.8 1.1 collective-permute-start.12
  72.9 1.6 collective-permute-done.15
  75.2 3.5 %states_forward.1 = (bf16[1024,512]{1,0:T(8,128)(2,1)S(1)}, bf16[1024,512]{1,0:T(8,128)(2,1)S(1)}, bf16[1024,512]{1,0:T(8,128)(2,1)S(1)}) custom-call(s32[1]{0:T(128)} %bitcast.17.me.order.me_ref, s32[1]{0:T(128)} %bitcast.9.place_ref, s32[8]{0:T(128)S(1)} %bitcast.74, s32[1]{0:T(128)} %mul.6.base_ref, f32[4,2,512]{2,1,0:T(2,128)S(1)} %pad_maximum_fusion.9.maps_ref, ...), custom_call_target="tpu_custom_call" | custom-call | flops 4000000000 | bytes 1048576 | tf_op jit(solution)/shard_map/states_forward/pallas_call | solution.py:398
  78.7 16.1 %collective-permute-done.12.q1 = bf16[8,64,768]{2,1,0:T(8,128)(2,1)S(1)} collective-permute-done((bf16[8,64,768]{2,1,0:T(8,128)(2,1)S(1)}, bf16[8,64,768]{2,1,0:T(8,128)(2,1)S(1)}, u32[]{:S(2)}, u32[]{:S(2)}) %collective-permute-start.12) | collective-permute-done | bytes 786464 | tf_op jit(solution)/shard_map/ppermute | solution.py:38
  95.3 1.3 pad_maximum_fusion.p0
  96.6 1.4 collective-permute-start.18
  98.2 0.9 copy-done.43
  99.1 31.1 %gate_forward.1 = (bf16[1024,3072]{1,0:T(8,128)(2,1)}, bf16[1024,3072]{1,0:T(8,128)(2,1)}, bf16[1024,3072]{1,0:T(8,128)(2,1)}, bf16[16,96,1024]{2,1,0:T(8,128)(2,1)}, bf16[16,96,1024]{2,1,0:T(8,128)(2,1)}) custom-call(s32[1]{0:T(128)} %bitcast.17.me.order.me_ref, bf16[1024,1024]{1,0:T(8,128)(2,1)} %get-tuple-element.233.x_ref.left_ref, ...), custom_call_target="tpu_custom_call" | custom-call | flops 16000000000 | bytes 1048576 | tf_op jit(solution)/shard_map/gate_forward/pallas_call | solution.py:458
  130.9 7.7 %collective-permute-done.20.p3 = bf16[8,96,1024]{2,1,0:T(8,128)(2,1)} collective-permute-done((bf16[8,96,1024]{2,1,0:T(8,128)(2,1)}, bf16[8,96,1024]{2,1,0:T(8,128)(2,1)}, u32[]{:S(2)}, u32[]{:S(2)}) %collective-permute-start.20) | collective-permute-done | bytes 1572896 | tf_op jit(solution)/shard_map/ppermute | solution.py:38
  138.6 5.0 %add_convert_fusion.3 = (bf16[8,96,1024]{2,1,0:T(8,128)(2,1)}, bf16[8,96,1024]{2,1,0:T(8,128)(2,1)}) fusion(bf16[16,96,1024]{2,1,0:T(8,128)(2,1)S(1)} %collective-permute-done.21, bf16[16,96,1024]{2,1,0:T(8,128)(2,1)} %get-tuple-element.240), kind=kLoop, calls=%fused_computation.4 | loop fusion | flops 6291456 | bytes 9437184 | tf_op jit(solution)/shard_map/convert_element_type | solution.py:993
  144.2 31.2 %gate_backward.1 = (bf16[1024,3072]{1,0:T(8,128)(2,1)}, f32[8,3072]{1,0:T(8,128)}, f32[8,3072]{1,0:T(8,128)}, f32[1024,512]{1,0:T(8,128)}, bf16[16,128,768]{2,1,...) custom-call(s32[1]{0:T(128)} %bitcast.17.me.order.me_ref, ...), custom_call_target="tpu_custom_call" | custom-call | flops 20000000000 | bytes 1048576 | tf_op jit(solution)/shard_map/gate_backward/pallas_call | solution.py:598
  176.0 1.7 add_convert_fusion.11
  177.7 1.5 collective-permute-start.23
  179.3 1.6 copy-done.15
  180.9 4.9 %state_backward.1 = (bf16[1024,512]{1,0:T(8,128)(2,1)S(1)}, f32[4,1024,128]{2,1,0:T(8,128)S(1)}, f32[2,8,512]{2,1,0:T(8,128)S(1)}, f32[2,512]{1,0:T(2,128)S(1)}, f32[8,512]{1,0:T(8,128)S(1)}) custom-call(s32[1]{0:T(128)} %bitcast.17.me.order.me_ref, s32[8]{0:T(128)S(1)} %bitcast.75, s32[1]{0:T(128)} %mul.6.base_ref, f32[1024,512]{1,0:T(8,128)S(1)} %copy-done.15, ...), custom_call_target="tpu_custom_call" | custom-call | flops 6000000000 | bytes 1048576 | tf_op jit(solution)/shard_map/state_backward/pallas_call | solution.py:655
  185.7 4.1 %collective-permute-done.23 = bf16[4,96,1024]{2,1,0:T(8,128)(2,1)S(1)} collective-permute-done((bf16[4,96,1024]{2,1,0:T(8,128)(2,1)S(1)}, bf16[4,96,1024]{2,1,0:T(8,128)(2,1)S(1)}, u32[]{:S(2)}, u32[]{:S(2)}) %collective-permute-start.23) | collective-permute-done | bytes 786464 | tf_op jit(solution)/shard_map/ppermute | solution.py:38
  189.9 0.9 add_convert_fusion
  191.0 1.5 collective-permute-start.27
  192.5 1.6 add_convert_fusion.9
  194.8 1.5 collective-permute-start.28
  196.8 1.6 collective-permute-start.29
  198.4 18.4 %input_backward.1 = (bf16[1024,512]{1,0:T(8,128)(2,1)S(1)}, bf16[1024,1024]{1,0:T(8,128)(2,1)}, f32[3,8,512]{2,1,0:T(8,128)S(1)}, f32[2,8,1024]{2,1,0:T(8,128)S(1)}) custom-call(s32[1]{0:T(128)} %bitcast.17.me.order.me_ref, s32[1]{0:T(128)} %bitcast.9.place_ref, s32[8]{0:T(128)S(1)} %bitcast.76, s32[1]{0:T(128)} %mul.6.base_ref, ...), custom_call_target="tpu_custom_call" | custom-call | flops 16000000000 | bytes 1048576 | tf_op jit(solution)/shard_map/input_backward/pallas_call | solution.py:750
  217.1 1.3 copy-done.16
  218.4 1.3 grad_reduce.1
  219.8 0.8 grad_state.1
  221.2 2.5 collective-permute-start.32
  224.7 1.5 collective-permute-start.30
  226.2 12.7 %out_forward.1 = bf16[1024,1024]{1,0:T(8,128)(2,1)} custom-call(s32[1]{0:T(128)} %bitcast.17.me.order.me_ref, s32[1]{0:T(128)} %bitcast.22.live_ref, s32[1]{0:T(128)} %mul.6.base_ref, bf16[1024,3072]{1,0:T(8,128)(2,1)S(1)} %bitcast.78, bf16[1024,1024]{1,0:T(8,128)(2,1)S(1)} %bitcast.72, f32[1,1024]{1,0:T(1,128)S(1)} %copy-done.19, ...), custom_call_target="tpu_custom_call" | custom-call | flops 12000000000 | bytes 1048576 | tf_op jit(solution)/shard_map/out_forward/pallas_call | solution.py:516
  238.9 5.1 %collective-permute-done.31 = bf16[8,64,768]{2,1,0:T(8,128)(2,1)S(1)} collective-permute-done((bf16[8,64,768]{2,1,0:T(8,128)(2,1)S(1)}, bf16[8,64,768]{2,1,0:T(8,128)(2,1)S(1)}, u32[]{:S(2)}, u32[]{:S(2)}) %collective-permute-start.31) | collective-permute-done | bytes 786464 | tf_op jit(solution)/shard_map/ppermute | solution.py:38
  245.3 1.2 collective-permute-start.36
  246.8 1.1 collective-permute-start.38
  248.0 7.7 %collective-permute-done.37 = bf16[4,64,768]{2,1,0:T(8,128)(2,1)S(1)} collective-permute-done((bf16[4,64,768]{2,1,0:T(8,128)(2,1)S(1)}, bf16[4,64,768]{2,1,0:T(8,128)(2,1)S(1)}, u32[]{:S(2)}, u32[]{:S(2)}) %collective-permute-start.37) | collective-permute-done | bytes 393248 | tf_op jit(solution)/shard_map/ppermute | solution.py:38
  256.5 1.0 collective-permute-start.41
  257.5 1.2 collective-permute-start.40
  259.3 7.8 %collective-permute-done.40 = bf16[2,64,768]{2,1,0:T(8,128)(2,1)S(1)} collective-permute-done((bf16[2,64,768]{2,1,0:T(8,128)(2,1)S(1)}, bf16[2,64,768]{2,1,0:T(8,128)(2,1)S(1)}, u32[]{:S(2)}, u32[]{:S(2)}) %collective-permute-start.40) | collective-permute-done | bytes 196640 | tf_op jit(solution)/shard_map/ppermute | solution.py:38
  267.1 3.7 %collective-permute-done.39.refs_2_ = bf16[128,768]{1,0:T(8,128)(2,1)S(1)} collective-permute-done((bf16[128,768]{1,0:T(8,128)(2,1)S(1)}, bf16[128,768]{1,0:T(8,128)(2,1)S(1)}, u32[]{:S(2)}, u32[]{:S(2)}) %collective-permute-start.39) | collective-permute-done | bytes 196640 | tf_op jit(solution)/shard_map/ppermute | solution.py:38
  271.1 0.8 collective-permute-start.44
  271.9 3.6 %collective-permute-start.43 = (bf16[56,512]{1,0:T(8,128)(2,1)S(1)}, bf16[56,512]{1,0:T(8,128)(2,1)S(1)}, u32[]{:S(2)}, u32[]{:S(2)}) collective-permute-start(bf16[56,512]{1,0:T(8,128)(2,1)S(1)} %get-tuple-element.363), channel_id=1, source_target_pairs={{0,16},{1,17},{2,18},{3,19},{4,20},{5,21},{6,22},{7,23},{8,24},{9,... | collective-permute-start | bytes 172040 | tf_op jit(solution)/shard_map/ppermute | solution.py:38
  275.5 2.0 collective-permute-done.45.refs_12_
  277.5 3.7 %collective-permute-done.43.refs_10_ = bf16[56,512]{1,0:T(8,128)(2,1)S(1)} collective-permute-done((bf16[56,512]{1,0:T(8,128)(2,1)S(1)}, bf16[56,512]{1,0:T(8,128)(2,1)S(1)}, u32[]{:S(2)}, u32[]{:S(2)}) %collective-permute-start.43) | collective-permute-done | bytes 57376 | tf_op jit(solution)/shard_map/ppermute | solution.py:38
  281.2 1.5 collective-permute-done.42.refs_5_
  282.8 1.1 finish.1
  (193 shorter events, 15.3 us)
Async XLA Ops:
  7.2 92.0 %all-gather.2.cloned.1.call-start = ((), (), s32[]{:S(2)}) async-start(), calls=%async_computation | async-start | bytes 6488064 | tf_op jit(solution)/shard_map/all_gather | solution.py:1068
  9.0 7.8 %copy-start.44 = (s32[1,8]{1,0:T(1,128)S(1)}, s32[1,8]{1,0:T(1,128)}, u32[]{:S(2)}) copy-start(s32[1,8]{1,0:T(1,128)} %param.17) | copy-start | bytes 100
  9.0 10.0 %copy-start = (bf16[1,1024,1024]{2,1,0:T(8,128)(2,1)S(1)}, bf16[1,1024,1024]{2,1,0:T(8,128)(2,1)}, u32[]{:S(2)}) copy-start(bf16[1,1024,1024]{2,1,0:T(8,128)(2,1)} %param.18) | copy-start | bytes 6291460
  11.1 10.0 %collective-permute-start.2 = (bf16[1,56,512]{2,1,0:T(8,128)(2,1)}, bf16[1,56,512]{2,1,0:T(8,128)(2,1)S(1)}, u32[]{:S(2)}, u32[]{:S(2)}) collective-permute-start(bf16[1,56,512]{2,1,0:T(8,128)(2,1)} %bitcast.87), channel_id=1, source_target_pairs={{0,24},{1,25},{2,26},{3,27},{4,28},{5,29},{6,30},{7,31},{8,16},{9,... | collective-permute-start | bytes 172040 | tf_op jit(solution)/shard_map/ppermute | solution.py:38
  16.2 4.9 %collective-permute-start.1 = (bf16[1,56,512]{2,1,0:T(8,128)(2,1)}, bf16[1,56,512]{2,1,0:T(8,128)(2,1)S(1)}, u32[]{:S(2)}, u32[]{:S(2)}) collective-permute-start(bf16[1,56,512]{2,1,0:T(8,128)(2,1)} %bitcast.88), channel_id=1, source_target_pairs={{0,8},{1,9},{2,10},{3,11},{4,12},{5,13},{6,14},{7,15},{8,0},{9,1},... | collective-permute-start | bytes 172040 | tf_op jit(solution)/shard_map/ppermute | solution.py:38
  16.2 5.7 %collective-permute-start = (bf16[1,56,512]{2,1,0:T(8,128)(2,1)}, bf16[1,56,512]{2,1,0:T(8,128)(2,1)S(1)}, u32[]{:S(2)}, u32[]{:S(2)}) collective-permute-start(bf16[1,56,512]{2,1,0:T(8,128)(2,1)} %bitcast.89), channel_id=1, source_target_pairs={{0,16},{1,17},{2,18},{3,19},{4,20},{5,21},{6,22},{7,23},{8,24},{9,... | collective-permute-start | bytes 172040 | tf_op jit(solution)/shard_map/ppermute | solution.py:38
  21.1 12.3 %copy-start.29 = (bf16[96,1024]{1,0:T(8,128)(2,1)S(1)}, bf16[96,1024]{1,0:T(8,128)(2,1)}, u32[]{:S(2)}) copy-start(bf16[96,1024]{1,0:T(8,128)(2,1)} %get-tuple-element.192) | copy-start | bytes 589828
  21.9 10.5 %collective-permute-start.3 = (bf16[4,56,512]{2,1,0:T(8,128)(2,1)S(1)}, bf16[4,56,512]{2,1,0:T(8,128)(2,1)S(1)}, u32[]{:S(2)}, u32[]{:S(2)}) collective-permute-start(bf16[4,56,512]{2,1,0:T(8,128)(2,1)S(1)} %pad_maximum_fusion.7), channel_id=1, source_target_pairs={{0,4},{1,3},{2,6},{3,1},{4,0},{5,7},{6,2},{7,5},{8,12},{9,11},{10,... | collective-permute-start | bytes 688136 | tf_op jit(solution)/shard_map/ppermute | solution.py:38
  23.5 8.9 %collective-permute-start.4 = (bf16[1,64,768]{2,1,0:T(8,128)(2,1)S(1)}, bf16[1,64,768]{2,1,0:T(8,128)(2,1)S(1)}, u32[]{:S(2)}, u32[]{:S(2)}) collective-permute-start(bf16[1,64,768]{2,1,0:T(8,128)(2,1)S(1)} %bitcast.84), channel_id=1, source_target_pairs={{0,16},{1,17},{2,18},{3,19},{4,20},{5,21},{6,22},{7,23},{8,24},{9,... | collective-permute-start | bytes 294920 | tf_op jit(solution)/shard_map/ppermute | solution.py:38
  32.4 12.8 %copy-start.36 = (bf16[1,64,768]{2,1,0:T(8,128)(2,1)}, bf16[1,64,768]{2,1,0:T(8,128)(2,1)S(1)}, u32[]{:S(2)}) copy-start(bf16[1,64,768]{2,1,0:T(8,128)(2,1)S(1)} %collective-permute-done.4) | copy-start | bytes 294916
  32.4 20.4 %copy-start.1 = (bf16[8,56,512]{2,1,0:T(8,128)(2,1)}, bf16[8,56,512]{2,1,0:T(8,128)(2,1)S(1)}, u32[]{:S(2)}) copy-start(bf16[8,56,512]{2,1,0:T(8,128)(2,1)S(1)} %constant_dynamic-update-slice_fusion.refs_0_.s0) | copy-start | bytes 1376260
  32.4 12.7 %collective-permute-start.6 = (bf16[8,56,512]{2,1,0:T(8,128)(2,1)S(1)}, bf16[8,56,512]{2,1,0:T(8,128)(2,1)S(1)}, u32[]{:S(2)}, u32[]{:S(2)}) collective-permute-start(bf16[8,56,512]{2,1,0:T(8,128)(2,1)S(1)} %constant_dynamic-update-slice_fusion.refs_0_.s0), channel_id=1, source_target_pairs={{0,2},{1,5},{2,0},{3,7},{4,6},{5,1},{6,4},{7,3},{8,10},{9,13},{10,... | collective-permute-start | bytes 1376264 | tf_op jit(solution)/shard_map/ppermute | solution.py:38
  32.5 10.6 %collective-permute-start.7 = (bf16[2,64,768]{2,1,0:T(8,128)(2,1)S(1)}, bf16[2,64,768]{2,1,0:T(8,128)(2,1)S(1)}, u32[]{:S(2)}, u32[]{:S(2)}) collective-permute-start(bf16[2,64,768]{2,1,0:T(8,128)(2,1)S(1)} %pad_maximum_fusion.8), channel_id=1, source_target_pairs={{0,8},{1,9},{2,10},{3,11},{4,12},{5,13},{6,14},{7,15},{8,0},{9,1},... | collective-permute-start | bytes 589832 | tf_op jit(solution)/shard_map/ppermute | solution.py:38
  33.3 11.8 %collective-permute-start.8 = (bf16[1,96,1024]{2,1,0:T(8,128)(2,1)S(1)}, bf16[1,96,1024]{2,1,0:T(8,128)(2,1)S(1)}, u32[]{:S(2)}, u32[]{:S(2)}) collective-permute-start(bf16[1,96,1024]{2,1,0:T(8,128)(2,1)S(1)} %bitcast.80), channel_id=1, source_target_pairs={{0,16},{1,17},{2,18},{3,19},{4,20},{5,21},{6,22},{7,23},{8,24},{9,... | collective-permute-start | bytes 589832 | tf_op jit(solution)/shard_map/ppermute | solution.py:38
  36.9 8.9 %collective-permute-start.5 = (bf16[8,56,512]{2,1,0:T(8,128)(2,1)S(1)}, bf16[8,56,512]{2,1,0:T(8,128)(2,1)S(1)}, u32[]{:S(2)}, u32[]{:S(2)}) collective-permute-start(bf16[8,56,512]{2,1,0:T(8,128)(2,1)S(1)} %constant_dynamic-update-slice_fusion.refs_0_.s0), channel_id=1, source_target_pairs={{0,1},{1,0},{2,3},{3,2},{4,5},{5,4},{6,7},{7,6},{8,9},{9,8},{10,11... | collective-permute-start | bytes 1376264 | tf_op jit(solution)/shard_map/ppermute | solution.py:38
  45.8 7.0 %copy-start.4 = (bf16[8,56,512]{2,1,0:T(8,128)(2,1)}, bf16[8,56,512]{2,1,0:T(8,128)(2,1)S(1)}, u32[]{:S(2)}) copy-start(bf16[8,56,512]{2,1,0:T(8,128)(2,1)S(1)} %collective-permute-done.6.refs_1_.s1) | copy-start | bytes 1376260
  45.8 1.9 collective-permute-start.9
  45.8 6.9 %copy-start.6 = (bf16[8,56,512]{2,1,0:T(8,128)(2,1)}, bf16[8,56,512]{2,1,0:T(8,128)(2,1)S(1)}, u32[]{:S(2)}) copy-start(bf16[8,56,512]{2,1,0:T(8,128)(2,1)S(1)} %collective-permute-done.5.refs_2_.s2) | copy-start | bytes 1376260
  51.4 18.1 %collective-permute-start.13 = (bf16[2,96,1024]{2,1,0:T(8,128)(2,1)}, bf16[2,96,1024]{2,1,0:T(8,128)(2,1)S(1)}, u32[]{:S(2)}, u32[]{:S(2)}) collective-permute-start(bf16[2,96,1024]{2,1,0:T(8,128)(2,1)} %pad_maximum_fusion.5), channel_id=1, source_target_pairs={{0,8},{1,9},{2,10},{3,11},{4,12},{5,13},{6,14},{7,15},{8,0},{9,1},... | collective-permute-start | bytes 1179656 | tf_op jit(solution)/shard_map/ppermute | solution.py:38
  51.7 11.4 %collective-permute-start.10 = (bf16[4,64,768]{2,1,0:T(8,128)(2,1)}, bf16[4,64,768]{2,1,0:T(8,128)(2,1)}, u32[]{:S(2)}, u32[]{:S(2)}) collective-permute-start(bf16[4,64,768]{2,1,0:T(8,128)(2,1)} %pad_maximum_fusion.6), channel_id=1, source_target_pairs={{0,4},{1,3},{2,6},{3,1},{4,0},{5,7},{6,2},{7,5},{8,12},{9,11},{10,... | collective-permute-start | bytes 1179656 | tf_op jit(solution)/shard_map/ppermute | solution.py:38
  54.6 8.5 %copy-start.35 = (bf16[64,768]{1,0:T(8,128)(2,1)S(1)}, bf16[64,768]{1,0:T(8,128)(2,1)}, u32[]{:S(2)}) copy-start(bf16[64,768]{1,0:T(8,128)(2,1)} %get-tuple-element.185) | copy-start | bytes 294916
  54.6 8.5 %copy-start.37 = (bf16[1,64,768]{2,1,0:T(8,128)(2,1)S(1)}, bf16[1,64,768]{2,1,0:T(8,128)(2,1)}, u32[]{:S(2)}) copy-start(bf16[1,64,768]{2,1,0:T(8,128)(2,1)} %copy-done.36) | copy-start | bytes 294916
  54.6 8.5 %copy-start.40 = (bf16[2,64,768]{2,1,0:T(8,128)(2,1)S(1)}, bf16[2,64,768]{2,1,0:T(8,128)(2,1)}, u32[]{:S(2)}) copy-start(bf16[2,64,768]{2,1,0:T(8,128)(2,1)} %copy-done.39) | copy-start | bytes 589828
  64.2 10.9 %copy-start.38 = (bf16[8,64,768]{2,1,0:T(8,128)(2,1)}, bf16[8,64,768]{2,1,0:T(8,128)(2,1)S(1)}, u32[]{:S(2)}) copy-start(bf16[8,64,768]{2,1,0:T(8,128)(2,1)S(1)} %pad_maximum_fusion.1.q0) | copy-start | bytes 2359300
  66.7 8.4 %copy-start.8 = (f32[1024,512]{1,0:T(8,128)S(1)}, f32[1024,512]{1,0:T(8,128)}, u32[]{:S(2)}) copy-start(f32[1024,512]{1,0:T(8,128)} %get-tuple-element.225.act_ref) | copy-start | bytes 6291460
  69.5 1.2 collective-permute-start.14
  70.7 3.8 %collective-permute-start.15 = (f32[2,2,512]{2,1,0:T(2,128)S(1)}, f32[2,2,512]{2,1,0:T(2,128)S(1)}, u32[]{:S(2)}, u32[]{:S(2)}) collective-permute-start(f32[2,2,512]{2,1,0:T(2,128)S(1)} %pad_maximum_fusion.11), channel_id=1, source_target_pairs={{0,2},{1,3},{2,0},{3,1},{4,6},{5,7},{6,4},{7,5},{8,10},{9,11},{10,... | collective-permute-start | bytes 24584 | tf_op jit(solution)/shard_map/ppermute | solution.py:38
  71.8 23.1 %collective-permute-start.12 = (bf16[8,64,768]{2,1,0:T(8,128)(2,1)S(1)}, bf16[8,64,768]{2,1,0:T(8,128)(2,1)S(1)}, u32[]{:S(2)}, u32[]{:S(2)}) collective-permute-start(bf16[8,64,768]{2,1,0:T(8,128)(2,1)S(1)} %pad_maximum_fusion.1.q0), channel_id=1, source_target_pairs={{0,2},{1,5},{2,0},{3,7},{4,6},{5,1},{6,4},{7,3},{8,10},{9,13},{10,... | collective-permute-start | bytes 2359304 | tf_op jit(solution)/shard_map/ppermute | solution.py:38
  74.5 20.7 %collective-permute-start.16 = (bf16[4,96,1024]{2,1,0:T(8,128)(2,1)S(1)}, bf16[4,96,1024]{2,1,0:T(8,128)(2,1)S(1)}, u32[]{:S(2)}, u32[]{:S(2)}) collective-permute-start(bf16[4,96,1024]{2,1,0:T(8,128)(2,1)S(1)} %pad_maximum_fusion.2), channel_id=1, source_target_pairs={{0,4},{1,3},{2,6},{3,1},{4,0},{5,7},{6,2},{7,5},{8,12},{9,11},{10,... | collective-permute-start | bytes 2359304 | tf_op jit(solution)/shard_map/ppermute | solution.py:38
  75.1 23.1 %collective-permute-start.11 = (bf16[8,64,768]{2,1,0:T(8,128)(2,1)S(1)}, bf16[8,64,768]{2,1,0:T(8,128)(2,1)S(1)}, u32[]{:S(2)}, u32[]{:S(2)}) collective-permute-start(bf16[8,64,768]{2,1,0:T(8,128)(2,1)S(1)} %pad_maximum_fusion.1.q0), channel_id=1, source_target_pairs={{0,1},{1,0},{2,3},{3,2},{4,5},{5,4},{6,7},{7,6},{8,9},{9,8},{10,11... | collective-permute-start | bytes 2359304 | tf_op jit(solution)/shard_map/ppermute | solution.py:38
  78.7 17.9 %copy-start.10 = (bf16[1024,512]{1,0:T(8,128)(2,1)}, bf16[1024,512]{1,0:T(8,128)(2,1)S(1)}, u32[]{:S(2)}) copy-start(bf16[1024,512]{1,0:T(8,128)(2,1)S(1)} %get-tuple-element.301.left_ref) | copy-start | bytes 3145732
  78.7 17.9 %copy-start.12 = (bf16[1024,512]{1,0:T(8,128)(2,1)}, bf16[1024,512]{1,0:T(8,128)(2,1)S(1)}, u32[]{:S(2)}) copy-start(bf16[1024,512]{1,0:T(8,128)(2,1)S(1)} %get-tuple-element.280.prior_ref) | copy-start | bytes 3145732
  78.7 17.9 %copy-start.14 = (bf16[1024,512]{1,0:T(8,128)(2,1)}, bf16[1024,512]{1,0:T(8,128)(2,1)S(1)}, u32[]{:S(2)}) copy-start(bf16[1024,512]{1,0:T(8,128)(2,1)S(1)} %get-tuple-element.234.ssm_ref) | copy-start | bytes 3145732
  95.2 3.9 %collective-permute-start.17 = (bf16[8,64,768]{2,1,0:T(8,128)(2,1)S(1)}, bf16[8,64,768]{2,1,0:T(8,128)(2,1)}, u32[]{:S(2)}, u32[]{:S(2)}) collective-permute-start(bf16[8,64,768]{2,1,0:T(8,128)(2,1)S(1)} %collective-permute-done.12.q1), channel_id=1, source_target_pairs={{0,1},{1,0},{2,3},{3,2},{4,5},{5,4},{6,7},{7,6},{8,9},{9,8},{10,11... | collective-permute-start | bytes 2359304 | tf_op jit(solution)/shard_map/ppermute | solution.py:38
  96.6 34.1 %collective-permute-start.18 = (bf16[8,96,1024]{2,1,0:T(8,128)(2,1)}, bf16[8,96,1024]{2,1,0:T(8,128)(2,1)}, u32[]{:S(2)}, u32[]{:S(2)}) collective-permute-start(bf16[8,96,1024]{2,1,0:T(8,128)(2,1)} %pad_maximum_fusion.p0), channel_id=1, source_target_pairs={{0,2},{1,5},{2,0},{3,7},{4,6},{5,1},{6,4},{7,3},{8,10},{9,13},{10,... | collective-permute-start | bytes 4718600 | tf_op jit(solution)/shard_map/ppermute | solution.py:38
  98.0 32.7 %collective-permute-start.19 = (bf16[8,96,1024]{2,1,0:T(8,128)(2,1)}, bf16[8,96,1024]{2,1,0:T(8,128)(2,1)}, u32[]{:S(2)}, u32[]{:S(2)}) collective-permute-start(bf16[8,96,1024]{2,1,0:T(8,128)(2,1)} %pad_maximum_fusion.p0), channel_id=1, source_target_pairs={{0,1},{1,0},{2,3},{3,2},{4,5},{5,4},{6,7},{7,6},{8,9},{9,8},{10,11... | collective-permute-start | bytes 4718600 | tf_op jit(solution)/shard_map/ppermute | solution.py:38
  130.3 8.3 %collective-permute-start.21 = (bf16[16,96,1024]{2,1,0:T(8,128)(2,1)}, bf16[16,96,1024]{2,1,0:T(8,128)(2,1)S(1)}, u32[]{:S(2)}, u32[]{:S(2)}) collective-permute-start(bf16[16,96,1024]{2,1,0:T(8,128)(2,1)} %get-tuple-element.245), channel_id=1, source_target_pairs={{0,1},{1,0},{2,3},{3,2},{4,5},{5,4},{6,7},{7,6},{8,9},{9,8},{10,11... | collective-permute-start | bytes 9437192 | tf_op jit(solution)/shard_map/ppermute | solution.py:38
  130.7 7.9 %collective-permute-start.20 = (bf16[8,96,1024]{2,1,0:T(8,128)(2,1)}, bf16[8,96,1024]{2,1,0:T(8,128)(2,1)}, u32[]{:S(2)}, u32[]{:S(2)}) collective-permute-start(bf16[8,96,1024]{2,1,0:T(8,128)(2,1)} %collective-permute-done.18.p1), channel_id=1, source_target_pairs={{0,1},{1,0},{2,3},{3,2},{4,5},{5,4},{6,7},{7,6},{8,9},{9,8},{10,11... | collective-permute-start | bytes 4718600 | tf_op jit(solution)/shard_map/ppermute | solution.py:38
  143.6 31.8 %collective-permute-start.22 = (bf16[8,96,1024]{2,1,0:T(8,128)(2,1)}, bf16[8,96,1024]{2,1,0:T(8,128)(2,1)}, u32[]{:S(2)}, u32[]{:S(2)}) collective-permute-start(bf16[8,96,1024]{2,1,0:T(8,128)(2,1)} %get-tuple-element.249), channel_id=1, source_target_pairs={{0,2},{1,5},{2,0},{3,7},{4,6},{5,1},{6,4},{7,3},{8,10},{9,13},{10,... | collective-permute-start | bytes 4718600 | tf_op jit(solution)/shard_map/ppermute | solution.py:38
  175.4 14.4 %collective-permute-start.24 = (bf16[16,128,768]{2,1,0:T(8,128)(2,1)}, bf16[16,128,768]{2,1,0:T(8,128)(2,1)S(1)}, u32[]{:S(2)}, u32[]{:S(2)}) collective-permute-start(bf16[16,128,768]{2,1,0:T(8,128)(2,1)} %get-tuple-element.263), channel_id=1, source_target_pairs={{0,1},{1,0},{2,3},{3,2},{4,5},{5,4},{6,7},{7,6},{8,9},{9,8},{10,11... | collective-permute-start | bytes 9437192 | tf_op jit(solution)/shard_map/ppermute | solution.py:38
  175.5 14.3 %collective-permute-start.25 = (bf16[16,64,768]{2,1,0:T(8,128)(2,1)}, bf16[16,64,768]{2,1,0:T(8,128)(2,1)S(1)}, u32[]{:S(2)}, u32[]{:S(2)}) collective-permute-start(bf16[16,64,768]{2,1,0:T(8,128)(2,1)} %get-tuple-element.264), channel_id=1, source_target_pairs={{0,1},{1,0},{2,3},{3,2},{4,5},{5,4},{6,7},{7,6},{8,9},{9,8},{10,11... | collective-permute-start | bytes 4718600 | tf_op jit(solution)/shard_map/ppermute | solution.py:38
  177.7 12.1 %collective-permute-start.23 = (bf16[4,96,1024]{2,1,0:T(8,128)(2,1)S(1)}, bf16[4,96,1024]{2,1,0:T(8,128)(2,1)S(1)}, u32[]{:S(2)}, u32[]{:S(2)}) collective-permute-start(bf16[4,96,1024]{2,1,0:T(8,128)(2,1)S(1)} %add_convert_fusion.11), channel_id=1, source_target_pairs={{0,4},{1,3},{2,6},{3,1},{4,0},{5,7},{6,2},{7,5},{8,12},{9,11},{10,... | collective-permute-start | bytes 2359304 | tf_op jit(solution)/shard_map/ppermute | solution.py:38
  180.9 9.0 %copy-start.28 = (bf16[16,128,768]{2,1,0:T(8,128)(2,1)S(1)}, bf16[16,128,768]{2,1,0:T(8,128)(2,1)}, u32[]{:S(2)}) copy-start(bf16[16,128,768]{2,1,0:T(8,128)(2,1)} %get-tuple-element.259) | copy-start | bytes 9437188
  189.8 1.2 collective-permute-start.26
  191.0 3.7 %collective-permute-start.27 = (f32[2,2,512]{2,1,0:T(2,128)S(1)}, f32[2,2,512]{2,1,0:T(2,128)S(1)}, u32[]{:S(2)}, u32[]{:S(2)}) collective-permute-start(f32[2,2,512]{2,1,0:T(2,128)S(1)} %pad_maximum_fusion.12), channel_id=1, source_target_pairs={{0,2},{1,3},{2,0},{3,1},{4,6},{5,7},{6,4},{7,5},{8,10},{9,11},{10,... | collective-permute-start | bytes 24584 | tf_op jit(solution)/shard_map/ppermute | solution.py:38
  194.8 22.0 %collective-permute-start.28 = (bf16[8,128,768]{2,1,0:T(8,128)(2,1)S(1)}, bf16[8,128,768]{2,1,0:T(8,128)(2,1)S(1)}, u32[]{:S(2)}, u32[]{:S(2)}) collective-permute-start(bf16[8,128,768]{2,1,0:T(8,128)(2,1)S(1)} %get-tuple-element.272), channel_id=1, source_target_pairs={{0,2},{1,5},{2,0},{3,7},{4,6},{5,1},{6,4},{7,3},{8,10},{9,13},{10,... | collective-permute-start | bytes 4718600 | tf_op jit(solution)/shard_map/ppermute | solution.py:38
  196.8 20.0 %collective-permute-start.29 = (bf16[2,96,1024]{2,1,0:T(8,128)(2,1)S(1)}, bf16[2,96,1024]{2,1,0:T(8,128)(2,1)S(1)}, u32[]{:S(2)}, u32[]{:S(2)}) collective-permute-start(bf16[2,96,1024]{2,1,0:T(8,128)(2,1)S(1)} %slice.247), channel_id=1, source_target_pairs={{0,8},{1,9},{2,10},{3,11},{4,12},{5,13},{6,14},{7,15},{8,0},{9,1},... | collective-permute-start | bytes 1179656 | tf_op jit(solution)/shard_map/ppermute | solution.py:38
  219.8 6.4 %slice-start = ((s8[6291456]{0:T(1024)(128)(4,1)}), s8[4194304]{0:T(1024)(128)(4,1)S(1)}, s32[]{:S(2)}) async-start(s8[6291456]{0:T(1024)(128)(4,1)} %bitcast.77), calls=%async_computation.1 | async-start | bytes 8388608
  221.1 3.6 %collective-permute-start.35 = (bf16[16,8,512]{2,1,0:T(8,128)(2,1)S(1)}, bf16[16,8,512]{2,1,0:T(8,128)(2,1)S(1)}, u32[]{:S(2)}, u32[]{:S(2)}) collective-permute-start(bf16[16,8,512]{2,1,0:T(8,128)(2,1)S(1)} %get-tuple-element.315), channel_id=1, source_target_pairs={{0,1},{1,0},{2,3},{3,2},{4,5},{5,4},{6,7},{7,6},{8,9},{9,8},{10,11... | collective-permute-start | bytes 393224 | tf_op jit(solution)/shard_map/ppermute | solution.py:38
  221.2 17.8 %collective-permute-start.32 = (bf16[96,1024]{1,0:T(8,128)(2,1)S(1)}, bf16[96,1024]{1,0:T(8,128)(2,1)S(1)}, u32[]{:S(2)}, u32[]{:S(2)}) collective-permute-start(bf16[96,1024]{1,0:T(8,128)(2,1)S(1)} %fusion), channel_id=1, source_target_pairs={{0,16},{1,17},{2,18},{3,19},{4,20},{5,21},{6,22},{7,23},{8,24},{9,... | collective-permute-start | bytes 589832 | tf_op jit(solution)/shard_map/ppermute | solution.py:38
  223.6 15.3 %collective-permute-start.34 = (bf16[16,16,512]{2,1,0:T(8,128)(2,1)S(1)}, bf16[16,16,512]{2,1,0:T(8,128)(2,1)S(1)}, u32[]{:S(2)}, u32[]{:S(2)}) collective-permute-start(bf16[16,16,512]{2,1,0:T(8,128)(2,1)S(1)} %get-tuple-element.314), channel_id=1, source_target_pairs={{0,1},{1,0},{2,3},{3,2},{4,5},{5,4},{6,7},{7,6},{8,9},{9,8},{10,11... | collective-permute-start | bytes 786440 | tf_op jit(solution)/shard_map/ppermute | solution.py:38
  223.8 15.1 %collective-permute-start.33 = (bf16[16,32,512]{2,1,0:T(8,128)(2,1)S(1)}, bf16[16,32,512]{2,1,0:T(8,128)(2,1)S(1)}, u32[]{:S(2)}, u32[]{:S(2)}) collective-permute-start(bf16[16,32,512]{2,1,0:T(8,128)(2,1)S(1)} %get-tuple-element.313), channel_id=1, source_target_pairs={{0,1},{1,0},{2,3},{3,2},{4,5},{5,4},{6,7},{7,6},{8,9},{9,8},{10,11... | collective-permute-start | bytes 1572872 | tf_op jit(solution)/shard_map/ppermute | solution.py:38
  224.1 19.9 %collective-permute-start.31 = (bf16[8,64,768]{2,1,0:T(8,128)(2,1)S(1)}, bf16[8,64,768]{2,1,0:T(8,128)(2,1)S(1)}, u32[]{:S(2)}, u32[]{:S(2)}) collective-permute-start(bf16[8,64,768]{2,1,0:T(8,128)(2,1)S(1)} %get-tuple-element.293), channel_id=1, source_target_pairs={{0,2},{1,5},{2,0},{3,7},{4,6},{5,1},{6,4},{7,3},{8,10},{9,13},{10,... | collective-permute-start | bytes 2359304 | tf_op jit(solution)/shard_map/ppermute | solution.py:38
  224.7 19.4 %collective-permute-start.30 = (bf16[4,128,768]{2,1,0:T(8,128)(2,1)S(1)}, bf16[4,128,768]{2,1,0:T(8,128)(2,1)S(1)}, u32[]{:S(2)}, u32[]{:S(2)}) collective-permute-start(bf16[4,128,768]{2,1,0:T(8,128)(2,1)S(1)} %add_convert_fusion.8), channel_id=1, source_target_pairs={{0,4},{1,3},{2,6},{3,1},{4,0},{5,7},{6,2},{7,5},{8,12},{9,11},{10,... | collective-permute-start | bytes 2359304 | tf_op jit(solution)/shard_map/ppermute | solution.py:38
  244.5 11.2 %collective-permute-start.37 = (bf16[4,64,768]{2,1,0:T(8,128)(2,1)S(1)}, bf16[4,64,768]{2,1,0:T(8,128)(2,1)S(1)}, u32[]{:S(2)}, u32[]{:S(2)}) collective-permute-start(bf16[4,64,768]{2,1,0:T(8,128)(2,1)S(1)} %add_convert_fusion.14), channel_id=1, source_target_pairs={{0,4},{1,3},{2,6},{3,1},{4,0},{5,7},{6,2},{7,5},{8,12},{9,11},{10,... | collective-permute-start | bytes 1179656 | tf_op jit(solution)/shard_map/ppermute | solution.py:38
  245.3 10.9 %collective-permute-start.36 = (bf16[2,128,768]{2,1,0:T(8,128)(2,1)S(1)}, bf16[2,128,768]{2,1,0:T(8,128)(2,1)S(1)}, u32[]{:S(2)}, u32[]{:S(2)}) collective-permute-start(bf16[2,128,768]{2,1,0:T(8,128)(2,1)S(1)} %slice.251), channel_id=1, source_target_pairs={{0,8},{1,9},{2,10},{3,11},{4,12},{5,13},{6,14},{7,15},{8,0},{9,1},... | collective-permute-start | bytes 1179656 | tf_op jit(solution)/shard_map/ppermute | solution.py:38
  246.8 9.4 %collective-permute-start.38 = (bf16[8,56,512]{2,1,0:T(8,128)(2,1)S(1)}, bf16[8,56,512]{2,1,0:T(8,128)(2,1)S(1)}, u32[]{:S(2)}, u32[]{:S(2)}) collective-permute-start(bf16[8,56,512]{2,1,0:T(8,128)(2,1)S(1)} %pad_maximum_fusion.3), channel_id=1, source_target_pairs={{0,2},{1,5},{2,0},{3,7},{4,6},{5,1},{6,4},{7,3},{8,10},{9,13},{10,... | collective-permute-start | bytes 1376264 | tf_op jit(solution)/shard_map/ppermute | solution.py:38
  256.5 14.4 %collective-permute-start.41 = (bf16[4,56,512]{2,1,0:T(8,128)(2,1)S(1)}, bf16[4,56,512]{2,1,0:T(8,128)(2,1)S(1)}, u32[]{:S(2)}, u32[]{:S(2)}) collective-permute-start(bf16[4,56,512]{2,1,0:T(8,128)(2,1)S(1)} %add_convert_fusion.19), channel_id=1, source_target_pairs={{0,4},{1,3},{2,6},{3,1},{4,0},{5,7},{6,2},{7,5},{8,12},{9,11},{10,... | collective-permute-start | bytes 688136 | tf_op jit(solution)/shard_map/ppermute | solution.py:38
  257.5 9.6 %collective-permute-start.40 = (bf16[2,64,768]{2,1,0:T(8,128)(2,1)S(1)}, bf16[2,64,768]{2,1,0:T(8,128)(2,1)S(1)}, u32[]{:S(2)}, u32[]{:S(2)}) collective-permute-start(bf16[2,64,768]{2,1,0:T(8,128)(2,1)S(1)} %slice.255), channel_id=1, source_target_pairs={{0,8},{1,9},{2,10},{3,11},{4,12},{5,13},{6,14},{7,15},{8,0},{9,1},... | collective-permute-start | bytes 589832 | tf_op jit(solution)/shard_map/ppermute | solution.py:38
  258.7 12.1 %collective-permute-start.39 = (bf16[128,768]{1,0:T(8,128)(2,1)S(1)}, bf16[128,768]{1,0:T(8,128)(2,1)S(1)}, u32[]{:S(2)}, u32[]{:S(2)}) collective-permute-start(bf16[128,768]{1,0:T(8,128)(2,1)S(1)} %fusion.1), channel_id=1, source_target_pairs={{0,16},{1,17},{2,18},{3,19},{4,20},{5,21},{6,22},{7,23},{8,24},{9,... | collective-permute-start | bytes 589832 | tf_op jit(solution)/shard_map/ppermute | solution.py:38
  271.0 6.5 %collective-permute-start.45 = (bf16[56,512]{1,0:T(8,128)(2,1)S(1)}, bf16[56,512]{1,0:T(8,128)(2,1)S(1)}, u32[]{:S(2)}, u32[]{:S(2)}) collective-permute-start(bf16[56,512]{1,0:T(8,128)(2,1)S(1)} %get-tuple-element.361), channel_id=1, source_target_pairs={{0,24},{1,25},{2,26},{3,27},{4,28},{5,29},{6,30},{7,31},{8,16},{9,... | collective-permute-start | bytes 172040 | tf_op jit(solution)/shard_map/ppermute | solution.py:38
  271.1 6.4 %collective-permute-start.44 = (bf16[56,512]{1,0:T(8,128)(2,1)S(1)}, bf16[56,512]{1,0:T(8,128)(2,1)S(1)}, u32[]{:S(2)}, u32[]{:S(2)}) collective-permute-start(bf16[56,512]{1,0:T(8,128)(2,1)S(1)} %get-tuple-element.362), channel_id=1, source_target_pairs={{0,8},{1,9},{2,10},{3,11},{4,12},{5,13},{6,14},{7,15},{8,0},{9,1},... | collective-permute-start | bytes 172040 | tf_op jit(solution)/shard_map/ppermute | solution.py:38
  271.9 9.3 %collective-permute-start.43 = (bf16[56,512]{1,0:T(8,128)(2,1)S(1)}, bf16[56,512]{1,0:T(8,128)(2,1)S(1)}, u32[]{:S(2)}, u32[]{:S(2)}) collective-permute-start(bf16[56,512]{1,0:T(8,128)(2,1)S(1)} %get-tuple-element.363), channel_id=1, source_target_pairs={{0,16},{1,17},{2,18},{3,19},{4,20},{5,21},{6,22},{7,23},{8,24},{9,... | collective-permute-start | bytes 172040 | tf_op jit(solution)/shard_map/ppermute | solution.py:38
  275.5 7.3 %collective-permute-start.42 = (bf16[64,768]{1,0:T(8,128)(2,1)S(1)}, bf16[64,768]{1,0:T(8,128)(2,1)S(1)}, u32[]{:S(2)}, u32[]{:S(2)}) collective-permute-start(bf16[64,768]{1,0:T(8,128)(2,1)S(1)} %fusion.2), channel_id=1, source_target_pairs={{0,16},{1,17},{2,18},{3,19},{4,20},{5,21},{6,22},{7,23},{8,24},{9,... | collective-permute-start | bytes 294920 | tf_op jit(solution)/shard_map/ppermute | solution.py:38
  (30 other events, 99.2 us)
Sparse Core Ops, SparseCore 0:
  10.9 80.2 all-gather.1

commit v5 on v4

--- a/solution.py
+++ b/solution.py
@@ -275,14 +275,15 @@
     return held
 
 
-def reduce_kernel(me, tokens, gain, shift, bias, inflow, parts):
+def reduce_kernel(me, ends, base, tokens, gain, shift, bias, decay, inflow, parts):
     block, width = tokens.shape
     channels = bias.shape[1]
     tile = 256
     columns = channels // 128
 
-    def body(me, x_ref, gain_ref, shift_ref, bias_ref, inflow_ref, s0, s1, s2, s3,
-             normed_ref, act_ref, slope_ref, state_ref, weight, sems):
+    def body(me, ends_ref, base_ref, x_ref, gain_ref, shift_ref, bias_ref, decay_ref, inflow_ref,
+             s0, s1, s2, s3, normed_ref, act_ref, slope_ref, state_ref, span_ref, map_ref,
+             weight, sems):
         load_weights(me[0], (s0, s1, s2, s3), weight, REDUCE_PIECES, sems)
 
         def norm(t, carry):
@@ -305,6 +306,11 @@
             return carry
 
         lax.fori_loop(0, block // tile, reduce, 0)
+        product, state = scan_block(
+            ends_ref, base_ref[0], decay_ref[...], state_ref, state_ref, False
+        )
+        span_ref[0], span_ref[1] = product, state
+        map_ref[0:1, :], map_ref[1:2, :] = whole_map(product, state, False)
 
     vm = pl.BlockSpec(memory_space=pltpu.VMEM)
     return pl.pallas_call(
@@ -315,42 +321,18 @@
             jax.ShapeDtypeStruct((block, channels), SINGLE),
             jax.ShapeDtypeStruct((block, channels), HALF),
             jax.ShapeDtypeStruct((columns, block, 128), SINGLE),
+            jax.ShapeDtypeStruct((2, SEGMENTS, channels), SINGLE),
+            jax.ShapeDtypeStruct((2, channels), SINGLE),
         ],
-        in_specs=[SMEM] + [vm] * 5 + [FAR] * 4,
-        out_specs=[vm] * 4,
+        in_specs=[SMEM] * 3 + [vm] * 6 + [FAR] * 4,
+        out_specs=[vm] * 6,
         scratch_shapes=[
             pltpu.VMEM((1, width, channels), HALF),
             pltpu.SemaphoreType.DMA((1,)),
         ],
         compiler_params=room(60),
         cost_estimate=cost(8),
-    )(me, tokens, gain, shift, bias, inflow, *parts)
-
-
-def scan_kernel(order, ends, base, flow, decay):
-    channels = decay.shape[1]
-
-    def body(order, ends_ref, base_ref, flow_ref, decay_ref, state_ref, span_ref, map_ref):
-        product, state = scan_block(
-            ends_ref, base_ref[0], decay_ref[...], flow_ref, state_ref, False
-        )
-        span_ref[0], span_ref[1] = product, state
-        map_ref[0:1, :], map_ref[1:2, :] = whole_map(product, state, False)
-
-    vm = pl.BlockSpec(memory_space=pltpu.VMEM)
-    return pl.pallas_call(
-        body,
-        name="state_scan",
-        out_shape=[
-            jax.ShapeDtypeStruct(flow.shape, SINGLE),
-            jax.ShapeDtypeStruct((2, SEGMENTS, channels), SINGLE),
-            jax.ShapeDtypeStruct((2, channels), SINGLE),
-        ],
-        in_specs=[SMEM] * 3 + [vm] * 2,
-        out_specs=[vm] * 3,
-        compiler_params=room(20),
-        cost_estimate=cost(12),
-    )(order, ends, base, flow, decay)
+    )(me, ends, base, tokens, gain, shift, bias, decay, inflow, *parts)
 
 
 def staged(count, product, finish):
@@ -1065,7 +1047,6 @@
     half, single = HALF, SINGLE
     shards = 1 << MAIN
     me = (device_number() >> low_bits()).reshape(1).astype(jnp.int32)
-    value_mat = lax.all_gather(value_weight.astype(half), ("dp", "seq"), axis=0, tiled=True)
     vectors = [
         gather_low(v)
         for v in (
@@ -1087,6 +1068,8 @@
         gather_low(expand_weight),
         gather_low(out_weight),
     )
+    value_part, small = tie((value_weight, small))
+    value_mat = lax.all_gather(value_part.astype(half), ("dp", "seq"), axis=0, tiled=True)
     channels = state_weight.shape[1]
     width = tokens.shape[-1]
     blocks = value_weight.shape[1] // width
@@ -1130,13 +1113,13 @@
     vectors = unpack_kernel(me, sizes, small_parts)
     gain, shift, value_add, reduce_add, _, skip, expand_add, out_add = vectors[:8]
     decays, inflow, inflow_pull = vectors[8:]
-    normed, act, reduce_slope, flow = reduce_kernel(
-        me, token_rows, gain, shift, reduce_add, inflow, small_parts
-    )
-    flow, expand_run.pending, me = tie((flow, expand_run.pending, me))
+    normed, act, reduce_slope, states, spans, own_map = reduce_kernel(
+        me, ends, base, token_rows, gain, shift, reduce_add, decays, inflow, small_parts
+    )
+    own_map, expand_run.pending, out_run.pending, me = tie(
+        (own_map, expand_run.pending, out_run.pending, me)
+    )
     me = expand_run.step(me)
-    states, spans, own_map = scan_kernel(me, ends, base, flow, decays)
-    own_map, out_run.pending, me = tie((own_map, out_run.pending, me))
     maps = gather_maps(own_map)
     maps, me = out_run.step((maps, me))
     states_low, prior, ssm_low = states_kernel(
@@ -1201,13 +1184,17 @@
     small_halves = (reduce_halves, state_halves, table_halves)
     reduce_halves, state_halves, table_halves, me = tie((*small_halves, me))
     small_halves = (reduce_halves, state_halves, table_halves)
-    small_others = [core_exchange(h[0]) for h in small_halves]
+    small_other = core_exchange(jnp.concatenate([h[0] for h in small_halves], axis=1))
     output = out_kernel(me, live, base, gated, token_rows, out_add, out_parts)
-    value_run.pending, expand_run.pending, out_run.pending, small_others, output = tie(
-        (value_run.pending, expand_run.pending, out_run.pending, small_others, output)
-    )
-
-    small_run = Run(reduce_steps([(h[1], other) for h, other in zip(small_halves, small_others)], True))
+    value_run.pending, expand_run.pending, out_run.pending, small_other, output = tie(
+        (value_run.pending, expand_run.pending, out_run.pending, small_other, output)
+    )
+
+    small_pairs, at = [], 0
+    for _, keep in small_halves:
+        small_pairs.append((keep, small_other[:, at : at + keep.shape[1]]))
+        at += keep.shape[1]
+    small_run = Run(reduce_steps(small_pairs, True))
     small_run.step()
     value_run.step()
     expand_run.step()

time: 291 us -> 287 us (0.986)
  waiting for transfers between devices: 81.8 us -> 73.9 us
    ppermute x46 -> x44, waiting for transfers between devices: 81.8 us -> 73.9 us  [exchange(): return lax.ppermute(values, axes, [(i, other(i)) for i in range(count)])]
    pallas_call x1, Pallas kernels: 8.44 us -> 11.5 us  [reduce_kernel(): pl.pallas_call(body, name='reduce_forward', out_shape=[jax.ShapeDtypeStru...]
    ppermute x46 -> x44, starting transfers between devices: 42.9 us -> 45.1 us  [exchange(): return lax.ppermute(values, axes, [(i, other(i)) for i in range(count)])]
    unnamed x98 -> x104, local copies, waits for them, and re-layouts: 7.2 us -> 9.19 us
  transfers between devices with their start and end apart: 47 -> 45, of which waited for: 21 -> 18; matrix products, arithmetic and copies ran while one was open for 5% -> 6% of each run, Pallas kernels for 40% -> 40%
where the time goes in v5:
time: 287 us
  Pallas kernels  121 us (42%)
  waiting for transfers between devices  73.9 us (26%)
  starting transfers between devices  45.2 us (16%)
  other arithmetic  21.9 us (8%)
  between operations  15 us (5%)
  local copies, waits for them, and re-layouts  10.1 us (4%)
    ppermute x44, waiting for transfers between devices, exchange(): return lax.ppermute(values, axes, [(i, other(i)) for i in range(count)])  73.9 us
    ppermute x44, starting transfers between devices, exchange(): return lax.ppermute(values, axes, [(i, other(i)) for i in range(count)])  45.1 us
    pallas_call x1, Pallas kernels, forward_kernel(): pl.pallas_call(body, name='gate_forward', out_shape=[jax.ShapeDtypeStruct...  31.2 us
    pallas_call x1, Pallas kernels, gate_kernel(): pl.pallas_call(body, name='gate_backward', out_shape=[jax.ShapeDtypeStruc...  31 us
    pallas_call x1, Pallas kernels, input_kernel(): pl.pallas_call(body, name='input_backward', out_shape=[jax.ShapeDtypeStru...  18.4 us
    pallas_call x1, Pallas kernels, out_kernel(): pl.pallas_call(body, name='out_forward', out_shape=jax.ShapeDtypeStruct((...  12.7 us
    pallas_call x1, Pallas kernels, reduce_kernel(): pl.pallas_call(body, name='reduce_forward', out_shape=[jax.ShapeDtypeStru...  11.5 us
    convert_element_type x17, other arithmetic, add_low(): return (first.astype(SINGLE) + second.astype(SINGLE)).astype(HALF)  11.1 us
  transfers between devices with their start and end apart: 45, of which 18 were waited for; matrix products, arithmetic and copies ran while one was open for 6% of the time, Pallas kernels for 40%

profile of v5, /device:TPU:0, one launch (start us, length us, event | category | flops | bytes accessed | tf_op | source)
XLA Modules:
  0.0 286.8 jit_solution(4210754181877345975)
XLA Ops:
  7.3 2.1 pack.1
  10.1 5.1 %collective-permute-start.2 = (bf16[1,56,512]{2,1,0:T(8,128)(2,1)}, bf16[1,56,512]{2,1,0:T(8,128)(2,1)S(1)}, u32[]{:S(2)}, u32[]{:S(2)}) collective-permute-start(bf16[1,56,512]{2,1,0:T(8,128)(2,1)} %bitcast.84), channel_id=1, source_target_pairs={{0,24},{1,25},{2,26},{3,27},{4,28},{5,29},{6,30},{7,31},{8,16},{9,... | collective-permute-start | bytes 172040 | tf_op jit(solution)/shard_map/ppermute | solution.py:38
  18.6 1.5 broadcast_select_fusion.grad_ref
  20.9 1.6 collective-permute-start.3
  22.5 1.7 collective-permute-start.4
  24.2 6.3 %collective-permute-done.4 = bf16[1,64,768]{2,1,0:T(8,128)(2,1)S(1)} collective-permute-done((bf16[1,64,768]{2,1,0:T(8,128)(2,1)S(1)}, bf16[1,64,768]{2,1,0:T(8,128)(2,1)S(1)}, u32[]{:S(2)}, u32[]{:S(2)}) %collective-permute-start.4) | collective-permute-done | bytes 98336 | tf_op jit(solution)/shard_map/ppermute | solution.py:38
  30.6 0.8 collective-permute-start.6
  31.4 1.0 collective-permute-start.7
  32.5 3.4 %collective-permute-start.8 = (bf16[1,96,1024]{2,1,0:T(8,128)(2,1)S(1)}, bf16[1,96,1024]{2,1,0:T(8,128)(2,1)S(1)}, u32[]{:S(2)}, u32[]{:S(2)}) collective-permute-start(bf16[1,96,1024]{2,1,0:T(8,128)(2,1)S(1)} %bitcast.77), channel_id=1, source_target_pairs={{0,16},{1,17},{2,18},{3,19},{4,20},{5,21},{6,22},{7,23},{8,24},{9,... | collective-permute-start | bytes 589832 | tf_op jit(solution)/shard_map/ppermute | solution.py:38
  35.9 6.5 %collective-permute-done.7 = bf16[2,64,768]{2,1,0:T(8,128)(2,1)S(1)} collective-permute-done((bf16[2,64,768]{2,1,0:T(8,128)(2,1)S(1)}, bf16[2,64,768]{2,1,0:T(8,128)(2,1)S(1)}, u32[]{:S(2)}, u32[]{:S(2)}) %collective-permute-start.7) | collective-permute-done | bytes 196640 | tf_op jit(solution)/shard_map/ppermute | solution.py:38
  42.4 3.5 %collective-permute-done.8 = bf16[1,96,1024]{2,1,0:T(8,128)(2,1)S(1)} collective-permute-done((bf16[1,96,1024]{2,1,0:T(8,128)(2,1)S(1)}, bf16[1,96,1024]{2,1,0:T(8,128)(2,1)S(1)}, u32[]{:S(2)}, u32[]{:S(2)}) %collective-permute-start.8) | collective-permute-done | bytes 196640 | tf_op jit(solution)/shard_map/ppermute | solution.py:38
  46.6 1.9 collective-permute-done.9.refs_3_.s3
  48.5 1.8 pad_maximum_fusion.7
  50.3 1.8 pad_maximum_fusion.6
  52.1 2.3 collective-permute-start.11
  54.4 1.9 unpack.1
  56.3 11.5 %reduce_forward.1 = (bf16[1024,1024]{1,0:T(8,128)(2,1)}, f32[1024,512]{1,0:T(8,128)}, bf16[1024,512]{1,0:T(8,128)(2,1)}, f32[4,1024,128]{2,1,0:T(8,128)}, f32[2,8,512]{2,1,0:T(8,128)}, /*index=5*/f32[2,512]{1,0:T(2,128)}) custom-call(s32[1]{0:T(128)} %bitcast.17.me.me_ref, s32[8]{0:T(128)} %bitcast.70, s32[1]{0:T(128)} %mul.6.base_ref, ...), custom_call_target="tpu_custom_call" | custom-call | flops 8000000000 | bytes 1048576 | tf_op jit(solution)/shard_map/reduce_forward/pallas_call | solution.py:316
  68.1 1.4 pad_maximum_fusion.2.q0
  69.5 1.4 collective-permute-start.15
  71.7 1.6 collective-permute-done.15
  73.4 2.1 collective-permute-start.16
  75.5 1.6 copy-done.10
  77.1 1.6 copy-done.12
  78.7 3.5 %states_forward.1 = (bf16[1024,512]{1,0:T(8,128)(2,1)S(1)}, bf16[1024,512]{1,0:T(8,128)(2,1)S(1)}, bf16[1024,512]{1,0:T(8,128)(2,1)S(1)}) custom-call(s32[1]{0:T(128)} %bitcast.17.me.me_ref, s32[1]{0:T(128)} %bitcast.9.place_ref, s32[8]{0:T(128)S(1)} %bitcast.71, s32[1]{0:T(128)} %mul.6.base_ref, f32[4,2,512]{2,1,0:T(2,128)S(1)} %pad_maximum_fusion.10.maps_ref, ...), custom_call_target="tpu_custom_call" | custom-call | flops 4000000000 | bytes 1048576 | tf_op jit(solution)/shard_map/states_forward/pallas_call | solution.py:380
  82.2 0.9 copy-done.17
  83.2 10.2 %collective-permute-done.13.q1 = bf16[8,64,768]{2,1,0:T(8,128)(2,1)S(1)} collective-permute-done((bf16[8,64,768]{2,1,0:T(8,128)(2,1)S(1)}, bf16[8,64,768]{2,1,0:T(8,128)(2,1)S(1)}, u32[]{:S(2)}, u32[]{:S(2)}) %collective-permute-start.13) | collective-permute-done | bytes 786464 | tf_op jit(solution)/shard_map/ppermute | solution.py:38
  93.6 1.3 pad_maximum_fusion.p0
  94.9 1.4 collective-permute-start.18
  96.3 0.9 copy-done.46
  97.2 31.2 %gate_forward.1 = (bf16[1024,3072]{1,0:T(8,128)(2,1)}, bf16[1024,3072]{1,0:T(8,128)(2,1)}, bf16[1024,3072]{1,0:T(8,128)(2,1)}, bf16[16,96,1024]{2,1,0:T(8,128)(2,1)}, bf16[16,96,1024]{2,1,0:T(8,128)(2,1)}) custom-call(s32[1]{0:T(128)} %bitcast.17.me.me_ref, bf16[1024,1024]{1,0:T(8,128)(2,1)} %get-tuple-element.228.x_ref.left_ref, ...), custom_call_target="tpu_custom_call" | custom-call | flops 16000000000 | bytes 1048576 | tf_op jit(solution)/shard_map/gate_forward/pallas_call | solution.py:440
  129.1 7.6 %collective-permute-done.20.p3 = bf16[8,96,1024]{2,1,0:T(8,128)(2,1)} collective-permute-done((bf16[8,96,1024]{2,1,0:T(8,128)(2,1)}, bf16[8,96,1024]{2,1,0:T(8,128)(2,1)}, u32[]{:S(2)}, u32[]{:S(2)}) %collective-permute-start.20) | collective-permute-done | bytes 1572896 | tf_op jit(solution)/shard_map/ppermute | solution.py:38
  136.8 5.0 %add_convert_fusion.3 = (bf16[8,96,1024]{2,1,0:T(8,128)(2,1)}, bf16[8,96,1024]{2,1,0:T(8,128)(2,1)}) fusion(bf16[16,96,1024]{2,1,0:T(8,128)(2,1)S(1)} %collective-permute-done.21, bf16[16,96,1024]{2,1,0:T(8,128)(2,1)} %get-tuple-element.236), kind=kLoop, calls=%fused_computation.4 | loop fusion | flops 6291456 | bytes 9437184 | tf_op jit(solution)/shard_map/convert_element_type | solution.py:975
  141.8 0.8 collective-permute-start.22
  142.6 31.0 %gate_backward.1 = (bf16[1024,3072]{1,0:T(8,128)(2,1)}, f32[8,3072]{1,0:T(8,128)}, f32[8,3072]{1,0:T(8,128)}, f32[1024,512]{1,0:T(8,128)}, bf16[16,128,768]{2,1,...) custom-call(s32[1]{0:T(128)} %bitcast.17.me.me_ref, ...), custom_call_target="tpu_custom_call" | custom-call | flops 20000000000 | bytes 1048576 | tf_op jit(solution)/shard_map/gate_backward/pallas_call | solution.py:580
  174.2 1.7 add_convert_fusion.11
  175.9 1.5 collective-permute-start.23
  177.4 1.6 copy-done.18
  179.0 4.9 %state_backward.1 = (bf16[1024,512]{1,0:T(8,128)(2,1)S(1)}, f32[4,1024,128]{2,1,0:T(8,128)S(1)}, f32[2,8,512]{2,1,0:T(8,128)S(1)}, f32[2,512]{1,0:T(2,128)S(1)}, f32[8,512]{1,0:T(8,128)S(1)}) custom-call(s32[1]{0:T(128)} %bitcast.17.me.me_ref, s32[8]{0:T(128)S(1)} %bitcast.72, s32[1]{0:T(128)} %mul.6.base_ref, f32[1024,512]{1,0:T(8,128)S(1)} %copy-done.18, ...), custom_call_target="tpu_custom_call" | custom-call | flops 6000000000 | bytes 1048576 | tf_op jit(solution)/shard_map/state_backward/pallas_call | solution.py:637
  183.9 4.1 %collective-permute-done.23 = bf16[4,96,1024]{2,1,0:T(8,128)(2,1)S(1)} collective-permute-done((bf16[4,96,1024]{2,1,0:T(8,128)(2,1)S(1)}, bf16[4,96,1024]{2,1,0:T(8,128)(2,1)S(1)}, u32[]{:S(2)}, u32[]{:S(2)}) %collective-permute-start.23) | collective-permute-done | bytes 786464 | tf_op jit(solution)/shard_map/ppermute | solution.py:38
  188.1 1.0 add_convert_fusion
  189.4 1.7 add_convert_fusion.9
  191.1 1.3 collective-permute-start.27
  192.9 2.0 collective-permute-done.27
  194.9 1.3 collective-permute-start.28
  196.2 1.5 collective-permute-start.29
  197.8 18.4 %input_backward.1 = (bf16[1024,512]{1,0:T(8,128)(2,1)S(1)}, bf16[1024,1024]{1,0:T(8,128)(2,1)}, f32[3,8,512]{2,1,0:T(8,128)S(1)}, f32[2,8,1024]{2,1,0:T(8,128)S(1)}) custom-call(s32[1]{0:T(128)} %bitcast.17.me.me_ref, s32[1]{0:T(128)} %bitcast.9.place_ref, s32[8]{0:T(128)S(1)} %bitcast.73, s32[1]{0:T(128)} %mul.6.base_ref, ...), custom_call_target="tpu_custom_call" | custom-call | flops 16000000000 | bytes 1048576 | tf_op jit(solution)/shard_map/input_backward/pallas_call | solution.py:732
  216.5 1.3 copy-done.19
  217.8 1.4 grad_reduce.1
  220.5 2.5 collective-permute-start.32
  223.7 1.5 collective-permute-start.30
  225.4 12.7 %out_forward.1 = bf16[1024,1024]{1,0:T(8,128)(2,1)} custom-call(s32[1]{0:T(128)} %bitcast.17.me.me_ref, s32[1]{0:T(128)} %bitcast.22.live_ref, s32[1]{0:T(128)} %mul.6.base_ref, bf16[1024,3072]{1,0:T(8,128)(2,1)S(1)} %bitcast.75, bf16[1024,1024]{1,0:T(8,128)(2,1)S(1)} %bitcast.69, f32[1,1024]{1,0:T(1,128)S(1)} %copy-done.21, ...), custom_call_target="tpu_custom_call" | custom-call | flops 12000000000 | bytes 1048576 | tf_op jit(solution)/shard_map/out_forward/pallas_call | solution.py:498
  238.2 3.0 %collective-permute-done.31 = bf16[8,64,768]{2,1,0:T(8,128)(2,1)S(1)} collective-permute-done((bf16[8,64,768]{2,1,0:T(8,128)(2,1)S(1)}, bf16[8,64,768]{2,1,0:T(8,128)(2,1)S(1)}, u32[]{:S(2)}, u32[]{:S(2)}) %collective-permute-start.31) | collective-permute-done | bytes 786464 | tf_op jit(solution)/shard_map/ppermute | solution.py:38
  241.8 1.6 collective-permute-start.35
  244.7 8.6 %collective-permute-done.35 = bf16[4,64,768]{2,1,0:T(8,128)(2,1)S(1)} collective-permute-done((bf16[4,64,768]{2,1,0:T(8,128)(2,1)S(1)}, bf16[4,64,768]{2,1,0:T(8,128)(2,1)S(1)}, u32[]{:S(2)}, u32[]{:S(2)}) %collective-permute-start.35) | collective-permute-done | bytes 393248 | tf_op jit(solution)/shard_map/ppermute | solution.py:38
  253.5 0.9 collective-permute-start.39
  254.4 1.6 collective-permute-start.38
  256.5 6.0 %collective-permute-done.38 = bf16[2,64,768]{2,1,0:T(8,128)(2,1)S(1)} collective-permute-done((bf16[2,64,768]{2,1,0:T(8,128)(2,1)S(1)}, bf16[2,64,768]{2,1,0:T(8,128)(2,1)S(1)}, u32[]{:S(2)}, u32[]{:S(2)}) %collective-permute-start.38) | collective-permute-done | bytes 196640 | tf_op jit(solution)/shard_map/ppermute | solution.py:38
  262.5 4.7 %collective-permute-done.37.refs_2_ = bf16[128,768]{1,0:T(8,128)(2,1)S(1)} collective-permute-done((bf16[128,768]{1,0:T(8,128)(2,1)S(1)}, bf16[128,768]{1,0:T(8,128)(2,1)S(1)}, u32[]{:S(2)}, u32[]{:S(2)}) %collective-permute-start.37) | collective-permute-done | bytes 196640 | tf_op jit(solution)/shard_map/ppermute | solution.py:38
  267.5 0.8 collective-permute-start.42
  268.3 3.5 %collective-permute-start.41 = (bf16[56,512]{1,0:T(8,128)(2,1)S(1)}, bf16[56,512]{1,0:T(8,128)(2,1)S(1)}, u32[]{:S(2)}, u32[]{:S(2)}) collective-permute-start(bf16[56,512]{1,0:T(8,128)(2,1)S(1)} %get-tuple-element.357), channel_id=1, source_target_pairs={{0,16},{1,17},{2,18},{3,19},{4,20},{5,21},{6,22},{7,23},{8,24},{9,... | collective-permute-start | bytes 172040 | tf_op jit(solution)/shard_map/ppermute | solution.py:38
  271.9 1.7 collective-permute-done.43.refs_12_
  273.6 3.7 %collective-permute-done.41.refs_10_ = bf16[56,512]{1,0:T(8,128)(2,1)S(1)} collective-permute-done((bf16[56,512]{1,0:T(8,128)(2,1)S(1)}, bf16[56,512]{1,0:T(8,128)(2,1)S(1)}, u32[]{:S(2)}, u32[]{:S(2)}) %collective-permute-start.41) | collective-permute-done | bytes 57376 | tf_op jit(solution)/shard_map/ppermute | solution.py:38
  277.4 1.5 collective-permute-done.40.refs_5_
  278.9 1.1 finish.1
  (195 shorter events, 14.4 us)
Async XLA Ops:
  7.2 90.1 %all-gather.2.cloned.1.call-start = ((), (), s32[]{:S(2)}) async-start(), calls=%async_computation | async-start | bytes 6488064 | tf_op jit(solution)/shard_map/all_gather | solution.py:1072
  7.2 8.6 %copy-start.47 = (s32[1,8]{1,0:T(1,128)S(1)}, s32[1,8]{1,0:T(1,128)}, u32[]{:S(2)}) copy-start(s32[1,8]{1,0:T(1,128)} %param.17) | copy-start | bytes 100
  7.2 10.8 %copy-start = (bf16[1,1024,1024]{2,1,0:T(8,128)(2,1)S(1)}, bf16[1,1024,1024]{2,1,0:T(8,128)(2,1)}, u32[]{:S(2)}) copy-start(bf16[1,1024,1024]{2,1,0:T(8,128)(2,1)} %param.18) | copy-start | bytes 6291460
  10.1 10.1 %collective-permute-start.2 = (bf16[1,56,512]{2,1,0:T(8,128)(2,1)}, bf16[1,56,512]{2,1,0:T(8,128)(2,1)S(1)}, u32[]{:S(2)}, u32[]{:S(2)}) collective-permute-start(bf16[1,56,512]{2,1,0:T(8,128)(2,1)} %bitcast.84), channel_id=1, source_target_pairs={{0,24},{1,25},{2,26},{3,27},{4,28},{5,29},{6,30},{7,31},{8,16},{9,... | collective-permute-start | bytes 172040 | tf_op jit(solution)/shard_map/ppermute | solution.py:38
  15.2 4.9 %collective-permute-start.1 = (bf16[1,56,512]{2,1,0:T(8,128)(2,1)}, bf16[1,56,512]{2,1,0:T(8,128)(2,1)S(1)}, u32[]{:S(2)}, u32[]{:S(2)}) collective-permute-start(bf16[1,56,512]{2,1,0:T(8,128)(2,1)} %bitcast.85), channel_id=1, source_target_pairs={{0,8},{1,9},{2,10},{3,11},{4,12},{5,13},{6,14},{7,15},{8,0},{9,1},... | collective-permute-start | bytes 172040 | tf_op jit(solution)/shard_map/ppermute | solution.py:38
  15.2 5.7 %collective-permute-start = (bf16[1,56,512]{2,1,0:T(8,128)(2,1)}, bf16[1,56,512]{2,1,0:T(8,128)(2,1)S(1)}, u32[]{:S(2)}, u32[]{:S(2)}) collective-permute-start(bf16[1,56,512]{2,1,0:T(8,128)(2,1)} %bitcast.86), channel_id=1, source_target_pairs={{0,16},{1,17},{2,18},{3,19},{4,20},{5,21},{6,22},{7,23},{8,24},{9,... | collective-permute-start | bytes 172040 | tf_op jit(solution)/shard_map/ppermute | solution.py:38
  20.1 12.3 %copy-start.32 = (bf16[96,1024]{1,0:T(8,128)(2,1)S(1)}, bf16[96,1024]{1,0:T(8,128)(2,1)}, u32[]{:S(2)}) copy-start(bf16[96,1024]{1,0:T(8,128)(2,1)} %get-tuple-element.190) | copy-start | bytes 589828
  20.9 9.6 %collective-permute-start.3 = (bf16[4,56,512]{2,1,0:T(8,128)(2,1)S(1)}, bf16[4,56,512]{2,1,0:T(8,128)(2,1)S(1)}, u32[]{:S(2)}, u32[]{:S(2)}) collective-permute-start(bf16[4,56,512]{2,1,0:T(8,128)(2,1)S(1)} %pad_maximum_fusion.8), channel_id=1, source_target_pairs={{0,4},{1,3},{2,6},{3,1},{4,0},{5,7},{6,2},{7,5},{8,12},{9,11},{10,... | collective-permute-start | bytes 688136 | tf_op jit(solution)/shard_map/ppermute | solution.py:38
  22.5 8.0 %collective-permute-start.4 = (bf16[1,64,768]{2,1,0:T(8,128)(2,1)S(1)}, bf16[1,64,768]{2,1,0:T(8,128)(2,1)S(1)}, u32[]{:S(2)}, u32[]{:S(2)}) collective-permute-start(bf16[1,64,768]{2,1,0:T(8,128)(2,1)S(1)} %bitcast.81), channel_id=1, source_target_pairs={{0,16},{1,17},{2,18},{3,19},{4,20},{5,21},{6,22},{7,23},{8,24},{9,... | collective-permute-start | bytes 294920 | tf_op jit(solution)/shard_map/ppermute | solution.py:38
  30.5 15.4 %copy-start.39 = (bf16[1,64,768]{2,1,0:T(8,128)(2,1)}, bf16[1,64,768]{2,1,0:T(8,128)(2,1)S(1)}, u32[]{:S(2)}) copy-start(bf16[1,64,768]{2,1,0:T(8,128)(2,1)S(1)} %collective-permute-done.4) | copy-start | bytes 294916
  30.6 23.9 %copy-start.1 = (bf16[8,56,512]{2,1,0:T(8,128)(2,1)}, bf16[8,56,512]{2,1,0:T(8,128)(2,1)S(1)}, u32[]{:S(2)}) copy-start(bf16[8,56,512]{2,1,0:T(8,128)(2,1)S(1)} %constant_dynamic-update-slice_fusion.refs_0_.s0) | copy-start | bytes 1376260
  30.6 15.3 %collective-permute-start.6 = (bf16[8,56,512]{2,1,0:T(8,128)(2,1)S(1)}, bf16[8,56,512]{2,1,0:T(8,128)(2,1)S(1)}, u32[]{:S(2)}, u32[]{:S(2)}) collective-permute-start(bf16[8,56,512]{2,1,0:T(8,128)(2,1)S(1)} %constant_dynamic-update-slice_fusion.refs_0_.s0), channel_id=1, source_target_pairs={{0,2},{1,5},{2,0},{3,7},{4,6},{5,1},{6,4},{7,3},{8,10},{9,13},{10,... | collective-permute-start | bytes 1376264 | tf_op jit(solution)/shard_map/ppermute | solution.py:38
  31.4 11.0 %collective-permute-start.7 = (bf16[2,64,768]{2,1,0:T(8,128)(2,1)S(1)}, bf16[2,64,768]{2,1,0:T(8,128)(2,1)S(1)}, u32[]{:S(2)}, u32[]{:S(2)}) collective-permute-start(bf16[2,64,768]{2,1,0:T(8,128)(2,1)S(1)} %pad_maximum_fusion.9), channel_id=1, source_target_pairs={{0,8},{1,9},{2,10},{3,11},{4,12},{5,13},{6,14},{7,15},{8,0},{9,1},... | collective-permute-start | bytes 589832 | tf_op jit(solution)/shard_map/ppermute | solution.py:38
  32.5 13.4 %collective-permute-start.8 = (bf16[1,96,1024]{2,1,0:T(8,128)(2,1)S(1)}, bf16[1,96,1024]{2,1,0:T(8,128)(2,1)S(1)}, u32[]{:S(2)}, u32[]{:S(2)}) collective-permute-start(bf16[1,96,1024]{2,1,0:T(8,128)(2,1)S(1)} %bitcast.77), channel_id=1, source_target_pairs={{0,16},{1,17},{2,18},{3,19},{4,20},{5,21},{6,22},{7,23},{8,24},{9,... | collective-permute-start | bytes 589832 | tf_op jit(solution)/shard_map/ppermute | solution.py:38
  35.9 10.7 %collective-permute-start.5 = (bf16[8,56,512]{2,1,0:T(8,128)(2,1)S(1)}, bf16[8,56,512]{2,1,0:T(8,128)(2,1)S(1)}, u32[]{:S(2)}, u32[]{:S(2)}) collective-permute-start(bf16[8,56,512]{2,1,0:T(8,128)(2,1)S(1)} %constant_dynamic-update-slice_fusion.refs_0_.s0), channel_id=1, source_target_pairs={{0,1},{1,0},{2,3},{3,2},{4,5},{5,4},{6,7},{7,6},{8,9},{9,8},{10,11... | collective-permute-start | bytes 1376264 | tf_op jit(solution)/shard_map/ppermute | solution.py:38
  46.6 7.9 %copy-start.4 = (bf16[8,56,512]{2,1,0:T(8,128)(2,1)}, bf16[8,56,512]{2,1,0:T(8,128)(2,1)S(1)}, u32[]{:S(2)}) copy-start(bf16[8,56,512]{2,1,0:T(8,128)(2,1)S(1)} %collective-permute-done.6.refs_1_.s1) | copy-start | bytes 1376260
  46.6 1.9 collective-permute-start.9
  46.6 7.8 %copy-start.6 = (bf16[8,56,512]{2,1,0:T(8,128)(2,1)}, bf16[8,56,512]{2,1,0:T(8,128)(2,1)S(1)}, u32[]{:S(2)}) copy-start(bf16[8,56,512]{2,1,0:T(8,128)(2,1)S(1)} %collective-permute-done.5.refs_2_.s2) | copy-start | bytes 1376260
  52.1 15.7 %collective-permute-start.11 = (bf16[2,96,1024]{2,1,0:T(8,128)(2,1)}, bf16[2,96,1024]{2,1,0:T(8,128)(2,1)S(1)}, u32[]{:S(2)}, u32[]{:S(2)}) collective-permute-start(bf16[2,96,1024]{2,1,0:T(8,128)(2,1)} %pad_maximum_fusion.6), channel_id=1, source_target_pairs={{0,8},{1,9},{2,10},{3,11},{4,12},{5,13},{6,14},{7,15},{8,0},{9,1},... | collective-permute-start | bytes 1179656 | tf_op jit(solution)/shard_map/ppermute | solution.py:38
  54.4 13.5 %collective-permute-start.10 = (bf16[4,64,768]{2,1,0:T(8,128)(2,1)}, bf16[4,64,768]{2,1,0:T(8,128)(2,1)}, u32[]{:S(2)}, u32[]{:S(2)}) collective-permute-start(bf16[4,64,768]{2,1,0:T(8,128)(2,1)} %pad_maximum_fusion.7), channel_id=1, source_target_pairs={{0,4},{1,3},{2,6},{3,1},{4,0},{5,7},{6,2},{7,5},{8,12},{9,11},{10,... | collective-permute-start | bytes 1179656 | tf_op jit(solution)/shard_map/ppermute | solution.py:38
  56.3 11.8 %copy-start.38 = (bf16[64,768]{1,0:T(8,128)(2,1)S(1)}, bf16[64,768]{1,0:T(8,128)(2,1)}, u32[]{:S(2)}) copy-start(bf16[64,768]{1,0:T(8,128)(2,1)} %get-tuple-element.183) | copy-start | bytes 294916
  67.9 7.5 %copy-start.2 = (bf16[8,56,512]{2,1,0:T(8,128)(2,1)S(1)}, bf16[8,56,512]{2,1,0:T(8,128)(2,1)}, u32[]{:S(2)}) copy-start(bf16[8,56,512]{2,1,0:T(8,128)(2,1)} %copy-done.1) | copy-start | bytes 1376260
  67.9 7.5 %copy-start.5 = (bf16[8,56,512]{2,1,0:T(8,128)(2,1)S(1)}, bf16[8,56,512]{2,1,0:T(8,128)(2,1)}, u32[]{:S(2)}) copy-start(bf16[8,56,512]{2,1,0:T(8,128)(2,1)} %copy-done.4) | copy-start | bytes 1376260
  67.9 7.5 %copy-start.7 = (bf16[8,56,512]{2,1,0:T(8,128)(2,1)S(1)}, bf16[8,56,512]{2,1,0:T(8,128)(2,1)}, u32[]{:S(2)}) copy-start(bf16[8,56,512]{2,1,0:T(8,128)(2,1)} %copy-done.6) | copy-start | bytes 1376260
  67.9 7.5 %copy-start.9 = (s32[1,8]{1,0:T(1,128)S(1)}, s32[1,8]{1,0:T(1,128)}, u32[]{:S(2)}) copy-start(s32[1,8]{1,0:T(1,128)} %copy-done.8) | copy-start | bytes 100
  67.9 7.5 %copy-start.24 = (f32[1,512]{1,0:T(1,128)S(1)}, f32[1,512]{1,0:T(1,128)}, u32[]{:S(2)}) copy-start(f32[1,512]{1,0:T(1,128)} %get-tuple-element.221.skip_ref) | copy-start | bytes 6148
  67.9 7.5 %copy-start.25 = (f32[1,512]{1,0:T(1,128)S(1)}, f32[1,512]{1,0:T(1,128)}, u32[]{:S(2)}) copy-start(f32[1,512]{1,0:T(1,128)} %get-tuple-element.204.decay_ref) | copy-start | bytes 6148
  68.0 7.5 %copy-start.26 = (f32[1,512]{1,0:T(1,128)S(1)}, f32[1,512]{1,0:T(1,128)}, u32[]{:S(2)}) copy-start(f32[1,512]{1,0:T(1,128)} %get-tuple-element.205.inflow_ref) | copy-start | bytes 6148
  68.0 1.5 collective-permute-start.14
  69.4 12.8 %copy-start.40 = (bf16[8,64,768]{2,1,0:T(8,128)(2,1)}, bf16[8,64,768]{2,1,0:T(8,128)(2,1)S(1)}, u32[]{:S(2)}) copy-start(bf16[8,64,768]{2,1,0:T(8,128)(2,1)S(1)} %pad_maximum_fusion.2.q0) | copy-start | bytes 2359300
  69.5 3.9 %collective-permute-start.15 = (f32[2,2,512]{2,1,0:T(2,128)S(1)}, f32[2,2,512]{2,1,0:T(2,128)S(1)}, u32[]{:S(2)}, u32[]{:S(2)}) collective-permute-start(f32[2,2,512]{2,1,0:T(2,128)S(1)} %pad_maximum_fusion.12), channel_id=1, source_target_pairs={{0,2},{1,3},{2,0},{3,1},{4,6},{5,7},{6,4},{7,5},{8,10},{9,11},{10,... | collective-permute-start | bytes 24584 | tf_op jit(solution)/shard_map/ppermute | solution.py:38
  71.0 22.3 %collective-permute-start.13 = (bf16[8,64,768]{2,1,0:T(8,128)(2,1)S(1)}, bf16[8,64,768]{2,1,0:T(8,128)(2,1)S(1)}, u32[]{:S(2)}, u32[]{:S(2)}) collective-permute-start(bf16[8,64,768]{2,1,0:T(8,128)(2,1)S(1)} %pad_maximum_fusion.2.q0), channel_id=1, source_target_pairs={{0,2},{1,5},{2,0},{3,7},{4,6},{5,1},{6,4},{7,3},{8,10},{9,13},{10,... | collective-permute-start | bytes 2359304 | tf_op jit(solution)/shard_map/ppermute | solution.py:38
  73.4 20.2 %collective-permute-start.16 = (bf16[4,96,1024]{2,1,0:T(8,128)(2,1)S(1)}, bf16[4,96,1024]{2,1,0:T(8,128)(2,1)S(1)}, u32[]{:S(2)}, u32[]{:S(2)}) collective-permute-start(bf16[4,96,1024]{2,1,0:T(8,128)(2,1)S(1)} %pad_maximum_fusion.3), channel_id=1, source_target_pairs={{0,4},{1,3},{2,6},{3,1},{4,0},{5,7},{6,2},{7,5},{8,12},{9,11},{10,... | collective-permute-start | bytes 2359304 | tf_op jit(solution)/shard_map/ppermute | solution.py:38
  75.4 20.9 %collective-permute-start.12 = (bf16[8,64,768]{2,1,0:T(8,128)(2,1)S(1)}, bf16[8,64,768]{2,1,0:T(8,128)(2,1)S(1)}, u32[]{:S(2)}, u32[]{:S(2)}) collective-permute-start(bf16[8,64,768]{2,1,0:T(8,128)(2,1)S(1)} %pad_maximum_fusion.2.q0), channel_id=1, source_target_pairs={{0,1},{1,0},{2,3},{3,2},{4,5},{5,4},{6,7},{7,6},{8,9},{9,8},{10,11... | collective-permute-start | bytes 2359304 | tf_op jit(solution)/shard_map/ppermute | solution.py:38
  83.2 11.7 %copy-start.13 = (bf16[1024,512]{1,0:T(8,128)(2,1)}, bf16[1024,512]{1,0:T(8,128)(2,1)S(1)}, u32[]{:S(2)}) copy-start(bf16[1024,512]{1,0:T(8,128)(2,1)S(1)} %get-tuple-element.297.left_ref) | copy-start | bytes 3145732
  83.2 11.7 %copy-start.15 = (bf16[1024,512]{1,0:T(8,128)(2,1)}, bf16[1024,512]{1,0:T(8,128)(2,1)S(1)}, u32[]{:S(2)}) copy-start(bf16[1024,512]{1,0:T(8,128)(2,1)S(1)} %get-tuple-element.276.prior_ref) | copy-start | bytes 3145732
  93.5 3.7 %collective-permute-start.17 = (bf16[8,64,768]{2,1,0:T(8,128)(2,1)S(1)}, bf16[8,64,768]{2,1,0:T(8,128)(2,1)}, u32[]{:S(2)}, u32[]{:S(2)}) collective-permute-start(bf16[8,64,768]{2,1,0:T(8,128)(2,1)S(1)} %collective-permute-done.13.q1), channel_id=1, source_target_pairs={{0,1},{1,0},{2,3},{3,2},{4,5},{5,4},{6,7},{7,6},{8,9},{9,8},{10,11... | collective-permute-start | bytes 2359304 | tf_op jit(solution)/shard_map/ppermute | solution.py:38
  94.9 34.1 %collective-permute-start.18 = (bf16[8,96,1024]{2,1,0:T(8,128)(2,1)}, bf16[8,96,1024]{2,1,0:T(8,128)(2,1)}, u32[]{:S(2)}, u32[]{:S(2)}) collective-permute-start(bf16[8,96,1024]{2,1,0:T(8,128)(2,1)} %pad_maximum_fusion.p0), channel_id=1, source_target_pairs={{0,2},{1,5},{2,0},{3,7},{4,6},{5,1},{6,4},{7,3},{8,10},{9,13},{10,... | collective-permute-start | bytes 4718600 | tf_op jit(solution)/shard_map/ppermute | solution.py:38
  96.3 32.7 %collective-permute-start.19 = (bf16[8,96,1024]{2,1,0:T(8,128)(2,1)}, bf16[8,96,1024]{2,1,0:T(8,128)(2,1)}, u32[]{:S(2)}, u32[]{:S(2)}) collective-permute-start(bf16[8,96,1024]{2,1,0:T(8,128)(2,1)} %pad_maximum_fusion.p0), channel_id=1, source_target_pairs={{0,1},{1,0},{2,3},{3,2},{4,5},{5,4},{6,7},{7,6},{8,9},{9,8},{10,11... | collective-permute-start | bytes 4718600 | tf_op jit(solution)/shard_map/ppermute | solution.py:38
  128.4 8.3 %collective-permute-start.21 = (bf16[16,96,1024]{2,1,0:T(8,128)(2,1)}, bf16[16,96,1024]{2,1,0:T(8,128)(2,1)S(1)}, u32[]{:S(2)}, u32[]{:S(2)}) collective-permute-start(bf16[16,96,1024]{2,1,0:T(8,128)(2,1)} %get-tuple-element.241), channel_id=1, source_target_pairs={{0,1},{1,0},{2,3},{3,2},{4,5},{5,4},{6,7},{7,6},{8,9},{9,8},{10,11... | collective-permute-start | bytes 9437192 | tf_op jit(solution)/shard_map/ppermute | solution.py:38
  129.0 7.7 %collective-permute-start.20 = (bf16[8,96,1024]{2,1,0:T(8,128)(2,1)}, bf16[8,96,1024]{2,1,0:T(8,128)(2,1)}, u32[]{:S(2)}, u32[]{:S(2)}) collective-permute-start(bf16[8,96,1024]{2,1,0:T(8,128)(2,1)} %collective-permute-done.18.p1), channel_id=1, source_target_pairs={{0,1},{1,0},{2,3},{3,2},{4,5},{5,4},{6,7},{7,6},{8,9},{9,8},{10,11... | collective-permute-start | bytes 4718600 | tf_op jit(solution)/shard_map/ppermute | solution.py:38
  141.8 31.8 %collective-permute-start.22 = (bf16[8,96,1024]{2,1,0:T(8,128)(2,1)}, bf16[8,96,1024]{2,1,0:T(8,128)(2,1)}, u32[]{:S(2)}, u32[]{:S(2)}) collective-permute-start(bf16[8,96,1024]{2,1,0:T(8,128)(2,1)} %get-tuple-element.245), channel_id=1, source_target_pairs={{0,2},{1,5},{2,0},{3,7},{4,6},{5,1},{6,4},{7,3},{8,10},{9,13},{10,... | collective-permute-start | bytes 4718600 | tf_op jit(solution)/shard_map/ppermute | solution.py:38
  173.6 14.4 %collective-permute-start.24 = (bf16[16,128,768]{2,1,0:T(8,128)(2,1)}, bf16[16,128,768]{2,1,0:T(8,128)(2,1)S(1)}, u32[]{:S(2)}, u32[]{:S(2)}) collective-permute-start(bf16[16,128,768]{2,1,0:T(8,128)(2,1)} %get-tuple-element.259), channel_id=1, source_target_pairs={{0,1},{1,0},{2,3},{3,2},{4,5},{5,4},{6,7},{7,6},{8,9},{9,8},{10,11... | collective-permute-start | bytes 9437192 | tf_op jit(solution)/shard_map/ppermute | solution.py:38
  173.7 14.3 %collective-permute-start.25 = (bf16[16,64,768]{2,1,0:T(8,128)(2,1)}, bf16[16,64,768]{2,1,0:T(8,128)(2,1)S(1)}, u32[]{:S(2)}, u32[]{:S(2)}) collective-permute-start(bf16[16,64,768]{2,1,0:T(8,128)(2,1)} %get-tuple-element.260), channel_id=1, source_target_pairs={{0,1},{1,0},{2,3},{3,2},{4,5},{5,4},{6,7},{7,6},{8,9},{9,8},{10,11... | collective-permute-start | bytes 4718600 | tf_op jit(solution)/shard_map/ppermute | solution.py:38
  175.9 12.1 %collective-permute-start.23 = (bf16[4,96,1024]{2,1,0:T(8,128)(2,1)S(1)}, bf16[4,96,1024]{2,1,0:T(8,128)(2,1)S(1)}, u32[]{:S(2)}, u32[]{:S(2)}) collective-permute-start(bf16[4,96,1024]{2,1,0:T(8,128)(2,1)S(1)} %add_convert_fusion.11), channel_id=1, source_target_pairs={{0,4},{1,3},{2,6},{3,1},{4,0},{5,7},{6,2},{7,5},{8,12},{9,11},{10,... | collective-permute-start | bytes 2359304 | tf_op jit(solution)/shard_map/ppermute | solution.py:38
  179.0 9.0 %copy-start.31 = (bf16[16,128,768]{2,1,0:T(8,128)(2,1)S(1)}, bf16[16,128,768]{2,1,0:T(8,128)(2,1)}, u32[]{:S(2)}) copy-start(bf16[16,128,768]{2,1,0:T(8,128)(2,1)} %get-tuple-element.255) | copy-start | bytes 9437188
  188.0 3.1 %collective-permute-start.26 = (f32[1,2,512]{2,1,0:T(2,128)S(1)}, f32[1,2,512]{2,1,0:T(2,128)S(1)}, u32[]{:S(2)}, u32[]{:S(2)}) collective-permute-start(f32[1,2,512]{2,1,0:T(2,128)S(1)} %bitcast.64), channel_id=1, source_target_pairs={{0,1},{1,0},{2,3},{3,2},{4,5},{5,4},{6,7},{7,6},{8,9},{9,8},{10,11... | collective-permute-start | bytes 12296 | tf_op jit(solution)/shard_map/ppermute | solution.py:38
  191.1 3.7 %collective-permute-start.27 = (f32[2,2,512]{2,1,0:T(2,128)S(1)}, f32[2,2,512]{2,1,0:T(2,128)S(1)}, u32[]{:S(2)}, u32[]{:S(2)}) collective-permute-start(f32[2,2,512]{2,1,0:T(2,128)S(1)} %pad_maximum_fusion.13), channel_id=1, source_target_pairs={{0,2},{1,3},{2,0},{3,1},{4,6},{5,7},{6,4},{7,5},{8,10},{9,11},{10,... | collective-permute-start | bytes 24584 | tf_op jit(solution)/shard_map/ppermute | solution.py:38
  194.9 21.3 %collective-permute-start.28 = (bf16[8,128,768]{2,1,0:T(8,128)(2,1)S(1)}, bf16[8,128,768]{2,1,0:T(8,128)(2,1)S(1)}, u32[]{:S(2)}, u32[]{:S(2)}) collective-permute-start(bf16[8,128,768]{2,1,0:T(8,128)(2,1)S(1)} %get-tuple-element.268), channel_id=1, source_target_pairs={{0,2},{1,5},{2,0},{3,7},{4,6},{5,1},{6,4},{7,3},{8,10},{9,13},{10,... | collective-permute-start | bytes 4718600 | tf_op jit(solution)/shard_map/ppermute | solution.py:38
  196.2 20.0 %collective-permute-start.29 = (bf16[2,96,1024]{2,1,0:T(8,128)(2,1)S(1)}, bf16[2,96,1024]{2,1,0:T(8,128)(2,1)S(1)}, u32[]{:S(2)}, u32[]{:S(2)}) collective-permute-start(bf16[2,96,1024]{2,1,0:T(8,128)(2,1)S(1)} %slice.256), channel_id=1, source_target_pairs={{0,8},{1,9},{2,10},{3,11},{4,12},{5,13},{6,14},{7,15},{8,0},{9,1},... | collective-permute-start | bytes 1179656 | tf_op jit(solution)/shard_map/ppermute | solution.py:38
  220.5 17.7 %collective-permute-start.32 = (bf16[96,1024]{1,0:T(8,128)(2,1)S(1)}, bf16[96,1024]{1,0:T(8,128)(2,1)S(1)}, u32[]{:S(2)}, u32[]{:S(2)}) collective-permute-start(bf16[96,1024]{1,0:T(8,128)(2,1)S(1)} %fusion), channel_id=1, source_target_pairs={{0,16},{1,17},{2,18},{3,19},{4,20},{5,21},{6,22},{7,23},{8,24},{9,... | collective-permute-start | bytes 589832 | tf_op jit(solution)/shard_map/ppermute | solution.py:38
  222.9 18.2 %collective-permute-start.31 = (bf16[8,64,768]{2,1,0:T(8,128)(2,1)S(1)}, bf16[8,64,768]{2,1,0:T(8,128)(2,1)S(1)}, u32[]{:S(2)}, u32[]{:S(2)}) collective-permute-start(bf16[8,64,768]{2,1,0:T(8,128)(2,1)S(1)} %get-tuple-element.289), channel_id=1, source_target_pairs={{0,2},{1,5},{2,0},{3,7},{4,6},{5,1},{6,4},{7,3},{8,10},{9,13},{10,... | collective-permute-start | bytes 2359304 | tf_op jit(solution)/shard_map/ppermute | solution.py:38
  223.7 17.4 %collective-permute-start.30 = (bf16[4,128,768]{2,1,0:T(8,128)(2,1)S(1)}, bf16[4,128,768]{2,1,0:T(8,128)(2,1)S(1)}, u32[]{:S(2)}, u32[]{:S(2)}) collective-permute-start(bf16[4,128,768]{2,1,0:T(8,128)(2,1)S(1)} %add_convert_fusion.8), channel_id=1, source_target_pairs={{0,4},{1,3},{2,6},{3,1},{4,0},{5,7},{6,2},{7,5},{8,12},{9,11},{10,... | collective-permute-start | bytes 2359304 | tf_op jit(solution)/shard_map/ppermute | solution.py:38
  225.3 15.8 %collective-permute-start.33 = (bf16[16,56,512]{2,1,0:T(8,128)(2,1)S(1)}, bf16[16,56,512]{2,1,0:T(8,128)(2,1)S(1)}, u32[]{:S(2)}, u32[]{:S(2)}) collective-permute-start(bf16[16,56,512]{2,1,0:T(8,128)(2,1)S(1)} %pad_maximum_fusion.1), channel_id=1, source_target_pairs={{0,1},{1,0},{2,3},{3,2},{4,5},{5,4},{6,7},{7,6},{8,9},{9,8},{10,11... | collective-permute-start | bytes 2752520 | tf_op jit(solution)/shard_map/ppermute | solution.py:38
  241.8 11.4 %collective-permute-start.35 = (bf16[4,64,768]{2,1,0:T(8,128)(2,1)S(1)}, bf16[4,64,768]{2,1,0:T(8,128)(2,1)S(1)}, u32[]{:S(2)}, u32[]{:S(2)}) collective-permute-start(bf16[4,64,768]{2,1,0:T(8,128)(2,1)S(1)} %add_convert_fusion.14), channel_id=1, source_target_pairs={{0,4},{1,3},{2,6},{3,1},{4,0},{5,7},{6,2},{7,5},{8,12},{9,11},{10,... | collective-permute-start | bytes 1179656 | tf_op jit(solution)/shard_map/ppermute | solution.py:38
  243.4 9.8 %collective-permute-start.34 = (bf16[2,128,768]{2,1,0:T(8,128)(2,1)S(1)}, bf16[2,128,768]{2,1,0:T(8,128)(2,1)S(1)}, u32[]{:S(2)}, u32[]{:S(2)}) collective-permute-start(bf16[2,128,768]{2,1,0:T(8,128)(2,1)S(1)} %slice.260), channel_id=1, source_target_pairs={{0,8},{1,9},{2,10},{3,11},{4,12},{5,13},{6,14},{7,15},{8,0},{9,1},... | collective-permute-start | bytes 1179656 | tf_op jit(solution)/shard_map/ppermute | solution.py:38
  244.0 9.3 %collective-permute-start.36 = (bf16[8,56,512]{2,1,0:T(8,128)(2,1)S(1)}, bf16[8,56,512]{2,1,0:T(8,128)(2,1)S(1)}, u32[]{:S(2)}, u32[]{:S(2)}) collective-permute-start(bf16[8,56,512]{2,1,0:T(8,128)(2,1)S(1)} %pad_maximum_fusion.4), channel_id=1, source_target_pairs={{0,2},{1,5},{2,0},{3,7},{4,6},{5,1},{6,4},{7,3},{8,10},{9,13},{10,... | collective-permute-start | bytes 1376264 | tf_op jit(solution)/shard_map/ppermute | solution.py:38
  253.5 13.7 %collective-permute-start.39 = (bf16[4,56,512]{2,1,0:T(8,128)(2,1)S(1)}, bf16[4,56,512]{2,1,0:T(8,128)(2,1)S(1)}, u32[]{:S(2)}, u32[]{:S(2)}) collective-permute-start(bf16[4,56,512]{2,1,0:T(8,128)(2,1)S(1)} %add_convert_fusion.19), channel_id=1, source_target_pairs={{0,4},{1,3},{2,6},{3,1},{4,0},{5,7},{6,2},{7,5},{8,12},{9,11},{10,... | collective-permute-start | bytes 688136 | tf_op jit(solution)/shard_map/ppermute | solution.py:38
  254.4 8.1 %collective-permute-start.38 = (bf16[2,64,768]{2,1,0:T(8,128)(2,1)S(1)}, bf16[2,64,768]{2,1,0:T(8,128)(2,1)S(1)}, u32[]{:S(2)}, u32[]{:S(2)}) collective-permute-start(bf16[2,64,768]{2,1,0:T(8,128)(2,1)S(1)} %slice.264), channel_id=1, source_target_pairs={{0,8},{1,9},{2,10},{3,11},{4,12},{5,13},{6,14},{7,15},{8,0},{9,1},... | collective-permute-start | bytes 589832 | tf_op jit(solution)/shard_map/ppermute | solution.py:38
  256.0 11.2 %collective-permute-start.37 = (bf16[128,768]{1,0:T(8,128)(2,1)S(1)}, bf16[128,768]{1,0:T(8,128)(2,1)S(1)}, u32[]{:S(2)}, u32[]{:S(2)}) collective-permute-start(bf16[128,768]{1,0:T(8,128)(2,1)S(1)} %fusion.1), channel_id=1, source_target_pairs={{0,16},{1,17},{2,18},{3,19},{4,20},{5,21},{6,22},{7,23},{8,24},{9,... | collective-permute-start | bytes 589832 | tf_op jit(solution)/shard_map/ppermute | solution.py:38
  267.4 6.2 %collective-permute-start.43 = (bf16[56,512]{1,0:T(8,128)(2,1)S(1)}, bf16[56,512]{1,0:T(8,128)(2,1)S(1)}, u32[]{:S(2)}, u32[]{:S(2)}) collective-permute-start(bf16[56,512]{1,0:T(8,128)(2,1)S(1)} %get-tuple-element.355), channel_id=1, source_target_pairs={{0,24},{1,25},{2,26},{3,27},{4,28},{5,29},{6,30},{7,31},{8,16},{9,... | collective-permute-start | bytes 172040 | tf_op jit(solution)/shard_map/ppermute | solution.py:38
  267.5 6.2 %collective-permute-start.42 = (bf16[56,512]{1,0:T(8,128)(2,1)S(1)}, bf16[56,512]{1,0:T(8,128)(2,1)S(1)}, u32[]{:S(2)}, u32[]{:S(2)}) collective-permute-start(bf16[56,512]{1,0:T(8,128)(2,1)S(1)} %get-tuple-element.356), channel_id=1, source_target_pairs={{0,8},{1,9},{2,10},{3,11},{4,12},{5,13},{6,14},{7,15},{8,0},{9,1},... | collective-permute-start | bytes 172040 | tf_op jit(solution)/shard_map/ppermute | solution.py:38
  268.3 9.1 %collective-permute-start.41 = (bf16[56,512]{1,0:T(8,128)(2,1)S(1)}, bf16[56,512]{1,0:T(8,128)(2,1)S(1)}, u32[]{:S(2)}, u32[]{:S(2)}) collective-permute-start(bf16[56,512]{1,0:T(8,128)(2,1)S(1)} %get-tuple-element.357), channel_id=1, source_target_pairs={{0,16},{1,17},{2,18},{3,19},{4,20},{5,21},{6,22},{7,23},{8,24},{9,... | collective-permute-start | bytes 172040 | tf_op jit(solution)/shard_map/ppermute | solution.py:38
  271.8 7.1 %collective-permute-start.40 = (bf16[64,768]{1,0:T(8,128)(2,1)S(1)}, bf16[64,768]{1,0:T(8,128)(2,1)S(1)}, u32[]{:S(2)}, u32[]{:S(2)}) collective-permute-start(bf16[64,768]{1,0:T(8,128)(2,1)S(1)} %fusion.2), channel_id=1, source_target_pairs={{0,16},{1,17},{2,18},{3,19},{4,20},{5,21},{6,22},{7,23},{8,24},{9,... | collective-permute-start | bytes 294920 | tf_op jit(solution)/shard_map/ppermute | solution.py:38
  (31 other events, 95.5 us)
Sparse Core Ops, SparseCore 0:
  10.9 78.1 all-gather.1
